TPU v7x, 32 devices: a whole 2x2x4 slice. The times are simulated.
32 devices in a mesh: dp: 8 (over z, x), tensor: 4 (over y, core).
Axes of the slice: x: 2, y: 2, z: 4, core: 2. Of those that a mesh axis runs over, the one named last changes fastest.
Arguments:
- layer_input: bfloat16 [8192, 512], P(('dp', 'tensor')), may hold values from -6 to 6
- segments: int32 [8, 1024], P('dp'), may hold values from 0 to 3, never falling along the last dimension, each value on 1 to 800 neighbouring positions
- norm1_gain: bfloat16 [512], replicated, may hold values from 0.5 to 1.5
- norm1_bias: bfloat16 [512], replicated, may hold values from -4 to 4
- w_query: bfloat16 [512, 512], P(None, 'tensor'), may hold values from -0.25 to 0.25
- b_query: bfloat16 [512], P('tensor'), may hold values from -6 to 6
- w_key: bfloat16 [512, 512], P(None, 'tensor'), may hold values from -0.25 to 0.25
- w_value: bfloat16 [512, 512], P(None, 'tensor'), may hold values from -0.25 to 0.25
- b_value: bfloat16 [512], P('tensor'), may hold values from -6 to 6
- w_out: bfloat16 [512, 512], P('tensor'), may hold values from -2 to 2
- b_out: bfloat16 [512], replicated, may hold values from -4 to 4
- gate1_w: bfloat16 [512, 512], P('tensor'), may hold values from -0.25 to 0.25
- gate1_b: bfloat16 [512], replicated, may hold values from -6 to 6
- norm2_gain: bfloat16 [512], replicated, may hold values from 0.5 to 1.5
- norm2_bias: bfloat16 [512], replicated, may hold values from -4 to 4
- w_in: bfloat16 [512, 2048], P(None, 'tensor'), may hold values from -0.25 to 0.25
- b_in: bfloat16 [2048], P('tensor'), may hold values from -6 to 6
- w_back: bfloat16 [2048, 512], P('tensor'), may hold values from -0.1875 to 0.1875
- b_back: bfloat16 [512], replicated, may hold values from -4 to 4
- gate2_w: bfloat16 [512, 512], P('tensor'), may hold values from -0.25 to 0.25
- gate2_b: bfloat16 [512], replicated, may hold values from -6 to 6
- cotangent: bfloat16 [8192, 512], P(('dp', 'tensor')), may hold values from -6 to 6
Outputs:
- output: bfloat16 [8192, 512], P(('dp', 'tensor'))
- input_grad: float32 [8192, 512], P(('dp', 'tensor'))
- grad_norm1_gain: float32 [512], replicated
- grad_norm1_bias: float32 [512], replicated
- grad_w_query: float32 [512, 512], P(None, 'tensor')
- grad_b_query: float32 [512], P('tensor')
- grad_w_key: float32 [512, 512], P(None, 'tensor')
- grad_w_value: float32 [512, 512], P(None, 'tensor')
- grad_b_value: float32 [512], P('tensor')
- grad_w_out: float32 [512, 512], P('tensor')
- grad_b_out: float32 [512], replicated
- grad_gate1_w: float32 [512, 512], P('tensor')
- grad_gate1_b: float32 [512], replicated
- grad_norm2_gain: float32 [512], replicated
- grad_norm2_bias: float32 [512], replicated
- grad_w_in: float32 [512, 2048], P(None, 'tensor')
- grad_b_in: float32 [2048], P('tensor')
- grad_w_back: float32 [2048, 512], P('tensor')
- grad_b_back: float32 [512], replicated
- grad_gate2_w: float32 [512, 512], P('tensor')
- grad_gate2_b: float32 [512], replicated
Inputs may be any that keep to these rules, and one draw needn't show every extreme that they name: `segments`: document numbers never fall along a sequence; every sequence holds 4 documents, none longer than 800 tokens, and one document reaches that length.
All inputs are finite; a program needn't handle non-finite values.
Results may differ from a plain program's by a relative error of at most 0.014.
Values may be sent and summed in bfloat16 or wider, within the bound.
No kernel may reach another device: no remote copies, remote signals or barrier semaphores. Data moves between devices by JAX's collectives and lax.ppermute only.
A program may use at most 64 MiB of HBM per device.

v0:
```python
import jax
import jax.numpy as jnp
from jax import lax
from jax.sharding import PartitionSpec as P

HD = 64


EPSILON = 1e-05


def matmul(left, right):
    return jnp.dot(left, right, preferred_element_type=jnp.float32)


def inner_left(left, right):
    return lax.dot_general(
        left, right, (((0,), (0,)), ((), ())), preferred_element_type=jnp.float32
    )


def outer_right(left, right):
    return lax.dot_general(
        left, right, (((1,), (1,)), ((), ())), preferred_element_type=jnp.float32
    )


def column_sum(matrix):
    return jnp.sum(matrix, axis=0, dtype=jnp.float32)


def place_columns(full, piece, start):
    current = lax.dynamic_slice_in_dim(full, start, piece.shape[1], 1)
    return lax.dynamic_update_slice_in_dim(full, current + piece, start, 1)


def smooth_unit(values):
    return jax.nn.gelu(values, approximate=True)


def norm_forward(values, gain, shift):
    centred = values - jnp.mean(values, axis=-1, keepdims=True)
    spread = jnp.mean(centred * centred, axis=-1, keepdims=True)
    inverse = lax.rsqrt(spread + EPSILON)
    unit = centred * inverse
    return (unit * gain + shift, unit, inverse)


def norm_backward(share_grad, unit, inverse, gain):
    scaled = share_grad * gain
    grad_gain = jnp.sum(share_grad * unit, axis=0)
    grad_shift = jnp.sum(share_grad, axis=0)
    average = jnp.mean(scaled, axis=-1, keepdims=True)
    project = jnp.mean(scaled * unit, axis=-1, keepdims=True)
    return (inverse * (scaled - average - unit * project), grad_gain, grad_shift)


def head_major(matrix):
    return matrix.reshape(matrix.shape[0], -1, HD).transpose(1, 0, 2)


def row_major(heads_array):
    return heads_array.transpose(1, 0, 2).reshape(heads_array.shape[1], -1)


def split_blocks(heads_array, count, block):
    return heads_array.reshape(heads_array.shape[0], count, block, HD).transpose(1, 0, 2, 3)


def join_blocks(blocks):
    count, heads, block, width = blocks.shape
    return blocks.transpose(0, 2, 1, 3).reshape(count * block, heads * width)


def build_mask(segment_row):
    places = lax.iota(jnp.int32, segment_row.shape[0])
    same_doc = segment_row[:, None] == segment_row[None, :]
    return same_doc & (places[None, :] <= places[:, None])


def attention_forward(query, keys, values, allowed):
    rows = query.shape[0]
    block = min(512, rows)
    count = rows // block
    scale_factor = HD ** (-0.5)
    heads_k = head_major(keys)
    heads_v = head_major(values)
    query_blocks = split_blocks(head_major(query), count, block)
    mask_blocks = allowed.reshape(count, block, rows)

    def one_block(pieces):
        query_block, mask_block = pieces
        scores = (
            jnp.einsum("hqd,hkd->hqk", query_block, heads_k, preferred_element_type=jnp.float32)
            * scale_factor
        )
        scores = jnp.where(mask_block[None], scores, -1e30)
        totals = jax.nn.logsumexp(scores, axis=-1, keepdims=True)
        probs = jnp.exp(scores - totals).astype(jnp.bfloat16)
        mixed = jnp.einsum("hqk,hkd->hqd", probs, heads_v, preferred_element_type=jnp.float32)
        return (mixed, totals)

    mixed, totals = lax.map(one_block, (query_blocks, mask_blocks))
    return (join_blocks(mixed).astype(jnp.bfloat16), totals)


def attention_backward(query, keys, values, allowed, totals, attended_grad):
    rows = query.shape[0]
    block = min(512, rows)
    count = rows // block
    scale_factor = HD ** (-0.5)
    heads_k = head_major(keys)
    heads_v = head_major(values)
    query_blocks = split_blocks(head_major(query), count, block)
    grad_blocks = split_blocks(head_major(attended_grad), count, block)
    mask_blocks = allowed.reshape(count, block, rows)

    def one_block(carry, pieces):
        key_acc, value_acc = carry
        query_block, grad_block, mask_block, total_block = pieces
        scores = (
            jnp.einsum("hqd,hkd->hqk", query_block, heads_k, preferred_element_type=jnp.float32)
            * scale_factor
        )
        scores = jnp.where(mask_block[None], scores, -1e30)
        probs = jnp.exp(scores - total_block)
        prob_low = probs.astype(jnp.bfloat16)
        prob_grad = jnp.einsum(
            "hqd,hkd->hqk", grad_block, heads_v, preferred_element_type=jnp.float32
        )
        weighted = jnp.sum(probs * prob_grad, axis=-1, keepdims=True)
        score_grad = (probs * (prob_grad - weighted)).astype(jnp.bfloat16)
        query_part = (
            jnp.einsum("hqk,hkd->hqd", score_grad, heads_k, preferred_element_type=jnp.float32)
            * scale_factor
        )
        key_acc = (
            key_acc
            + jnp.einsum(
                "hqk,hqd->hkd", score_grad, query_block, preferred_element_type=jnp.float32
            )
            * scale_factor
        )
        value_acc = value_acc + jnp.einsum(
            "hqk,hqd->hkd", prob_low, grad_block, preferred_element_type=jnp.float32
        )
        return ((key_acc, value_acc), query_part.astype(jnp.bfloat16))

    empty = jnp.zeros(heads_k.shape, jnp.float32)
    (key_acc, value_acc), query_parts = lax.scan(
        one_block, (empty, empty), (query_blocks, grad_blocks, mask_blocks, totals)
    )
    return (
        join_blocks(query_parts),
        row_major(key_acc).astype(jnp.bfloat16),
        row_major(value_acc).astype(jnp.bfloat16),
    )


def forward_pass(layer_input, segments, weights):
    (
        norm1_gain,
        norm1_bias,
        w_query,
        b_query,
        w_key,
        w_value,
        b_value,
        w_out,
        b_out,
        gate1_w,
        gate1_b,
        norm2_gain,
        norm2_bias,
        w_in,
        b_in,
        w_back,
        b_back,
        gate2_w,
        gate2_b,
    ) = weights
    start_col = lax.axis_index("tensor") * gate1_w.shape[0]
    inputs = layer_input.astype(jnp.float32)
    normed_part, unit_one, inverse_one = norm_forward(
        inputs, norm1_gain.astype(jnp.float32), norm1_bias.astype(jnp.float32)
    )
    normed_low = normed_part.astype(jnp.bfloat16)
    normed = lax.all_gather(normed_low, "tensor", axis=0, tiled=True)
    query = (matmul(normed, w_query) + b_query.astype(jnp.float32)).astype(jnp.bfloat16)
    keys = matmul(normed, w_key).astype(jnp.bfloat16)
    values = (matmul(normed, w_value) + b_value.astype(jnp.float32)).astype(jnp.bfloat16)
    allowed = build_mask(segments[0])
    attended, totals = attention_forward(query, keys, values, allowed)
    gate_rows = lax.dynamic_slice_in_dim(normed, start_col, gate1_w.shape[0], 1)
    branch_part, logit_one = (
        lax.psum_scatter(matmul(attended, w_out), "tensor", scatter_dimension=0, tiled=True),
        lax.psum_scatter(matmul(gate_rows, gate1_w), "tensor", scatter_dimension=0, tiled=True),
    )
    branch = branch_part + b_out.astype(jnp.float32)
    gate_one = jax.nn.sigmoid(logit_one + gate1_b.astype(jnp.float32))
    middle = inputs + gate_one * branch
    normed_two_part, unit_two, inverse_two = norm_forward(
        middle, norm2_gain.astype(jnp.float32), norm2_bias.astype(jnp.float32)
    )
    normed_two = lax.all_gather(normed_two_part.astype(jnp.bfloat16), "tensor", axis=0, tiled=True)
    hidden_input = matmul(normed_two, w_in) + b_in.astype(jnp.float32)
    hidden = smooth_unit(hidden_input).astype(jnp.bfloat16)
    gate_rows_two = lax.dynamic_slice_in_dim(normed_two, start_col, gate2_w.shape[0], 1)
    ffn_part, logit_two = (
        lax.psum_scatter(matmul(hidden, w_back), "tensor", scatter_dimension=0, tiled=True),
        lax.psum_scatter(matmul(gate_rows_two, gate2_w), "tensor", scatter_dimension=0, tiled=True),
    )
    ffn_out = ffn_part + b_back.astype(jnp.float32)
    gate_two = jax.nn.sigmoid(logit_two + gate2_b.astype(jnp.float32))
    result = middle + gate_two * ffn_out
    saved = (
        normed,
        normed_low,
        query,
        keys,
        values,
        allowed,
        attended,
        totals,
        branch,
        gate_one,
        unit_one,
        inverse_one,
        normed_two,
        hidden,
        hidden_input,
        ffn_out,
        gate_two,
        unit_two,
        inverse_two,
    )
    return (result, saved)


def body(
    layer_input,
    segments,
    norm1_gain,
    norm1_bias,
    w_query,
    b_query,
    w_key,
    w_value,
    b_value,
    w_out,
    b_out,
    gate1_w,
    gate1_b,
    norm2_gain,
    norm2_bias,
    w_in,
    b_in,
    w_back,
    b_back,
    gate2_w,
    gate2_b,
    cotangent,
):
    weights = (
        norm1_gain,
        norm1_bias,
        w_query,
        b_query,
        w_key,
        w_value,
        b_value,
        w_out,
        b_out,
        gate1_w,
        gate1_b,
        norm2_gain,
        norm2_bias,
        w_in,
        b_in,
        w_back,
        b_back,
        gate2_w,
        gate2_b,
    )
    result, saved = forward_pass(layer_input, segments, weights)
    barrier = lax.optimization_barrier((layer_input, weights))
    unused, saved = forward_pass(barrier[0], segments, barrier[1])
    (
        normed,
        normed_low,
        query,
        keys,
        values,
        allowed,
        attended,
        totals,
        branch,
        gate_one,
        unit_one,
        inverse_one,
        normed_two,
        hidden,
        hidden_input,
        ffn_out,
        gate_two,
        unit_two,
        inverse_two,
    ) = saved
    start_col = lax.axis_index("tensor") * gate1_w.shape[0]
    upstream = cotangent.astype(jnp.float32)
    ffn_grad = (gate_two * upstream).astype(jnp.bfloat16)
    logit_two_grad = (upstream * ffn_out * (gate_two * (1.0 - gate_two))).astype(jnp.bfloat16)
    ffn_grad_all, logit_two_all = (
        lax.all_gather(ffn_grad, "tensor", axis=0, tiled=True),
        lax.all_gather(logit_two_grad, "tensor", axis=0, tiled=True),
    )
    grad_b_back = column_sum(ffn_grad_all)
    grad_gate2_b = column_sum(logit_two_all)
    grad_w_back = inner_left(hidden, ffn_grad_all)
    unused_value, smooth_pull = jax.vjp(smooth_unit, hidden_input)
    hidden_grad = smooth_pull(outer_right(ffn_grad_all, w_back))[0].astype(jnp.bfloat16)
    grad_w_in = inner_left(normed_two, hidden_grad)
    grad_b_in = column_sum(hidden_grad)
    rows_two = lax.dynamic_slice_in_dim(normed_two, start_col, gate2_w.shape[0], 1)
    grad_gate2_w = inner_left(rows_two, logit_two_all)
    normed_two_grad = place_columns(
        outer_right(hidden_grad, w_in), outer_right(logit_two_all, gate2_w), start_col
    )
    normed_two_share = lax.psum_scatter(normed_two_grad, "tensor", scatter_dimension=0, tiled=True)
    middle_back, grad_norm2_gain, grad_norm2_bias = norm_backward(
        normed_two_share, unit_two, inverse_two, norm2_gain.astype(jnp.float32)
    )
    middle_grad = upstream + middle_back
    ffn_grads = (grad_w_in, grad_b_in, grad_w_back, grad_b_back, grad_gate2_w, grad_gate2_b)
    branch_grad = (gate_one * middle_grad).astype(jnp.bfloat16)
    logit_one_grad = (middle_grad * branch * (gate_one * (1.0 - gate_one))).astype(jnp.bfloat16)
    grad_b_out = column_sum(branch_grad)
    grad_gate1_b = column_sum(logit_one_grad)
    branch_all, logit_one_all = (
        lax.all_gather(branch_grad, "tensor", axis=0, tiled=True),
        lax.all_gather(logit_one_grad, "tensor", axis=0, tiled=True),
    )
    grad_w_out = inner_left(attended, branch_all)
    attended_grad = outer_right(branch_all, w_out).astype(jnp.bfloat16)
    rows_one = lax.dynamic_slice_in_dim(normed, start_col, gate1_w.shape[0], 1)
    grad_gate1_w = inner_left(rows_one, logit_one_all)
    query_grad, keys_grad, values_grad = attention_backward(
        query, keys, values, allowed, totals, attended_grad
    )
    grad_w_query = inner_left(normed, query_grad)
    grad_b_query = column_sum(query_grad)
    grad_w_key = inner_left(normed, keys_grad)
    grad_w_value = inner_left(normed, values_grad)
    grad_b_value = column_sum(values_grad)
    normed_grad = (
        outer_right(query_grad, w_query)
        + outer_right(keys_grad, w_key)
        + outer_right(values_grad, w_value)
    )
    normed_grad = place_columns(normed_grad, outer_right(logit_one_all, gate1_w), start_col)
    normed_share = lax.psum_scatter(
        normed_grad.astype(jnp.bfloat16), "tensor", scatter_dimension=0, tiled=True
    ).astype(jnp.float32)
    input_back, grad_norm1_gain, grad_norm1_bias = norm_backward(
        normed_share, unit_one, inverse_one, norm1_gain.astype(jnp.float32)
    )
    input_grad = middle_grad + input_back
    norm_sums = lax.psum(
        (
            grad_norm1_gain,
            grad_norm1_bias,
            grad_norm2_gain,
            grad_norm2_bias,
            grad_b_out,
            grad_gate1_b,
        ),
        ("dp", "tensor"),
    )
    attention_grads = (
        grad_w_query,
        grad_b_query,
        grad_w_key,
        grad_w_value,
        grad_b_value,
        grad_w_out,
        grad_gate1_w,
    )
    every_grad = lax.psum(
        (
            grad_w_query,
            grad_b_query,
            grad_w_key,
            grad_w_value,
            grad_b_value,
            grad_w_out,
            grad_gate1_w,
            grad_w_in,
            grad_b_in,
            grad_w_back,
            grad_b_back,
            grad_gate2_w,
            grad_gate2_b,
        ),
        "dp",
    )
    attention_grads = every_grad[0:7]
    ffn_grads = every_grad[7:13]
    return (
        result.astype(jnp.bfloat16),
        input_grad,
        norm_sums[0],
        norm_sums[1],
        attention_grads[0],
        attention_grads[1],
        attention_grads[2],
        attention_grads[3],
        attention_grads[4],
        attention_grads[5],
        norm_sums[4],
        attention_grads[6],
        norm_sums[5],
        norm_sums[2],
        norm_sums[3],
        ffn_grads[0],
        ffn_grads[1],
        ffn_grads[2],
        ffn_grads[3],
        ffn_grads[4],
        ffn_grads[5],
    )


def solution(mesh):
    placed = (
        P(("dp", "tensor"), None),
        P("dp", None),
        P(),
        P(),
        P(None, "tensor"),
        P("tensor"),
        P(None, "tensor"),
        P(None, "tensor"),
        P("tensor"),
        P("tensor", None),
        P(),
        P("tensor", None),
        P(),
        P(),
        P(),
        P(None, "tensor"),
        P("tensor"),
        P("tensor", None),
        P(),
        P("tensor", None),
        P(),
        P(("dp", "tensor"), None),
    )
    return jax.shard_map(
        body,
        mesh=mesh,
        in_specs=placed,
        out_specs=(
            P(("dp", "tensor"), None),
            P(("dp", "tensor"), None),
            P(),
            P(),
            P(None, "tensor"),
            P("tensor"),
            P(None, "tensor"),
            P(None, "tensor"),
            P("tensor"),
            P("tensor", None),
            P(),
            P("tensor", None),
            P(),
            P(),
            P(),
            P(None, "tensor"),
            P("tensor"),
            P("tensor", None),
            P(),
            P("tensor", None),
            P(),
        ),
        check_vma=False,
    )
```

profile of v0, /device:TPU:0, one launch (start us, length us, event | category | flops | bytes accessed | tf_op | source)
XLA Modules:
  0.0 718.7 jit_solution(1008536278620861501)
XLA Ops:
  11.0 1.9 fusion.90
  16.1 1.9 fusion.52
  18.0 14.4 %all-gather.13.cloned.1.call-done = bf16[1024,512]{1,0:T(8,128)(2,1)} async-done(((bf16[256,512]{1,0:T(8,128)(2,1)}), bf16[1024,512]{1,0:T(8,128)(2,1)}) %all-gather.13.cloned.1.call-update) | async-done | bytes 1048592 | tf_op jit(solution)/shard_map/all_gather | solution.py:188
  32.5 1.8 fusion.73
  36.2 8.7 %while.38 = (s32[]{:T(128)}, bf16[2,2,512,64]{2,3,1,0:T(8,128)(2,1)}, f32[2,2,512,1]{2,1,3,0:T(2,128)S(1)}, pred[2,512,1024]{2,1,0:T(8,128)(4,1)S(1)}, bf16[2,2,...) while((s32[]{:T(128)}, ...), condition=%wide.region_18.19_spmd, body=%wide.region_15.18_spmd.sunk | while | flops 279977984 | bytes 18268324 | solution.py:103
  46.9 1.8 fusion.133
  48.9 2.7 fusion.116
  54.8 25.5 %reduce-scatter.21.cloned.1.call-done = f32[256,512]{1,0:T(8,128)} async-done(((f32[1024,512]{1,0:T(8,128)}), f32[256,512]{1,0:T(8,128)}) %reduce-scatter.21.cloned.1.call-update) | async-done | bytes 524304 | tf_op jit(solution)/shard_map/reduce_scatter | solution.py:196
  80.3 34.1 %reduce-scatter.19.cloned.1.call-done = f32[256,512]{1,0:T(8,128)} async-done(((f32[1024,512]{1,0:T(8,128)}), f32[256,512]{1,0:T(8,128)}) %reduce-scatter.19.cloned.1.call-update) | async-done | bytes 524304 | tf_op jit(solution)/shard_map/reduce_scatter | solution.py:197
  118.3 16.8 %all-gather.15.cloned.1.call-done = bf16[1024,512]{1,0:T(8,128)(2,1)} async-done(((bf16[256,512]{1,0:T(8,128)(2,1)}), bf16[1024,512]{1,0:T(8,128)(2,1)}) %all-gather.15.cloned.1.call-update) | async-done | bytes 1048592 | tf_op jit(solution)/shard_map/all_gather | solution.py:205
  135.1 2.7 fusion.112
  138.6 30.8 %reduce-scatter.23.cloned.1.call-done = f32[256,512]{1,0:T(8,128)} async-done(((f32[1024,512]{1,0:T(8,128)}), f32[256,512]{1,0:T(8,128)}) %reduce-scatter.23.cloned.1.call-update) | async-done | bytes 524304 | tf_op jit(solution)/shard_map/reduce_scatter | solution.py:211
  169.5 2.0 fusion.100
  172.8 3.4 fusion.134
  176.2 12.2 %all-gather.17.cloned.1.call-done = bf16[1024,512]{1,0:T(8,128)(2,1)} async-done(((bf16[256,512]{1,0:T(8,128)(2,1)}), bf16[1024,512]{1,0:T(8,128)(2,1)}) %all-gather.17.cloned.1.call-update) | async-done | bytes 1048592 | tf_op jit(solution)/shard_map/all_gather | solution.py:314
  188.4 5.5 convert_reduce_fusion.2
  194.8 2.0 fusion.136
  198.2 30.3 %reduce-scatter.25.cloned.1.call-done = f32[256,512]{1,0:T(8,128)} async-done(((f32[1024,512]{1,0:T(8,128)}), f32[256,512]{1,0:T(8,128)}) %reduce-scatter.25.cloned.1.call-update) | async-done | bytes 524304 | tf_op jit(solution)/shard_map/reduce_scatter | solution.py:210
  228.5 2.2 fusion.102
  230.9 3.4 fusion.135
  234.4 13.2 %all-gather.19.cloned.1.call-done = bf16[1024,512]{1,0:T(8,128)(2,1)} async-done(((bf16[256,512]{1,0:T(8,128)(2,1)}), bf16[1024,512]{1,0:T(8,128)(2,1)}) %all-gather.19.cloned.1.call-update) | async-done | bytes 1048592 | tf_op jit(solution)/shard_map/all_gather | solution.py:315
  247.6 2.7 fusion.69
  251.1 30.8 %reduce-scatter.27.cloned.1.call-done = f32[256,512]{1,0:T(8,128)} async-done(((f32[1024,512]{1,0:T(8,128)}), f32[256,512]{1,0:T(8,128)}) %reduce-scatter.27.cloned.1.call-update) | async-done | bytes 524304 | tf_op jit(solution)/shard_map/reduce_scatter | solution.py:329
  281.9 2.1 multiply_reduce_fusion.1
  284.1 3.3 convert_reduce_fusion.6
  289.6 16.1 %all-gather.21.cloned.1.call-done = bf16[1024,512]{1,0:T(8,128)(2,1)} async-done(((bf16[256,512]{1,0:T(8,128)(2,1)}), bf16[1024,512]{1,0:T(8,128)(2,1)}) %all-gather.21.cloned.1.call-update) | async-done | bytes 1048592 | tf_op jit(solution)/shard_map/all_gather | solution.py:340
  305.7 2.4 convolution_convert_fusion
  308.1 1.9 reshape.269
  310.0 1.7 copy.48
  311.7 16.5 %while.39 = (s32[]{:T(128)}, f32[2,1024,64]{1,2,0:T(8,128)}, f32[2,1024,64]{1,2,0:T(8,128)}, bf16[2,2,512,64]{2,3,1,0:T(8,128)(2,1)}, pred[2,512,1024]{2,1,0:T(8...) while((s32[]{:T(128)}, f32[2,1024,64]{1,2,0:T(8,128)}, ...), condition=%wide.region_29.30_spmd.clone, body=%wide.region_27.29_spmd.clone.sunk | while | flops 687602688 | bytes 50229632 | solution.py:150
  314.3 1.8 multiply_reduce_fusion.7
  322.5 1.8 multiply_reduce_fusion.7
  332.4 1.8 add_add_fusion
  334.2 2.7 fusion.68
  336.9 2.7 convert_element_type.273
  343.1 21.6 %reduce-scatter.29.cloned.1.call-done = bf16[256,512]{1,0:T(8,128)(2,1)} async-done(((bf16[1024,512]{1,0:T(8,128)(2,1)}), bf16[256,512]{1,0:T(8,128)(2,1)}) %reduce-scatter.29.cloned.1.call-update) | async-done | bytes 262160 | tf_op jit(solution)/shard_map/reduce_scatter | solution.py:361
  364.7 1.9 fusion.105
  366.6 2.4 fusion.93
  370.4 15.5 %all-gather.9.cloned.1.call-done = bf16[1024,512]{1,0:T(8,128)(2,1)} async-done(((bf16[256,512]{1,0:T(8,128)(2,1)}), bf16[1024,512]{1,0:T(8,128)(2,1)}) %all-gather.9.cloned.1.call-update) | async-done | bytes 1048592 | tf_op jit(solution)/shard_map/all_gather | solution.py:188
  385.9 2.4 fusion.71
  388.3 1.9 reshape.261
  390.2 1.7 copy.43
  391.9 2.7 fusion.108
  394.9 2.4 convolution_convert_fusion.2
  397.3 2.4 fusion.72
  400.4 10.8 %while.37 = (s32[]{:T(128)}, bf16[2,2,512,64]{2,3,1,0:T(8,128)(2,1)}, pred[2,512,1024]{2,1,0:T(8,128)(4,1)S(1)}, bf16[2,2,512,64]{2,3,1,0:T(8,128)(2,1)}, bf16[2...) while((s32[]{:T(128)}, bf16[2,2,512,64]{2,3,1,0:T(8,128)(2,1)}, ...), condition=%wide.region_6.7_spmd, body=%wide.region_3.0_spmd.sunk | while | flops 279973888 | bytes 19304628 | solution.py:103
  400.5 2.1 fusion.236
  405.9 2.1 fusion.236
  412.6 1.8 fusion.132
  414.5 11.7 %reduce-scatter.11.cloned.1.call-done = f32[256,512]{1,0:T(8,128)} async-done(((f32[1024,512]{1,0:T(8,128)}), f32[256,512]{1,0:T(8,128)}) %reduce-scatter.11.cloned.1.call-update) | async-done | bytes 524304 | tf_op jit(solution)/shard_map/reduce_scatter | solution.py:197
  426.2 34.0 %reduce-scatter.13.cloned.1.call-done = f32[256,512]{1,0:T(8,128)} async-done(((f32[1024,512]{1,0:T(8,128)}), f32[256,512]{1,0:T(8,128)}) %reduce-scatter.13.cloned.1.call-update) | async-done | bytes 524304 | tf_op jit(solution)/shard_map/reduce_scatter | solution.py:196
  462.9 16.8 %all-gather.11.cloned.1.call-done = bf16[1024,512]{1,0:T(8,128)(2,1)} async-done(((bf16[256,512]{1,0:T(8,128)(2,1)}), bf16[1024,512]{1,0:T(8,128)(2,1)}) %all-gather.11.cloned.1.call-update) | async-done | bytes 1048592 | tf_op jit(solution)/shard_map/all_gather | solution.py:205
  479.7 4.1 fusion.70
  484.7 2.7 fusion.106
  487.4 3.4 fusion.144
  490.8 1.7 fusion.143
  501.2 22.1 %all-reduce.1 = (f32[128]{0:T(128)}, f32[128]{0:T(128)}, f32[512]{0:T(512)}, f32[512]{0:T(512)}, f32[512]{0:T(512)}) all-reduce(f32[128]{0:T(128)S(1)} %reduce_sum.253, f32[128]{0:T(128)S(1)} %reduce_sum.255, f32[512]{0:T(512)S(1)} %copy-done.71, f32[512]{0:T(512)S(1)} %convert_reduce_fusion.1, ...), channel_id=1, replica_groups=mesh['dp'=8,'tensor'=4] {'dp'}, use_global_device_ids=true, to_apply=%region_39.40 | all-reduce | flops 1792 | bytes 14336 | tf_op jit(solution)/shard_map/psum | solution.py:388
  523.4 37.1 %all-reduce = (f32[512]{0:T(512)}, f32[512]{0:T(512)}, f32[512]{0:T(512)}, f32[512]{0:T(512)}, f32[512]{0:T(512)}, /*index=5*/f32[512]{0:T(512)}) all-reduce(f32[512]{0:T(512)S(1)} %copy-done.62, f32[512]{0:T(512)S(1)} %copy-done.63, f32[512]{0:T(512)S(1)} %copy-done.61, ...), channel_id=1, replica_groups=mesh['dp'=8,'tensor'=4] {'dp','tensor'}, use_global_device_ids=true, to_apply=%region_34.35 | all-reduce | flops 3072 | bytes 24576 | tf_op jit(solution)/shard_map/psum | solution.py:368
  560.4 2.2 add_convert_fusion.1
  562.6 139.3 %all-reduce.5.cloned.1.call-done = (f32[512,128]{1,0:T(8,128)}, f32[512,128]{1,0:T(8,128)}, f32[512,128]{1,0:T(8,128)}, f32[128,512]{1,0:T(8,128)}, f32[128,512]...) async-done(((f32[512,128]{1,0:T(8,128)}, f32[512,128]{1,0:T(8,128)}, f32[512,128]{1,0:T(8,128)}, f32[128,512]{1,0:T(8,128)}, ...) | async-done | bytes 3670032 | tf_op jit(solution)/shard_map/psum | solution.py:388
  701.9 1.8 copy.96
  703.7 1.8 copy.97
  705.4 1.7 copy.98
  707.1 1.7 copy.99
  (334 shorter events, 80.2 us)
Async XLA Ops:
  7.2 181.2 %copy-start = (bf16[512,512]{1,0:T(8,128)(2,1)S(1)}, bf16[512,512]{1,0:T(8,128)(2,1)}, u32[]{:S(2)}) copy-start(bf16[512,512]{1,0:T(8,128)(2,1)} %param.45) | copy-start | bytes 1572868
  7.2 25.2 %copy-start.23 = (bf16[512,128]{1,0:T(8,128)(2,1)S(1)}, bf16[512,128]{1,0:T(8,128)(2,1)}, u32[]{:S(2)}) copy-start(bf16[512,128]{1,0:T(8,128)(2,1)} %param.32) | copy-start | bytes 393220
  7.2 25.2 %all-gather.13.cloned.1.call-start = ((), (), s32[]{:S(2)}) async-start(), calls=%async_computation.16 | async-start | bytes 1310720 | tf_op jit(solution)/shard_map/all_gather | solution.py:188
  8.4 25.8 %copy-start.48 = (f32[256]{0:T(256)}, f32[256]{0:T(256)S(1)}, u32[]{:S(2)}) copy-start(f32[256]{0:T(256)S(1)} %broadcast_multiply_fusion.5) | copy-start | bytes 3076
  9.6 24.7 %copy-start.52 = (f32[256]{0:T(256)}, f32[256]{0:T(256)S(1)}, u32[]{:S(2)}) copy-start(f32[256]{0:T(256)S(1)} %add_rsqrt_fusion.1) | copy-start | bytes 3076
  11.0 23.5 %copy-start.25 = (bf16[512,128]{1,0:T(8,128)(2,1)S(1)}, bf16[512,128]{1,0:T(8,128)(2,1)}, u32[]{:S(2)}) copy-start(bf16[512,128]{1,0:T(8,128)(2,1)} %param.34) | copy-start | bytes 393220
  12.9 67.5 %reduce-scatter.21.cloned.1.call-start = ((), (), s32[]{:S(2)}) async-start(), calls=%async_computation.18 | async-start | bytes 2621440 | tf_op jit(solution)/shard_map/reduce_scatter | solution.py:196
  18.0 17.0 %copy-start.27 = (bf16[512,128]{1,0:T(8,128)(2,1)S(1)}, bf16[512,128]{1,0:T(8,128)(2,1)}, u32[]{:S(2)}) copy-start(bf16[512,128]{1,0:T(8,128)(2,1)} %param.35) | copy-start | bytes 393220
  32.4 2.1 copy-start.1
  36.2 10.7 %copy-start.22 = (bf16[128,512]{1,0:T(8,128)(2,1)S(1)}, bf16[128,512]{1,0:T(8,128)(2,1)}, u32[]{:S(2)}) copy-start(bf16[128,512]{1,0:T(8,128)(2,1)} %param.37) | copy-start | bytes 393220
  44.9 3.9 copy-start.6
  48.8 65.7 %reduce-scatter.19.cloned.1.call-start = ((), (), s32[]{:S(2)}) async-start(), calls=%async_computation.17 | async-start | bytes 2621440 | tf_op jit(solution)/shard_map/reduce_scatter | solution.py:197
  48.8 2.8 copy-start.65
  48.8 65.6 %copy-start.2 = (bf16[256,512]{1,0:T(8,128)(2,1)S(1)}, bf16[256,512]{1,0:T(8,128)(2,1)}, u32[]{:S(2)}) copy-start(bf16[256,512]{1,0:T(8,128)(2,1)} %param.28) | copy-start | bytes 786436
  51.6 83.6 %all-gather.15.cloned.1.call-start = ((), (), s32[]{:S(2)}) async-start(), calls=%async_computation.19 | async-start | bytes 1310720 | tf_op jit(solution)/shard_map/all_gather | solution.py:205
  52.3 63.7 %copy-start.51 = (f32[512]{0:T(512)}, f32[512]{0:T(512)S(1)}, u32[]{:S(2)}) copy-start(f32[512]{0:T(512)S(1)} %convert_element_type.253) | copy-start | bytes 6148
  114.5 2.9 copy-start.56
  114.5 2.9 copy-start.57
  116.0 21.9 %copy-start.50 = (f32[256]{0:T(256)}, f32[256]{0:T(256)S(1)}, u32[]{:S(2)}) copy-start(f32[256]{0:T(256)S(1)} %broadcast_multiply_fusion.4) | copy-start | bytes 3076
  118.2 51.2 %reduce-scatter.23.cloned.1.call-start = ((), (), s32[]{:S(2)}) async-start(), calls=%async_computation.20 | async-start | bytes 2621440 | tf_op jit(solution)/shard_map/reduce_scatter | solution.py:211
  137.9 50.5 %all-gather.17.cloned.1.call-start = ((), (), s32[]{:S(2)}) async-start(), calls=%async_computation.21 | async-start | bytes 1310720 | tf_op jit(solution)/shard_map/all_gather | solution.py:314
  171.5 57.0 %reduce-scatter.25.cloned.1.call-start = ((), (), s32[]{:S(2)}) async-start(), calls=%async_computation.22 | async-start | bytes 2621440 | tf_op jit(solution)/shard_map/reduce_scatter | solution.py:210
  196.9 50.7 %all-gather.19.cloned.1.call-start = ((), (), s32[]{:S(2)}) async-start(), calls=%async_computation.23 | async-start | bytes 1310720 | tf_op jit(solution)/shard_map/all_gather | solution.py:315
  230.7 51.2 %reduce-scatter.27.cloned.1.call-start = ((), (), s32[]{:S(2)}) async-start(), calls=%async_computation.24 | async-start | bytes 2621440 | tf_op jit(solution)/shard_map/reduce_scatter | solution.py:329
  250.3 55.4 %all-gather.21.cloned.1.call-start = ((), (), s32[]{:S(2)}) async-start(), calls=%async_computation.25 | async-start | bytes 1310720 | tf_op jit(solution)/shard_map/all_gather | solution.py:340
  281.9 5.5 copy-start.11
  288.8 45.3 %all-gather.23.cloned.1.call-start = ((), (), s32[]{:S(2)}) async-start(), calls=%async_computation.26 | async-start | bytes 1310720 | tf_op jit(solution)/shard_map/all_gather | solution.py:341
  289.6 75.1 %reduce-scatter.29.cloned.1.call-start = ((), (), s32[]{:S(2)}) async-start(), calls=%async_computation.27 | async-start | bytes 1310720 | tf_op jit(solution)/shard_map/reduce_scatter | solution.py:361
  314.2 1.8 copy-start.43
  328.2 2.5 copy-start.44
  328.2 3.1 copy-start.24
  329.4 2.5 copy-start.26
  336.9 27.8 %copy-start.49 = (f32[256]{0:T(256)S(1)}, f32[256]{0:T(256)}, u32[]{:S(2)}) copy-start(f32[256]{0:T(256)} %copy-done.48) | copy-start | bytes 3076
  336.9 27.8 %copy-start.53 = (f32[256]{0:T(256)S(1)}, f32[256]{0:T(256)}, u32[]{:S(2)}) copy-start(f32[256]{0:T(256)} %copy-done.52) | copy-start | bytes 3076
  339.6 46.3 %all-gather.9.cloned.1.call-start = ((), (), s32[]{:S(2)}) async-start(), calls=%async_computation.10 | async-start | bytes 1310720 | tf_op jit(solution)/shard_map/all_gather | solution.py:188
  369.0 57.2 %reduce-scatter.11.cloned.1.call-start = ((), (), s32[]{:S(2)}) async-start(), calls=%async_computation.11 | async-start | bytes 2621440 | tf_op jit(solution)/shard_map/reduce_scatter | solution.py:197
  394.6 65.6 %reduce-scatter.13.cloned.1.call-start = ((), (), s32[]{:S(2)}) async-start(), calls=%async_computation.12 | async-start | bytes 2621440 | tf_op jit(solution)/shard_map/reduce_scatter | solution.py:196
  412.5 1.9 copy-start.64
  412.5 1.9 copy-start.66
  412.6 1.9 copy-start.67
  414.4 48.5 %copy-start.68 = (bf16[512]{0:T(512)(128)(2,1)S(1)}, bf16[512]{0:T(512)(128)(2,1)}, u32[]{:S(2)}) copy-start(bf16[512]{0:T(512)(128)(2,1)} %param.44) | copy-start | bytes 3076
  414.4 65.3 %copy-start.21 = (bf16[512,512]{1,0:T(8,128)(2,1)S(1)}, bf16[512,512]{1,0:T(8,128)(2,1)}, u32[]{:S(2)}) copy-start(bf16[512,512]{1,0:T(8,128)(2,1)} %param.43) | copy-start | bytes 1572868
  414.4 65.3 %all-gather.11.cloned.1.call-start = ((), (), s32[]{:S(2)}) async-start(), calls=%async_computation.13 | async-start | bytes 1310720 | tf_op jit(solution)/shard_map/all_gather | solution.py:205
  461.7 22.1 %copy-start.9 = (f32[256,512]{1,0:T(8,128)}, f32[256,512]{1,0:T(8,128)S(1)}, u32[]{:S(2)}) copy-start(f32[256,512]{1,0:T(8,128)S(1)} %get-tuple-element.332) | copy-start | bytes 1572868
  462.8 97.6 %reduce-scatter.17.cloned.1.call-start = ((), (), s32[]{:S(2)}) async-start(), calls=%async_computation.15 | async-start | bytes 2621440 | tf_op jit(solution)/shard_map/reduce_scatter | solution.py:210
  483.8 76.7 %reduce-scatter.15.cloned.1.call-start = ((), (), s32[]{:S(2)}) async-start(), calls=%async_computation.14 | async-start | bytes 2621440 | tf_op jit(solution)/shard_map/reduce_scatter | solution.py:211
  487.4 214.6 %all-reduce.5.cloned.1.call-start = ((), (), s32[]{:S(2)}) async-start(), calls=%async_computation.28 | async-start | bytes 7340032 | tf_op jit(solution)/shard_map/psum | solution.py:388
  487.4 3.4 copy-start.16
  487.4 3.4 copy-start.30
  490.8 2.8 copy-start.13
  492.5 2.1 copy-start.14
  492.5 2.1 copy-start.18
  494.6 3.4 copy-start.20
  499.9 23.4 %copy-start.58 = (f32[512]{0:T(512)S(1)}, f32[512]{0:T(512)}, u32[]{:S(2)}) copy-start(f32[512]{0:T(512)} %get-tuple-element.247) | copy-start | bytes 6148
  499.9 23.4 %copy-start.59 = (f32[512]{0:T(512)S(1)}, f32[512]{0:T(512)}, u32[]{:S(2)}) copy-start(f32[512]{0:T(512)} %get-tuple-element.252) | copy-start | bytes 6148
  499.9 23.4 %copy-start.60 = (f32[512]{0:T(512)S(1)}, f32[512]{0:T(512)}, u32[]{:S(2)}) copy-start(f32[512]{0:T(512)} %get-tuple-element.324) | copy-start | bytes 6148
  499.9 23.4 %copy-start.61 = (f32[512]{0:T(512)S(1)}, f32[512]{0:T(512)}, u32[]{:S(2)}) copy-start(f32[512]{0:T(512)} %get-tuple-element.327) | copy-start | bytes 6148
  499.9 23.4 %copy-start.62 = (f32[512]{0:T(512)S(1)}, f32[512]{0:T(512)}, u32[]{:S(2)}) copy-start(f32[512]{0:T(512)} %get-tuple-element.250) | copy-start | bytes 6148
  499.9 23.4 %copy-start.63 = (f32[512]{0:T(512)S(1)}, f32[512]{0:T(512)}, u32[]{:S(2)}) copy-start(f32[512]{0:T(512)} %get-tuple-element.254) | copy-start | bytes 6148
  499.9 60.5 %copy-start.10 = (f32[256,512]{1,0:T(8,128)S(1)}, f32[256,512]{1,0:T(8,128)}, u32[]{:S(2)}) copy-start(f32[256,512]{1,0:T(8,128)} %copy-done.9) | copy-start | bytes 1572868
  701.9 6.9 copy-start.46
  701.9 7.6 %copy-start.34 = (f32[512,512]{1,0:T(8,128)S(1)}, f32[512,512]{1,0:T(8,128)}, u32[]{:S(2)}) copy-start(f32[512,512]{1,0:T(8,128)} %get-tuple-element.593) | copy-start | bytes 3145732
  703.7 6.8 copy-start.33
  709.5 1.9 copy-start.45
  (41 other events, 43.0 us)
Sparse Core Ops, SparseCore 0:
  13.0 19.4 all-gather.12
  48.9 31.4 reduce-scatter.20
  83.0 31.3 reduce-scatter.18
  118.4 16.7 all-gather.14
  138.0 31.4 reduce-scatter.22
  171.6 16.7 all-gather.16
  197.0 31.4 reduce-scatter.24
  230.8 16.7 all-gather.18
  250.5 31.4 reduce-scatter.26
  289.0 16.7 all-gather.20
  307.9 16.7 all-gather.22
  339.7 24.8 reduce-scatter.28
  369.1 16.7 all-gather.8
  394.7 31.4 reduce-scatter.10
  428.7 31.4 reduce-scatter.12
  462.9 16.7 all-gather.10
  483.9 31.4 reduce-scatter.16
  517.9 31.5 reduce-scatter.14
  555.9 145.9 all-reduce.4
where the time goes:
time: 720 us; the launch traced here: 719 us
  waiting for transfers between devices  464 us (64%)
  matrix products  87.1 us (12%)
  blocking collectives  59.2 us (8%)
  other arithmetic  56.5 us (8%)
  local copies, waits for them, and re-layouts  35.3 us (5%)
  between operations  14.7 us (2%)
    psum x1, waiting for transfers between devices, body(): lax.psum((grad_w_query, grad_b_query, grad_w_key, grad_w_value, grad_b_va...  139 us
    reduce_scatter x2, waiting for transfers between devices, forward_pass(): lax.psum_scatter(matmul(attended, w_out), 'tensor', scatter_dimension=0,...  59.5 us
    reduce_scatter x2, waiting for transfers between devices, forward_pass(): lax.psum_scatter(matmul(gate_rows, gate1_w), 'tensor', scatter_dimension=...  45.8 us
    psum x1, blocking collectives, body(): lax.psum((grad_norm1_gain, grad_norm1_bias, grad_norm2_gain, grad_norm2_b...  37.1 us
    dot_general x15, matrix products, matmul(): return jnp.dot(left, right, preferred_element_type=jnp.float32)  33.9 us
    all_gather x2, waiting for transfers between devices, forward_pass(): lax.all_gather(normed_two_part.astype(jnp.bfloat16), 'tensor', axis=0, ti...  33.6 us
    reduce_scatter x1, waiting for transfers between devices, body(): lax.psum_scatter(normed_two_grad, 'tensor', scatter_dimension=0, tiled=True)  30.8 us
    reduce_scatter x2, waiting for transfers between devices, forward_pass(): lax.psum_scatter(matmul(gate_rows_two, gate2_w), 'tensor', scatter_dimens...  30.8 us
  transfers between devices with their start and end apart: 19, of which 16 were waited for; matrix products, arithmetic and copies ran while one was open for 12% of the time, Pallas kernels for 0%

commit v1 on v0

v1 whole, which is shorter than its diff:
```python
import functools

import jax
import jax.numpy as jnp
from jax import lax
from jax.experimental import pallas as pl
from jax.experimental.pallas import tpu as pltpu
from jax.sharding import PartitionSpec as P

HD = 64
EPSILON = 1e-05
F32 = jnp.float32
BF16 = jnp.bfloat16
NEG = -1e30
PX = 2
LOCAL = (0, PX, 1, 1 ^ PX)
VMEM_LIMIT = 60 * 1024 * 1024


def nn(a, b):
    return lax.dot_general(a, b, (((1,), (0,)), ((), ())), preferred_element_type=F32)


def nt(a, b):
    return lax.dot_general(a, b, (((1,), (1,)), ((), ())), preferred_element_type=F32)


def tn(a, b):
    return lax.dot_general(a, b, (((0,), (0,)), ((), ())), preferred_element_type=F32)


VM = pl.BlockSpec(memory_space=pltpu.VMEM)
SM = pl.BlockSpec(memory_space=pltpu.SMEM)


def call(body, outs, args, smem=0, scratch=(), flops=0, nbytes=None, name=None, aliases=None):
    if nbytes is None:
        nbytes = sum(a.size * a.dtype.itemsize for a in args) + sum(
            o.size * o.dtype.itemsize for o in outs
        )
    return pl.pallas_call(
        body,
        out_shape=tuple(outs),
        in_specs=[SM] * smem + [VM] * (len(args) - smem),
        out_specs=tuple([VM] * len(outs)),
        scratch_shapes=list(scratch),
        compiler_params=pltpu.CompilerParams(vmem_limit_bytes=VMEM_LIMIT),
        cost_estimate=pl.CostEstimate(flops=flops, bytes_accessed=nbytes, transcendentals=0),
        name=name,
        input_output_aliases=aliases or {},
    )(*args)


def sds(shape, dtype):
    return jax.ShapeDtypeStruct(shape, dtype)


def norm_unit(values):
    centred = values - jnp.mean(values, axis=-1, keepdims=True)
    spread = jnp.mean(centred * centred, axis=-1, keepdims=True)
    inverse = lax.rsqrt(spread + EPSILON)
    return centred * inverse, inverse


def sigmoid(v):
    return 1.0 / (1.0 + jnp.exp(-v))


C0 = 0.7978845608028654
C1 = 0.044715


def gelu_parts(u):
    square = u * u
    t = jnp.tanh(C0 * u * (1.0 + C1 * square))
    half = 0.5 * (1.0 + t)
    value = u * half
    slope = half + (0.5 * C0) * u * (1.0 - t * t) * (1.0 + (3.0 * C1) * square)
    return value, slope


def attend_query_block(qb, tb, segs, segv, qz, k, vt, p_ref, ot_ref, invl_ref, s_sc, m_sc, l_sc, o_sc, segc):
    rows = 256
    tq = tb[qb]
    m_sc[...] = jnp.full(m_sc.shape, NEG, F32)
    l_sc[...] = jnp.zeros(l_sc.shape, F32)
    o_sc[...] = jnp.zeros(o_sc.shape, F32)
    seg_q = segv[tq].astype(F32)

    def active(kb):
        tk = tb[kb]
        return (tk <= tq) & (segs[tk, 0, rows - 1] >= segs[tq, 0, 0])

    @pl.loop(0, 4)
    def _(kb):
        @pl.when(active(kb))
        def _():
            tk = tb[kb]
            krows = pl.ds(pl.multiple_of(kb * rows, rows), rows)
            kpos = tk * rows + lax.broadcasted_iota(jnp.int32, (rows, rows), 0)
            qpos = tq * rows + lax.broadcasted_iota(jnp.int32, (rows, rows), 1)
            seg_k = segc[pl.ds(pl.multiple_of(tk * rows, rows), rows), 0:1]
            bias = jnp.where((kpos <= qpos) & (seg_k == seg_q), 0.0, NEG)
            for h in range(4):
                pair = 128 * (h // 2)
                s = nn(k[krows, pair : pair + 128], qz[h]) + bias
                s_sc[h, krows, :] = s
                m_sc[h] = jnp.maximum(m_sc[h], jnp.max(s.reshape(rows // 8, 8, rows), axis=0))

    for h in range(4):
        m_sc[h] = jnp.broadcast_to(jnp.max(m_sc[h], axis=0, keepdims=True), (8, rows))

    @pl.loop(0, 4)
    def _(kb):
        @pl.when(active(kb))
        def _():
            krows = pl.ds(pl.multiple_of(kb * rows, rows), rows)
            for h in range(4):
                e = jnp.exp(s_sc[h, krows, :] - m_sc[h, 0:1, :])
                l_sc[h] = l_sc[h] + jnp.sum(e.reshape(rows // 8, 8, rows), axis=0)
                pb = e.astype(BF16)
                p_ref[h, krows, :] = pb
                o_sc[h] = o_sc[h] + nn(vt[64 * h : 64 * h + 64, krows], pb)

    for h in range(4):
        invl = 1.0 / jnp.sum(l_sc[h], axis=0, keepdims=True)
        invl_ref[h] = jnp.broadcast_to(invl, (8, rows))
        ot_ref[64 * h : 64 * h + 64, :] = (o_sc[h] * invl).astype(BF16)


def fill_qz(qz, qt):
    zero = jnp.zeros((64, 256), BF16)
    for h in range(4):
        mine = qt[64 * h : 64 * h + 64, :]
        qz[h] = jnp.concatenate([mine, zero] if h % 2 == 0 else [zero, mine], axis=0)


def fill_segc(segc, segv):
    for t in range(4):
        row = jnp.broadcast_to(segv[t].astype(F32), (128, 256))
        segc[256 * t : 256 * t + 256, :] = row.T


def first_kernel(
    tb, segs, segv, x0, x1, x2, x3, vecs, qkv0, qkv1,
    n_ref, qt0_ref, qt1_ref, k_ref, vt_ref, p_ref, ot_ref, att_ref, invl_ref,
    qz, s_sc, m_sc, l_sc, o_sc, segc,
):
    for i, x in enumerate((x0, x1, x2, x3)):
        unit, _ = norm_unit(x[...].astype(F32))
        n_ref[256 * i : 256 * i + 256, :] = (unit * vecs[0:1, :] + vecs[1:2, :]).astype(BF16)
    n = n_ref[...]
    for c, w in enumerate((qkv0, qkv1)):
        cols = slice(128 * c, 128 * c + 128)
        q = nn(n[0:512], w[0:512, 0:128]) + w[512:513, 0:128].astype(F32)
        qt = (q.astype(BF16).astype(F32) * HD ** (-0.5)).T.astype(BF16)
        qt0_ref[cols, :] = qt[:, 0:256]
        qt1_ref[cols, :] = qt[:, 256:512]
        k_ref[:, cols] = nn(n, w[0:512, 128:256]).astype(BF16)
        v = nn(n, w[0:512, 256:384]) + w[512:513, 256:384].astype(F32)
        vt_ref[cols, :] = v.T.astype(BF16)
    fill_segc(segc, segv)
    fill_qz(qz, qt1_ref)
    attend_query_block(1, tb, segs, segv, qz, k_ref, vt_ref, p_ref, ot_ref, invl_ref, s_sc, m_sc, l_sc, o_sc, segc)
    att_ref[...] = ot_ref[...].astype(F32).T.astype(BF16)


def second_kernel(
    tb, segs, segv, qt0, k, vt,
    p_ref, ot_ref, att_ref, invl_ref,
    qz, s_sc, m_sc, l_sc, o_sc, segc,
):
    fill_segc(segc, segv)
    fill_qz(qz, qt0)
    attend_query_block(0, tb, segs, segv, qz, k, vt, p_ref, ot_ref, invl_ref, s_sc, m_sc, l_sc, o_sc, segc)
    att_ref[...] = ot_ref[...].astype(F32).T.astype(BF16)


ATT_SCRATCH = (
    pltpu.VMEM((4, 128, 256), BF16),
    pltpu.VMEM((4, 1024, 256), F32),
    pltpu.VMEM((4, 8, 256), F32),
    pltpu.VMEM((4, 8, 256), F32),
    pltpu.VMEM((4, 64, 256), F32),
    pltpu.VMEM((1024, 128), F32),
)


def gather_gate(tb, pieces, start, scratch):
    for i, piece in enumerate(pieces):
        scratch[pl.ds(pl.multiple_of(tb[i] * 128, 128), 128), :] = piece[start : start + 128, :]


def out_kernel(
    tb, x0, n, att, attp, vecs, e0, e1, e2, e3,
    n2_ref, mid_ref, branch_ref, gate_ref,
    gw,
):
    gather_gate(tb, (e0, e1, e2, e3), 128, gw)
    branch = nn(att[:, 0:128], e0[0:128, :]) + nn(att[:, 128:256], e2[0:128, :])
    branch = branch + nn(attp[:, 0:128], e1[0:128, :]) + nn(attp[:, 128:256], e3[0:128, :])
    branch = branch + vecs[2:3, :]
    gate = sigmoid(nn(n[0:256, :], gw[...]) + vecs[3:4, :])
    middle = x0[...].astype(F32) + gate * branch
    unit, _ = norm_unit(middle)
    n2_ref[...] = (unit * vecs[4:5, :] + vecs[5:6, :]).astype(BF16)
    mid_ref[...] = middle
    branch_ref[...] = branch
    gate_ref[...] = gate


def ffn_kernel(
    tb, n2, mid, ct, vecs, f0, f1, f2, f3,
    out_ref, fg_ref, ltg_ref, hid_ref, slope_ref,
    gw,
):
    gather_gate(tb, (f0, f1, f2, f3), 1024, gw)
    n2v = n2[...]
    total = jnp.zeros((256, 512), F32)
    for i, f in enumerate((f0, f2, f1, f3)):
        u = nn(n2v, f[0:512, :]) + f[1152:1153, :].astype(F32)
        value, slope = gelu_parts(u)
        value = value.astype(BF16)
        hid_ref[:, 512 * i : 512 * i + 512] = value
        slope_ref[:, 512 * i : 512 * i + 512] = slope.astype(BF16)
        total = total + nn(value, f[512:1024, :])
    ffn = total + vecs[6:7, :]
    gate = sigmoid(nn(n2v, gw[...]) + vecs[7:8, :])
    up = ct[...].astype(F32)
    out_ref[...] = (mid[...] + gate * ffn).astype(BF16)
    fg_ref[...] = (gate * up).astype(BF16)
    ltg_ref[...] = (up * ffn * (gate * (1.0 - gate))).astype(BF16)


def back_kernel(
    tb, fg, ltg, slope, mid, branch, gate, ct, vecs, f0, f1, f2, f3, e0, e1, e2, e3,
    dot_ref, dotp_ref, mg_ref, bg_ref, log_ref, hg_ref, sums_ref,
    gw,
):
    gather_gate(tb, (f0, f1, f2, f3), 1024, gw)
    fgv = fg[...]
    ltgv = ltg[...]
    ng = nt(ltgv, gw[...])
    for i, f in enumerate((f0, f2, f1, f3)):
        hg = nt(fgv, f[512:1024, :]) * slope[:, 512 * i : 512 * i + 512].astype(F32)
        hg = hg.astype(BF16)
        if i < 2:
            hg_ref[:, 512 * i : 512 * i + 512] = hg
        ng = ng + nt(hg, f[0:512, :])
    unit, inverse = norm_unit(mid[...])
    g = ng * vecs[4:5, :]
    back = inverse * (g - jnp.mean(g, axis=-1, keepdims=True) - unit * jnp.mean(g * unit, axis=-1, keepdims=True))
    mg = ct[...].astype(F32) + back
    mg_ref[...] = mg
    gatev = gate[...]
    bg = (gatev * mg).astype(BF16)
    log = (mg * branch[...] * (gatev * (1.0 - gatev))).astype(BF16)
    bg_ref[...] = bg
    log_ref[...] = log
    dot_ref[0:128, :] = nt(e0[0:128, :], bg).astype(BF16)
    dot_ref[128:256, :] = nt(e2[0:128, :], bg).astype(BF16)
    dotp_ref[0:128, :] = nt(e1[0:128, :], bg).astype(BF16)
    dotp_ref[128:256, :] = nt(e3[0:128, :], bg).astype(BF16)
    rows = [fgv.astype(F32), ltgv.astype(F32), bg.astype(F32), log.astype(F32), ng * unit, ng]
    sums_ref[...] = jnp.zeros((8, 512), F32)
    for i, r in enumerate(rows):
        sums_ref[i : i + 1, :] = jnp.sum(r, axis=0, keepdims=True)


def ffn_weight_kernel(
    n2, n2p, fg, fgp, hid, hg, f0, f2,
    keep_ref, send_ref,
):
    n2v, n2pv, fgv, fgpv = n2[...], n2p[...], fg[...], fgp[...]
    for i, f in enumerate((f0, f2)):
        cols = slice(512 * i, 512 * i + 512)
        u = nn(n2pv, f[0:512, :]) + f[1152:1153, :].astype(F32)
        value, slope = gelu_parts(u)
        hidp = value.astype(BF16)
        hgp = (nt(fgpv, f[512:1024, :]) * slope).astype(BF16)
        hgo = hg[:, cols]
        win = tn(n2v, hgo) + tn(n2pv, hgp)
        wback = tn(hid[:, cols], fgv) + tn(hidp, fgpv)
        bias = jnp.sum(hgo.astype(F32), axis=0, keepdims=True) + jnp.sum(hgp.astype(F32), axis=0, keepdims=True)
        dst = keep_ref if i == 0 else send_ref
        dst[0:512, :] = win.astype(dst.dtype)
        dst[512:1024, :] = wback.astype(dst.dtype)
        dst[1024:1032, :] = jnp.broadcast_to(bias, (8, 512)).astype(dst.dtype)


def small_weight_kernel(
    tb, n, n2, ltg, log, att, attp, bg,
    keep_ref, send_ref,
    g1, g2,
):
    g2[...] = tn(n2[...], ltg[...])
    g1[...] = tn(n[0:256, :], log[...])
    bgv = bg[...]
    wo = (tn(att[:, 0:128], bgv), tn(attp[:, 0:128], bgv), tn(att[:, 128:256], bgv), tn(attp[:, 128:256], bgv))
    for i in range(4):
        src = pl.ds(pl.multiple_of(tb[i] * 128, 128), 128)
        dst = keep_ref if i < 2 else send_ref
        base = 384 * (i % 2)
        dst[base : base + 128, :] = g2[src, :].astype(dst.dtype)
        dst[base + 128 : base + 256, :] = g1[src, :].astype(dst.dtype)
        dst[base + 256 : base + 384, :] = wo[i].astype(dst.dtype)


def prepare_kernel(n, k, qkv0, qkv1, v_ref, kt_ref):
    nv = n[...]
    for c, w in enumerate((qkv0, qkv1)):
        v = nn(nv, w[0:512, 256:384]) + w[512:513, 256:384].astype(F32)
        v_ref[:, 128 * c : 128 * c + 128] = v.astype(BF16)
    kt_ref[...] = k[...].astype(F32).T.astype(BF16)


def attend_back(qb, tb, segs, p, dot, ot, invl, qt, kt, v, dk, dv, dq, doz, dos, dlt):
    rows = 256
    tq = tb[qb]
    zero = jnp.zeros((64, rows), BF16)
    for h in range(4):
        hs = slice(64 * h, 64 * h + 64)
        scale = invl[h, 0:1, :]
        dv_h = dot[hs, :].astype(F32)
        delta = jnp.sum(dv_h * ot[hs, :].astype(F32), axis=0, keepdims=True) * scale
        dlt[h] = jnp.broadcast_to(delta, (8, rows))
        mine = (dv_h * scale).astype(BF16)
        dos[hs, :] = mine
        doz[h] = jnp.concatenate([mine, zero] if h % 2 == 0 else [zero, mine], axis=0)
    dq[...] = jnp.zeros(dq.shape, F32)

    @pl.loop(0, 4)
    def _(kb):
        tk = tb[kb]

        @pl.when((tk <= tq) & (segs[tk, 0, rows - 1] >= segs[tq, 0, 0]))
        def _():
            ks = pl.ds(pl.multiple_of(kb * rows, rows), rows)
            for h in range(4):
                pair = 128 * (h // 2)
                hs = slice(64 * h, 64 * h + 64)
                ph = p[h, ks, :]
                dp = nn(v[ks, pair : pair + 128], doz[h])
                ds = (ph.astype(F32) * (dp - dlt[h, 0:1, :])).astype(BF16)
                dv[hs, ks] = dv[hs, ks] + nt(dos[hs, :], ph)
                dk[hs, ks] = dk[hs, ks] + nt(qt[hs, :], ds)
                dq[hs, :] = dq[hs, :] + nn(kt[hs, ks], ds)


def back_first_kernel(
    tb, segs, p, dot, ot, invl, qt, kt, v,
    dk_ref, dv_ref, dq_ref,
    dq, doz, dos, dlt,
):
    dk_ref[...] = jnp.zeros(dk_ref.shape, F32)
    dv_ref[...] = jnp.zeros(dv_ref.shape, F32)
    attend_back(0, tb, segs, p, dot, ot, invl, qt, kt, v, dk_ref, dv_ref, dq, doz, dos, dlt)
    dq_ref[...] = (dq[...] * HD ** (-0.5)).astype(BF16)


def back_second_kernel(
    tb, segs, p, dot, ot, invl, qt, kt, v, dk0, dv0, dq0, n,
    dqt_ref, dkt_ref, dvt_ref, keep_ref, send_ref, bias_ref,
    dk, dv, dq, doz, dos, dlt,
):
    dk[...] = dk0[...]
    dv[...] = dv0[...]
    attend_back(1, tb, segs, p, dot, ot, invl, qt, kt, v, dk, dv, dq, doz, dos, dlt)
    dqt_ref[:, 0:256] = dq0[...]
    dqt_ref[:, 256:512] = (dq[...] * HD ** (-0.5)).astype(BF16)
    dkt_ref[...] = dk[...].astype(BF16)
    dvt_ref[...] = dv[...].astype(BF16)
    nv = n[...]
    wq = nn(dqt_ref[...], nv[0:512, :])
    wk = nn(dkt_ref[...], nv)
    wv = nn(dvt_ref[...], nv)
    for i, w in enumerate((wq, wk, wv)):
        keep_ref[128 * i : 128 * i + 128, :] = w[0:128, :]
        send_ref[128 * i : 128 * i + 128, :] = w[128:256, :].astype(BF16)
    ones_q = jnp.ones((8, 512), BF16)
    ones_v = jnp.ones((8, 1024), BF16)
    bias_ref[:, 0:256] = nt(ones_q, dqt_ref[...])
    bias_ref[:, 256:512] = nt(ones_v, dvt_ref[...])


def input_kernel(dqt, dkt, dvt, qkv0, qkv1, own_ref, par_ref, send_ref):
    def weight(part):
        cols = slice(128 * part, 128 * part + 128)
        return jnp.concatenate([qkv0[0:512, cols], qkv1[0:512, cols]], axis=1)

    wk, wv = weight(1), weight(2)
    g = nn(wk, dkt[...]) + nn(wv, dvt[...])
    send_ref[...] = g[:, 512:1024].astype(BF16)
    g0 = g[:, 0:512] + nn(weight(0), dqt[...])
    own_ref[...] = g0[:, 0:256]
    par_ref[...] = g0[:, 256:512]


def last_kernel(tb, own, sib, par, x0, mg, log, vecs, e0, e1, e2, e3, grad_ref, sums_ref, gw):
    gather_gate(tb, (e0, e1, e2, e3), 128, gw)
    total = own[...] + sib[:, 0:256].astype(F32) + par[...].astype(F32)
    ng = total.T + nt(log[...], gw[...])
    unit, inverse = norm_unit(x0[...].astype(F32))
    g = ng * vecs[0:1, :]
    back = inverse * (g - jnp.mean(g, axis=-1, keepdims=True) - unit * jnp.mean(g * unit, axis=-1, keepdims=True))
    grad_ref[...] = mg[...] + back
    sums_ref[...] = jnp.zeros((8, 512), F32)
    sums_ref[0:1, :] = jnp.sum(ng * unit, axis=0, keepdims=True)
    sums_ref[1:2, :] = jnp.sum(ng, axis=0, keepdims=True)


def body(
    layer_input, segments, norm1_gain, norm1_bias, w_query, b_query, w_key, w_value, b_value,
    w_out, b_out, gate1_w, gate1_b, norm2_gain, norm2_bias, w_in, b_in, w_back, b_back,
    gate2_w, gate2_b, cotangent, *, n_dp,
):
    def hop(value, mask):
        return lax.ppermute(value, "tensor", [(i, i ^ mask) for i in range(4)])

    t = lax.axis_index("tensor").astype(jnp.int32)
    tb = t ^ jnp.array(LOCAL, jnp.int32)
    seg = segments.reshape(4, 1, 256)
    x0 = layer_input
    x1 = hop(x0, PX)
    x2 = hop(x0, 1)
    x3 = hop(x1, 1)
    zero128 = jnp.zeros((128,), BF16)
    row_qkv = jnp.concatenate([b_query, zero128, b_value])[None]
    qkv0 = jnp.concatenate(
        [jnp.concatenate([w_query, w_key, w_value], axis=1), row_qkv, jnp.zeros((7, 384), BF16)], axis=0
    )
    qkv1 = hop(qkv0, 1)
    e0 = jnp.concatenate([w_out, gate1_w], axis=0)
    f0 = jnp.concatenate([w_in, w_back, gate2_w, b_in[None], jnp.zeros((7, 512), BF16)], axis=0)
    e2 = hop(e0, 1)
    f2 = hop(f0, 1)
    x1b, e0b, f0b = lax.optimization_barrier((x1, e0, f0))
    e1 = hop(e0b, PX)
    e3 = hop(e1, 1)
    f1 = hop(f0b, PX)
    f3 = hop(f1, 1)
    vecs = jnp.stack(
        [norm1_gain, norm1_bias, b_out, gate1_b, norm2_gain, norm2_bias, b_back, gate2_b]
    ).astype(F32)

    n, qt0, qt1, k, vt, p1, ot1, att1, invl1 = call(
        first_kernel,
        [
            sds((1024, 512), BF16), sds((256, 256), BF16), sds((256, 256), BF16), sds((1024, 256), BF16),
            sds((256, 1024), BF16), sds((4, 1024, 256), BF16), sds((256, 256), BF16), sds((256, 256), BF16),
            sds((4, 8, 256), F32),
        ],
        [tb, seg, seg, x0, x1b, x2, x3, vecs, qkv0, qkv1],
        smem=2, scratch=ATT_SCRATCH, flops=2_000_000_000, name="first",
    )
    attp = hop(att1, PX)
    p0, ot0, att0, invl0 = call(
        second_kernel,
        [sds((4, 1024, 256), BF16), sds((256, 256), BF16), sds((256, 256), BF16), sds((4, 8, 256), F32)],
        [tb, seg, seg, qt0, k, vt],
        smem=2, scratch=ATT_SCRATCH, flops=2_000_000_000, name="second",
    )
    n2, mid, branch, gate = call(
        out_kernel,
        [sds((256, 512), BF16), sds((256, 512), F32), sds((256, 512), F32), sds((256, 512), F32)],
        [tb, x0, n, att0, attp, vecs, e0, e1, e2, e3],
        smem=1, scratch=[pltpu.VMEM((512, 512), BF16)], flops=270_000_000, name="out",
    )
    n2p = hop(n2, PX)
    result, fg, ltg, hid, slope = call(
        ffn_kernel,
        [
            sds((256, 512), BF16), sds((256, 512), BF16), sds((256, 512), BF16), sds((256, 2048), BF16),
            sds((256, 2048), BF16),
        ],
        [tb, n2, mid, cotangent, vecs, f0, f1, f2, f3],
        smem=1, scratch=[pltpu.VMEM((512, 512), BF16)], flops=1_200_000_000, name="ffn",
    )
    fgp = hop(fg, PX)
    dot0, dotp, mg, bg, log, hg, sums = call(
        back_kernel,
        [
            sds((256, 256), BF16), sds((256, 256), BF16), sds((256, 512), F32), sds((256, 512), BF16),
            sds((256, 512), BF16), sds((256, 1024), BF16), sds((8, 512), F32),
        ],
        [tb, fg, ltg, slope, mid, branch, gate, cotangent, vecs, f0, f1, f2, f3, e0, e1, e2, e3],
        smem=1, scratch=[pltpu.VMEM((512, 512), BF16)], flops=1_400_000_000, name="back",
    )
    dot1 = hop(dotp, PX)
    fkeep, fsend = call(
        ffn_weight_kernel,
        [sds((1032, 512), F32), sds((1032, 512), BF16)],
        [n2, n2p, fg, fgp, hid, hg, f0, f2],
        flops=1_600_000_000, name="ffn_weight",
    )
    frecv = hop(fsend, 1)
    fsum = fkeep + frecv.astype(F32)
    skeep, ssend = call(
        small_weight_kernel,
        [sds((768, 512), F32), sds((768, 512), BF16)],
        [tb, n, n2, ltg, log, att0, attp, bg],
        smem=1, scratch=[pltpu.VMEM((512, 512), F32), pltpu.VMEM((512, 512), F32)],
        flops=400_000_000, name="small_weight",
    )
    srecv = hop(ssend, 1)
    ssum = skeep + srecv.astype(F32)
    spar = hop(ssum[384:768].astype(BF16), PX)
    stot = (ssum[0:384] + spar.astype(F32)).astype(BF16)
    sums = sums + hop(sums, 1)
    sums = sums + hop(sums, PX)

    v, kt = call(
        prepare_kernel, [sds((1024, 256), BF16), sds((256, 1024), BF16)], [n, k, qkv0, qkv1],
        flops=270_000_000, name="prepare",
    )
    back_scratch = [
        pltpu.VMEM((256, 256), F32), pltpu.VMEM((4, 128, 256), BF16), pltpu.VMEM((256, 256), BF16),
        pltpu.VMEM((4, 8, 256), F32),
    ]
    dk0, dv0, dq0 = call(
        back_first_kernel,
        [sds((256, 1024), F32), sds((256, 1024), F32), sds((256, 256), BF16)],
        [tb, seg, p0, dot0, ot0, invl0, qt0, kt, v],
        smem=2, scratch=back_scratch, flops=2_000_000_000, name="attn_back0",
    )
    dqt, dkt, dvt, akeep, asend, abias = call(
        back_second_kernel,
        [
            sds((256, 512), BF16), sds((256, 1024), BF16), sds((256, 1024), BF16), sds((384, 512), F32),
            sds((384, 512), BF16), sds((8, 512), F32),
        ],
        [tb, seg, p1, dot1, ot1, invl1, qt1, kt, v, dk0, dv0, dq0, n],
        smem=2, scratch=[pltpu.VMEM((256, 1024), F32), pltpu.VMEM((256, 1024), F32)] + back_scratch,
        flops=2_500_000_000, name="attn_back1",
    )
    arecv = hop(asend, 1)
    asum = (akeep + arecv.astype(F32)).astype(BF16)
    bq_s = abias[0, 128:256]
    bv_s = abias[0, 384:512]
    brecv = hop(jnp.concatenate([bq_s, bv_s])[None], 1)[0]
    bq = abias[0, 0:128] + brecv[0:128]
    bv = abias[0, 256:384] + brecv[128:256]
    gown, gpar, gsend = call(
        input_kernel,
        [sds((512, 256), F32), sds((512, 256), F32), sds((512, 512), BF16)],
        [dqt, dkt, dvt, qkv0, qkv1],
        flops=700_000_000, name="input_grad",
    )
    gsib = hop(gsend, 1)
    gp = hop((gpar + gsib[:, 256:512].astype(F32)).astype(BF16), PX)
    input_grad, sums1 = call(
        last_kernel,
        [sds((256, 512), F32), sds((8, 512), F32)],
        [tb, gown, gsib, gp, x0, mg, log, vecs, e0, e1, e2, e3],
        smem=1, scratch=[pltpu.VMEM((512, 512), BF16)], flops=140_000_000, name="last",
    )
    sums1 = sums1 + hop(sums1, 1)
    sums1 = sums1 + hop(sums1, PX)

    def scatter(matrix):
        pieces = matrix.astype(BF16).reshape(n_dp, -1, 512)
        got = lax.all_to_all(pieces, "dp", 0, 0, tiled=True)
        return jnp.sum(got.astype(F32), axis=0).astype(BF16)

    def gather(piece, small):
        rows = piece.shape[0]
        both = jnp.concatenate([piece, small.astype(BF16)], axis=0)
        got = lax.all_to_all(jnp.broadcast_to(both[None], (n_dp,) + both.shape), "dp", 0, 0, tiled=True)
        return (
            got[:, :rows].astype(F32).reshape(n_dp * rows, 512),
            jnp.sum(got[:, rows:].astype(F32), axis=0),
        )

    small_f = jnp.concatenate([sums[0:6], fsum[1024:1025], jnp.zeros((1, 512), F32)], axis=0)
    f_all, f_small = gather(scatter(fsum[0:1024]), small_f)
    s_all, s_small = gather(scatter(stot), jnp.zeros((8, 512), F32))
    small_a = jnp.concatenate(
        [sums1[0:2], jnp.concatenate([bq, bv, jnp.zeros((256,), F32)])[None], jnp.zeros((5, 512), F32)], axis=0
    )
    a_all, a_small = gather(scatter(asum), small_a)
    return (
        result,
        input_grad,
        a_small[0],
        a_small[1],
        a_all[0:128].T,
        a_small[2, 0:128],
        a_all[128:256].T,
        a_all[256:384].T,
        a_small[2, 128:256],
        s_all[256:384],
        f_small[2],
        s_all[128:256],
        f_small[3],
        f_small[4],
        f_small[5],
        f_all[0:512],
        f_small[6],
        f_all[512:1024],
        f_small[0],
        s_all[0:128],
        f_small[1],
    )


def solution(mesh):
    tok = P(("dp", "tensor"), None)
    col = P(None, "tensor")
    row = P("tensor", None)
    vec = P("tensor")
    rep = P()
    return jax.shard_map(
        functools.partial(body, n_dp=mesh.shape["dp"]),
        mesh=mesh,
        in_specs=(
            tok, P("dp", None), rep, rep, col, vec, col, col, vec, row, rep, row, rep, rep, rep,
            col, vec, row, rep, row, rep, tok,
        ),
        out_specs=(
            tok, tok, rep, rep, col, vec, col, col, vec, row, rep, row, rep, rep, rep,
            col, vec, row, rep, row, rep,
        ),
        check_vma=False,
    )
```

time: 720 us -> 260 us (0.36)
  waiting for transfers between devices: 464 us -> 119 us
  matrix products: 87.1 us -> 0 us
  Pallas kernels: 0 us -> 61 us
  blocking collectives: 59.2 us -> 0 us
  other arithmetic: 56.5 us -> 9.61 us
  starting transfers between devices: 1.19 us -> 45.8 us
  local copies, waits for them, and re-layouts: 35.3 us -> 21.6 us
  between operations: 14.7 us -> 1.35 us
    reduce_scatter x10 -> x0, waiting for transfers between devices: 219 us -> none  [the longest x2 59.5 us: forward_pass(): lax.psum_scatter(matmul(attended, w_out), 'tensor', scatter_dimension=0,...]
    psum x1 -> x0, waiting for transfers between devices: 139 us -> none  [body(): lax.psum((grad_w_query, grad_b_query, grad_w_key, grad_w_value, grad_b_va...]
    all_gather x8 -> x0, waiting for transfers between devices: 105 us -> none  [the longest x2 33.6 us: forward_pass(): lax.all_gather(normed_two_part.astype(jnp.bfloat16), 'tensor', axis=0, ti...]
    dot_general x49 -> x0, matrix products: 87.1 us -> none  [the longest x15 33.9 us: matmul(): return jnp.dot(left, right, preferred_element_type=jnp.float32)]
    all_to_all x0 -> x6, waiting for transfers between devices: none -> 71.2 us  [the longest x3 38.9 us: gather(): lax.all_to_all(jnp.broadcast_to(both[None], (n_dp,) + both.shape), 'dp',...]
    pallas_call x0 -> x12, Pallas kernels: none -> 61 us  [call(): pl.pallas_call(body, out_shape=tuple(outs), in_specs=[SM] * smem + [VM] *...]
    psum x2 -> x0, blocking collectives: 59.2 us -> none  [the longest x1 37.1 us: body(): lax.psum((grad_norm1_gain, grad_norm1_bias, grad_norm2_gain, grad_norm2_b...]
    ppermute x0 -> x25, waiting for transfers between devices: none -> 48 us  [hop(): return lax.ppermute(value, 'tensor', [(i, i ^ mask) for i in range(4)])]
  transfers between devices with their start and end apart: 19 -> 31, of which waited for: 16 -> 13; matrix products, arithmetic and copies ran while one was open for 12% -> 9% of each run, Pallas kernels for 0% -> 17%
where the time goes in v1:
time: 260 us; the launch traced here: 258 us
  waiting for transfers between devices  119 us (46%)
  Pallas kernels  61 us (23%)
  starting transfers between devices  45.8 us (18%)
  local copies, waits for them, and re-layouts  21.6 us (8%)
  other arithmetic  9.61 us (4%)
    pallas_call x12, Pallas kernels, call(): pl.pallas_call(body, out_shape=tuple(outs), in_specs=[SM] * smem + [VM] *...  61 us
    ppermute x25, waiting for transfers between devices, hop(): return lax.ppermute(value, 'tensor', [(i, i ^ mask) for i in range(4)])  48 us
    all_to_all x3, waiting for transfers between devices, gather(): lax.all_to_all(jnp.broadcast_to(both[None], (n_dp,) + both.shape), 'dp',...  38.9 us
    all_to_all x3, waiting for transfers between devices, scatter(): got = lax.all_to_all(pieces, 'dp', 0, 0, tiled=True)  32.3 us
    ppermute x25, starting transfers between devices, hop(): return lax.ppermute(value, 'tensor', [(i, i ^ mask) for i in range(4)])  19.2 us
    all_to_all x3, starting transfers between devices, scatter(): got = lax.all_to_all(pieces, 'dp', 0, 0, tiled=True)  15.3 us
    all_to_all x3, starting transfers between devices, gather(): lax.all_to_all(jnp.broadcast_to(both[None], (n_dp,) + both.shape), 'dp',...  11.3 us
    unnamed x80, local copies, waits for them, and re-layouts  5.81 us
  transfers between devices with their start and end apart: 31, of which 13 were waited for; matrix products, arithmetic and copies ran while one was open for 9% of the time, Pallas kernels for 17%

profile of v1, /device:TPU:0, one launch (start us, length us, event | category | flops | bytes accessed | tf_op | source)
XLA Modules:
  0.0 258.5 jit_solution(9345673596343374756)
XLA Ops:
  0.7 3.0 %collective-permute-start = (bf16[256,512]{1,0:T(8,128)(2,1)}, bf16[256,512]{1,0:T(8,128)(2,1)S(1)}, u32[]{:S(2)}, u32[]{:S(2)}) collective-permute-start(bf16[256,512]{1,0:T(8,128)(2,1)} %x0.5), channel_id=1, source_target_pairs={{0,2},{1,3},{2,0},{3,1},{4,6},{5,7},{6,4},{7,5},{8,10},{9,11},{10,... | collective-permute-start | bytes 786440 | tf_op jit(solution)/shard_map/ppermute | solution.py:418
  3.8 0.7 broadcast_in_dim.49
  4.5 4.8 %concatenate.38.f0 = bf16[1160,512]{1,0:T(8,128)(2,1)S(1)} concatenate(bf16[512,512]{1,0:T(8,128)(2,1)} %param.38, bf16[512,512]{1,0:T(8,128)(2,1)} %param.40, bf16[128,512]{1,0:T(8,128)(2,1)} %param.42, bf16[1,512]{1,0:T(2,128)(2,1)S(1)} %broadcast_in_dim.49, bf16[7,512]{1,0:T(8,128)(2,1)S(1)} %broadcast_in_dim.50), dimensions={0} | concatenate | bytes 2375680 | tf_op jit(solution)/shard_map/concatenate | solution.py:434
  9.4 0.8 collective-permute-done.x1
  10.3 1.7 collective-permute-start.8
  12.0 25.7 %collective-permute-done.8.f1 = bf16[1160,512]{1,0:T(8,128)(2,1)} collective-permute-done((bf16[1160,512]{1,0:T(8,128)(2,1)S(1)}, bf16[1160,512]{1,0:T(8,128)(2,1)}, u32[]{:S(2)}, u32[]{:S(2)}) %collective-permute-start.8) | collective-permute-done | bytes 1187872 | tf_op jit(solution)/shard_map/ppermute | solution.py:418
  38.6 1.5 collective-permute-start.5
  40.1 1.6 collective-permute-done.1.x2
  43.5 3.8 %collective-permute-done.5.e1 = bf16[256,512]{1,0:T(8,128)(2,1)S(1)} collective-permute-done((bf16[256,512]{1,0:T(8,128)(2,1)S(1)}, bf16[256,512]{1,0:T(8,128)(2,1)S(1)}, u32[]{:S(2)}, u32[]{:S(2)}) %collective-permute-start.5) | collective-permute-done | bytes 262176 | tf_op jit(solution)/shard_map/ppermute | solution.py:418
  47.3 7.8 %first.1 = (bf16[1024,512]{1,0:T(8,128)(2,1)}, bf16[256,256]{1,0:T(8,128)(2,1)}, bf16[256,256]{1,0:T(8,128)(2,1)}, bf16[1024,256]{1,0:T(8,128)(2,1)}, bf16[256,1...) custom-call(s32[4]{0:T(128)} %broadcast_xor_fusion.tb, ...), custom_call_target="tpu_custom_call" | custom-call | flops 2000000000 | bytes 6623248 | tf_op jit(solution)/shard_map/first/pallas_call | solution.py:41
  55.5 3.3 %prepare.1 = (bf16[1024,256]{1,0:T(8,128)(2,1)}, bf16[256,1024]{1,0:T(8,128)(2,1)}) custom-call(bf16[1024,512]{1,0:T(8,128)(2,1)} %get-tuple-element.74.n, bf16[1024,256]{1,0:T(8,128)(2,1)} %get-tuple-element.76.k, bf16[520,384]{1,0:T(8,128)(2,1)} %copy-done.7, bf16[520,384]{1,0:T(8,128)(2,1)} %collective-permute-done.3.qkv1), custom_call_target="tpu_custom_call" | custom-call | flops 270000000 | bytes 3420160 | tf_op jit(solution)/shard_map/prepare/pallas_call | solution.py:41
  58.8 3.7 %second.1 = (bf16[4,1024,256]{2,1,0:T(8,128)(2,1)}, bf16[256,256]{1,0:T(8,128)(2,1)}, bf16[256,256]{1,0:T(8,128)(2,1)}, f32[4,8,256]{2,1,0:T(8,128)}) custom-call(s32[4]{0:T(128)} %broadcast_xor_fusion.tb, s32[4,1,256]{2,1,0:T(1,128)} %bitcast.55, s32[4,1,256]{2,1,0:T(1,128)} %bitcast.56, bf16[256,256]{1,0:T(8,128)(2,1)} %get-tuple-element.75.qt0.qt, ...), custom_call_target="tpu_custom_call" | custom-call | flops 2000000000 | bytes 3579920 | tf_op jit(solution)/shard_map/second/pallas_call | solution.py:41
  62.5 0.7 copy-done.4
  63.3 3.6 %out.1 = (bf16[256,512]{1,0:T(8,128)(2,1)}, f32[256,512]{1,0:T(8,128)}, f32[256,512]{1,0:T(8,128)}, f32[256,512]{1,0:T(8,128)}) custom-call(s32[4]{0:T(128)} %broadcast_xor_fusion.tb, bf16[256,512]{1,0:T(8,128)(2,1)} %x0.5, bf16[1024,512]{1,0:T(8,128)(2,1)} %get-tuple-element.74.n, bf16[256,256]{1,0:T(8,128)(2,1)} %get-tuple-element.78.att, ...), custom_call_target="tpu_custom_call" | custom-call | flops 270000000 | bytes 4472848 | tf_op jit(solution)/shard_map/out/pallas_call | solution.py:41
  66.9 1.0 copy-done.1
  67.9 6.3 %ffn.1 = (bf16[256,512]{1,0:T(8,128)(2,1)}, bf16[256,512]{1,0:T(8,128)(2,1)}, bf16[256,512]{1,0:T(8,128)(2,1)}, bf16[256,2048]{1,0:T(8,128)(2,1)}, bf16[256,2048]{1,0:T(8,128)(2,1)}) custom-call(s32[4]{0:T(128)} %broadcast_xor_fusion.tb, bf16[256,512]{1,0:T(8,128)(2,1)} %get-tuple-element.81.n2, f32[256,512]{1,0:T(8,128)} %get-tuple-element.82.mid, ...), custom_call_target="tpu_custom_call" | custom-call | flops 1200000000 | bytes 8699920 | tf_op jit(solution)/shard_map/ffn/pallas_call | solution.py:41
  74.3 7.0 %back.1 = (bf16[256,256]{1,0:T(8,128)(2,1)}, bf16[256,256]{1,0:T(8,128)(2,1)}, f32[256,512]{1,0:T(8,128)}, bf16[256,512]{1,0:T(8,128)(2,1)}, bf16[256,512]{1,0:T...) custom-call(s32[4]{0:T(128)} %broadcast_xor_fusion.tb, bf16[256,512]{1,0:T(8,128)(2,1)} %get-tuple-element.86.fg, ...), custom_call_target="tpu_custom_call" | custom-call | flops 1400000000 | bytes 11075600 | tf_op jit(solution)/shard_map/back/pallas_call | solution.py:41
  81.2 3.6 %small_weight.1 = (f32[768,512]{1,0:T(8,128)}, bf16[768,512]{1,0:T(8,128)(2,1)}) custom-call(s32[4]{0:T(128)} %broadcast_xor_fusion.tb, bf16[1024,512]{1,0:T(8,128)(2,1)} %get-tuple-element.74.n, bf16[256,512]{1,0:T(8,128)(2,1)} %get-tuple-element.81.n2, bf16[256,512]{1,0:T(8,128)(2,1)} %get-tuple-element.87.ltg, bf16[256,512]{1,0:T(8,128)(2,1)} %get-tuple-element.111.log, ...), custom_call_target="tpu_custom_call" | custom-call | flops 400000000 | bytes 4718608 | tf_op jit(solution)/shard_map/small_weight/pallas_call | solution.py:41
  84.9 1.4 collective-permute-start.18
  86.2 2.9 %collective-permute-start.11 = (bf16[256,256]{1,0:T(8,128)(2,1)S(1)}, bf16[256,256]{1,0:T(8,128)(2,1)S(1)}, u32[]{:S(2)}, u32[]{:S(2)}) collective-permute-start(bf16[256,256]{1,0:T(8,128)(2,1)S(1)} %copy-done.35), channel_id=1, source_target_pairs={{0,2},{1,3},{2,0},{3,1},{4,6},{5,7},{6,4},{7,5},{8,10},{9,11},{10,... | collective-permute-start | bytes 393224 | tf_op jit(solution)/shard_map/ppermute | solution.py:418
  89.2 4.6 %attn_back0.1 = (f32[256,1024]{1,0:T(8,128)}, f32[256,1024]{1,0:T(8,128)}, bf16[256,256]{1,0:T(8,128)(2,1)}) custom-call(s32[4]{0:T(128)} %broadcast_xor_fusion.tb, s32[4,1,256]{2,1,0:T(1,128)} %bitcast.57, bf16[4,1024,256]{2,1,0:T(8,128)(2,1)} %get-tuple-element.97.p, bf16[256,256]{1,0:T(8,128)(2,1)} %get-tuple-element.98.dot, ...), custom_call_target="tpu_custom_call" | custom-call | flops 2000000000 | bytes 5804048 | tf_op jit(solution)/shard_map/attn_back0/pallas_call | solution.py:41
  93.8 0.6 copy-done.36
  94.4 8.3 %attn_back1.1 = (bf16[256,512]{1,0:T(8,128)(2,1)}, bf16[256,1024]{1,0:T(8,128)(2,1)}, bf16[256,1024]{1,0:T(8,128)(2,1)}, f32[384,512]{1,0:T(8,128)}, bf16[384,512]{1,0:T(8,128)(2,1)}, /*index=5*/f32[8,512]{1,0:T(8,128)}) custom-call(s32[4]{0:T(128)} %broadcast_xor_fusion.tb, s32[4,1,256]{2,1,0:T(1,128)} %bitcast.58, ...), custom_call_target="tpu_custom_call" | custom-call | flops 2500000000 | bytes 9359376 | tf_op jit(solution)/shard_map/attn_back1/pallas_call | solution.py:41
  102.7 1.8 collective-permute-start.14
  104.9 1.7 collective-permute-start.21
  106.6 3.5 %input_grad.1 = (f32[512,256]{1,0:T(8,128)}, f32[512,256]{1,0:T(8,128)}, bf16[512,512]{1,0:T(8,128)(2,1)}) custom-call(bf16[256,512]{1,0:T(8,128)(2,1)} %get-tuple-element.104.dqt, bf16[256,1024]{1,0:T(8,128)(2,1)} %get-tuple-element.105.dkt, bf16[256,1024]{1,0:T(8,128)(2,1)} %get-tuple-element.106.dvt, bf16[520,384]{1,0:T(8,128)(2,1)} %copy-done.7, ...), custom_call_target="tpu_custom_call" | custom-call | flops 700000000 | bytes 3682304 | tf_op jit(solution)/shard_map/input_grad/pallas_call | solution.py:41
  110.2 0.8 slice_bitcast_fusion.6
  111.0 0.9 add_convert_fusion.1
  111.8 5.7 %all-to-all-start = ((bf16[8,48,512]{2,1,0:T(8,128)(2,1)}), bf16[8,48,512]{2,1,0:T(8,128)(2,1)}, u32[]{:S(2)}, u32[]{:S(2)}) async-start(bf16[8,48,512]{2,1,0:T(8,128)(2,1)} %bitcast.1), calls=%async_computation | async-start | bytes 786432 | tf_op jit(solution)/shard_map/all_to_all | solution.py:562
  117.6 1.4 convert_add_fusion
  119.6 1.8 collective-permute-start.13
  121.4 5.9 %ffn_weight.1 = (f32[1032,512]{1,0:T(8,128)}, bf16[1032,512]{1,0:T(8,128)(2,1)}) custom-call(bf16[256,512]{1,0:T(8,128)(2,1)} %get-tuple-element.81.n2, bf16[256,512]{1,0:T(8,128)(2,1)} %collective-permute-done.20.n2p, bf16[256,512]{1,0:T(8,128)(2,1)} %get-tuple-element.86.fg, bf16[256,512]{1,0:T(8,128)(2,1)} %collective-permute-done.21.fgp, ...), custom_call_target="tpu_custom_call" | custom-call | flops 1600000000 | bytes 8167424 | tf_op jit(solution)/shard_map/ffn_weight/pallas_call | solution.py:41
  127.8 8.1 %collective-permute-done.13.par = bf16[512,256]{1,0:T(8,128)(2,1)S(1)} collective-permute-done((bf16[512,256]{1,0:T(8,128)(2,1)S(1)}, bf16[512,256]{1,0:T(8,128)(2,1)S(1)}, u32[]{:S(2)}, u32[]{:S(2)}) %collective-permute-start.13) | collective-permute-done | bytes 262176 | tf_op jit(solution)/shard_map/ppermute | solution.py:418
  135.9 0.7 copy-done.16
  136.6 3.4 %last.1 = (f32[256,512]{1,0:T(8,128)}, f32[8,512]{1,0:T(8,128)}) custom-call(s32[4]{0:T(128)} %broadcast_xor_fusion.tb, f32[512,256]{1,0:T(8,128)} %get-tuple-element.107.own, bf16[512,512]{1,0:T(8,128)(2,1)} %copy-done.11, bf16[512,256]{1,0:T(8,128)(2,1)} %copy-done.16, bf16[256,512]{1,0:T(8,128)(2,1)} %x0.5, f32[256,512]{1,0:T(8,128)} %get-tuple-element.110.mg, ...), custom_call_target="tpu_custom_call" | custom-call | flops 140000000 | bytes 3964944 | tf_op jit(solution)/shard_map/last/pallas_call | solution.py:41
  140.0 0.9 fusion
  140.8 5.8 %all-to-all-start.2 = ((bf16[8,48,512]{2,1,0:T(8,128)(2,1)}), bf16[8,48,512]{2,1,0:T(8,128)(2,1)S(1)}, u32[]{:S(2)}, u32[]{:S(2)}) async-start(bf16[8,48,512]{2,1,0:T(8,128)(2,1)} %bitcast.16), calls=%async_computation.2 | async-start | bytes 786432 | tf_op jit(solution)/shard_map/all_to_all | solution.py:562
  146.7 0.7 fusion.6
  147.8 3.4 %collective-permute-done.16 = f32[8,512]{1,0:T(8,128)S(1)} collective-permute-done((f32[8,512]{1,0:T(8,128)S(1)}, f32[8,512]{1,0:T(8,128)S(1)}, u32[]{:S(2)}, u32[]{:S(2)}) %collective-permute-start.16) | collective-permute-done | bytes 16416 | tf_op jit(solution)/shard_map/ppermute | solution.py:418
  151.2 1.1 reduce_sum.54
  152.3 6.7 %all-to-all-done.2 = bf16[8,48,512]{2,1,0:T(8,128)(2,1)S(1)} async-done(((bf16[8,48,512]{2,1,0:T(8,128)(2,1)}), bf16[8,48,512]{2,1,0:T(8,128)(2,1)S(1)}, u32[]{:S(2)}, u32[]{:S(2)}) %all-to-all-start.2) | async-done | bytes 393248 | tf_op jit(solution)/shard_map/all_to_all | solution.py:562
  159.0 0.8 broadcast_in_dim.58
  159.9 4.1 %all-to-all-start.1 = ((bf16[8,56,512]{2,1,0:T(8,128)(2,1)}), bf16[8,56,512]{2,1,0:T(8,128)(2,1)}, u32[]{:S(2)}, u32[]{:S(2)}) async-start(bf16[8,56,512]{2,1,0:T(8,128)(2,1)} %broadcast_in_dim.58), calls=%async_computation.1 | async-start | bytes 917504 | tf_op jit(solution)/shard_map/all_to_all | solution.py:568
  164.0 1.6 add_convert_fusion
  165.6 1.0 slice.181
  166.6 10.3 %all-to-all-done.1 = bf16[8,56,512]{2,1,0:T(8,128)(2,1)} async-done(((bf16[8,56,512]{2,1,0:T(8,128)(2,1)}), bf16[8,56,512]{2,1,0:T(8,128)(2,1)}, u32[]{:S(2)}, u32[]{:S(2)}) %all-to-all-start.1) | async-done | bytes 458784 | tf_op jit(solution)/shard_map/all_to_all | solution.py:568
  176.9 3.7 %all-to-all-start.4 = ((bf16[8,128,512]{2,1,0:T(8,128)(2,1)}), bf16[8,128,512]{2,1,0:T(8,128)(2,1)S(1)}, u32[]{:S(2)}, u32[]{:S(2)}) async-start(bf16[8,128,512]{2,1,0:T(8,128)(2,1)} %bitcast.18), calls=%async_computation.4 | async-start | bytes 2097152 | tf_op jit(solution)/shard_map/all_to_all | solution.py:562
  180.8 25.6 %all-to-all-done.4 = bf16[8,128,512]{2,1,0:T(8,128)(2,1)S(1)} async-done(((bf16[8,128,512]{2,1,0:T(8,128)(2,1)}), bf16[8,128,512]{2,1,0:T(8,128)(2,1)S(1)}, u32[]{:S(2)}, u32[]{:S(2)}) %all-to-all-start.4) | async-done | bytes 1048608 | tf_op jit(solution)/shard_map/all_to_all | solution.py:562
  206.4 0.8 broadcast_in_dim.59
  207.2 3.5 %all-to-all-start.3 = ((bf16[8,56,512]{2,1,0:T(8,128)(2,1)}), bf16[8,56,512]{2,1,0:T(8,128)(2,1)S(1)}, u32[]{:S(2)}, u32[]{:S(2)}) async-start(bf16[8,56,512]{2,1,0:T(8,128)(2,1)} %broadcast_in_dim.59), calls=%async_computation.3 | async-start | bytes 917504 | tf_op jit(solution)/shard_map/all_to_all | solution.py:568
  210.8 1.2 collective-permute-done.23
  212.3 3.4 %collective-permute-done.24 = f32[8,512]{1,0:T(8,128)S(1)} collective-permute-done((f32[8,512]{1,0:T(8,128)S(1)}, f32[8,512]{1,0:T(8,128)S(1)}, u32[]{:S(2)}, u32[]{:S(2)}) %collective-permute-start.24) | collective-permute-done | bytes 16416 | tf_op jit(solution)/shard_map/ppermute | solution.py:418
  216.0 8.0 %all-to-all-done.3 = bf16[8,56,512]{2,1,0:T(8,128)(2,1)S(1)} async-done(((bf16[8,56,512]{2,1,0:T(8,128)(2,1)}), bf16[8,56,512]{2,1,0:T(8,128)(2,1)S(1)}, u32[]{:S(2)}, u32[]{:S(2)}) %all-to-all-start.3) | async-done | bytes 458784 | tf_op jit(solution)/shard_map/all_to_all | solution.py:568
  224.0 1.1 broadcast_in_dim.61
  225.0 3.6 %all-to-all-start.5 = ((bf16[8,136,512]{2,1,0:T(8,128)(2,1)}), bf16[8,136,512]{2,1,0:T(8,128)(2,1)S(1)}, u32[]{:S(2)}, u32[]{:S(2)}) async-start(bf16[8,136,512]{2,1,0:T(8,128)(2,1)} %broadcast_in_dim.61), calls=%async_computation.5 | async-start | bytes 2228224 | tf_op jit(solution)/shard_map/all_to_all | solution.py:568
  228.7 1.0 slice.171
  229.9 0.8 copy.45
  230.7 0.8 copy.46
  231.5 0.8 copy.47
  232.4 0.9 convert_reduce_fusion.1
  234.5 0.9 fusion.8
  235.4 20.6 %all-to-all-done.5 = bf16[8,136,512]{2,1,0:T(8,128)(2,1)S(1)} async-done(((bf16[8,136,512]{2,1,0:T(8,128)(2,1)}), bf16[8,136,512]{2,1,0:T(8,128)(2,1)S(1)}, u32[]{:S(2)}, u32[]{:S(2)}) %all-to-all-start.5) | async-done | bytes 1114144 | tf_op jit(solution)/shard_map/all_to_all | solution.py:568
  256.3 1.6 fusion.7
  257.9 0.6 fusion.9
  (154 shorter events, 7.5 us)
Async XLA Ops:
  0.7 8.7 %copy-start.17 = (bf16[128,512]{1,0:T(8,128)(2,1)S(1)}, bf16[128,512]{1,0:T(8,128)(2,1)}, u32[]{:S(2)}) copy-start(bf16[128,512]{1,0:T(8,128)(2,1)} %param.32) | copy-start | bytes 393220
  0.7 8.7 %copy-start.18 = (bf16[128,512]{1,0:T(8,128)(2,1)S(1)}, bf16[128,512]{1,0:T(8,128)(2,1)}, u32[]{:S(2)}) copy-start(bf16[128,512]{1,0:T(8,128)(2,1)} %param.34) | copy-start | bytes 393220
  0.7 37.6 %copy-start.33 = (bf16[128]{0:T(256)(128)(2,1)S(1)}, bf16[128]{0:T(256)(128)(2,1)}, u32[]{:S(2)}) copy-start(bf16[128]{0:T(256)(128)(2,1)} %param.28) | copy-start | bytes 772
  0.7 37.5 %copy-start.32 = (bf16[128]{0:T(256)(128)(2,1)S(1)}, bf16[128]{0:T(256)(128)(2,1)}, u32[]{:S(2)}) copy-start(bf16[128]{0:T(256)(128)(2,1)} %param.31) | copy-start | bytes 772
  0.7 37.7 %copy-start.21 = (bf16[512,128]{1,0:T(8,128)(2,1)S(1)}, bf16[512,128]{1,0:T(8,128)(2,1)}, u32[]{:S(2)}) copy-start(bf16[512,128]{1,0:T(8,128)(2,1)} %param.27) | copy-start | bytes 393220
  0.7 37.7 %copy-start.20 = (bf16[512,128]{1,0:T(8,128)(2,1)S(1)}, bf16[512,128]{1,0:T(8,128)(2,1)}, u32[]{:S(2)}) copy-start(bf16[512,128]{1,0:T(8,128)(2,1)} %param.29) | copy-start | bytes 393220
  0.7 37.7 %copy-start.19 = (bf16[512,128]{1,0:T(8,128)(2,1)S(1)}, bf16[512,128]{1,0:T(8,128)(2,1)}, u32[]{:S(2)}) copy-start(bf16[512,128]{1,0:T(8,128)(2,1)} %param.30) | copy-start | bytes 393220
  0.7 9.6 %collective-permute-start = (bf16[256,512]{1,0:T(8,128)(2,1)}, bf16[256,512]{1,0:T(8,128)(2,1)S(1)}, u32[]{:S(2)}, u32[]{:S(2)}) collective-permute-start(bf16[256,512]{1,0:T(8,128)(2,1)} %x0.5), channel_id=1, source_target_pairs={{0,2},{1,3},{2,0},{3,1},{4,6},{5,7},{6,4},{7,5},{8,10},{9,11},{10,... | collective-permute-start | bytes 786440 | tf_op jit(solution)/shard_map/ppermute | solution.py:418
  4.4 37.4 %copy-start.24 = (bf16[512]{0:T(512)(128)(2,1)S(1)}, bf16[512]{0:T(512)(128)(2,1)}, u32[]{:S(2)}) copy-start(bf16[512]{0:T(512)(128)(2,1)} %param.25) | copy-start | bytes 3076
  4.5 37.4 %copy-start.25 = (bf16[512]{0:T(512)(128)(2,1)S(1)}, bf16[512]{0:T(512)(128)(2,1)}, u32[]{:S(2)}) copy-start(bf16[512]{0:T(512)(128)(2,1)} %param.26) | copy-start | bytes 3076
  4.5 37.4 %copy-start.26 = (bf16[512]{0:T(512)(128)(2,1)S(1)}, bf16[512]{0:T(512)(128)(2,1)}, u32[]{:S(2)}) copy-start(bf16[512]{0:T(512)(128)(2,1)} %param.33) | copy-start | bytes 3076
  4.5 37.4 %copy-start.27 = (bf16[512]{0:T(512)(128)(2,1)S(1)}, bf16[512]{0:T(512)(128)(2,1)}, u32[]{:S(2)}) copy-start(bf16[512]{0:T(512)(128)(2,1)} %param.35) | copy-start | bytes 3076
  4.5 37.4 %copy-start.28 = (bf16[512]{0:T(512)(128)(2,1)S(1)}, bf16[512]{0:T(512)(128)(2,1)}, u32[]{:S(2)}) copy-start(bf16[512]{0:T(512)(128)(2,1)} %param.36) | copy-start | bytes 3076
  4.5 37.4 %copy-start.29 = (bf16[512]{0:T(512)(128)(2,1)S(1)}, bf16[512]{0:T(512)(128)(2,1)}, u32[]{:S(2)}) copy-start(bf16[512]{0:T(512)(128)(2,1)} %param.37) | copy-start | bytes 3076
  4.5 37.4 %copy-start.30 = (bf16[512]{0:T(512)(128)(2,1)S(1)}, bf16[512]{0:T(512)(128)(2,1)}, u32[]{:S(2)}) copy-start(bf16[512]{0:T(512)(128)(2,1)} %param.41) | copy-start | bytes 3076
  4.5 37.4 %copy-start.31 = (bf16[512]{0:T(512)(128)(2,1)S(1)}, bf16[512]{0:T(512)(128)(2,1)}, u32[]{:S(2)}) copy-start(bf16[512]{0:T(512)(128)(2,1)} %param.43) | copy-start | bytes 3076
  4.5 38.1 %copy-start.37 = (s32[4]{0:T(128)S(1)}, s32[4]{0:T(128)}, u32[]{:S(2)}) copy-start(s32[4]{0:T(128)} %constant.9.clone) | copy-start | bytes 52
  9.4 45.8 %copy-start = (bf16[1160,512]{1,0:T(8,128)(2,1)}, bf16[1160,512]{1,0:T(8,128)(2,1)S(1)}, u32[]{:S(2)}) copy-start(bf16[1160,512]{1,0:T(8,128)(2,1)S(1)} %concatenate.38.f0) | copy-start | bytes 3563524
  9.4 45.7 %copy-start.2 = (bf16[256,512]{1,0:T(8,128)(2,1)}, bf16[256,512]{1,0:T(8,128)(2,1)S(1)}, u32[]{:S(2)}) copy-start(bf16[256,512]{1,0:T(8,128)(2,1)S(1)} %constant_dynamic-update-slice_fusion.e0) | copy-start | bytes 786436
  10.3 28.0 %copy-start.34 = (bf16[256,512]{1,0:T(8,128)(2,1)}, bf16[256,512]{1,0:T(8,128)(2,1)S(1)}, u32[]{:S(2)}) copy-start(bf16[256,512]{1,0:T(8,128)(2,1)S(1)} %collective-permute-done.x1) | copy-start | bytes 786436
  10.3 27.4 %collective-permute-start.8 = (bf16[1160,512]{1,0:T(8,128)(2,1)S(1)}, bf16[1160,512]{1,0:T(8,128)(2,1)}, u32[]{:S(2)}, u32[]{:S(2)}) collective-permute-start(bf16[1160,512]{1,0:T(8,128)(2,1)S(1)} %concatenate.38.f0), channel_id=1, source_target_pairs={{0,2},{1,3},{2,0},{3,1},{4,6},{5,7},{6,4},{7,5},{8,10},{9,11},{10,... | collective-permute-start | bytes 3563528 | tf_op jit(solution)/shard_map/ppermute | solution.py:418
  12.0 54.9 %collective-permute-start.9 = (bf16[1160,512]{1,0:T(8,128)(2,1)S(1)}, bf16[1160,512]{1,0:T(8,128)(2,1)S(1)}, u32[]{:S(2)}, u32[]{:S(2)}) collective-permute-start(bf16[1160,512]{1,0:T(8,128)(2,1)S(1)} %concatenate.38.f0), channel_id=1, source_target_pairs={{0,1},{1,0},{2,3},{3,2},{4,5},{5,4},{6,7},{7,6},{8,9},{9,8},{10,11... | collective-permute-start | bytes 3563528 | tf_op jit(solution)/shard_map/ppermute | solution.py:418
  37.7 29.2 %collective-permute-start.10 = (bf16[1160,512]{1,0:T(8,128)(2,1)}, bf16[1160,512]{1,0:T(8,128)(2,1)}, u32[]{:S(2)}, u32[]{:S(2)}) collective-permute-start(bf16[1160,512]{1,0:T(8,128)(2,1)} %collective-permute-done.8.f1), channel_id=1, source_target_pairs={{0,1},{1,0},{2,3},{3,2},{4,5},{5,4},{6,7},{7,6},{8,9},{9,8},{10,11... | collective-permute-start | bytes 3563528 | tf_op jit(solution)/shard_map/ppermute | solution.py:418
  37.7 3.9 %collective-permute-start.1 = (bf16[256,512]{1,0:T(8,128)(2,1)}, bf16[256,512]{1,0:T(8,128)(2,1)}, u32[]{:S(2)}, u32[]{:S(2)}) collective-permute-start(bf16[256,512]{1,0:T(8,128)(2,1)} %x0.5), channel_id=1, source_target_pairs={{0,1},{1,0},{2,3},{3,2},{4,5},{5,4},{6,7},{7,6},{8,9},{9,8},{10,11... | collective-permute-start | bytes 786440 | tf_op jit(solution)/shard_map/ppermute | solution.py:418
  38.5 4.6 %copy-start.7 = (bf16[520,384]{1,0:T(8,128)(2,1)}, bf16[520,384]{1,0:T(8,128)(2,1)S(1)}, u32[]{:S(2)}) copy-start(bf16[520,384]{1,0:T(8,128)(2,1)S(1)} %maximum_maximum_fusion.qkv0) | copy-start | bytes 1198084
  38.5 4.6 %collective-permute-start.3 = (bf16[520,384]{1,0:T(8,128)(2,1)S(1)}, bf16[520,384]{1,0:T(8,128)(2,1)}, u32[]{:S(2)}, u32[]{:S(2)}) collective-permute-start(bf16[520,384]{1,0:T(8,128)(2,1)S(1)} %maximum_maximum_fusion.qkv0), channel_id=1, source_target_pairs={{0,1},{1,0},{2,3},{3,2},{4,5},{5,4},{6,7},{7,6},{8,9},{9,8},{10,11... | collective-permute-start | bytes 1198088 | tf_op jit(solution)/shard_map/ppermute | solution.py:418
  38.6 8.7 %collective-permute-start.5 = (bf16[256,512]{1,0:T(8,128)(2,1)S(1)}, bf16[256,512]{1,0:T(8,128)(2,1)S(1)}, u32[]{:S(2)}, u32[]{:S(2)}) collective-permute-start(bf16[256,512]{1,0:T(8,128)(2,1)S(1)} %constant_dynamic-update-slice_fusion.e0), channel_id=1, source_target_pairs={{0,2},{1,3},{2,0},{3,1},{4,6},{5,7},{6,4},{7,5},{8,10},{9,11},{10,... | collective-permute-start | bytes 786440 | tf_op jit(solution)/shard_map/ppermute | solution.py:418
  41.7 5.7 %collective-permute-start.2 = (bf16[256,512]{1,0:T(8,128)(2,1)}, bf16[256,512]{1,0:T(8,128)(2,1)}, u32[]{:S(2)}, u32[]{:S(2)}) collective-permute-start(bf16[256,512]{1,0:T(8,128)(2,1)} %copy-done.34), channel_id=1, source_target_pairs={{0,1},{1,0},{2,3},{3,2},{4,5},{5,4},{6,7},{7,6},{8,9},{9,8},{10,11... | collective-permute-start | bytes 786440 | tf_op jit(solution)/shard_map/ppermute | solution.py:418
  43.1 19.4 %collective-permute-start.6 = (bf16[256,512]{1,0:T(8,128)(2,1)S(1)}, bf16[256,512]{1,0:T(8,128)(2,1)S(1)}, u32[]{:S(2)}, u32[]{:S(2)}) collective-permute-start(bf16[256,512]{1,0:T(8,128)(2,1)S(1)} %constant_dynamic-update-slice_fusion.e0), channel_id=1, source_target_pairs={{0,1},{1,0},{2,3},{3,2},{4,5},{5,4},{6,7},{7,6},{8,9},{9,8},{10,11... | collective-permute-start | bytes 786440 | tf_op jit(solution)/shard_map/ppermute | solution.py:418
  47.3 7.8 %copy-start.3 = (bf16[256,512]{1,0:T(8,128)(2,1)}, bf16[256,512]{1,0:T(8,128)(2,1)S(1)}, u32[]{:S(2)}) copy-start(bf16[256,512]{1,0:T(8,128)(2,1)S(1)} %collective-permute-done.5.e1) | copy-start | bytes 786436
  47.3 15.2 %collective-permute-start.7 = (bf16[256,512]{1,0:T(8,128)(2,1)S(1)}, bf16[256,512]{1,0:T(8,128)(2,1)S(1)}, u32[]{:S(2)}, u32[]{:S(2)}) collective-permute-start(bf16[256,512]{1,0:T(8,128)(2,1)S(1)} %collective-permute-done.5.e1), channel_id=1, source_target_pairs={{0,1},{1,0},{2,3},{3,2},{4,5},{5,4},{6,7},{7,6},{8,9},{9,8},{10,11... | collective-permute-start | bytes 786440 | tf_op jit(solution)/shard_map/ppermute | solution.py:418
  55.2 7.3 %collective-permute-start.4 = (bf16[256,256]{1,0:T(8,128)(2,1)}, bf16[256,256]{1,0:T(8,128)(2,1)S(1)}, u32[]{:S(2)}, u32[]{:S(2)}) collective-permute-start(bf16[256,256]{1,0:T(8,128)(2,1)} %get-tuple-element.79), channel_id=1, source_target_pairs={{0,2},{1,3},{2,0},{3,1},{4,6},{5,7},{6,4},{7,5},{8,10},{9,11},{10,... | collective-permute-start | bytes 393224 | tf_op jit(solution)/shard_map/ppermute | solution.py:418
  66.9 1.0 copy-start.1
  81.2 5.0 %copy-start.35 = (bf16[256,256]{1,0:T(8,128)(2,1)S(1)}, bf16[256,256]{1,0:T(8,128)(2,1)}, u32[]{:S(2)}) copy-start(bf16[256,256]{1,0:T(8,128)(2,1)} %get-tuple-element.91) | copy-start | bytes 393220
  84.9 32.7 %collective-permute-start.18 = (bf16[768,512]{1,0:T(8,128)(2,1)}, bf16[768,512]{1,0:T(8,128)(2,1)}, u32[]{:S(2)}, u32[]{:S(2)}) collective-permute-start(bf16[768,512]{1,0:T(8,128)(2,1)} %get-tuple-element.119), channel_id=1, source_target_pairs={{0,1},{1,0},{2,3},{3,2},{4,5},{5,4},{6,7},{7,6},{8,9},{9,8},{10,11... | collective-permute-start | bytes 2359304 | tf_op jit(solution)/shard_map/ppermute | solution.py:418
  86.2 7.5 %collective-permute-start.11 = (bf16[256,256]{1,0:T(8,128)(2,1)S(1)}, bf16[256,256]{1,0:T(8,128)(2,1)S(1)}, u32[]{:S(2)}, u32[]{:S(2)}) collective-permute-start(bf16[256,256]{1,0:T(8,128)(2,1)S(1)} %copy-done.35), channel_id=1, source_target_pairs={{0,2},{1,3},{2,0},{3,1},{4,6},{5,7},{6,4},{7,5},{8,10},{9,11},{10,... | collective-permute-start | bytes 393224 | tf_op jit(solution)/shard_map/ppermute | solution.py:418
  94.4 10.2 %copy-start.12 = (bf16[256,512]{1,0:T(8,128)(2,1)S(1)}, bf16[256,512]{1,0:T(8,128)(2,1)}, u32[]{:S(2)}) copy-start(bf16[256,512]{1,0:T(8,128)(2,1)} %get-tuple-element.81.n2) | copy-start | bytes 786436
  102.7 8.2 %copy-start.13 = (f32[384,512]{1,0:T(8,128)S(1)}, f32[384,512]{1,0:T(8,128)}, u32[]{:S(2)}) copy-start(f32[384,512]{1,0:T(8,128)} %get-tuple-element.113) | copy-start | bytes 2359300
  102.7 8.2 %collective-permute-start.14 = (bf16[384,512]{1,0:T(8,128)(2,1)}, bf16[384,512]{1,0:T(8,128)(2,1)S(1)}, u32[]{:S(2)}, u32[]{:S(2)}) collective-permute-start(bf16[384,512]{1,0:T(8,128)(2,1)} %get-tuple-element.114), channel_id=1, source_target_pairs={{0,1},{1,0},{2,3},{3,2},{4,5},{5,4},{6,7},{7,6},{8,9},{9,8},{10,11... | collective-permute-start | bytes 1179656 | tf_op jit(solution)/shard_map/ppermute | solution.py:418
  104.6 16.7 %collective-permute-start.20 = (bf16[256,512]{1,0:T(8,128)(2,1)S(1)}, bf16[256,512]{1,0:T(8,128)(2,1)}, u32[]{:S(2)}, u32[]{:S(2)}) collective-permute-start(bf16[256,512]{1,0:T(8,128)(2,1)S(1)} %copy-done.12), channel_id=1, source_target_pairs={{0,2},{1,3},{2,0},{3,1},{4,6},{5,7},{6,4},{7,5},{8,10},{9,11},{10,... | collective-permute-start | bytes 786440 | tf_op jit(solution)/shard_map/ppermute | solution.py:418
  104.9 16.4 %collective-permute-start.21 = (bf16[256,512]{1,0:T(8,128)(2,1)}, bf16[256,512]{1,0:T(8,128)(2,1)}, u32[]{:S(2)}, u32[]{:S(2)}) collective-permute-start(bf16[256,512]{1,0:T(8,128)(2,1)} %get-tuple-element.86.fg), channel_id=1, source_target_pairs={{0,2},{1,3},{2,0},{3,1},{4,6},{5,7},{6,4},{7,5},{8,10},{9,11},{10,... | collective-permute-start | bytes 786440 | tf_op jit(solution)/shard_map/ppermute | solution.py:418
  110.2 7.4 %copy-start.10 = (f32[768,512]{1,0:T(8,128)S(1)}, f32[768,512]{1,0:T(8,128)}, u32[]{:S(2)}) copy-start(f32[768,512]{1,0:T(8,128)} %get-tuple-element.118) | copy-start | bytes 4718596
  110.2 9.3 %collective-permute-start.12 = (bf16[512,512]{1,0:T(8,128)(2,1)}, bf16[512,512]{1,0:T(8,128)(2,1)S(1)}, u32[]{:S(2)}, u32[]{:S(2)}) collective-permute-start(bf16[512,512]{1,0:T(8,128)(2,1)} %get-tuple-element.108), channel_id=1, source_target_pairs={{0,1},{1,0},{2,3},{3,2},{4,5},{5,4},{6,7},{7,6},{8,9},{9,8},{10,11... | collective-permute-start | bytes 1572872 | tf_op jit(solution)/shard_map/ppermute | solution.py:418
  111.8 29.0 %all-to-all-start = ((bf16[8,48,512]{2,1,0:T(8,128)(2,1)}), bf16[8,48,512]{2,1,0:T(8,128)(2,1)}, u32[]{:S(2)}, u32[]{:S(2)}) async-start(bf16[8,48,512]{2,1,0:T(8,128)(2,1)} %bitcast.1), calls=%async_computation | async-start | bytes 786432 | tf_op jit(solution)/shard_map/all_to_all | solution.py:562
  117.6 1.9 copy-start.15
  119.1 20.9 %collective-permute-start.19 = (bf16[384,512]{1,0:T(8,128)(2,1)S(1)}, bf16[384,512]{1,0:T(8,128)(2,1)S(1)}, u32[]{:S(2)}, u32[]{:S(2)}) collective-permute-start(bf16[384,512]{1,0:T(8,128)(2,1)S(1)} %slice.233), channel_id=1, source_target_pairs={{0,2},{1,3},{2,0},{3,1},{4,6},{5,7},{6,4},{7,5},{8,10},{9,11},{10,... | collective-permute-start | bytes 1179656 | tf_op jit(solution)/shard_map/ppermute | solution.py:418
  119.5 7.8 %copy-start.11 = (bf16[512,512]{1,0:T(8,128)(2,1)}, bf16[512,512]{1,0:T(8,128)(2,1)S(1)}, u32[]{:S(2)}) copy-start(bf16[512,512]{1,0:T(8,128)(2,1)S(1)} %collective-permute-done.12.sib) | copy-start | bytes 1572868
  119.6 16.3 %collective-permute-start.13 = (bf16[512,256]{1,0:T(8,128)(2,1)S(1)}, bf16[512,256]{1,0:T(8,128)(2,1)S(1)}, u32[]{:S(2)}, u32[]{:S(2)}) collective-permute-start(bf16[512,256]{1,0:T(8,128)(2,1)S(1)} %add_convert_fusion.2), channel_id=1, source_target_pairs={{0,2},{1,3},{2,0},{3,1},{4,6},{5,7},{6,4},{7,5},{8,10},{9,11},{10,... | collective-permute-start | bytes 786440 | tf_op jit(solution)/shard_map/ppermute | solution.py:418
  121.3 25.3 %collective-permute-start.17 = (f32[1,256]{1,0:T(1,128)S(1)}, f32[1,256]{1,0:T(1,128)S(1)}, u32[]{:S(2)}, u32[]{:S(2)}) collective-permute-start(f32[1,256]{1,0:T(1,128)S(1)} %bitcast.52), channel_id=1, source_target_pairs={{0,1},{1,0},{2,3},{3,2},{4,5},{5,4},{6,7},{7,6},{8,9},{9,8},{10,11... | collective-permute-start | bytes 3080 | tf_op jit(solution)/shard_map/ppermute | solution.py:418
  127.3 36.7 %collective-permute-start.22 = (bf16[1032,512]{1,0:T(8,128)(2,1)}, bf16[1032,512]{1,0:T(8,128)(2,1)}, u32[]{:S(2)}, u32[]{:S(2)}) collective-permute-start(bf16[1032,512]{1,0:T(8,128)(2,1)} %get-tuple-element.123), channel_id=1, source_target_pairs={{0,1},{1,0},{2,3},{3,2},{4,5},{5,4},{6,7},{7,6},{8,9},{9,8},{10,11... | collective-permute-start | bytes 3170312 | tf_op jit(solution)/shard_map/ppermute | solution.py:418
  139.9 7.4 %copy-start.23 = (f32[8,512]{1,0:T(8,128)S(1)}, f32[8,512]{1,0:T(8,128)}, u32[]{:S(2)}) copy-start(f32[8,512]{1,0:T(8,128)} %get-tuple-element.115) | copy-start | bytes 49156
  139.9 7.4 %collective-permute-start.15 = (f32[8,512]{1,0:T(8,128)}, f32[8,512]{1,0:T(8,128)S(1)}, u32[]{:S(2)}, u32[]{:S(2)}) collective-permute-start(f32[8,512]{1,0:T(8,128)} %get-tuple-element.115), channel_id=1, source_target_pairs={{0,1},{1,0},{2,3},{3,2},{4,5},{5,4},{6,7},{7,6},{8,9},{9,8},{10,11... | collective-permute-start | bytes 49160 | tf_op jit(solution)/shard_map/ppermute | solution.py:418
  140.8 23.2 %copy-start.6 = (f32[1032,512]{1,0:T(8,128)S(1)}, f32[1032,512]{1,0:T(8,128)}, u32[]{:S(2)}) copy-start(f32[1032,512]{1,0:T(8,128)} %get-tuple-element.122) | copy-start | bytes 6340612
  140.8 18.2 %all-to-all-start.2 = ((bf16[8,48,512]{2,1,0:T(8,128)(2,1)}), bf16[8,48,512]{2,1,0:T(8,128)(2,1)S(1)}, u32[]{:S(2)}, u32[]{:S(2)}) async-start(bf16[8,48,512]{2,1,0:T(8,128)(2,1)} %bitcast.16), calls=%async_computation.2 | async-start | bytes 786432 | tf_op jit(solution)/shard_map/all_to_all | solution.py:562
  147.4 3.8 %collective-permute-start.16 = (f32[8,512]{1,0:T(8,128)S(1)}, f32[8,512]{1,0:T(8,128)S(1)}, u32[]{:S(2)}, u32[]{:S(2)}) collective-permute-start(f32[8,512]{1,0:T(8,128)S(1)} %add.43), channel_id=1, source_target_pairs={{0,2},{1,3},{2,0},{3,1},{4,6},{5,7},{6,4},{7,5},{8,10},{9,11},{10,... | collective-permute-start | bytes 49160 | tf_op jit(solution)/shard_map/ppermute | solution.py:418
  159.0 5.0 %copy-start.8 = (bf16[8,48,512]{2,1,0:T(8,128)(2,1)}, bf16[8,48,512]{2,1,0:T(8,128)(2,1)S(1)}, u32[]{:S(2)}) copy-start(bf16[8,48,512]{2,1,0:T(8,128)(2,1)S(1)} %all-to-all-done.2) | copy-start | bytes 1179652
  159.9 17.1 %all-to-all-start.1 = ((bf16[8,56,512]{2,1,0:T(8,128)(2,1)}), bf16[8,56,512]{2,1,0:T(8,128)(2,1)}, u32[]{:S(2)}, u32[]{:S(2)}) async-start(bf16[8,56,512]{2,1,0:T(8,128)(2,1)} %broadcast_in_dim.58), calls=%async_computation.1 | async-start | bytes 917504 | tf_op jit(solution)/shard_map/all_to_all | solution.py:568
  166.6 14.0 %copy-start.9 = (bf16[8,48,512]{2,1,0:T(8,128)(2,1)S(1)}, bf16[8,48,512]{2,1,0:T(8,128)(2,1)}, u32[]{:S(2)}) copy-start(bf16[8,48,512]{2,1,0:T(8,128)(2,1)} %copy-done.8) | copy-start | bytes 1179652
  176.9 33.8 %copy-start.22 = (f32[8,512]{1,0:T(8,128)S(1)}, f32[8,512]{1,0:T(8,128)}, u32[]{:S(2)}) copy-start(f32[8,512]{1,0:T(8,128)} %get-tuple-element.124) | copy-start | bytes 49156
  176.9 29.4 %all-to-all-start.4 = ((bf16[8,128,512]{2,1,0:T(8,128)(2,1)}), bf16[8,128,512]{2,1,0:T(8,128)(2,1)S(1)}, u32[]{:S(2)}, u32[]{:S(2)}) async-start(bf16[8,128,512]{2,1,0:T(8,128)(2,1)} %bitcast.18), calls=%async_computation.4 | async-start | bytes 2097152 | tf_op jit(solution)/shard_map/all_to_all | solution.py:562
  207.2 16.8 %all-to-all-start.3 = ((bf16[8,56,512]{2,1,0:T(8,128)(2,1)}), bf16[8,56,512]{2,1,0:T(8,128)(2,1)S(1)}, u32[]{:S(2)}, u32[]{:S(2)}) async-start(bf16[8,56,512]{2,1,0:T(8,128)(2,1)} %broadcast_in_dim.59), calls=%async_computation.3 | async-start | bytes 917504 | tf_op jit(solution)/shard_map/all_to_all | solution.py:568
  210.7 1.2 collective-permute-start.23
  212.0 3.7 %collective-permute-start.24 = (f32[8,512]{1,0:T(8,128)S(1)}, f32[8,512]{1,0:T(8,128)S(1)}, u32[]{:S(2)}, u32[]{:S(2)}) collective-permute-start(f32[8,512]{1,0:T(8,128)S(1)} %add.52), channel_id=1, source_target_pairs={{0,2},{1,3},{2,0},{3,1},{4,6},{5,7},{6,4},{7,5},{8,10},{9,11},{10,... | collective-permute-start | bytes 49160 | tf_op jit(solution)/shard_map/ppermute | solution.py:418
  225.0 31.0 %all-to-all-start.5 = ((bf16[8,136,512]{2,1,0:T(8,128)(2,1)}), bf16[8,136,512]{2,1,0:T(8,128)(2,1)S(1)}, u32[]{:S(2)}, u32[]{:S(2)}) async-start(bf16[8,136,512]{2,1,0:T(8,128)(2,1)} %broadcast_in_dim.61), calls=%async_computation.5 | async-start | bytes 2228224 | tf_op jit(solution)/shard_map/all_to_all | solution.py:568
  (5 other events, 3.6 us)

commit v2 on v1

--- a/solution.py
+++ b/solution.py
@@ -1,4 +1,5 @@
 import functools
+import math
 
 import jax
 import jax.numpy as jnp
@@ -14,7 +15,7 @@
 NEG = -1e30
 PX = 2
 LOCAL = (0, PX, 1, 1 ^ PX)
-VMEM_LIMIT = 60 * 1024 * 1024
+SPARE = 4 * 1024 * 1024
 
 
 def nn(a, b):
@@ -33,21 +34,19 @@
 SM = pl.BlockSpec(memory_space=pltpu.SMEM)
 
 
-def call(body, outs, args, smem=0, scratch=(), flops=0, nbytes=None, name=None, aliases=None):
-    if nbytes is None:
-        nbytes = sum(a.size * a.dtype.itemsize for a in args) + sum(
-            o.size * o.dtype.itemsize for o in outs
-        )
+def call(body, outs, args, smem=0, scratch=(), name=None, space=VM, limit=None):
+    nbytes = sum(a.size * a.dtype.itemsize for a in args) + sum(o.size * o.dtype.itemsize for o in outs)
+    held = sum(math.prod(s.shape) * 4 for s in scratch)
+    limit = limit or nbytes + held + SPARE
     return pl.pallas_call(
         body,
         out_shape=tuple(outs),
-        in_specs=[SM] * smem + [VM] * (len(args) - smem),
+        in_specs=[SM] * smem + [space] * (len(args) - smem),
         out_specs=tuple([VM] * len(outs)),
         scratch_shapes=list(scratch),
-        compiler_params=pltpu.CompilerParams(vmem_limit_bytes=VMEM_LIMIT),
-        cost_estimate=pl.CostEstimate(flops=flops, bytes_accessed=nbytes, transcendentals=0),
+        compiler_params=pltpu.CompilerParams(vmem_limit_bytes=limit),
+        cost_estimate=pl.CostEstimate(flops=0, bytes_accessed=0, transcendentals=0),
         name=name,
-        input_output_aliases=aliases or {},
     )(*args)
 
 
@@ -85,11 +84,11 @@
     m_sc[...] = jnp.full(m_sc.shape, NEG, F32)
     l_sc[...] = jnp.zeros(l_sc.shape, F32)
     o_sc[...] = jnp.zeros(o_sc.shape, F32)
-    seg_q = segv[tq].astype(F32)
+    seg_q = segv[0:1, pl.ds(pl.multiple_of(tq * rows, rows), rows)].astype(F32)
 
     def active(kb):
         tk = tb[kb]
-        return (tk <= tq) & (segs[tk, 0, rows - 1] >= segs[tq, 0, 0])
+        return (tk <= tq) & (segs[0, tk * rows + rows - 1] >= segs[0, tq * rows])
 
     @pl.loop(0, 4)
     def _(kb):
@@ -137,7 +136,7 @@
 
 def fill_segc(segc, segv):
     for t in range(4):
-        row = jnp.broadcast_to(segv[t].astype(F32), (128, 256))
+        row = jnp.broadcast_to(segv[0:1, 256 * t : 256 * t + 256].astype(F32), (128, 256))
         segc[256 * t : 256 * t + 256, :] = row.T
 
 
@@ -209,21 +208,41 @@
     gate_ref[...] = gate
 
 
-def ffn_kernel(
-    tb, n2, mid, ct, vecs, f0, f1, f2, f3,
-    out_ref, fg_ref, ltg_ref, hid_ref, slope_ref,
-    gw,
-):
-    gather_gate(tb, (f0, f1, f2, f3), 1024, gw)
+def pair_up(a, b, start):
+    return jnp.concatenate([a[start : start + 128, :], b[start : start + 128, :]], axis=0)
+
+
+def pair_bias(a, b):
+    return jnp.concatenate([a[256:257, 0:128], b[256:257, 0:128]], axis=1).astype(F32)
+
+
+def ffn_first_kernel(
+    tb, n2, vecs, win0, wback0, c2,
+    total_ref, hid_ref, slope_ref,
+):
     n2v = n2[...]
     total = jnp.zeros((256, 512), F32)
-    for i, f in enumerate((f0, f2, f1, f3)):
-        u = nn(n2v, f[0:512, :]) + f[1152:1153, :].astype(F32)
-        value, slope = gelu_parts(u)
+    for i, (b, w, wb) in enumerate(((vecs[8:9, :], win0[...], wback0[...]), (c2[384:385, :], c2[392:904, :], c2[904:1416, :]))):
+        value, slope = gelu_parts(nn(n2v, w) + b.astype(F32))
         value = value.astype(BF16)
         hid_ref[:, 512 * i : 512 * i + 512] = value
         slope_ref[:, 512 * i : 512 * i + 512] = slope.astype(BF16)
-        total = total + nn(value, f[512:1024, :])
+        total = total + nn(value, wb)
+    total_ref[...] = total
+
+
+def ffn_kernel(
+    tb, n2, mid, ct, vecs, e0, e1, e2, e3, total0, s0, s1, s2, s3, s4, s5, s6, s7,
+    out_ref, fg_ref, ltg_ref, slope_ref,
+    gw,
+):
+    gather_gate(tb, (e0, e1, e2, e3), 256, gw)
+    n2v = n2[...]
+    total = total0[...]
+    for i, (a, b) in enumerate(((s0, s1), (s2, s3), (s4, s5), (s6, s7))):
+        value, slope = gelu_parts(nt(n2v, pair_up(a, b, 0)) + pair_bias(a, b))
+        slope_ref[:, 256 * i : 256 * i + 256] = slope.astype(BF16)
+        total = total + nn(value.astype(BF16), pair_up(a, b, 128))
     ffn = total + vecs[6:7, :]
     gate = sigmoid(nn(n2v, gw[...]) + vecs[7:8, :])
     up = ct[...].astype(F32)
@@ -233,20 +252,22 @@
 
 
 def back_kernel(
-    tb, fg, ltg, slope, mid, branch, gate, ct, vecs, f0, f1, f2, f3, e0, e1, e2, e3,
+    tb, fg, ltg, slope0, slope1, mid, branch, gate, ct, vecs, e0, e1, e2, e3,
+    win0, wback0, s0, s1, s2, s3, s4, s5, s6, s7,
     dot_ref, dotp_ref, mg_ref, bg_ref, log_ref, hg_ref, sums_ref,
     gw,
 ):
-    gather_gate(tb, (f0, f1, f2, f3), 1024, gw)
+    gather_gate(tb, (e0, e1, e2, e3), 256, gw)
     fgv = fg[...]
     ltgv = ltg[...]
     ng = nt(ltgv, gw[...])
-    for i, f in enumerate((f0, f2, f1, f3)):
-        hg = nt(fgv, f[512:1024, :]) * slope[:, 512 * i : 512 * i + 512].astype(F32)
-        hg = hg.astype(BF16)
-        if i < 2:
-            hg_ref[:, 512 * i : 512 * i + 512] = hg
-        ng = ng + nt(hg, f[0:512, :])
+    for i, (w, wb) in enumerate(((win0[...], wback0[...]), (e2[392:904, :], e2[904:1416, :]))):
+        hg = (nt(fgv, wb) * slope0[:, 512 * i : 512 * i + 512].astype(F32)).astype(BF16)
+        hg_ref[:, 512 * i : 512 * i + 512] = hg
+        ng = ng + nt(hg, w)
+    for i, (a, b) in enumerate(((s0, s1), (s2, s3), (s4, s5), (s6, s7))):
+        hg = (nt(fgv, pair_up(a, b, 128)) * slope1[:, 256 * i : 256 * i + 256].astype(F32)).astype(BF16)
+        ng = ng + nn(hg, pair_up(a, b, 0))
     unit, inverse = norm_unit(mid[...])
     g = ng * vecs[4:5, :]
     back = inverse * (g - jnp.mean(g, axis=-1, keepdims=True) - unit * jnp.mean(g * unit, axis=-1, keepdims=True))
@@ -267,32 +288,43 @@
         sums_ref[i : i + 1, :] = jnp.sum(r, axis=0, keepdims=True)
 
 
-def ffn_weight_kernel(
-    n2, n2p, fg, fgp, hid, hg, f0, f2,
+def ffn_back_weight_kernel(
+    tb, n2p, fg, fgp, hid, vecs, win0, c2,
+    keep_ref, send_ref, slope_ref,
+):
+    fgv, fgpv, n2pv = fg[...], fgp[...], n2p[...]
+    for i, (b, w) in enumerate(((vecs[8:9, :], win0[...]), (c2[384:385, :], c2[392:904, :]))):
+        cols = slice(512 * i, 512 * i + 512)
+        value, slope = gelu_parts(nn(n2pv, w) + b.astype(F32))
+        slope_ref[:, cols] = slope.astype(BF16)
+        wback = tn(hid[:, cols], fgv) + tn(value.astype(BF16), fgpv)
+        dst = keep_ref if i == 0 else send_ref
+        dst[...] = wback.astype(dst.dtype)
+
+
+def ffn_in_weight_kernel(
+    tb, n2, n2p, fgp, hg, slope, wback0, c2,
     keep_ref, send_ref,
 ):
-    n2v, n2pv, fgv, fgpv = n2[...], n2p[...], fg[...], fgp[...]
-    for i, f in enumerate((f0, f2)):
+    n2v, n2pv, fgpv = n2[...], n2p[...], fgp[...]
+    for i, wb in enumerate((wback0[...], c2[904:1416, :])):
         cols = slice(512 * i, 512 * i + 512)
-        u = nn(n2pv, f[0:512, :]) + f[1152:1153, :].astype(F32)
-        value, slope = gelu_parts(u)
-        hidp = value.astype(BF16)
-        hgp = (nt(fgpv, f[512:1024, :]) * slope).astype(BF16)
+        hgp = (nt(fgpv, wb) * slope[:, cols].astype(F32)).astype(BF16)
         hgo = hg[:, cols]
         win = tn(n2v, hgo) + tn(n2pv, hgp)
-        wback = tn(hid[:, cols], fgv) + tn(hidp, fgpv)
         bias = jnp.sum(hgo.astype(F32), axis=0, keepdims=True) + jnp.sum(hgp.astype(F32), axis=0, keepdims=True)
         dst = keep_ref if i == 0 else send_ref
         dst[0:512, :] = win.astype(dst.dtype)
-        dst[512:1024, :] = wback.astype(dst.dtype)
-        dst[1024:1032, :] = jnp.broadcast_to(bias, (8, 512)).astype(dst.dtype)
+        dst[512:520, :] = jnp.broadcast_to(bias, (8, 512)).astype(dst.dtype)
 
 
 def small_weight_kernel(
-    tb, n, n2, ltg, log, att, attp, bg,
+    tb, n, n2, ltg, log, att, attp, bg, sums,
     keep_ref, send_ref,
     g1, g2,
 ):
+    keep_ref[768:776, :] = sums[...]
+    send_ref[768:776, :] = sums[...].astype(BF16)
     g2[...] = tn(n2[...], ltg[...])
     g1[...] = tn(n[0:256, :], log[...])
     bgv = bg[...]
@@ -306,7 +338,7 @@
         dst[base + 256 : base + 384, :] = wo[i].astype(dst.dtype)
 
 
-def prepare_kernel(n, k, qkv0, qkv1, v_ref, kt_ref):
+def prepare_kernel(tb, n, k, qkv0, qkv1, v_ref, kt_ref):
     nv = n[...]
     for c, w in enumerate((qkv0, qkv1)):
         v = nn(nv, w[0:512, 256:384]) + w[512:513, 256:384].astype(F32)
@@ -333,7 +365,7 @@
     def _(kb):
         tk = tb[kb]
 
-        @pl.when((tk <= tq) & (segs[tk, 0, rows - 1] >= segs[tq, 0, 0]))
+        @pl.when((tk <= tq) & (segs[0, tk * rows + rows - 1] >= segs[0, tq * rows]))
         def _():
             ks = pl.ds(pl.multiple_of(kb * rows, rows), rows)
             for h in range(4):
@@ -360,7 +392,7 @@
 
 def back_second_kernel(
     tb, segs, p, dot, ot, invl, qt, kt, v, dk0, dv0, dq0, n,
-    dqt_ref, dkt_ref, dvt_ref, keep_ref, send_ref, bias_ref,
+    dqt_ref, dkt_ref, dvt_ref, keep_ref, send_ref,
     dk, dv, dq, doz, dos, dlt,
 ):
     dk[...] = dk0[...]
@@ -379,11 +411,14 @@
         send_ref[128 * i : 128 * i + 128, :] = w[128:256, :].astype(BF16)
     ones_q = jnp.ones((8, 512), BF16)
     ones_v = jnp.ones((8, 1024), BF16)
-    bias_ref[:, 0:256] = nt(ones_q, dqt_ref[...])
-    bias_ref[:, 256:512] = nt(ones_v, dvt_ref[...])
-
-
-def input_kernel(dqt, dkt, dvt, qkv0, qkv1, own_ref, par_ref, send_ref):
+    bq = nt(ones_q, dqt_ref[...])
+    bv = nt(ones_v, dvt_ref[...])
+    empty = jnp.zeros((8, 256), F32)
+    keep_ref[384:392, :] = jnp.concatenate([bq[:, 0:128], bv[:, 0:128], empty], axis=1)
+    send_ref[384:392, :] = jnp.concatenate([bq[:, 128:256], bv[:, 128:256], empty], axis=1).astype(BF16)
+
+
+def input_kernel(tb, dqt, dkt, dvt, qkv0, qkv1, own_ref, par_ref, send_ref):
     def weight(part):
         cols = slice(128 * part, 128 * part + 128)
         return jnp.concatenate([qkv0[0:512, cols], qkv1[0:512, cols]], axis=1)
@@ -409,6 +444,149 @@
     sums_ref[1:2, :] = jnp.sum(ng, axis=0, keepdims=True)
 
 
+def pack_kernel(
+    pos, w_in, w_back, w_out, g1, g2, wq, wk, wv, *refs,
+):
+    vectors, (s_ref, e_ref, c_ref, qkv_ref, vecs), (sems, cut, *lines) = refs[:11], refs[11:16], refs[16:]
+    start = pl.multiple_of((pos[4] & 3) * 128, 128)
+    moves = [
+        (w_in.at[:, pl.ds(start, 128)], cut),
+        (w_back.at[pl.ds(start, 128), :], s_ref.at[128:256, :]),
+        (w_out, e_ref.at[0:128, :]),
+        (g1, e_ref.at[128:256, :]),
+        (g2, e_ref.at[256:384, :]),
+        (w_out, c_ref.at[0:128, :]),
+        (g1, c_ref.at[128:256, :]),
+        (g2, c_ref.at[256:384, :]),
+        (w_in, c_ref.at[392:904, :]),
+        (w_back, c_ref.at[904:1416, :]),
+        (wq, qkv_ref.at[0:512, 0:128]),
+        (wk, qkv_ref.at[0:512, 128:256]),
+        (wv, qkv_ref.at[0:512, 256:384]),
+    ] + list(zip(vectors, lines))
+    copies = [pltpu.make_async_copy(src, dst, sems.at[i]) for i, (src, dst) in enumerate(moves)]
+    for copy in copies:
+        copy.start()
+    for copy in copies:
+        copy.wait()
+    for i, v in enumerate(lines[:9]):
+        vecs[i : i + 1, :] = v[...].astype(F32).reshape(1, 512)
+    bq = lines[9][...].astype(F32).reshape(1, 128)
+    bv = lines[10][...].astype(F32).reshape(1, 128)
+    vecs[9:16, :] = jnp.zeros((7, 512), F32)
+    s_ref[0:128, :] = cut[...].astype(F32).T.astype(BF16)
+    bias = vecs[8:9, pl.ds(start, 128)]
+    s_ref[256:264, :] = jnp.broadcast_to(jnp.concatenate([bias] * 4, axis=1), (8, 512)).astype(BF16)
+    b_in = jnp.broadcast_to(vecs[8:9, :], (8, 512)).astype(BF16)
+    e_ref[384:392, :] = b_in
+    c_ref[384:392, :] = b_in
+    for i, bias in enumerate((bq, jnp.zeros_like(bq), bv)):
+        qkv_ref[512:520, 128 * i : 128 * i + 128] = jnp.broadcast_to(bias, (8, 128)).astype(BF16)
+
+
+def half_rows_kernel(tb, keep, recv, out_ref):
+    out_ref[...] = (keep[384:, :] + recv[384:, :].astype(F32)).astype(BF16)
+
+
+def half_columns_kernel(tb, keep, recv, out_ref):
+    half = keep.shape[1]
+    out_ref[...] = (keep[...] + recv[:, half:].astype(F32)).astype(BF16)
+
+
+def stages_of(n_dp):
+    return [(shift, 2) for shift in range(n_dp.bit_length() - 1)]
+
+
+def dp_hop(value, mask, n_dp):
+    return lax.ppermute(value, "dp", [(i, i ^ mask) for i in range(n_dp)])
+
+
+def padded(rows, n_dp):
+    unit = 8 * n_dp
+    return -(-rows // unit) * unit
+
+
+def split_into(total, pos, shift, size, outs):
+    rows = total.shape[0] // size
+    mine = (pos[4] >> shift) & (size - 1)
+    for k, out in enumerate(outs):
+        at = pl.multiple_of((mine ^ k) * rows, 8)
+        out[...] = total[pl.ds(at, rows), :].astype(out.dtype)
+
+
+def split_kernel(pos, *refs, parts, shift, size):
+    count = sum(len(p[1]) for p in parts)
+    ins, outs, total = refs[:count], refs[count:-1], refs[-1]
+    at, used = 0, 0
+    for rows, takes in parts:
+        value = ins[used][takes[0] : takes[0] + rows, :].astype(F32)
+        for ref, start in zip(ins[used + 1 : used + len(takes)], takes[1:]):
+            value = value + ref[start : start + rows, :].astype(F32)
+        total[at : at + rows, :] = value
+        used += len(takes)
+        at += rows
+    if at < total.shape[0]:
+        total[at:, :] = jnp.zeros((total.shape[0] - at, 512), F32)
+    split_into(total, pos, shift, size, outs)
+
+
+def small_kernel(pos, *refs, rows, count, small):
+    out = refs[-1]
+    value = refs[0][...].astype(F32)
+    for r in refs[1:count]:
+        value = value + r[...].astype(F32)
+    out[0:rows, :] = value.astype(BF16)
+    if small:
+        at = count
+        out[rows : rows + 8, :] = jnp.zeros((8, 512), BF16)
+        for first, size, starts in small:
+            block = refs[at][starts[0] : starts[0] + size, :].astype(F32)
+            for r, start in zip(refs[at + 1 : at + len(starts)], starts[1:]):
+                block = block + r[start : start + size, :].astype(F32)
+            out[rows + first : rows + first + size, :] = block.astype(BF16)
+            at += len(starts)
+
+
+def join_kernel(pos, *refs):
+    out = refs[-1]
+    size = refs[0].shape[0]
+    for i, r in enumerate(refs[:-1]):
+        out[i * size : i * size + size] = r[...]
+
+
+def unpack_kernel(pos, *refs, count, plan, rows, has_small, stages):
+    place = 0
+    for shift, size in stages:
+        place = place * size + ((pos[4] >> shift) & (size - 1))
+    blocks, outs, scratch = refs[:count], refs[count:-1], refs[-1]
+    each = blocks[0].shape[0]
+    for i in range(count * each):
+        at = pl.multiple_of((place ^ i) * rows, 8)
+        scratch[pl.ds(at, rows), :] = blocks[i // each][i % each, 0:rows, :].astype(F32)
+    for out, (start, size, flip) in zip(outs, plan):
+        block = scratch[start : start + size, :]
+        out[...] = block.T if flip else block
+    if has_small:
+        total = jnp.zeros((8, 512), F32)
+        for b in blocks:
+            total = total + jnp.sum(b[:, rows:, :].astype(F32), axis=0)
+        outs[len(plan)][...] = total
+
+
+def unpack_call(pos, blocks, stages, plan, small):
+    rows = blocks[0].shape[1] - (8 if small else 0)
+    shapes = [sds((512, size) if flip else (size, 512), F32) for _, size, flip in plan]
+    if small:
+        shapes = shapes + [sds((8, 512), F32)]
+    total = rows * sum(b.shape[0] for b in blocks)
+    return call(
+        functools.partial(
+            unpack_kernel, count=len(blocks), plan=plan, rows=rows, has_small=bool(small), stages=tuple(stages)
+        ),
+        shapes, [pos] + blocks, smem=1, scratch=[pltpu.VMEM((total, 512), F32)], name="unpack",
+    )
+
+
 def body(
     layer_input, segments, norm1_gain, norm1_bias, w_query, b_query, w_key, w_value, b_value,
     w_out, b_out, gate1_w, gate1_b, norm2_gain, norm2_bias, w_in, b_in, w_back, b_back,
@@ -417,189 +595,252 @@
     def hop(value, mask):
         return lax.ppermute(value, "tensor", [(i, i ^ mask) for i in range(4)])
 
+    def dhop(value, mask):
+        return dp_hop(value, mask, n_dp)
+
+    def after(value, *deps):
+        return lax.optimization_barrier((value,) + deps)[0]
+
     t = lax.axis_index("tensor").astype(jnp.int32)
-    tb = t ^ jnp.array(LOCAL, jnp.int32)
-    seg = segments.reshape(4, 1, 256)
+    me = lax.axis_index("dp").astype(jnp.int32)
+    tb = jnp.where(jnp.arange(8) < 4, t ^ jnp.array(LOCAL + (0,) * 4, jnp.int32), me)
+    seg = segments
     x0 = layer_input
+    last = [None]
+
+    def step(kernel, outs, args, name, scratch=(), smem=1, space=VM, then=(), limit=None):
+        pos = tb if last[0] is None else after(tb, last[0], *then)
+        got = call(kernel, outs, [pos] + args, smem=smem, scratch=scratch, name=name, space=space, limit=limit)
+        last[0] = got[0]
+        return got
+
     x1 = hop(x0, PX)
     x2 = hop(x0, 1)
+    s0, e0, c0, qkv0, vecs = step(
+        pack_kernel,
+        [sds((264, 512), BF16), sds((392, 512), BF16), sds((1416, 512), BF16), sds((520, 384), BF16), sds((16, 512), F32)],
+        [w_in, w_back, w_out, gate1_w, gate2_w, w_query, w_key, w_value, norm1_gain, norm1_bias, b_out, gate1_b,
+         norm2_gain, norm2_bias, b_back, gate2_b, b_in, b_query, b_value],
+        "pack",
+        [pltpu.SemaphoreType.DMA((24,)), pltpu.VMEM((512, 128), BF16)]
+        + [pltpu.VMEM((512,), BF16)] * 9 + [pltpu.VMEM((128,), BF16)] * 2,
+        space=pl.BlockSpec(memory_space=pltpu.MemorySpace.HBM), limit=60 * 1024 * 1024,
+    )
+    qkv1 = hop(qkv0, 1)
+    sy = hop(s0, PX)
     x3 = hop(x1, 1)
-    zero128 = jnp.zeros((128,), BF16)
-    row_qkv = jnp.concatenate([b_query, zero128, b_value])[None]
-    qkv0 = jnp.concatenate(
-        [jnp.concatenate([w_query, w_key, w_value], axis=1), row_qkv, jnp.zeros((7, 384), BF16)], axis=0
-    )
-    qkv1 = hop(qkv0, 1)
-    e0 = jnp.concatenate([w_out, gate1_w], axis=0)
-    f0 = jnp.concatenate([w_in, w_back, gate2_w, b_in[None], jnp.zeros((7, 512), BF16)], axis=0)
-    e2 = hop(e0, 1)
-    f2 = hop(f0, 1)
-    x1b, e0b, f0b = lax.optimization_barrier((x1, e0, f0))
-    e1 = hop(e0b, PX)
-    e3 = hop(e1, 1)
-    f1 = hop(f0b, PX)
-    f3 = hop(f1, 1)
-    vecs = jnp.stack(
-        [norm1_gain, norm1_bias, b_out, gate1_b, norm2_gain, norm2_bias, b_back, gate2_b]
-    ).astype(F32)
-
-    n, qt0, qt1, k, vt, p1, ot1, att1, invl1 = call(
+    e1 = hop(after(e0, x1), PX)
+    c2 = hop(after(c0, qkv1), 1)
+
+    n, qt0, qt1, k, vt, p1, ot1, att1, invl1 = step(
         first_kernel,
         [
             sds((1024, 512), BF16), sds((256, 256), BF16), sds((256, 256), BF16), sds((1024, 256), BF16),
             sds((256, 1024), BF16), sds((4, 1024, 256), BF16), sds((256, 256), BF16), sds((256, 256), BF16),
             sds((4, 8, 256), F32),
         ],
-        [tb, seg, seg, x0, x1b, x2, x3, vecs, qkv0, qkv1],
-        smem=2, scratch=ATT_SCRATCH, flops=2_000_000_000, name="first",
+        [seg, seg, x0, x1, x2, x3, vecs, qkv0, qkv1],
+        "first", ATT_SCRATCH, 2,
     )
     attp = hop(att1, PX)
-    p0, ot0, att0, invl0 = call(
+    sy = after(sy, att1)
+    sx = dhop(sy, 1)
+    sz = dhop(sy, 2)
+    e3 = hop(after(e1, att1), 1)
+    p0, ot0, att0, invl0 = step(
         second_kernel,
         [sds((4, 1024, 256), BF16), sds((256, 256), BF16), sds((256, 256), BF16), sds((4, 8, 256), F32)],
-        [tb, seg, seg, qt0, k, vt],
-        smem=2, scratch=ATT_SCRATCH, flops=2_000_000_000, name="second",
-    )
-    n2, mid, branch, gate = call(
+        [seg, seg, qt0, k, vt],
+        "second", ATT_SCRATCH, 2,
+    )
+    v, kt = step(prepare_kernel, [sds((1024, 256), BF16), sds((256, 1024), BF16)], [n, k, qkv0, qkv1], "prepare")
+    n2, mid, branch, gate = step(
         out_kernel,
         [sds((256, 512), BF16), sds((256, 512), F32), sds((256, 512), F32), sds((256, 512), F32)],
-        [tb, x0, n, att0, attp, vecs, e0, e1, e2, e3],
-        smem=1, scratch=[pltpu.VMEM((512, 512), BF16)], flops=270_000_000, name="out",
+        [x0, n, att0, attp, vecs, e0, e1, c2, e3],
+        "out", [pltpu.VMEM((512, 512), BF16)],
     )
     n2p = hop(n2, PX)
-    result, fg, ltg, hid, slope = call(
+    sxz = dhop(after(sz, n2), 1)
+    total0, hid, slope0 = step(
+        ffn_first_kernel,
+        [sds((256, 512), F32), sds((256, 1024), BF16), sds((256, 1024), BF16)],
+        [n2, vecs, w_in, w_back, c2],
+        "ffn_first",
+    )
+    quarters = [sy, hop(sy, 1), sx, hop(sx, 1), sz, hop(sz, 1)]
+    sxz = after(sxz, total0)
+    quarters = quarters + [sxz, hop(sxz, 1)]
+    result, fg, ltg, slope1 = step(
         ffn_kernel,
-        [
-            sds((256, 512), BF16), sds((256, 512), BF16), sds((256, 512), BF16), sds((256, 2048), BF16),
-            sds((256, 2048), BF16),
-        ],
-        [tb, n2, mid, cotangent, vecs, f0, f1, f2, f3],
-        smem=1, scratch=[pltpu.VMEM((512, 512), BF16)], flops=1_200_000_000, name="ffn",
+        [sds((256, 512), BF16), sds((256, 512), BF16), sds((256, 512), BF16), sds((256, 1024), BF16)],
+        [n2, mid, cotangent, vecs, e0, e1, c2, e3, total0] + quarters,
+        "ffn", [pltpu.VMEM((512, 512), BF16)],
     )
     fgp = hop(fg, PX)
-    dot0, dotp, mg, bg, log, hg, sums = call(
+    dot0, dotp, mg, bg, log, hg, sums = step(
         back_kernel,
         [
             sds((256, 256), BF16), sds((256, 256), BF16), sds((256, 512), F32), sds((256, 512), BF16),
             sds((256, 512), BF16), sds((256, 1024), BF16), sds((8, 512), F32),
         ],
-        [tb, fg, ltg, slope, mid, branch, gate, cotangent, vecs, f0, f1, f2, f3, e0, e1, e2, e3],
-        smem=1, scratch=[pltpu.VMEM((512, 512), BF16)], flops=1_400_000_000, name="back",
+        [fg, ltg, slope0, slope1, mid, branch, gate, cotangent, vecs, e0, e1, c2, e3, w_in, w_back] + quarters,
+        "back", [pltpu.VMEM((512, 512), BF16)],
     )
     dot1 = hop(dotp, PX)
-    fkeep, fsend = call(
-        ffn_weight_kernel,
-        [sds((1032, 512), F32), sds((1032, 512), BF16)],
-        [n2, n2p, fg, fgp, hid, hg, f0, f2],
-        flops=1_600_000_000, name="ffn_weight",
-    )
-    frecv = hop(fsend, 1)
-    fsum = fkeep + frecv.astype(F32)
-    skeep, ssend = call(
-        small_weight_kernel,
-        [sds((768, 512), F32), sds((768, 512), BF16)],
-        [tb, n, n2, ltg, log, att0, attp, bg],
-        smem=1, scratch=[pltpu.VMEM((512, 512), F32), pltpu.VMEM((512, 512), F32)],
-        flops=400_000_000, name="small_weight",
-    )
-    srecv = hop(ssend, 1)
-    ssum = skeep + srecv.astype(F32)
-    spar = hop(ssum[384:768].astype(BF16), PX)
-    stot = (ssum[0:384] + spar.astype(F32)).astype(BF16)
-    sums = sums + hop(sums, 1)
-    sums = sums + hop(sums, PX)
-
-    v, kt = call(
-        prepare_kernel, [sds((1024, 256), BF16), sds((256, 1024), BF16)], [n, k, qkv0, qkv1],
-        flops=270_000_000, name="prepare",
-    )
     back_scratch = [
         pltpu.VMEM((256, 256), F32), pltpu.VMEM((4, 128, 256), BF16), pltpu.VMEM((256, 256), BF16),
         pltpu.VMEM((4, 8, 256), F32),
     ]
-    dk0, dv0, dq0 = call(
+    dk0, dv0, dq0 = step(
         back_first_kernel,
         [sds((256, 1024), F32), sds((256, 1024), F32), sds((256, 256), BF16)],
-        [tb, seg, p0, dot0, ot0, invl0, qt0, kt, v],
-        smem=2, scratch=back_scratch, flops=2_000_000_000, name="attn_back0",
-    )
-    dqt, dkt, dvt, akeep, asend, abias = call(
+        [seg, p0, dot0, ot0, invl0, qt0, kt, v],
+        "attn_back0", back_scratch, 2,
+    )
+    bkeep, bsend, slopep = step(
+        ffn_back_weight_kernel,
+        [sds((512, 512), F32), sds((512, 512), BF16), sds((256, 1024), BF16)],
+        [n2p, fg, fgp, hid, vecs, w_in, c2],
+        "ffn_back_weight",
+    )
+    brecv = hop(bsend, 1)
+    ikeep, isend = step(
+        ffn_in_weight_kernel,
+        [sds((520, 512), F32), sds((520, 512), BF16)],
+        [n2, n2p, fgp, hg, slopep, w_back, c2],
+        "ffn_in_weight",
+    )
+    irecv = hop(isend, 1)
+    skeep, ssend = step(
+        small_weight_kernel,
+        [sds((776, 512), F32), sds((776, 512), BF16)],
+        [n, n2, ltg, log, att0, attp, bg, sums],
+        "small_weight", [pltpu.VMEM((512, 512), F32), pltpu.VMEM((512, 512), F32)], then=(dot1,),
+    )
+    srecv = hop(ssend, 1)
+    stages = stages_of(n_dp)
+
+    def split(parts, rows, stage):
+        shift, size = stage
+        arrays = [a for _, addends in parts for a, _ in addends]
+        static = tuple((r, tuple(start for _, start in addends)) for r, addends in parts)
+        return step(
+            functools.partial(split_kernel, parts=static, shift=shift, size=size),
+            [sds((rows // size, 512), F32)] + [sds((rows // size, 512), BF16)] * (size - 1),
+            arrays, "split", [pltpu.VMEM((rows, 512), F32)],
+        )
+
+    def send(pieces, stage):
+        return [pieces[0]] + [dhop(p, k << stage[0]) for k, p in enumerate(pieces[1:], 1)]
+
+    def resplit(pieces, i):
+        rows = pieces[0].shape[0]
+        return send(split([(rows, [(p, 0) for p in pieces])], rows, stages[i]), stages[i])
+
+    def fold(pieces, small):
+        rows = pieces[0].shape[0]
+        static = tuple((f, m, tuple(start for _, start in group)) for f, m, group in small)
+        arrays = [a for _, _, group in small for a, _ in group]
+        return step(
+            functools.partial(small_kernel, rows=rows, count=len(pieces), small=static),
+            [sds((rows + (8 if small else 0), 512), BF16)], list(pieces) + arrays, "fold",
+        )[0]
+
+    def spread(held, i):
+        shift, size = stages[i]
+        return [held] + [dhop(held, k << shift) for k in range(1, size)]
+
+    def join(blocks):
+        shape = (len(blocks) * blocks[0].shape[0],) + blocks[0].shape[1:]
+        return step(join_kernel, [sds(shape, BF16)], blocks, "join")[0]
+
+    depth = len(stages)
+    rows_f, rows_a = padded(1024, n_dp), padded(768, n_dp)
+    f = send(split([(512, [(bkeep, 0), (brecv, 0)]), (512, [(ikeep, 0), (irecv, 0)])], rows_f, stages[0]), stages[0])
+    (spar,) = step(half_rows_kernel, [sds((392, 512), BF16)], [skeep, srecv], "half_rows")
+    sparr = hop(spar, PX)
+
+    dqt, dkt, dvt, akeep, asend = step(
         back_second_kernel,
         [
-            sds((256, 512), BF16), sds((256, 1024), BF16), sds((256, 1024), BF16), sds((384, 512), F32),
-            sds((384, 512), BF16), sds((8, 512), F32),
+            sds((256, 512), BF16), sds((256, 1024), BF16), sds((256, 1024), BF16), sds((392, 512), F32),
+            sds((392, 512), BF16),
         ],
-        [tb, seg, p1, dot1, ot1, invl1, qt1, kt, v, dk0, dv0, dq0, n],
-        smem=2, scratch=[pltpu.VMEM((256, 1024), F32), pltpu.VMEM((256, 1024), F32)] + back_scratch,
-        flops=2_500_000_000, name="attn_back1",
+        [seg, p1, dot1, ot1, invl1, qt1, kt, v, dk0, dv0, dq0, n],
+        "attn_back1", [pltpu.VMEM((256, 1024), F32), pltpu.VMEM((256, 1024), F32)] + back_scratch, 2,
     )
     arecv = hop(asend, 1)
-    asum = (akeep + arecv.astype(F32)).astype(BF16)
-    bq_s = abias[0, 128:256]
-    bv_s = abias[0, 384:512]
-    brecv = hop(jnp.concatenate([bq_s, bv_s])[None], 1)[0]
-    bq = abias[0, 0:128] + brecv[0:128]
-    bv = abias[0, 256:384] + brecv[128:256]
-    gown, gpar, gsend = call(
+    gown, gpar, gsend = step(
         input_kernel,
         [sds((512, 256), F32), sds((512, 256), F32), sds((512, 512), BF16)],
         [dqt, dkt, dvt, qkv0, qkv1],
-        flops=700_000_000, name="input_grad",
+        "input_grad",
     )
     gsib = hop(gsend, 1)
-    gp = hop((gpar + gsib[:, 256:512].astype(F32)).astype(BF16), PX)
-    input_grad, sums1 = call(
+    f = resplit(f, 1)
+    a = send(
+        split([(384, [(akeep, 0), (arecv, 0)]), (384, [(skeep, 0), (srecv, 0), (sparr, 0)])], rows_a, stages[0]),
+        stages[0],
+    )
+    (gsum,) = step(half_columns_kernel, [sds((512, 256), BF16)], [gpar, gsib], "half_columns")
+    gp = hop(gsum, PX)
+    f = resplit(f, 2)
+    a = resplit(a, 1)
+    input_grad, sums1 = step(
         last_kernel,
         [sds((256, 512), F32), sds((8, 512), F32)],
-        [tb, gown, gsib, gp, x0, mg, log, vecs, e0, e1, e2, e3],
-        smem=1, scratch=[pltpu.VMEM((512, 512), BF16)], flops=140_000_000, name="last",
-    )
-    sums1 = sums1 + hop(sums1, 1)
-    sums1 = sums1 + hop(sums1, PX)
-
-    def scatter(matrix):
-        pieces = matrix.astype(BF16).reshape(n_dp, -1, 512)
-        got = lax.all_to_all(pieces, "dp", 0, 0, tiled=True)
-        return jnp.sum(got.astype(F32), axis=0).astype(BF16)
-
-    def gather(piece, small):
-        rows = piece.shape[0]
-        both = jnp.concatenate([piece, small.astype(BF16)], axis=0)
-        got = lax.all_to_all(jnp.broadcast_to(both[None], (n_dp,) + both.shape), "dp", 0, 0, tiled=True)
-        return (
-            got[:, :rows].astype(F32).reshape(n_dp * rows, 512),
-            jnp.sum(got[:, rows:].astype(F32), axis=0),
-        )
-
-    small_f = jnp.concatenate([sums[0:6], fsum[1024:1025], jnp.zeros((1, 512), F32)], axis=0)
-    f_all, f_small = gather(scatter(fsum[0:1024]), small_f)
-    s_all, s_small = gather(scatter(stot), jnp.zeros((8, 512), F32))
-    small_a = jnp.concatenate(
-        [sums1[0:2], jnp.concatenate([bq, bv, jnp.zeros((256,), F32)])[None], jnp.zeros((5, 512), F32)], axis=0
-    )
-    a_all, a_small = gather(scatter(asum), small_a)
+        [gown, gsib, gp, x0, mg, log, vecs, e0, e1, c2, e3],
+        "last", [pltpu.VMEM((512, 512), BF16)],
+    )
+    sums1_b = hop(sums1, PX)
+    sums1_a = hop(sums1, 1)
+    for i in range(3, depth):
+        f = resplit(f, i)
+    for i in range(2, depth - 1):
+        a = resplit(a, i)
+    tail = [(skeep, 773), (srecv, 773), (sparr, 389)]
+    f = fold(f, [(0, 1, [(ikeep, 512), (irecv, 512)]), (1, 1, tail)])[None]
+    f = spread(f, depth - 1)
+    a = resplit(a, depth - 1)
+    sums1_c = hop(after(sums1_b, a[0]), 1)
+    f = spread(join(f), depth - 2)
+    group = [(skeep, 768), (srecv, 768), (sparr, 384)]
+    a = fold(
+        a,
+        [(0, 2, [(sums1, 0), (sums1_a, 0), (sums1_b, 0), (sums1_c, 0)]), (2, 1, [(akeep, 384), (arecv, 384)]),
+         (3, 5, group)],
+    )[None]
+    a = spread(a, depth - 1)
+    for i in range(depth - 3, -1, -1):
+        f = spread(join(f), i)
+        a = spread(join(a), i + 1)
+    a = spread(join(a), 0)
+    g_wback, g_win, f_small = unpack_call(tb, f, stages, ((0, 512, False), (512, 512, False)), True)
+    plan = ((0, 128, True), (128, 128, True), (256, 128, True), (384, 128, False), (512, 128, False), (640, 128, False))
+    g_q, g_k, g_v, g_g2, g_g1, g_wo, a_small = unpack_call(tb, a, stages, plan, True)
     return (
         result,
         input_grad,
         a_small[0],
         a_small[1],
-        a_all[0:128].T,
+        g_q,
         a_small[2, 0:128],
-        a_all[128:256].T,
-        a_all[256:384].T,
+        g_k,
+        g_v,
         a_small[2, 128:256],
-        s_all[256:384],
-        f_small[2],
-        s_all[128:256],
-        f_small[3],
-        f_small[4],
-        f_small[5],
-        f_all[0:512],
-        f_small[6],
-        f_all[512:1024],
+        g_wo,
+        a_small[5],
+        g_g1,
+        a_small[6],
+        a_small[7],
+        f_small[1],
+        g_win,
         f_small[0],
-        s_all[0:128],
-        f_small[1],
+        g_wback,
+        a_small[3],
+        g_g2,
+        a_small[4],
     )
 
 

time: 260 us -> 160 us (0.62)
  waiting for transfers between devices: 119 us -> 71.6 us
  local copies, waits for them, and re-layouts: 21.6 us -> 3.51 us
  starting transfers between devices: 45.8 us -> 32.3 us
  Pallas kernels: 61 us -> 50.2 us
  other arithmetic: 9.61 us -> 1.21 us
    all_to_all x6 -> x0, waiting for transfers between devices: 71.2 us -> none  [the longest x3 38.9 us: gather(): lax.all_to_all(jnp.broadcast_to(both[None], (n_dp,) + both.shape), 'dp',...]
    ppermute x0 -> x15, waiting for transfers between devices: none -> 42 us  [dp_hop(): return lax.ppermute(value, 'dp', [(i, i ^ mask) for i in range(n_dp)])]
    all_to_all x6 -> x0, starting transfers between devices: 26.6 us -> none  [the longest x3 15.3 us: scatter(): got = lax.all_to_all(pieces, 'dp', 0, 0, tiled=True)]
    ppermute x25 -> x26, waiting for transfers between devices: 48 us -> 29.5 us  [hop(): return lax.ppermute(value, 'tensor', [(i, i ^ mask) for i in range(4)])]
    ppermute x0 -> x15, starting transfers between devices: none -> 17.2 us  [dp_hop(): return lax.ppermute(value, 'dp', [(i, i ^ mask) for i in range(n_dp)])]
    pallas_call x12 -> x31, Pallas kernels: 61 us -> 50.2 us  [call(): pl.pallas_call(body, out_shape=tuple(outs), in_specs=[SM] * smem + [space...]
    concatenate x6 -> x0, local copies, waits for them, and re-layouts: 5.08 us -> none  [the longest x1 4.83 us: body(): jnp.concatenate([w_in, w_back, gate2_w, b_in[None], jnp.zeros((7, 512), B...]
    slice x9 -> x2, local copies, waits for them, and re-layouts: 5.8 us -> 1.19 us  [the longest x1 0.61 us: body(): a_small[4]]
  transfers between devices with their start and end apart: 31 -> 41, of which waited for: 13 -> 20; matrix products, arithmetic and copies ran while one was open for 9% -> 0% of each run, Pallas kernels for 17% -> 26%
where the time goes in v2:
time: 160 us
  waiting for transfers between devices  71.6 us (45%)
  Pallas kernels  50.2 us (31%)
  starting transfers between devices  32.3 us (20%)
  local copies, waits for them, and re-layouts  3.51 us (2%)
    pallas_call x31, Pallas kernels, call(): pl.pallas_call(body, out_shape=tuple(outs), in_specs=[SM] * smem + [space...  50.2 us
    ppermute x15, waiting for transfers between devices, dp_hop(): return lax.ppermute(value, 'dp', [(i, i ^ mask) for i in range(n_dp)])  42 us
    ppermute x26, waiting for transfers between devices, hop(): return lax.ppermute(value, 'tensor', [(i, i ^ mask) for i in range(4)])  29.5 us
    ppermute x15, starting transfers between devices, dp_hop(): return lax.ppermute(value, 'dp', [(i, i ^ mask) for i in range(n_dp)])  17.2 us
    ppermute x26, starting transfers between devices, hop(): return lax.ppermute(value, 'tensor', [(i, i ^ mask) for i in range(4)])  15.1 us
  transfers between devices with their start and end apart: 41, of which 20 were waited for; matrix products, arithmetic and copies ran while one was open for 0% of the time, Pallas kernels for 26%

profile of v2, /device:TPU:0, one launch (start us, length us, event | category | flops | bytes accessed | tf_op | source)
XLA Modules:
  0.0 159.9 jit_solution(14299818898210955810)
XLA Ops:
  0.7 1.2 compare_select_fusion.pos.tb
  1.9 4.2 %pack.1 = (bf16[264,512]{1,0:T(8,128)(2,1)}, bf16[392,512]{1,0:T(8,128)(2,1)}, bf16[1416,512]{1,0:T(8,128)(2,1)}, bf16[520,384]{1,0:T(8,128)(2,1)}, f32[16,512]{1,0:T(8,128)}) custom-call(s32[8]{0:T(128)} %compare_select_fusion.pos.tb, bf16[512,512]{1,0:T(8,128)(2,1)} %win0.5, bf16[512,512]{1,0:T(8,128)(2,1)} %wback0.5, bf16[128,512]{1,0:T(8,128)(2,1)} %w_out.1, ...), custom_call_target="tpu_custom_call" | custom-call | tf_op jit(solution)/shard_map/pack/pallas_call | solution.py:41
  6.7 1.6 collective-permute-done.3.qkv1
  8.6 2.7 %collective-permute-start = (bf16[256,512]{1,0:T(8,128)(2,1)S(1)}, bf16[256,512]{1,0:T(8,128)(2,1)S(1)}, u32[]{:S(2)}, u32[]{:S(2)}) collective-permute-start(bf16[256,512]{1,0:T(8,128)(2,1)S(1)} %copy-done.5), channel_id=1, source_target_pairs={{0,2},{1,3},{2,0},{3,1},{4,6},{5,7},{6,4},{7,5},{8,10},{9,11},{10,... | collective-permute-start | bytes 786440 | tf_op jit(solution)/shard_map/ppermute | solution.py:596
  11.3 6.8 %collective-permute-done.x1 = bf16[256,512]{1,0:T(8,128)(2,1)S(1)} collective-permute-done((bf16[256,512]{1,0:T(8,128)(2,1)S(1)}, bf16[256,512]{1,0:T(8,128)(2,1)S(1)}, u32[]{:S(2)}, u32[]{:S(2)}) %collective-permute-start) | collective-permute-done | bytes 262176 | tf_op jit(solution)/shard_map/ppermute | solution.py:596
  18.1 1.7 %collective-permute-start.5 = (bf16[392,512]{1,0:T(8,128)(2,1)}, bf16[392,512]{1,0:T(8,128)(2,1)S(1)}, u32[]{:S(2)}, u32[]{:S(2)}) collective-permute-start(bf16[392,512]{1,0:T(8,128)(2,1)} %get-tuple-element.152.e0), channel_id=1, source_target_pairs={{0,2},{1,3},{2,0},{3,1},{4,6},{5,7},{6,4},{7,5},{8,10},{9,11},{10,... | collective-permute-start | bytes 1204232 | tf_op jit(solution)/shard_map/ppermute | solution.py:596
  20.6 0.7 collective-permute-done.1.x2
  21.8 1.0 copy-done.3
  22.8 0.8 copy-done.6
  23.5 4.8 %first.1 = (bf16[1024,512]{1,0:T(8,128)(2,1)S(1)}, bf16[256,256]{1,0:T(8,128)(2,1)S(1)}, bf16[256,256]{1,0:T(8,128)(2,1)S(1)}, bf16[1024,256]{1,0:T(8,128)(2,1)S...) custom-call(s32[8]{0:T(128)S(1)} %copy-done.9, ...), custom_call_target="tpu_custom_call" | custom-call | tf_op jit(solution)/shard_map/first/pallas_call | solution.py:41
  28.3 2.2 %collective-permute-done.5.e1 = bf16[392,512]{1,0:T(8,128)(2,1)S(1)} collective-permute-done((bf16[392,512]{1,0:T(8,128)(2,1)}, bf16[392,512]{1,0:T(8,128)(2,1)S(1)}, u32[]{:S(2)}, u32[]{:S(2)}) %collective-permute-start.5) | collective-permute-done | bytes 401440 | tf_op jit(solution)/shard_map/ppermute | solution.py:596
  30.5 4.6 %collective-permute-done.8.s0 = bf16[264,512]{1,0:T(8,128)(2,1)S(1)} collective-permute-done((bf16[264,512]{1,0:T(8,128)(2,1)}, bf16[264,512]{1,0:T(8,128)(2,1)S(1)}, u32[]{:S(2)}, u32[]{:S(2)}) %collective-permute-start.8) | collective-permute-done | bytes 270368 | tf_op jit(solution)/shard_map/ppermute | solution.py:596
  35.1 1.6 collective-permute-start.12
  36.7 1.5 collective-permute-start.4
  38.2 1.5 collective-permute-start.10
  39.7 1.6 %second.1 = (bf16[4,1024,256]{2,1,0:T(8,128)(2,1)S(1)}, bf16[256,256]{1,0:T(8,128)(2,1)S(1)}, bf16[256,256]{1,0:T(8,128)(2,1)S(1)}, f32[4,8,256]{2,1,0:T(8,128)S(1)}) custom-call(s32[8]{0:T(128)S(1)} %copy-done.9, s32[1,1024]{1,0:T(1,128)S(1)} %copy-done.10, s32[1,1024]{1,0:T(1,128)S(1)} %copy-done.10, bf16[256,256]{1,0:T(8,128)(2,1)S(1)} %get-tuple-element.142.qt0.qt, ...), custom_call_target="tpu_custom_call" | custom-call | tf_op jit(solution)/shard_map/second/pallas_call | solution.py:41
  41.3 1.3 prepare.1
  42.7 1.4 out.1
  45.2 1.7 %ffn_first.1 = (f32[256,512]{1,0:T(8,128)S(1)}, bf16[256,1024]{1,0:T(8,128)(2,1)S(1)}, bf16[256,1024]{1,0:T(8,128)(2,1)S(1)}) custom-call(s32[8]{0:T(128)S(1)} %copy-done.9, bf16[256,512]{1,0:T(8,128)(2,1)S(1)} %get-tuple-element.156.n2, f32[16,512]{1,0:T(8,128)S(1)} %copy-done.7, bf16[512,512]{1,0:T(8,128)(2,1)S(1)} %copy-done, ...), custom_call_target="tpu_custom_call" | custom-call | tf_op jit(solution)/shard_map/ffn_first/pallas_call | solution.py:41
  46.9 4.0 %collective-permute-done.14.s6 = bf16[264,512]{1,0:T(8,128)(2,1)S(1)} collective-permute-done((bf16[264,512]{1,0:T(8,128)(2,1)S(1)}, bf16[264,512]{1,0:T(8,128)(2,1)S(1)}, u32[]{:S(2)}, u32[]{:S(2)}) %collective-permute-start.14) | collective-permute-done | bytes 270368 | tf_op jit(solution)/shard_map/ppermute | solution.py:501
  50.9 1.7 %collective-permute-start.16 = (bf16[256,512]{1,0:T(8,128)(2,1)S(1)}, bf16[256,512]{1,0:T(8,128)(2,1)S(1)}, u32[]{:S(2)}, u32[]{:S(2)}) collective-permute-start(bf16[256,512]{1,0:T(8,128)(2,1)S(1)} %get-tuple-element.156.n2), channel_id=1, source_target_pairs={{0,2},{1,3},{2,0},{3,1},{4,6},{5,7},{6,4},{7,5},{8,10},{9,11},{10,... | collective-permute-start | bytes 786440 | tf_op jit(solution)/shard_map/ppermute | solution.py:596
  52.7 2.8 %ffn.1 = (bf16[256,512]{1,0:T(8,128)(2,1)}, bf16[256,512]{1,0:T(8,128)(2,1)S(1)}, bf16[256,512]{1,0:T(8,128)(2,1)S(1)}, bf16[256,1024]{1,0:T(8,128)(2,1)S(1)}) custom-call(s32[8]{0:T(128)S(1)} %copy-done.9, bf16[256,512]{1,0:T(8,128)(2,1)S(1)} %get-tuple-element.156.n2, f32[256,512]{1,0:T(8,128)S(1)} %get-tuple-element.160.mid, ...), custom_call_target="tpu_custom_call" | custom-call | tf_op jit(solution)/shard_map/ffn/pallas_call | solution.py:41
  55.5 1.5 collective-permute-start.17
  57.0 3.5 %back.1 = (bf16[256,256]{1,0:T(8,128)(2,1)S(1)}, bf16[256,256]{1,0:T(8,128)(2,1)S(1)}, f32[256,512]{1,0:T(8,128)S(1)}, bf16[256,512]{1,0:T(8,128)(2,1)S(1)}, bf1...) custom-call(s32[8]{0:T(128)S(1)} %copy-done.9, ...), custom_call_target="tpu_custom_call" | custom-call | tf_op jit(solution)/shard_map/back/pallas_call | solution.py:41
  61.1 2.0 %attn_back0.1 = (f32[256,1024]{1,0:T(8,128)S(1)}, f32[256,1024]{1,0:T(8,128)S(1)}, bf16[256,256]{1,0:T(8,128)(2,1)S(1)}) custom-call(s32[8]{0:T(128)S(1)} %copy-done.9, s32[1,1024]{1,0:T(1,128)S(1)} %copy-done.10, bf16[4,1024,256]{2,1,0:T(8,128)(2,1)S(1)} %get-tuple-element.145.p, bf16[256,256]{1,0:T(8,128)(2,1)S(1)} %get-tuple-element.172.dot, ...), custom_call_target="tpu_custom_call" | custom-call | tf_op jit(solution)/shard_map/attn_back0/pallas_call | solution.py:41
  63.1 2.5 %collective-permute-done.17.fgp = bf16[256,512]{1,0:T(8,128)(2,1)S(1)} collective-permute-done((bf16[256,512]{1,0:T(8,128)(2,1)S(1)}, bf16[256,512]{1,0:T(8,128)(2,1)S(1)}, u32[]{:S(2)}, u32[]{:S(2)}) %collective-permute-start.17) | collective-permute-done | bytes 262176 | tf_op jit(solution)/shard_map/ppermute | solution.py:596
  65.6 2.3 %ffn_back_weight.1 = (f32[512,512]{1,0:T(8,128)S(1)}, bf16[512,512]{1,0:T(8,128)(2,1)S(1)}, bf16[256,1024]{1,0:T(8,128)(2,1)S(1)}) custom-call(s32[8]{0:T(128)S(1)} %copy-done.9, bf16[256,512]{1,0:T(8,128)(2,1)S(1)} %collective-permute-done.16.n2p, bf16[256,512]{1,0:T(8,128)(2,1)S(1)} %get-tuple-element.166.fg, ...), custom_call_target="tpu_custom_call" | custom-call | tf_op jit(solution)/shard_map/ffn_back_weight/pallas_call | solution.py:41
  67.9 1.9 %ffn_in_weight.1 = (f32[520,512]{1,0:T(8,128)S(1)}, bf16[520,512]{1,0:T(8,128)(2,1)S(1)}) custom-call(s32[8]{0:T(128)S(1)} %copy-done.9, bf16[256,512]{1,0:T(8,128)(2,1)S(1)} %get-tuple-element.156.n2, bf16[256,512]{1,0:T(8,128)(2,1)S(1)} %collective-permute-done.16.n2p, bf16[256,512]{1,0:T(8,128)(2,1)S(1)} %collective-permute-done.17.fgp, ...), custom_call_target="tpu_custom_call" | custom-call | tf_op jit(solution)/shard_map/ffn_in_weight/pallas_call | solution.py:41
  69.8 1.2 small_weight.1
  71.7 3.2 %collective-permute-done.19.refs_1_ = bf16[512,512]{1,0:T(8,128)(2,1)S(1)} collective-permute-done((bf16[512,512]{1,0:T(8,128)(2,1)S(1)}, bf16[512,512]{1,0:T(8,128)(2,1)S(1)}, u32[]{:S(2)}, u32[]{:S(2)}) %collective-permute-start.19) | collective-permute-done | bytes 524320 | tf_op jit(solution)/shard_map/ppermute | solution.py:596
  74.9 1.0 split.6
  75.9 1.1 collective-permute-start.22
  77.0 0.6 half_rows.1
  77.6 4.8 %attn_back1.1 = (bf16[256,512]{1,0:T(8,128)(2,1)S(1)}, bf16[256,1024]{1,0:T(8,128)(2,1)S(1)}, bf16[256,1024]{1,0:T(8,128)(2,1)S(1)}, f32[392,512]{1,0:T(8,128)S(1)}, bf16[392,512]{1,0:T(8,128)(2,1)S(1)}) custom-call(s32[8]{0:T(128)S(1)} %copy-done.9, s32[1,1024]{1,0:T(1,128)S(1)} %copy-done.10, bf16[4,1024,256]{2,1,0:T(8,128)(2,1)S(1)} %get-tuple-element.198.p, ...), custom_call_target="tpu_custom_call" | custom-call | tf_op jit(solution)/shard_map/attn_back1/pallas_call | solution.py:41
  82.4 0.8 collective-permute-start.23
  83.2 1.4 input_grad.1
  84.8 5.2 %collective-permute-done.22.refs_1_ = bf16[512,512]{1,0:T(8,128)(2,1)S(1)} collective-permute-done((bf16[512,512]{1,0:T(8,128)(2,1)S(1)}, bf16[512,512]{1,0:T(8,128)(2,1)S(1)}, u32[]{:S(2)}, u32[]{:S(2)}) %collective-permute-start.22) | collective-permute-done | bytes 524320 | tf_op jit(solution)/shard_map/ppermute | solution.py:501
  90.0 0.8 split.7
  90.7 3.7 %collective-permute-done.24.refs_4_.refs_6_.refs_10_ = bf16[392,512]{1,0:T(8,128)(2,1)S(1)} collective-permute-done((bf16[392,512]{1,0:T(8,128)(2,1)S(1)}, bf16[392,512]{1,0:T(8,128)(2,1)S(1)}, u32[]{:S(2)}, u32[]{:S(2)}) %collective-permute-start.24) | collective-permute-done | bytes 401440 | tf_op jit(solution)/shard_map/ppermute | solution.py:596
  94.5 1.0 split.8
  95.5 1.1 collective-permute-start.27
  98.0 5.8 %collective-permute-done.26.refs_1_ = bf16[256,512]{1,0:T(8,128)(2,1)S(1)} collective-permute-done((bf16[256,512]{1,0:T(8,128)(2,1)S(1)}, bf16[256,512]{1,0:T(8,128)(2,1)S(1)}, u32[]{:S(2)}, u32[]{:S(2)}) %collective-permute-start.26) | collective-permute-done | bytes 262176 | tf_op jit(solution)/shard_map/ppermute | solution.py:501
  103.7 0.6 split.9
  104.4 2.7 %collective-permute-start.29 = (bf16[128,512]{1,0:T(8,128)(2,1)S(1)}, bf16[128,512]{1,0:T(8,128)(2,1)S(1)}, u32[]{:S(2)}, u32[]{:S(2)}) collective-permute-start(bf16[128,512]{1,0:T(8,128)(2,1)S(1)} %get-tuple-element.229), channel_id=1, source_target_pairs={{0,16},{4,20},{8,24},{12,28},{16,0},{20,4},{24,8},{28,12},{1,17},{... | collective-permute-start | bytes 393224 | tf_op jit(solution)/shard_map/ppermute | solution.py:501
  107.0 0.7 split.10
  108.3 2.0 %last.1 = (f32[256,512]{1,0:T(8,128)}, f32[8,512]{1,0:T(8,128)S(1)}) custom-call(s32[8]{0:T(128)S(1)} %copy-done.9, f32[512,256]{1,0:T(8,128)S(1)} %get-tuple-element.208.own, bf16[512,512]{1,0:T(8,128)(2,1)S(1)} %collective-permute-done.25.recv.sib, bf16[512,256]{1,0:T(8,128)(2,1)S(1)} %collective-permute-done.28.par, bf16[256,512]{1,0:T(8,128)(2,1)S(1)} %copy-done.5, ...), custom_call_target="tpu_custom_call" | custom-call | tf_op jit(solution)/shard_map/last/pallas_call | solution.py:41
  110.3 1.4 collective-permute-done.29.refs_1_
  112.2 1.9 %collective-permute-start.31 = (bf16[1,136,512]{2,1,0:T(8,128)(2,1)S(1)}, bf16[1,136,512]{2,1,0:T(8,128)(2,1)S(1)}, u32[]{:S(2)}, u32[]{:S(2)}) collective-permute-start(bf16[1,136,512]{2,1,0:T(8,128)(2,1)S(1)} %bitcast.15), channel_id=1, source_target_pairs={{0,16},{4,20},{8,24},{12,28},{16,0},{20,4},{24,8},{28,12},{1,17},{... | collective-permute-start | bytes 417800 | tf_op jit(solution)/shard_map/ppermute | solution.py:501
  114.2 1.6 %collective-permute-done.30.refs_1_ = bf16[192,512]{1,0:T(8,128)(2,1)S(1)} collective-permute-done((bf16[192,512]{1,0:T(8,128)(2,1)S(1)}, bf16[192,512]{1,0:T(8,128)(2,1)S(1)}, u32[]{:S(2)}, u32[]{:S(2)}) %collective-permute-start.30) | collective-permute-done | bytes 196640 | tf_op jit(solution)/shard_map/ppermute | solution.py:501
  115.8 0.6 split.11
  116.4 3.1 %collective-permute-done.31.refs_1_ = bf16[1,136,512]{2,1,0:T(8,128)(2,1)S(1)} collective-permute-done((bf16[1,136,512]{2,1,0:T(8,128)(2,1)S(1)}, bf16[1,136,512]{2,1,0:T(8,128)(2,1)S(1)}, u32[]{:S(2)}, u32[]{:S(2)}) %collective-permute-start.31) | collective-permute-done | bytes 139296 | tf_op jit(solution)/shard_map/ppermute | solution.py:501
  120.1 2.3 %collective-permute-start.32 = (bf16[96,512]{1,0:T(8,128)(2,1)S(1)}, bf16[96,512]{1,0:T(8,128)(2,1)S(1)}, u32[]{:S(2)}, u32[]{:S(2)}) collective-permute-start(bf16[96,512]{1,0:T(8,128)(2,1)S(1)} %get-tuple-element.235), channel_id=1, source_target_pairs={{0,16},{4,20},{8,24},{12,28},{16,0},{20,4},{24,8},{28,12},{1,17},{... | collective-permute-start | bytes 294920 | tf_op jit(solution)/shard_map/ppermute | solution.py:501
  122.4 1.2 collective-permute-start.34
  123.6 2.5 %collective-permute-done.34.refs_4_ = f32[8,512]{1,0:T(8,128)S(1)} collective-permute-done((f32[8,512]{1,0:T(8,128)S(1)}, f32[8,512]{1,0:T(8,128)S(1)}, u32[]{:S(2)}, u32[]{:S(2)}) %collective-permute-start.34) | collective-permute-done | bytes 16416 | tf_op jit(solution)/shard_map/ppermute | solution.py:596
  126.1 1.2 collective-permute-done.35.refs_5_
  128.5 1.1 collective-permute-start.40
  129.6 1.3 collective-permute-start.37
  130.8 6.6 %collective-permute-done.37.refs_1_ = bf16[1,104,512]{2,1,0:T(8,128)(2,1)S(1)} collective-permute-done((bf16[1,104,512]{2,1,0:T(8,128)(2,1)S(1)}, bf16[1,104,512]{2,1,0:T(8,128)(2,1)S(1)}, u32[]{:S(2)}, u32[]{:S(2)}) %collective-permute-start.37) | collective-permute-done | bytes 106528 | tf_op jit(solution)/shard_map/ppermute | solution.py:501
  138.1 7.2 %collective-permute-done.38.refs_1_ = bf16[2,104,512]{2,1,0:T(8,128)(2,1)S(1)} collective-permute-done((bf16[2,104,512]{2,1,0:T(8,128)(2,1)S(1)}, bf16[2,104,512]{2,1,0:T(8,128)(2,1)S(1)}, u32[]{:S(2)}, u32[]{:S(2)}) %collective-permute-start.38) | collective-permute-done | bytes 213024 | tf_op jit(solution)/shard_map/ppermute | solution.py:501
  145.8 1.1 collective-permute-start.39
  146.9 2.1 %unpack.3 = (f32[512,512]{1,0:T(8,128)}, f32[512,512]{1,0:T(8,128)}, f32[8,512]{1,0:T(8,128)S(1)}) custom-call(s32[8]{0:T(128)S(1)} %copy-done.9, bf16[4,136,512]{2,1,0:T(8,128)(2,1)S(1)} %join.5.refs_0_, bf16[4,136,512]{2,1,0:T(8,128)(2,1)S(1)} %collective-permute-done.40.refs_1_), custom_call_target="tpu_custom_call" | custom-call | tf_op jit(solution)/shard_map/unpack/pallas_call | solution.py:41
  149.6 7.2 %collective-permute-done.39.refs_1_ = bf16[4,104,512]{2,1,0:T(8,128)(2,1)S(1)} collective-permute-done((bf16[4,104,512]{2,1,0:T(8,128)(2,1)S(1)}, bf16[4,104,512]{2,1,0:T(8,128)(2,1)S(1)}, u32[]{:S(2)}, u32[]{:S(2)}) %collective-permute-start.39) | collective-permute-done | bytes 426016 | tf_op jit(solution)/shard_map/ppermute | solution.py:501
  156.8 2.0 %unpack.2 = (f32[512,128]{1,0:T(8,128)}, f32[512,128]{1,0:T(8,128)}, f32[512,128]{1,0:T(8,128)}, f32[128,512]{1,0:T(8,128)}, f32[128,512]{1,0:T(8,128)}, /*index=5*/f32[128,512]{1,0:T(8,128)}, f32[8,512]{1,0:T(8,128)S(1)}) custom-call(s32[8]{0:T(128)S(1)} %copy-done.9, bf16[4,104,512]{2,1,0:T(8,128)(2,1)S(1)} %join.7.refs_0_, ...), custom_call_target="tpu_custom_call" | custom-call | tf_op jit(solution)/shard_map/unpack/pallas_call | solution.py:41
  159.3 0.6 fusion
  (75 shorter events, 11.3 us)
Async XLA Ops:
  0.7 8.0 %copy-start.5 = (bf16[256,512]{1,0:T(8,128)(2,1)S(1)}, bf16[256,512]{1,0:T(8,128)(2,1)}, u32[]{:S(2)}) copy-start(bf16[256,512]{1,0:T(8,128)(2,1)} %x0.5) | copy-start | bytes 786436
  0.7 21.1 %copy-start.10 = (s32[1,1024]{1,0:T(1,128)S(1)}, s32[1,1024]{1,0:T(1,128)}, u32[]{:S(2)}) copy-start(s32[1,1024]{1,0:T(1,128)} %segs.7) | copy-start | bytes 12292
  1.9 19.9 %copy-start.9 = (s32[8]{0:T(128)S(1)}, s32[8]{0:T(128)}, u32[]{:S(2)}) copy-start(s32[8]{0:T(128)} %compare_select_fusion.pos.tb) | copy-start | bytes 100
  6.1 2.1 %collective-permute-start.3 = (bf16[520,384]{1,0:T(8,128)(2,1)}, bf16[520,384]{1,0:T(8,128)(2,1)S(1)}, u32[]{:S(2)}, u32[]{:S(2)}) collective-permute-start(bf16[520,384]{1,0:T(8,128)(2,1)} %get-tuple-element.139.qkv0), channel_id=1, source_target_pairs={{0,1},{1,0},{2,3},{3,2},{4,5},{5,4},{6,7},{7,6},{8,9},{9,8},{10,11... | collective-permute-start | bytes 1198088 | tf_op jit(solution)/shard_map/ppermute | solution.py:596
  8.2 34.4 %collective-permute-start.6 = (bf16[1416,512]{1,0:T(8,128)(2,1)}, bf16[1416,512]{1,0:T(8,128)(2,1)S(1)}, u32[]{:S(2)}, u32[]{:S(2)}) collective-permute-start(bf16[1416,512]{1,0:T(8,128)(2,1)} %get-tuple-element.154), channel_id=1, source_target_pairs={{0,1},{1,0},{2,3},{3,2},{4,5},{5,4},{6,7},{7,6},{8,9},{9,8},{10,11... | collective-permute-start | bytes 4349960 | tf_op jit(solution)/shard_map/ppermute | solution.py:596
  8.6 9.5 %collective-permute-start = (bf16[256,512]{1,0:T(8,128)(2,1)S(1)}, bf16[256,512]{1,0:T(8,128)(2,1)S(1)}, u32[]{:S(2)}, u32[]{:S(2)}) collective-permute-start(bf16[256,512]{1,0:T(8,128)(2,1)S(1)} %copy-done.5), channel_id=1, source_target_pairs={{0,2},{1,3},{2,0},{3,1},{4,6},{5,7},{6,4},{7,5},{8,10},{9,11},{10,... | collective-permute-start | bytes 786440 | tf_op jit(solution)/shard_map/ppermute | solution.py:596
  18.1 12.4 %collective-permute-start.5 = (bf16[392,512]{1,0:T(8,128)(2,1)}, bf16[392,512]{1,0:T(8,128)(2,1)S(1)}, u32[]{:S(2)}, u32[]{:S(2)}) collective-permute-start(bf16[392,512]{1,0:T(8,128)(2,1)} %get-tuple-element.152.e0), channel_id=1, source_target_pairs={{0,2},{1,3},{2,0},{3,1},{4,6},{5,7},{6,4},{7,5},{8,10},{9,11},{10,... | collective-permute-start | bytes 1204232 | tf_op jit(solution)/shard_map/ppermute | solution.py:596
  19.8 1.5 collective-permute-start.1
  19.8 1.9 %collective-permute-start.2 = (bf16[256,512]{1,0:T(8,128)(2,1)S(1)}, bf16[256,512]{1,0:T(8,128)(2,1)S(1)}, u32[]{:S(2)}, u32[]{:S(2)}) collective-permute-start(bf16[256,512]{1,0:T(8,128)(2,1)S(1)} %collective-permute-done.x1), channel_id=1, source_target_pairs={{0,1},{1,0},{2,3},{3,2},{4,5},{5,4},{6,7},{7,6},{8,9},{9,8},{10,11... | collective-permute-start | bytes 786440 | tf_op jit(solution)/shard_map/ppermute | solution.py:596
  20.4 14.7 %collective-permute-start.8 = (bf16[264,512]{1,0:T(8,128)(2,1)}, bf16[264,512]{1,0:T(8,128)(2,1)S(1)}, u32[]{:S(2)}, u32[]{:S(2)}) collective-permute-start(bf16[264,512]{1,0:T(8,128)(2,1)} %get-tuple-element.136), channel_id=1, source_target_pairs={{0,2},{1,3},{2,0},{3,1},{4,6},{5,7},{6,4},{7,5},{8,10},{9,11},{10,... | collective-permute-start | bytes 811016 | tf_op jit(solution)/shard_map/ppermute | solution.py:596
  21.8 1.0 copy-start.3
  22.8 0.8 copy-start.6
  23.5 17.8 %copy-start.4 = (bf16[520,384]{1,0:T(8,128)(2,1)S(1)}, bf16[520,384]{1,0:T(8,128)(2,1)}, u32[]{:S(2)}) copy-start(bf16[520,384]{1,0:T(8,128)(2,1)} %get-tuple-element.139.qkv0) | copy-start | bytes 1198084
  30.5 12.1 %collective-permute-start.7 = (bf16[392,512]{1,0:T(8,128)(2,1)S(1)}, bf16[392,512]{1,0:T(8,128)(2,1)S(1)}, u32[]{:S(2)}, u32[]{:S(2)}) collective-permute-start(bf16[392,512]{1,0:T(8,128)(2,1)S(1)} %collective-permute-done.5.e1), channel_id=1, source_target_pairs={{0,1},{1,0},{2,3},{3,2},{4,5},{5,4},{6,7},{7,6},{8,9},{9,8},{10,11... | collective-permute-start | bytes 1204232 | tf_op jit(solution)/shard_map/ppermute | solution.py:596
  35.1 9.0 %collective-permute-start.12 = (bf16[264,512]{1,0:T(8,128)(2,1)S(1)}, bf16[264,512]{1,0:T(8,128)(2,1)S(1)}, u32[]{:S(2)}, u32[]{:S(2)}) collective-permute-start(bf16[264,512]{1,0:T(8,128)(2,1)S(1)} %collective-permute-done.8.s0), channel_id=1, source_target_pairs={{0,8},{4,12},{8,0},{12,4},{16,24},{20,28},{24,16},{28,20},{1,9},{5... | collective-permute-start | bytes 811016 | tf_op jit(solution)/shard_map/ppermute | solution.py:501
  36.7 5.9 %collective-permute-start.4 = (bf16[256,256]{1,0:T(8,128)(2,1)S(1)}, bf16[256,256]{1,0:T(8,128)(2,1)S(1)}, u32[]{:S(2)}, u32[]{:S(2)}) collective-permute-start(bf16[256,256]{1,0:T(8,128)(2,1)S(1)} %get-tuple-element.150), channel_id=1, source_target_pairs={{0,2},{1,3},{2,0},{3,1},{4,6},{5,7},{6,4},{7,5},{8,10},{9,11},{10,... | collective-permute-start | bytes 393224 | tf_op jit(solution)/shard_map/ppermute | solution.py:596
  38.2 7.0 %collective-permute-start.10 = (bf16[264,512]{1,0:T(8,128)(2,1)S(1)}, bf16[264,512]{1,0:T(8,128)(2,1)S(1)}, u32[]{:S(2)}, u32[]{:S(2)}) collective-permute-start(bf16[264,512]{1,0:T(8,128)(2,1)S(1)} %collective-permute-done.8.s0), channel_id=1, source_target_pairs={{0,4},{4,0},{8,12},{12,8},{16,20},{20,16},{24,28},{28,24},{1,5},{5... | collective-permute-start | bytes 811016 | tf_op jit(solution)/shard_map/ppermute | solution.py:501
  39.7 3.0 %copy-start.2 = (bf16[392,512]{1,0:T(8,128)(2,1)S(1)}, bf16[392,512]{1,0:T(8,128)(2,1)}, u32[]{:S(2)}) copy-start(bf16[392,512]{1,0:T(8,128)(2,1)} %get-tuple-element.152.e0) | copy-start | bytes 1204228
  39.7 3.0 %copy-start.7 = (f32[16,512]{1,0:T(8,128)S(1)}, f32[16,512]{1,0:T(8,128)}, u32[]{:S(2)}) copy-start(f32[16,512]{1,0:T(8,128)} %get-tuple-element.138.vecs) | copy-start | bytes 98308
  42.6 2.6 %copy-start = (bf16[512,512]{1,0:T(8,128)(2,1)S(1)}, bf16[512,512]{1,0:T(8,128)(2,1)}, u32[]{:S(2)}) copy-start(bf16[512,512]{1,0:T(8,128)(2,1)} %win0.5) | copy-start | bytes 1572868
  42.7 2.5 %copy-start.1 = (bf16[512,512]{1,0:T(8,128)(2,1)S(1)}, bf16[512,512]{1,0:T(8,128)(2,1)}, u32[]{:S(2)}) copy-start(bf16[512,512]{1,0:T(8,128)(2,1)} %wback0.5) | copy-start | bytes 1572868
  44.1 8.6 %copy-start.8 = (bf16[256,512]{1,0:T(8,128)(2,1)S(1)}, bf16[256,512]{1,0:T(8,128)(2,1)}, u32[]{:S(2)}) copy-start(bf16[256,512]{1,0:T(8,128)(2,1)} %ct.3) | copy-start | bytes 786436
  44.1 6.8 %collective-permute-start.14 = (bf16[264,512]{1,0:T(8,128)(2,1)S(1)}, bf16[264,512]{1,0:T(8,128)(2,1)S(1)}, u32[]{:S(2)}, u32[]{:S(2)}) collective-permute-start(bf16[264,512]{1,0:T(8,128)(2,1)S(1)} %collective-permute-done.12.s4), channel_id=1, source_target_pairs={{0,4},{4,0},{8,12},{12,8},{16,20},{20,16},{24,28},{28,24},{1,5},{5... | collective-permute-start | bytes 811016 | tf_op jit(solution)/shard_map/ppermute | solution.py:501
  44.7 7.9 %collective-permute-start.9 = (bf16[264,512]{1,0:T(8,128)(2,1)S(1)}, bf16[264,512]{1,0:T(8,128)(2,1)S(1)}, u32[]{:S(2)}, u32[]{:S(2)}) collective-permute-start(bf16[264,512]{1,0:T(8,128)(2,1)S(1)} %collective-permute-done.8.s0), channel_id=1, source_target_pairs={{0,1},{1,0},{2,3},{3,2},{4,5},{5,4},{6,7},{7,6},{8,9},{9,8},{10,11... | collective-permute-start | bytes 811016 | tf_op jit(solution)/shard_map/ppermute | solution.py:596
  44.7 7.9 %collective-permute-start.13 = (bf16[264,512]{1,0:T(8,128)(2,1)S(1)}, bf16[264,512]{1,0:T(8,128)(2,1)S(1)}, u32[]{:S(2)}, u32[]{:S(2)}) collective-permute-start(bf16[264,512]{1,0:T(8,128)(2,1)S(1)} %collective-permute-done.12.s4), channel_id=1, source_target_pairs={{0,1},{1,0},{2,3},{3,2},{4,5},{5,4},{6,7},{7,6},{8,9},{9,8},{10,11... | collective-permute-start | bytes 811016 | tf_op jit(solution)/shard_map/ppermute | solution.py:596
  45.2 7.4 %collective-permute-start.11 = (bf16[264,512]{1,0:T(8,128)(2,1)S(1)}, bf16[264,512]{1,0:T(8,128)(2,1)S(1)}, u32[]{:S(2)}, u32[]{:S(2)}) collective-permute-start(bf16[264,512]{1,0:T(8,128)(2,1)S(1)} %collective-permute-done.10.s2), channel_id=1, source_target_pairs={{0,1},{1,0},{2,3},{3,2},{4,5},{5,4},{6,7},{7,6},{8,9},{9,8},{10,11... | collective-permute-start | bytes 811016 | tf_op jit(solution)/shard_map/ppermute | solution.py:596
  50.9 1.7 %collective-permute-start.15 = (bf16[264,512]{1,0:T(8,128)(2,1)S(1)}, bf16[264,512]{1,0:T(8,128)(2,1)S(1)}, u32[]{:S(2)}, u32[]{:S(2)}) collective-permute-start(bf16[264,512]{1,0:T(8,128)(2,1)S(1)} %collective-permute-done.14.s6), channel_id=1, source_target_pairs={{0,1},{1,0},{2,3},{3,2},{4,5},{5,4},{6,7},{7,6},{8,9},{9,8},{10,11... | collective-permute-start | bytes 811016 | tf_op jit(solution)/shard_map/ppermute | solution.py:596
  50.9 12.2 %collective-permute-start.16 = (bf16[256,512]{1,0:T(8,128)(2,1)S(1)}, bf16[256,512]{1,0:T(8,128)(2,1)S(1)}, u32[]{:S(2)}, u32[]{:S(2)}) collective-permute-start(bf16[256,512]{1,0:T(8,128)(2,1)S(1)} %get-tuple-element.156.n2), channel_id=1, source_target_pairs={{0,2},{1,3},{2,0},{3,1},{4,6},{5,7},{6,4},{7,5},{8,10},{9,11},{10,... | collective-permute-start | bytes 786440 | tf_op jit(solution)/shard_map/ppermute | solution.py:596
  55.5 10.1 %collective-permute-start.17 = (bf16[256,512]{1,0:T(8,128)(2,1)S(1)}, bf16[256,512]{1,0:T(8,128)(2,1)S(1)}, u32[]{:S(2)}, u32[]{:S(2)}) collective-permute-start(bf16[256,512]{1,0:T(8,128)(2,1)S(1)} %get-tuple-element.166.fg), channel_id=1, source_target_pairs={{0,2},{1,3},{2,0},{3,1},{4,6},{5,7},{6,4},{7,5},{8,10},{9,11},{10,... | collective-permute-start | bytes 786440 | tf_op jit(solution)/shard_map/ppermute | solution.py:596
  60.5 9.3 %collective-permute-start.18 = (bf16[256,256]{1,0:T(8,128)(2,1)S(1)}, bf16[256,256]{1,0:T(8,128)(2,1)S(1)}, u32[]{:S(2)}, u32[]{:S(2)}) collective-permute-start(bf16[256,256]{1,0:T(8,128)(2,1)S(1)} %get-tuple-element.185), channel_id=1, source_target_pairs={{0,2},{1,3},{2,0},{3,1},{4,6},{5,7},{6,4},{7,5},{8,10},{9,11},{10,... | collective-permute-start | bytes 393224 | tf_op jit(solution)/shard_map/ppermute | solution.py:596
  71.0 6.0 %collective-permute-start.21 = (bf16[776,512]{1,0:T(8,128)(2,1)S(1)}, bf16[776,512]{1,0:T(8,128)(2,1)S(1)}, u32[]{:S(2)}, u32[]{:S(2)}) collective-permute-start(bf16[776,512]{1,0:T(8,128)(2,1)S(1)} %get-tuple-element.196), channel_id=1, source_target_pairs={{0,1},{1,0},{2,3},{3,2},{4,5},{5,4},{6,7},{7,6},{8,9},{9,8},{10,11... | collective-permute-start | bytes 2383880 | tf_op jit(solution)/shard_map/ppermute | solution.py:596
  71.1 3.8 %collective-permute-start.20 = (bf16[520,512]{1,0:T(8,128)(2,1)S(1)}, bf16[520,512]{1,0:T(8,128)(2,1)S(1)}, u32[]{:S(2)}, u32[]{:S(2)}) collective-permute-start(bf16[520,512]{1,0:T(8,128)(2,1)S(1)} %get-tuple-element.193), channel_id=1, source_target_pairs={{0,1},{1,0},{2,3},{3,2},{4,5},{5,4},{6,7},{7,6},{8,9},{9,8},{10,11... | collective-permute-start | bytes 1597448 | tf_op jit(solution)/shard_map/ppermute | solution.py:596
  71.6 3.3 %collective-permute-start.19 = (bf16[512,512]{1,0:T(8,128)(2,1)S(1)}, bf16[512,512]{1,0:T(8,128)(2,1)S(1)}, u32[]{:S(2)}, u32[]{:S(2)}) collective-permute-start(bf16[512,512]{1,0:T(8,128)(2,1)S(1)} %get-tuple-element.192), channel_id=1, source_target_pairs={{0,1},{1,0},{2,3},{3,2},{4,5},{5,4},{6,7},{7,6},{8,9},{9,8},{10,11... | collective-permute-start | bytes 1572872 | tf_op jit(solution)/shard_map/ppermute | solution.py:596
  75.9 14.0 %collective-permute-start.22 = (bf16[512,512]{1,0:T(8,128)(2,1)S(1)}, bf16[512,512]{1,0:T(8,128)(2,1)S(1)}, u32[]{:S(2)}, u32[]{:S(2)}) collective-permute-start(bf16[512,512]{1,0:T(8,128)(2,1)S(1)} %get-tuple-element.210), channel_id=1, source_target_pairs={{0,4},{4,0},{8,12},{12,8},{16,20},{20,16},{24,28},{28,24},{1,5},{5... | collective-permute-start | bytes 1572872 | tf_op jit(solution)/shard_map/ppermute | solution.py:501
  82.4 8.4 %collective-permute-start.23 = (bf16[392,512]{1,0:T(8,128)(2,1)S(1)}, bf16[392,512]{1,0:T(8,128)(2,1)S(1)}, u32[]{:S(2)}, u32[]{:S(2)}) collective-permute-start(bf16[392,512]{1,0:T(8,128)(2,1)S(1)} %get-tuple-element.214), channel_id=1, source_target_pairs={{0,1},{1,0},{2,3},{3,2},{4,5},{5,4},{6,7},{7,6},{8,9},{9,8},{10,11... | collective-permute-start | bytes 1204232 | tf_op jit(solution)/shard_map/ppermute | solution.py:596
  83.2 11.3 %collective-permute-start.24 = (bf16[392,512]{1,0:T(8,128)(2,1)S(1)}, bf16[392,512]{1,0:T(8,128)(2,1)S(1)}, u32[]{:S(2)}, u32[]{:S(2)}) collective-permute-start(bf16[392,512]{1,0:T(8,128)(2,1)S(1)} %half_rows.1), channel_id=1, source_target_pairs={{0,2},{1,3},{2,0},{3,1},{4,6},{5,7},{6,4},{7,5},{8,10},{9,11},{10,... | collective-permute-start | bytes 1204232 | tf_op jit(solution)/shard_map/ppermute | solution.py:596
  84.6 12.4 %collective-permute-start.25 = (bf16[512,512]{1,0:T(8,128)(2,1)S(1)}, bf16[512,512]{1,0:T(8,128)(2,1)S(1)}, u32[]{:S(2)}, u32[]{:S(2)}) collective-permute-start(bf16[512,512]{1,0:T(8,128)(2,1)S(1)} %get-tuple-element.218), channel_id=1, source_target_pairs={{0,1},{1,0},{2,3},{3,2},{4,5},{5,4},{6,7},{7,6},{8,9},{9,8},{10,11... | collective-permute-start | bytes 1572872 | tf_op jit(solution)/shard_map/ppermute | solution.py:596
  95.5 11.6 %collective-permute-start.27 = (bf16[384,512]{1,0:T(8,128)(2,1)S(1)}, bf16[384,512]{1,0:T(8,128)(2,1)S(1)}, u32[]{:S(2)}, u32[]{:S(2)}) collective-permute-start(bf16[384,512]{1,0:T(8,128)(2,1)S(1)} %get-tuple-element.223), channel_id=1, source_target_pairs={{0,4},{4,0},{8,12},{12,8},{16,20},{20,16},{24,28},{28,24},{1,5},{5... | collective-permute-start | bytes 1179656 | tf_op jit(solution)/shard_map/ppermute | solution.py:501
  96.6 7.2 %collective-permute-start.26 = (bf16[256,512]{1,0:T(8,128)(2,1)S(1)}, bf16[256,512]{1,0:T(8,128)(2,1)S(1)}, u32[]{:S(2)}, u32[]{:S(2)}) collective-permute-start(bf16[256,512]{1,0:T(8,128)(2,1)S(1)} %get-tuple-element.220), channel_id=1, source_target_pairs={{0,8},{4,12},{8,0},{12,4},{16,24},{20,28},{24,16},{28,20},{1,9},{5... | collective-permute-start | bytes 786440 | tf_op jit(solution)/shard_map/ppermute | solution.py:501
  97.6 10.7 %collective-permute-start.28 = (bf16[512,256]{1,0:T(8,128)(2,1)S(1)}, bf16[512,256]{1,0:T(8,128)(2,1)S(1)}, u32[]{:S(2)}, u32[]{:S(2)}) collective-permute-start(bf16[512,256]{1,0:T(8,128)(2,1)S(1)} %half_columns.1), channel_id=1, source_target_pairs={{0,2},{1,3},{2,0},{3,1},{4,6},{5,7},{6,4},{7,5},{8,10},{9,11},{10,... | collective-permute-start | bytes 786440 | tf_op jit(solution)/shard_map/ppermute | solution.py:596
  104.4 7.3 %collective-permute-start.29 = (bf16[128,512]{1,0:T(8,128)(2,1)S(1)}, bf16[128,512]{1,0:T(8,128)(2,1)S(1)}, u32[]{:S(2)}, u32[]{:S(2)}) collective-permute-start(bf16[128,512]{1,0:T(8,128)(2,1)S(1)} %get-tuple-element.229), channel_id=1, source_target_pairs={{0,16},{4,20},{8,24},{12,28},{16,0},{20,4},{24,8},{28,12},{1,17},{... | collective-permute-start | bytes 393224 | tf_op jit(solution)/shard_map/ppermute | solution.py:501
  107.7 8.0 %collective-permute-start.30 = (bf16[192,512]{1,0:T(8,128)(2,1)S(1)}, bf16[192,512]{1,0:T(8,128)(2,1)S(1)}, u32[]{:S(2)}, u32[]{:S(2)}) collective-permute-start(bf16[192,512]{1,0:T(8,128)(2,1)S(1)} %get-tuple-element.231), channel_id=1, source_target_pairs={{0,8},{4,12},{8,0},{12,4},{16,24},{20,28},{24,16},{28,20},{1,9},{5... | collective-permute-start | bytes 589832 | tf_op jit(solution)/shard_map/ppermute | solution.py:501
  112.2 7.2 %collective-permute-start.31 = (bf16[1,136,512]{2,1,0:T(8,128)(2,1)S(1)}, bf16[1,136,512]{2,1,0:T(8,128)(2,1)S(1)}, u32[]{:S(2)}, u32[]{:S(2)}) collective-permute-start(bf16[1,136,512]{2,1,0:T(8,128)(2,1)S(1)} %bitcast.15), channel_id=1, source_target_pairs={{0,16},{4,20},{8,24},{12,28},{16,0},{20,4},{24,8},{28,12},{1,17},{... | collective-permute-start | bytes 417800 | tf_op jit(solution)/shard_map/ppermute | solution.py:501
  120.0 7.9 %collective-permute-start.36 = (bf16[2,136,512]{2,1,0:T(8,128)(2,1)S(1)}, bf16[2,136,512]{2,1,0:T(8,128)(2,1)S(1)}, u32[]{:S(2)}, u32[]{:S(2)}) collective-permute-start(bf16[2,136,512]{2,1,0:T(8,128)(2,1)S(1)} %join.4.refs_0_), channel_id=1, source_target_pairs={{0,8},{4,12},{8,0},{12,4},{16,24},{20,28},{24,16},{28,20},{1,9},{5... | collective-permute-start | bytes 835592 | tf_op jit(solution)/shard_map/ppermute | solution.py:501
  120.1 7.2 %collective-permute-start.32 = (bf16[96,512]{1,0:T(8,128)(2,1)S(1)}, bf16[96,512]{1,0:T(8,128)(2,1)S(1)}, u32[]{:S(2)}, u32[]{:S(2)}) collective-permute-start(bf16[96,512]{1,0:T(8,128)(2,1)S(1)} %get-tuple-element.235), channel_id=1, source_target_pairs={{0,16},{4,20},{8,24},{12,28},{16,0},{20,4},{24,8},{28,12},{1,17},{... | collective-permute-start | bytes 294920 | tf_op jit(solution)/shard_map/ppermute | solution.py:501
  122.4 3.7 %collective-permute-start.34 = (f32[8,512]{1,0:T(8,128)S(1)}, f32[8,512]{1,0:T(8,128)S(1)}, u32[]{:S(2)}, u32[]{:S(2)}) collective-permute-start(f32[8,512]{1,0:T(8,128)S(1)} %get-tuple-element.236.refs_2_), channel_id=1, source_target_pairs={{0,2},{1,3},{2,0},{3,1},{4,6},{5,7},{6,4},{7,5},{8,10},{9,11},{10,... | collective-permute-start | bytes 49160 | tf_op jit(solution)/shard_map/ppermute | solution.py:596
  123.6 2.5 %collective-permute-start.33 = (f32[8,512]{1,0:T(8,128)S(1)}, f32[8,512]{1,0:T(8,128)S(1)}, u32[]{:S(2)}, u32[]{:S(2)}) collective-permute-start(f32[8,512]{1,0:T(8,128)S(1)} %get-tuple-element.236.refs_2_), channel_id=1, source_target_pairs={{0,1},{1,0},{2,3},{3,2},{4,5},{5,4},{6,7},{7,6},{8,9},{9,8},{10,11... | collective-permute-start | bytes 49160 | tf_op jit(solution)/shard_map/ppermute | solution.py:596
  126.1 1.2 collective-permute-start.35
  128.5 18.4 %collective-permute-start.40 = (bf16[4,136,512]{2,1,0:T(8,128)(2,1)S(1)}, bf16[4,136,512]{2,1,0:T(8,128)(2,1)S(1)}, u32[]{:S(2)}, u32[]{:S(2)}) collective-permute-start(bf16[4,136,512]{2,1,0:T(8,128)(2,1)S(1)} %join.5.refs_0_), channel_id=1, source_target_pairs={{0,4},{4,0},{8,12},{12,8},{16,20},{20,16},{24,28},{28,24},{1,5},{5... | collective-permute-start | bytes 1671176 | tf_op jit(solution)/shard_map/ppermute | solution.py:501
  129.6 7.9 %collective-permute-start.37 = (bf16[1,104,512]{2,1,0:T(8,128)(2,1)S(1)}, bf16[1,104,512]{2,1,0:T(8,128)(2,1)S(1)}, u32[]{:S(2)}, u32[]{:S(2)}) collective-permute-start(bf16[1,104,512]{2,1,0:T(8,128)(2,1)S(1)} %bitcast.17), channel_id=1, source_target_pairs={{0,16},{4,20},{8,24},{12,28},{16,0},{20,4},{24,8},{28,12},{1,17},{... | collective-permute-start | bytes 319496 | tf_op jit(solution)/shard_map/ppermute | solution.py:501
  138.0 7.2 %collective-permute-start.38 = (bf16[2,104,512]{2,1,0:T(8,128)(2,1)S(1)}, bf16[2,104,512]{2,1,0:T(8,128)(2,1)S(1)}, u32[]{:S(2)}, u32[]{:S(2)}) collective-permute-start(bf16[2,104,512]{2,1,0:T(8,128)(2,1)S(1)} %join.6.refs_0_), channel_id=1, source_target_pairs={{0,8},{4,12},{8,0},{12,4},{16,24},{20,28},{24,16},{28,20},{1,9},{5... | collective-permute-start | bytes 638984 | tf_op jit(solution)/shard_map/ppermute | solution.py:501
  145.8 11.0 %collective-permute-start.39 = (bf16[4,104,512]{2,1,0:T(8,128)(2,1)S(1)}, bf16[4,104,512]{2,1,0:T(8,128)(2,1)S(1)}, u32[]{:S(2)}, u32[]{:S(2)}) collective-permute-start(bf16[4,104,512]{2,1,0:T(8,128)(2,1)S(1)} %join.7.refs_0_), channel_id=1, source_target_pairs={{0,4},{4,0},{8,12},{12,8},{16,20},{20,16},{24,28},{28,24},{1,5},{5... | collective-permute-start | bytes 1277960 | tf_op jit(solution)/shard_map/ppermute | solution.py:501

commit v3 on v2

--- a/solution.py
+++ b/solution.py
@@ -16,6 +16,7 @@
 PX = 2
 LOCAL = (0, PX, 1, 1 ^ PX)
 SPARE = 4 * 1024 * 1024
+COST = 10**10
 
 
 def nn(a, b):
@@ -45,7 +46,7 @@
         out_specs=tuple([VM] * len(outs)),
         scratch_shapes=list(scratch),
         compiler_params=pltpu.CompilerParams(vmem_limit_bytes=limit),
-        cost_estimate=pl.CostEstimate(flops=0, bytes_accessed=0, transcendentals=0),
+        cost_estimate=pl.CostEstimate(flops=COST, bytes_accessed=0, transcendentals=0),
         name=name,
     )(*args)
 
@@ -493,98 +494,123 @@
     out_ref[...] = (keep[...] + recv[:, half:].astype(F32)).astype(BF16)
 
 
-def stages_of(n_dp):
-    return [(shift, 2) for shift in range(n_dp.bit_length() - 1)]
-
-
-def dp_hop(value, mask, n_dp):
-    return lax.ppermute(value, "dp", [(i, i ^ mask) for i in range(n_dp)])
-
-
 def padded(rows, n_dp):
     unit = 8 * n_dp
     return -(-rows // unit) * unit
 
 
-def split_into(total, pos, shift, size, outs):
-    rows = total.shape[0] // size
-    mine = (pos[4] >> shift) & (size - 1)
-    for k, out in enumerate(outs):
-        at = pl.multiple_of((mine ^ k) * rows, 8)
-        out[...] = total[pl.ds(at, rows), :].astype(out.dtype)
-
-
-def split_kernel(pos, *refs, parts, shift, size):
-    count = sum(len(p[1]) for p in parts)
-    ins, outs, total = refs[:count], refs[count:-1], refs[-1]
-    at, used = 0, 0
-    for rows, takes in parts:
-        value = ins[used][takes[0] : takes[0] + rows, :].astype(F32)
-        for ref, start in zip(ins[used + 1 : used + len(takes)], takes[1:]):
-            value = value + ref[start : start + rows, :].astype(F32)
-        total[at : at + rows, :] = value
-        used += len(takes)
-        at += rows
-    if at < total.shape[0]:
-        total[at:, :] = jnp.zeros((total.shape[0] - at, 512), F32)
-    split_into(total, pos, shift, size, outs)
-
-
-def small_kernel(pos, *refs, rows, count, small):
+def bit_of(pos, b):
+    return (pos[4] >> b) & 1
+
+
+def sum_into(dst, at, addends, rows):
+    value = None
+    for ref, start in addends:
+        block = ref[start : start + rows, :].astype(F32)
+        value = block if value is None else value + block
+    dst[at : at + rows, :] = value
+
+
+def cut_rows(total, at, rows, bit, own, own_at, send, send_at):
+    half = rows // 2
+    mine = pl.multiple_of(at + bit * half, 8)
+    other = pl.multiple_of(at + (1 - bit) * half, 8)
+    own[own_at : own_at + half, :] = total[pl.ds(mine, half), :]
+    send[send_at : send_at + half, :] = total[pl.ds(other, half), :].astype(BF16)
+
+
+def pick(refs, groups):
+    it = iter(refs)
+    return [(rows, [(next(it), start) for start in starts]) for rows, starts in groups]
+
+
+def halves_kernel(pos, *refs, parts, rows, bits):
+    count = sum(len(starts) for groups in parts for _, starts in groups)
+    ins, (own1, send1, own2, send2, total) = refs[:count], refs[count:]
+    used = 0
+    for groups, bit, own, send in zip(parts, bits, (own1, own2), (send1, send2)):
+        need = sum(len(starts) for _, starts in groups)
+        at = 0
+        for size, addends in pick(ins[used : used + need], groups):
+            sum_into(total, at, addends, size)
+            at += size
+        used += need
+        if at < rows:
+            total[at:, :] = jnp.zeros((rows - at, 512), F32)
+        cut_rows(total, 0, rows, bit_of(pos, bit), own, 0, send, 0)
+
+
+def merge_kernel(pos, own1, recv1, own2, recv2, own, send, total, *, bit):
+    rows = own1.shape[0]
+    for i, (o, r) in enumerate(((own1, recv1), (own2, recv2))):
+        total[...] = o[...] + r[...].astype(F32)
+        cut_rows(total, 0, rows, bit_of(pos, bit), own, i * rows // 2, send, i * rows // 2)
+
+
+def both_kernel(pos, own0, recv0, own, send, total, *, bit):
+    rows = own0.shape[0] // 2
+    total[...] = own0[...] + recv0[...].astype(F32)
+    for i in range(2):
+        cut_rows(total, i * rows, rows, bit_of(pos, bit), own, i * rows // 2, send, i * rows // 2)
+
+
+def fold_kernel(pos, own, recv, *refs, small):
     out = refs[-1]
-    value = refs[0][...].astype(F32)
-    for r in refs[1:count]:
-        value = value + r[...].astype(F32)
-    out[0:rows, :] = value.astype(BF16)
-    if small:
-        at = count
-        out[rows : rows + 8, :] = jnp.zeros((8, 512), BF16)
-        for first, size, starts in small:
-            block = refs[at][starts[0] : starts[0] + size, :].astype(F32)
-            for r, start in zip(refs[at + 1 : at + len(starts)], starts[1:]):
-                block = block + r[start : start + size, :].astype(F32)
-            out[rows + first : rows + first + size, :] = block.astype(BF16)
-            at += len(starts)
-
-
-def join_kernel(pos, *refs):
-    out = refs[-1]
-    size = refs[0].shape[0]
-    for i, r in enumerate(refs[:-1]):
-        out[i * size : i * size + size] = r[...]
-
-
-def unpack_kernel(pos, *refs, count, plan, rows, has_small, stages):
-    place = 0
-    for shift, size in stages:
-        place = place * size + ((pos[4] >> shift) & (size - 1))
-    blocks, outs, scratch = refs[:count], refs[count:-1], refs[-1]
-    each = blocks[0].shape[0]
-    for i in range(count * each):
-        at = pl.multiple_of((place ^ i) * rows, 8)
-        scratch[pl.ds(at, rows), :] = blocks[i // each][i % each, 0:rows, :].astype(F32)
-    for out, (start, size, flip) in zip(outs, plan):
-        block = scratch[start : start + size, :]
-        out[...] = block.T if flip else block
-    if has_small:
-        total = jnp.zeros((8, 512), F32)
-        for b in blocks:
-            total = total + jnp.sum(b[:, rows:, :].astype(F32), axis=0)
-        outs[len(plan)][...] = total
-
-
-def unpack_call(pos, blocks, stages, plan, small):
-    rows = blocks[0].shape[1] - (8 if small else 0)
-    shapes = [sds((512, size) if flip else (size, 512), F32) for _, size, flip in plan]
-    if small:
-        shapes = shapes + [sds((8, 512), F32)]
-    total = rows * sum(b.shape[0] for b in blocks)
-    return call(
-        functools.partial(
-            unpack_kernel, count=len(blocks), plan=plan, rows=rows, has_small=bool(small), stages=tuple(stages)
-        ),
-        shapes, [pos] + blocks, smem=1, scratch=[pltpu.VMEM((total, 512), F32)], name="unpack",
-    )
+    rows = own.shape[0]
+    out[0:rows, :] = (own[...] + recv[...].astype(F32)).astype(BF16)
+    out[rows : rows + 8, :] = jnp.zeros((8, 512), BF16)
+    at = 0
+    for first, size, starts in small:
+        value = None
+        for ref, start in zip(refs[at : at + len(starts)], starts):
+            block = ref[start : start + size, :].astype(F32)
+            value = block if value is None else value + block
+        out[rows + first : rows + first + size, :] = value.astype(BF16)
+        at += len(starts)
+
+
+def stack_kernel(pos, held, recv, out):
+    size = held.shape[0]
+    out[0:size] = held[...]
+    out[size:] = recv[...]
+
+
+def part_kernel(pos, held, recv, out1, out2):
+    size, rows = held.shape[0], (held.shape[1] - 8) // 2
+    for i, r in enumerate((held, recv)):
+        at = slice(i * size, i * size + size)
+        out1[at, 0:rows, :] = r[:, 0:rows, :]
+        out1[at, rows : rows + 8, :] = r[:, 2 * rows :, :]
+        out2[at] = r[:, rows : 2 * rows, :]
+
+
+def pair_kernel(pos, held1, recv1, held2, recv2, out1, out2):
+    for out, h, r in ((out1, held1, recv1), (out2, held2, recv2)):
+        size = h.shape[0]
+        out[0:size] = h[...]
+        out[size:] = r[...]
+
+
+def unpack_kernel(pos, held1, recv1, held2, recv2, *refs, plans, orders):
+    outs, scratch = refs[:-1], refs[-1]
+    rows = held2.shape[1]
+    used = 0
+    for plan, order, blocks in zip(plans, orders, ((held1, recv1), (held2, recv2))):
+        place = 0
+        for b in order:
+            place = place * 2 + bit_of(pos, b)
+        each = blocks[0].shape[0]
+        for i in range(2 * each):
+            at = pl.multiple_of((place ^ i) * rows, 8)
+            scratch[pl.ds(at, rows), :] = blocks[i // each][i % each, 0:rows, :].astype(F32)
+        for start, size, flip in plan:
+            block = scratch[start : start + size, :]
+            outs[used][...] = block.T if flip else block
+            used += 1
+    total = jnp.zeros((8, 512), F32)
+    for r in (held1, recv1):
+        total = total + jnp.sum(r[:, rows:, :].astype(F32), axis=0)
+    outs[used][...] = total
 
 
 def body(
@@ -596,7 +622,7 @@
         return lax.ppermute(value, "tensor", [(i, i ^ mask) for i in range(4)])
 
     def dhop(value, mask):
-        return dp_hop(value, mask, n_dp)
+        return lax.ppermute(value, "dp", [(i, i ^ mask) for i in range(n_dp)])
 
     def after(value, *deps):
         return lax.optimization_barrier((value,) + deps)[0]
@@ -719,45 +745,77 @@
         "small_weight", [pltpu.VMEM((512, 512), F32), pltpu.VMEM((512, 512), F32)], then=(dot1,),
     )
     srecv = hop(ssend, 1)
-    stages = stages_of(n_dp)
-
-    def split(parts, rows, stage):
-        shift, size = stage
-        arrays = [a for _, addends in parts for a, _ in addends]
-        static = tuple((r, tuple(start for _, start in addends)) for r, addends in parts)
-        return step(
-            functools.partial(split_kernel, parts=static, shift=shift, size=size),
-            [sds((rows // size, 512), F32)] + [sds((rows // size, 512), BF16)] * (size - 1),
-            arrays, "split", [pltpu.VMEM((rows, 512), F32)],
+    bits = n_dp.bit_length() - 1
+
+    def halves(parts1, parts2, rows):
+        arrays = [a for parts in (parts1, parts2) for _, group in parts for a, _ in group]
+        static = tuple(
+            tuple((m, tuple(start for _, start in group)) for m, group in parts) for parts in (parts1, parts2)
         )
-
-    def send(pieces, stage):
-        return [pieces[0]] + [dhop(p, k << stage[0]) for k, p in enumerate(pieces[1:], 1)]
-
-    def resplit(pieces, i):
-        rows = pieces[0].shape[0]
-        return send(split([(rows, [(p, 0) for p in pieces])], rows, stages[i]), stages[i])
-
-    def fold(pieces, small):
-        rows = pieces[0].shape[0]
+        shapes = [sds((rows // 2, 512), F32), sds((rows // 2, 512), BF16)] * 2
+        o1, s1, o2, s2 = step(
+            functools.partial(halves_kernel, parts=static, rows=rows, bits=(0, 1)),
+            shapes, arrays, "halves", [pltpu.VMEM((rows, 512), F32)],
+        )
+        return o1, dhop(s1, 1), o2, dhop(s2, 2)
+
+    def quarter_step(o1, r1, o2, r2):
+        rows = o1.shape[0]
+        shapes = [sds((rows // 2, 512), F32), sds((rows // 2, 512), BF16)] * 2
+        o1, s1, o2, s2 = step(
+            functools.partial(halves_kernel, parts=(((rows, (0, 0)),),) * 2, rows=rows, bits=(1, 0)),
+            shapes, [o1, r1, o2, r2], "quarters", [pltpu.VMEM((rows, 512), F32)],
+        )
+        return o1, dhop(s1, 2), o2, dhop(s2, 1)
+
+    def merge_step(o1, r1, o2, r2):
+        rows = o1.shape[0]
+        own, sent = step(
+            functools.partial(merge_kernel, bit=2), [sds((rows, 512), F32), sds((rows, 512), BF16)],
+            [o1, r1, o2, r2], "merge", [pltpu.VMEM((rows, 512), F32)],
+        )
+        pair = own, dhop(sent, 4)
+        for b in range(3, bits):
+            rows = rows // 2
+            own, sent = step(
+                functools.partial(both_kernel, bit=b), [sds((rows, 512), F32), sds((rows, 512), BF16)],
+                list(pair), "both", [pltpu.VMEM((2 * rows, 512), F32)],
+            )
+            pair = own, dhop(sent, 1 << b)
+        return pair
+
+    def fold_step(own, recv, small):
+        rows = own.shape[0]
         static = tuple((f, m, tuple(start for _, start in group)) for f, m, group in small)
         arrays = [a for _, _, group in small for a, _ in group]
+        held = step(
+            functools.partial(fold_kernel, small=static), [sds((rows + 8, 512), BF16)], [own, recv] + arrays, "fold"
+        )[0][None]
+        for b in range(bits - 1, 2, -1):
+            shape = (2 * held.shape[0],) + held.shape[1:]
+            held = step(stack_kernel, [sds(shape, BF16)], [held, dhop(held, 1 << b)], "stack")[0]
+        return held, dhop(held, 4)
+
+    def part_step(held, recv):
+        size, rows = 2 * held.shape[0], (held.shape[1] - 8) // 2
+        h1, h2 = step(part_kernel, [sds((size, rows + 8, 512), BF16), sds((size, rows, 512), BF16)], [held, recv], "part")
+        return h1, dhop(h1, 2), h2, dhop(h2, 1)
+
+    def pair_step(h1, r1, h2, r2):
+        shapes = [sds((2 * h.shape[0],) + h.shape[1:], BF16) for h in (h1, h2)]
+        h1, h2 = step(pair_kernel, shapes, [h1, r1, h2, r2], "pair")
+        return h1, dhop(h1, 1), h2, dhop(h2, 2)
+
+    def unpack_step(h1, r1, h2, r2, plans):
+        shapes = [sds((512, size) if flip else (size, 512), F32) for plan in plans for _, size, flip in plan]
+        rest = tuple(range(2, bits))
+        rows = 2 * h2.shape[0] * h2.shape[1]
         return step(
-            functools.partial(small_kernel, rows=rows, count=len(pieces), small=static),
-            [sds((rows + (8 if small else 0), 512), BF16)], list(pieces) + arrays, "fold",
-        )[0]
-
-    def spread(held, i):
-        shift, size = stages[i]
-        return [held] + [dhop(held, k << shift) for k in range(1, size)]
-
-    def join(blocks):
-        shape = (len(blocks) * blocks[0].shape[0],) + blocks[0].shape[1:]
-        return step(join_kernel, [sds(shape, BF16)], blocks, "join")[0]
-
-    depth = len(stages)
-    rows_f, rows_a = padded(1024, n_dp), padded(768, n_dp)
-    f = send(split([(512, [(bkeep, 0), (brecv, 0)]), (512, [(ikeep, 0), (irecv, 0)])], rows_f, stages[0]), stages[0])
+            functools.partial(unpack_kernel, plans=plans, orders=((0, 1) + rest, (1, 0) + rest)),
+            shapes + [sds((8, 512), F32)], [h1, r1, h2, r2], "unpack", [pltpu.VMEM((rows, 512), F32)],
+        )
+
+    f = halves([(512, [(bkeep, 0), (brecv, 0)])], [(512, [(ikeep, 0), (irecv, 0)])], padded(512, n_dp))
     (spar,) = step(half_rows_kernel, [sds((392, 512), BF16)], [skeep, srecv], "half_rows")
     sparr = hop(spar, PX)
 
@@ -778,15 +836,14 @@
         "input_grad",
     )
     gsib = hop(gsend, 1)
-    f = resplit(f, 1)
-    a = send(
-        split([(384, [(akeep, 0), (arecv, 0)]), (384, [(skeep, 0), (srecv, 0), (sparr, 0)])], rows_a, stages[0]),
-        stages[0],
+    f = quarter_step(*f)
+    a = halves(
+        [(384, [(akeep, 0), (arecv, 0)])], [(384, [(skeep, 0), (srecv, 0), (sparr, 0)])], padded(384, n_dp)
     )
     (gsum,) = step(half_columns_kernel, [sds((512, 256), BF16)], [gpar, gsib], "half_columns")
     gp = hop(gsum, PX)
-    f = resplit(f, 2)
-    a = resplit(a, 1)
+    f = merge_step(*f)
+    a = quarter_step(*a)
     input_grad, sums1 = step(
         last_kernel,
         [sds((256, 512), F32), sds((8, 512), F32)],
@@ -795,30 +852,26 @@
     )
     sums1_b = hop(sums1, PX)
     sums1_a = hop(sums1, 1)
-    for i in range(3, depth):
-        f = resplit(f, i)
-    for i in range(2, depth - 1):
-        a = resplit(a, i)
     tail = [(skeep, 773), (srecv, 773), (sparr, 389)]
-    f = fold(f, [(0, 1, [(ikeep, 512), (irecv, 512)]), (1, 1, tail)])[None]
-    f = spread(f, depth - 1)
-    a = resplit(a, depth - 1)
+    f = fold_step(*f, [(0, 1, [(ikeep, 512), (irecv, 512)]), (1, 1, tail)])
+    a = merge_step(*a)
     sums1_c = hop(after(sums1_b, a[0]), 1)
-    f = spread(join(f), depth - 2)
+    f = part_step(*f)
     group = [(skeep, 768), (srecv, 768), (sparr, 384)]
-    a = fold(
-        a,
+    a = fold_step(
+        *a,
         [(0, 2, [(sums1, 0), (sums1_a, 0), (sums1_b, 0), (sums1_c, 0)]), (2, 1, [(akeep, 384), (arecv, 384)]),
          (3, 5, group)],
-    )[None]
-    a = spread(a, depth - 1)
-    for i in range(depth - 3, -1, -1):
-        f = spread(join(f), i)
-        a = spread(join(a), i + 1)
-    a = spread(join(a), 0)
-    g_wback, g_win, f_small = unpack_call(tb, f, stages, ((0, 512, False), (512, 512, False)), True)
-    plan = ((0, 128, True), (128, 128, True), (256, 128, True), (384, 128, False), (512, 128, False), (640, 128, False))
-    g_q, g_k, g_v, g_g2, g_g1, g_wo, a_small = unpack_call(tb, a, stages, plan, True)
+    )
+    f = pair_step(*f)
+    a = part_step(*a)
+    g_wback, g_win, f_small = unpack_step(*f, (((0, 512, False),), ((0, 512, False),)))
+    a = pair_step(*a)
+    plans = (
+        ((0, 128, True), (128, 128, True), (256, 128, True)),
+        ((0, 128, False), (128, 128, False), (256, 128, False)),
+    )
+    g_q, g_k, g_v, g_g2, g_g1, g_wo, a_small = unpack_step(*a, plans)
     return (
         result,
         input_grad,

time: 160 us -> 137 us (0.86)
  waiting for transfers between devices: 71.6 us -> 33.4 us
  starting transfers between devices: 32.3 us -> 47.1 us
    ppermute x26, waiting for transfers between devices: 29.5 us -> 7.21 us  [hop(): return lax.ppermute(value, 'tensor', [(i, i ^ mask) for i in range(4)])]
    ppermute x15 -> x23, waiting for transfers between devices: 42 us -> 26.2 us  [dhop(): return lax.ppermute(value, 'dp', [(i, i ^ mask) for i in range(n_dp)])]
    ppermute x15 -> x23, starting transfers between devices: 17.2 us -> 30.6 us  [dhop(): return lax.ppermute(value, 'dp', [(i, i ^ mask) for i in range(n_dp)])]
  transfers between devices with their start and end apart: 41 -> 49, of which waited for: 20 -> 16; matrix products, arithmetic and copies ran while one was open for 0% -> 1% of each run, Pallas kernels for 26% -> 35%
where the time goes in v3:
time: 137 us; the launch traced here: 136 us
  Pallas kernels  50.2 us (37%)
  starting transfers between devices  47.1 us (34%)
  waiting for transfers between devices  33.4 us (24%)
  local copies, waits for them, and re-layouts  3.5 us (3%)
    pallas_call x31, Pallas kernels, call(): pl.pallas_call(body, out_shape=tuple(outs), in_specs=[SM] * smem + [space...  50.2 us
    ppermute x23, starting transfers between devices, dhop(): return lax.ppermute(value, 'dp', [(i, i ^ mask) for i in range(n_dp)])  30.6 us
    ppermute x23, waiting for transfers between devices, dhop(): return lax.ppermute(value, 'dp', [(i, i ^ mask) for i in range(n_dp)])  26.2 us
    ppermute x26, starting transfers between devices, hop(): return lax.ppermute(value, 'tensor', [(i, i ^ mask) for i in range(4)])  16.5 us
    ppermute x26, waiting for transfers between devices, hop(): return lax.ppermute(value, 'tensor', [(i, i ^ mask) for i in range(4)])  7.21 us
  transfers between devices with their start and end apart: 49, of which 16 were waited for; matrix products, arithmetic and copies ran while one was open for 1% of the time, Pallas kernels for 35%

profile of v3, /device:TPU:0, one launch (start us, length us, event | category | flops | bytes accessed | tf_op | source)
XLA Modules:
  0.0 136.4 jit_solution(6561997103062404781)
XLA Ops:
  0.7 3.0 %collective-permute-start = (bf16[256,512]{1,0:T(8,128)(2,1)}, bf16[256,512]{1,0:T(8,128)(2,1)S(1)}, u32[]{:S(2)}, u32[]{:S(2)}) collective-permute-start(bf16[256,512]{1,0:T(8,128)(2,1)} %x0.5), channel_id=1, source_target_pairs={{0,2},{1,3},{2,0},{3,1},{4,6},{5,7},{6,4},{7,5},{8,10},{9,11},{10,... | collective-permute-start | bytes 786440 | tf_op jit(solution)/shard_map/ppermute | solution.py:622
  3.7 1.2 compare_select_fusion.pos.tb
  4.9 4.2 %pack.1 = (bf16[264,512]{1,0:T(8,128)(2,1)}, bf16[392,512]{1,0:T(8,128)(2,1)}, bf16[1416,512]{1,0:T(8,128)(2,1)}, bf16[520,384]{1,0:T(8,128)(2,1)}, f32[16,512]{1,0:T(8,128)}) custom-call(s32[8]{0:T(128)} %compare_select_fusion.pos.tb, bf16[512,512]{1,0:T(8,128)(2,1)} %win0.5, bf16[512,512]{1,0:T(8,128)(2,1)} %wback0.5, bf16[128,512]{1,0:T(8,128)(2,1)} %w_out.1, ...), custom_call_target="tpu_custom_call" | custom-call | flops 10000000000 | tf_op jit(solution)/shard_map/pack/pallas_call | solution.py:42
  10.2 1.7 %collective-permute-start.8 = (bf16[264,512]{1,0:T(8,128)(2,1)}, bf16[264,512]{1,0:T(8,128)(2,1)S(1)}, u32[]{:S(2)}, u32[]{:S(2)}) collective-permute-start(bf16[264,512]{1,0:T(8,128)(2,1)} %get-tuple-element.154), channel_id=1, source_target_pairs={{0,2},{1,3},{2,0},{3,1},{4,6},{5,7},{6,4},{7,5},{8,10},{9,11},{10,... | collective-permute-start | bytes 811016 | tf_op jit(solution)/shard_map/ppermute | solution.py:622
  12.3 1.0 copy-done.4
  13.3 0.8 copy-done.9
  14.0 4.8 %first.1 = (bf16[1024,512]{1,0:T(8,128)(2,1)S(1)}, bf16[256,256]{1,0:T(8,128)(2,1)S(1)}, bf16[256,256]{1,0:T(8,128)(2,1)S(1)}, bf16[1024,256]{1,0:T(8,128)(2,1)S...) custom-call(s32[8]{0:T(128)S(1)} %copy-done, ...), custom_call_target="tpu_custom_call" | custom-call | flops 10000000000 | tf_op jit(solution)/shard_map/first/pallas_call | solution.py:42
  18.9 0.6 collective-permute-start.4
  19.7 1.8 %collective-permute-start.12 = (bf16[264,512]{1,0:T(8,128)(2,1)S(1)}, bf16[264,512]{1,0:T(8,128)(2,1)S(1)}, u32[]{:S(2)}, u32[]{:S(2)}) collective-permute-start(bf16[264,512]{1,0:T(8,128)(2,1)S(1)} %collective-permute-done.8.s0), channel_id=1, source_target_pairs={{0,8},{4,12},{8,0},{12,4},{16,24},{20,28},{24,16},{28,20},{1,9},{5... | collective-permute-start | bytes 811016 | tf_op jit(solution)/shard_map/ppermute | solution.py:625
  21.5 1.5 %collective-permute-start.10 = (bf16[264,512]{1,0:T(8,128)(2,1)S(1)}, bf16[264,512]{1,0:T(8,128)(2,1)S(1)}, u32[]{:S(2)}, u32[]{:S(2)}) collective-permute-start(bf16[264,512]{1,0:T(8,128)(2,1)S(1)} %collective-permute-done.8.s0), channel_id=1, source_target_pairs={{0,4},{4,0},{8,12},{12,8},{16,20},{20,16},{24,28},{28,24},{1,5},{5... | collective-permute-start | bytes 811016 | tf_op jit(solution)/shard_map/ppermute | solution.py:625
  23.0 1.6 %second.1 = (bf16[4,1024,256]{2,1,0:T(8,128)(2,1)S(1)}, bf16[256,256]{1,0:T(8,128)(2,1)S(1)}, bf16[256,256]{1,0:T(8,128)(2,1)S(1)}, f32[4,8,256]{2,1,0:T(8,128)S(1)}) custom-call(s32[8]{0:T(128)S(1)} %copy-done, s32[1,1024]{1,0:T(1,128)S(1)} %copy-done.8, s32[1,1024]{1,0:T(1,128)S(1)} %copy-done.8, bf16[256,256]{1,0:T(8,128)(2,1)S(1)} %get-tuple-element.160.qt0.qt, ...), custom_call_target="tpu_custom_call" | custom-call | flops 10000000000 | tf_op jit(solution)/shard_map/second/pallas_call | solution.py:42
  24.7 3.6 %collective-permute-done.5.e1 = bf16[392,512]{1,0:T(8,128)(2,1)S(1)} collective-permute-done((bf16[392,512]{1,0:T(8,128)(2,1)}, bf16[392,512]{1,0:T(8,128)(2,1)S(1)}, u32[]{:S(2)}, u32[]{:S(2)}) %collective-permute-start.5) | collective-permute-done | bytes 401440 | tf_op jit(solution)/shard_map/ppermute | solution.py:622
  28.3 1.3 prepare.1
  29.6 1.2 collective-permute-done.4.attp
  31.3 1.4 %out.1 = (bf16[256,512]{1,0:T(8,128)(2,1)S(1)}, f32[256,512]{1,0:T(8,128)S(1)}, f32[256,512]{1,0:T(8,128)S(1)}, f32[256,512]{1,0:T(8,128)S(1)}) custom-call(s32[8]{0:T(128)S(1)} %copy-done, bf16[256,512]{1,0:T(8,128)(2,1)S(1)} %copy-done.7, bf16[1024,512]{1,0:T(8,128)(2,1)S(1)} %get-tuple-element.158.n, bf16[256,256]{1,0:T(8,128)(2,1)S(1)} %get-tuple-element.167.att, ...), custom_call_target="tpu_custom_call" | custom-call | flops 10000000000 | tf_op jit(solution)/shard_map/out/pallas_call | solution.py:42
  32.8 1.8 %collective-permute-start.14 = (bf16[264,512]{1,0:T(8,128)(2,1)S(1)}, bf16[264,512]{1,0:T(8,128)(2,1)S(1)}, u32[]{:S(2)}, u32[]{:S(2)}) collective-permute-start(bf16[264,512]{1,0:T(8,128)(2,1)S(1)} %collective-permute-done.12.s4), channel_id=1, source_target_pairs={{0,4},{4,0},{8,12},{12,8},{16,20},{20,16},{24,28},{28,24},{1,5},{5... | collective-permute-start | bytes 811016 | tf_op jit(solution)/shard_map/ppermute | solution.py:625
  34.5 1.7 %ffn_first.1 = (f32[256,512]{1,0:T(8,128)S(1)}, bf16[256,1024]{1,0:T(8,128)(2,1)S(1)}, bf16[256,1024]{1,0:T(8,128)(2,1)S(1)}) custom-call(s32[8]{0:T(128)S(1)} %copy-done, bf16[256,512]{1,0:T(8,128)(2,1)S(1)} %get-tuple-element.174.n2, f32[16,512]{1,0:T(8,128)S(1)} %copy-done.9, bf16[512,512]{1,0:T(8,128)(2,1)S(1)} %copy-done.1, ...), custom_call_target="tpu_custom_call" | custom-call | flops 10000000000 | tf_op jit(solution)/shard_map/ffn_first/pallas_call | solution.py:42
  36.2 5.4 %collective-permute-done.14.s6 = bf16[264,512]{1,0:T(8,128)(2,1)S(1)} collective-permute-done((bf16[264,512]{1,0:T(8,128)(2,1)S(1)}, bf16[264,512]{1,0:T(8,128)(2,1)S(1)}, u32[]{:S(2)}, u32[]{:S(2)}) %collective-permute-start.14) | collective-permute-done | bytes 270368 | tf_op jit(solution)/shard_map/ppermute | solution.py:625
  41.6 1.7 %collective-permute-start.16 = (bf16[256,512]{1,0:T(8,128)(2,1)S(1)}, bf16[256,512]{1,0:T(8,128)(2,1)S(1)}, u32[]{:S(2)}, u32[]{:S(2)}) collective-permute-start(bf16[256,512]{1,0:T(8,128)(2,1)S(1)} %get-tuple-element.174.n2), channel_id=1, source_target_pairs={{0,2},{1,3},{2,0},{3,1},{4,6},{5,7},{6,4},{7,5},{8,10},{9,11},{10,... | collective-permute-start | bytes 786440 | tf_op jit(solution)/shard_map/ppermute | solution.py:622
  43.4 2.8 %ffn.1 = (bf16[256,512]{1,0:T(8,128)(2,1)}, bf16[256,512]{1,0:T(8,128)(2,1)S(1)}, bf16[256,512]{1,0:T(8,128)(2,1)S(1)}, bf16[256,1024]{1,0:T(8,128)(2,1)S(1)}) custom-call(s32[8]{0:T(128)S(1)} %copy-done, bf16[256,512]{1,0:T(8,128)(2,1)S(1)} %get-tuple-element.174.n2, f32[256,512]{1,0:T(8,128)S(1)} %get-tuple-element.178.mid, ...), custom_call_target="tpu_custom_call" | custom-call | flops 10000000000 | tf_op jit(solution)/shard_map/ffn/pallas_call | solution.py:42
  46.3 1.5 %collective-permute-start.17 = (bf16[256,512]{1,0:T(8,128)(2,1)S(1)}, bf16[256,512]{1,0:T(8,128)(2,1)S(1)}, u32[]{:S(2)}, u32[]{:S(2)}) collective-permute-start(bf16[256,512]{1,0:T(8,128)(2,1)S(1)} %get-tuple-element.184.fg), channel_id=1, source_target_pairs={{0,2},{1,3},{2,0},{3,1},{4,6},{5,7},{6,4},{7,5},{8,10},{9,11},{10,... | collective-permute-start | bytes 786440 | tf_op jit(solution)/shard_map/ppermute | solution.py:622
  47.8 3.5 %back.1 = (bf16[256,256]{1,0:T(8,128)(2,1)S(1)}, bf16[256,256]{1,0:T(8,128)(2,1)S(1)}, f32[256,512]{1,0:T(8,128)S(1)}, bf16[256,512]{1,0:T(8,128)(2,1)S(1)}, bf1...) custom-call(s32[8]{0:T(128)S(1)} %copy-done, ...), custom_call_target="tpu_custom_call" | custom-call | flops 10000000000 | tf_op jit(solution)/shard_map/back/pallas_call | solution.py:42
  51.2 2.0 %attn_back0.1 = (f32[256,1024]{1,0:T(8,128)S(1)}, f32[256,1024]{1,0:T(8,128)S(1)}, bf16[256,256]{1,0:T(8,128)(2,1)S(1)}) custom-call(s32[8]{0:T(128)S(1)} %copy-done, s32[1,1024]{1,0:T(1,128)S(1)} %copy-done.8, bf16[4,1024,256]{2,1,0:T(8,128)(2,1)S(1)} %get-tuple-element.163.p, bf16[256,256]{1,0:T(8,128)(2,1)S(1)} %get-tuple-element.190.dot, ...), custom_call_target="tpu_custom_call" | custom-call | flops 10000000000 | tf_op jit(solution)/shard_map/attn_back0/pallas_call | solution.py:42
  53.3 2.6 %collective-permute-start.18 = (bf16[256,256]{1,0:T(8,128)(2,1)S(1)}, bf16[256,256]{1,0:T(8,128)(2,1)S(1)}, u32[]{:S(2)}, u32[]{:S(2)}) collective-permute-start(bf16[256,256]{1,0:T(8,128)(2,1)S(1)} %get-tuple-element.203), channel_id=1, source_target_pairs={{0,2},{1,3},{2,0},{3,1},{4,6},{5,7},{6,4},{7,5},{8,10},{9,11},{10,... | collective-permute-start | bytes 393224 | tf_op jit(solution)/shard_map/ppermute | solution.py:622
  56.0 2.3 %ffn_back_weight.1 = (f32[512,512]{1,0:T(8,128)S(1)}, bf16[512,512]{1,0:T(8,128)(2,1)S(1)}, bf16[256,1024]{1,0:T(8,128)(2,1)S(1)}) custom-call(s32[8]{0:T(128)S(1)} %copy-done, bf16[256,512]{1,0:T(8,128)(2,1)S(1)} %collective-permute-done.16.n2p, bf16[256,512]{1,0:T(8,128)(2,1)S(1)} %get-tuple-element.184.fg, ...), custom_call_target="tpu_custom_call" | custom-call | flops 10000000000 | tf_op jit(solution)/shard_map/ffn_back_weight/pallas_call | solution.py:42
  58.3 1.9 %ffn_in_weight.1 = (f32[520,512]{1,0:T(8,128)S(1)}, bf16[520,512]{1,0:T(8,128)(2,1)S(1)}) custom-call(s32[8]{0:T(128)S(1)} %copy-done, bf16[256,512]{1,0:T(8,128)(2,1)S(1)} %get-tuple-element.174.n2, bf16[256,512]{1,0:T(8,128)(2,1)S(1)} %collective-permute-done.16.n2p, bf16[256,512]{1,0:T(8,128)(2,1)S(1)} %collective-permute-done.17.fgp, ...), custom_call_target="tpu_custom_call" | custom-call | flops 10000000000 | tf_op jit(solution)/shard_map/ffn_in_weight/pallas_call | solution.py:42
  60.8 1.2 small_weight.1
  63.0 1.0 halves.2
  64.0 1.7 %collective-permute-start.22 = (bf16[256,512]{1,0:T(8,128)(2,1)S(1)}, bf16[256,512]{1,0:T(8,128)(2,1)S(1)}, u32[]{:S(2)}, u32[]{:S(2)}) collective-permute-start(bf16[256,512]{1,0:T(8,128)(2,1)S(1)} %get-tuple-element.228), channel_id=1, source_target_pairs={{0,4},{4,0},{8,12},{12,8},{16,20},{20,16},{24,28},{28,24},{1,5},{5... | collective-permute-start | bytes 786440 | tf_op jit(solution)/shard_map/ppermute | solution.py:625
  65.7 1.6 %collective-permute-start.23 = (bf16[256,512]{1,0:T(8,128)(2,1)S(1)}, bf16[256,512]{1,0:T(8,128)(2,1)S(1)}, u32[]{:S(2)}, u32[]{:S(2)}) collective-permute-start(bf16[256,512]{1,0:T(8,128)(2,1)S(1)} %get-tuple-element.230), channel_id=1, source_target_pairs={{0,8},{4,12},{8,0},{12,4},{16,24},{20,28},{24,16},{28,20},{1,9},{5... | collective-permute-start | bytes 786440 | tf_op jit(solution)/shard_map/ppermute | solution.py:625
  67.2 0.6 half_rows.1
  67.9 1.8 %collective-permute-start.25 = (bf16[392,512]{1,0:T(8,128)(2,1)S(1)}, bf16[392,512]{1,0:T(8,128)(2,1)S(1)}, u32[]{:S(2)}, u32[]{:S(2)}) collective-permute-start(bf16[392,512]{1,0:T(8,128)(2,1)S(1)} %half_rows.1), channel_id=1, source_target_pairs={{0,2},{1,3},{2,0},{3,1},{4,6},{5,7},{6,4},{7,5},{8,10},{9,11},{10,... | collective-permute-start | bytes 1204232 | tf_op jit(solution)/shard_map/ppermute | solution.py:622
  69.6 4.8 %attn_back1.1 = (bf16[256,512]{1,0:T(8,128)(2,1)S(1)}, bf16[256,1024]{1,0:T(8,128)(2,1)S(1)}, bf16[256,1024]{1,0:T(8,128)(2,1)S(1)}, f32[392,512]{1,0:T(8,128)S(1)}, bf16[392,512]{1,0:T(8,128)(2,1)S(1)}) custom-call(s32[8]{0:T(128)S(1)} %copy-done, s32[1,1024]{1,0:T(1,128)S(1)} %copy-done.8, bf16[4,1024,256]{2,1,0:T(8,128)(2,1)S(1)} %get-tuple-element.216.p, ...), custom_call_target="tpu_custom_call" | custom-call | flops 10000000000 | tf_op jit(solution)/shard_map/attn_back1/pallas_call | solution.py:42
  74.4 1.4 %input_grad.1 = (f32[512,256]{1,0:T(8,128)S(1)}, f32[512,256]{1,0:T(8,128)S(1)}, bf16[512,512]{1,0:T(8,128)(2,1)S(1)}) custom-call(s32[8]{0:T(128)S(1)} %copy-done, bf16[256,512]{1,0:T(8,128)(2,1)S(1)} %get-tuple-element.222.dqt, bf16[256,1024]{1,0:T(8,128)(2,1)S(1)} %get-tuple-element.224.dkt, bf16[256,1024]{1,0:T(8,128)(2,1)S(1)} %get-tuple-element.225.dvt, ...), custom_call_target="tpu_custom_call" | custom-call | flops 10000000000 | tf_op jit(solution)/shard_map/input_grad/pallas_call | solution.py:42
  76.2 0.7 quarters.2
  78.0 0.8 collective-permute-done.25.refs_4_.refs_8_
  78.8 1.0 halves.3
  79.8 0.7 collective-permute-start.29
  80.5 1.6 %collective-permute-start.30 = (bf16[192,512]{1,0:T(8,128)(2,1)S(1)}, bf16[192,512]{1,0:T(8,128)(2,1)S(1)}, u32[]{:S(2)}, u32[]{:S(2)}) collective-permute-start(bf16[192,512]{1,0:T(8,128)(2,1)S(1)} %get-tuple-element.247), channel_id=1, source_target_pairs={{0,8},{4,12},{8,0},{12,4},{16,24},{20,28},{24,16},{28,20},{1,9},{5... | collective-permute-start | bytes 589832 | tf_op jit(solution)/shard_map/ppermute | solution.py:625
  82.1 0.6 half_columns.1
  83.5 0.6 merge.2
  84.1 2.7 %collective-permute-start.32 = (bf16[128,512]{1,0:T(8,128)(2,1)S(1)}, bf16[128,512]{1,0:T(8,128)(2,1)S(1)}, u32[]{:S(2)}, u32[]{:S(2)}) collective-permute-start(bf16[128,512]{1,0:T(8,128)(2,1)S(1)} %get-tuple-element.253), channel_id=1, source_target_pairs={{0,16},{4,20},{8,24},{12,28},{16,0},{20,4},{24,8},{28,12},{1,17},{... | collective-permute-start | bytes 393224 | tf_op jit(solution)/shard_map/ppermute | solution.py:625
  87.0 2.5 %collective-permute-done.30.refs_3_ = bf16[192,512]{1,0:T(8,128)(2,1)S(1)} collective-permute-done((bf16[192,512]{1,0:T(8,128)(2,1)S(1)}, bf16[192,512]{1,0:T(8,128)(2,1)S(1)}, u32[]{:S(2)}, u32[]{:S(2)}) %collective-permute-start.30) | collective-permute-done | bytes 196640 | tf_op jit(solution)/shard_map/ppermute | solution.py:625
  89.5 0.7 quarters.3
  90.9 2.0 %last.1 = (f32[256,512]{1,0:T(8,128)}, f32[8,512]{1,0:T(8,128)S(1)}) custom-call(s32[8]{0:T(128)S(1)} %copy-done, f32[512,256]{1,0:T(8,128)S(1)} %get-tuple-element.226.own, bf16[512,512]{1,0:T(8,128)(2,1)S(1)} %collective-permute-done.26.recv.sib, bf16[512,256]{1,0:T(8,128)(2,1)S(1)} %collective-permute-done.31.par, bf16[256,512]{1,0:T(8,128)(2,1)S(1)} %copy-done.7, ...), custom_call_target="tpu_custom_call" | custom-call | flops 10000000000 | tf_op jit(solution)/shard_map/last/pallas_call | solution.py:42
  93.2 0.6 fold.2
  93.8 3.2 %collective-permute-start.35 = (bf16[1,136,512]{2,1,0:T(8,128)(2,1)S(1)}, bf16[1,136,512]{2,1,0:T(8,128)(2,1)S(1)}, u32[]{:S(2)}, u32[]{:S(2)}) collective-permute-start(bf16[1,136,512]{2,1,0:T(8,128)(2,1)S(1)} %bitcast.15), channel_id=1, source_target_pairs={{0,16},{4,20},{8,24},{12,28},{16,0},{20,4},{24,8},{28,12},{1,17},{... | collective-permute-start | bytes 417800 | tf_op jit(solution)/shard_map/ppermute | solution.py:625
  97.1 0.6 merge.3
  97.7 1.4 %collective-permute-start.36 = (bf16[96,512]{1,0:T(8,128)(2,1)S(1)}, bf16[96,512]{1,0:T(8,128)(2,1)S(1)}, u32[]{:S(2)}, u32[]{:S(2)}) collective-permute-start(bf16[96,512]{1,0:T(8,128)(2,1)S(1)} %get-tuple-element.262), channel_id=1, source_target_pairs={{0,16},{4,20},{8,24},{12,28},{16,0},{20,4},{24,8},{28,12},{1,17},{... | collective-permute-start | bytes 294920 | tf_op jit(solution)/shard_map/ppermute | solution.py:625
  99.1 7.6 %collective-permute-done.35.recv = bf16[1,136,512]{2,1,0:T(8,128)(2,1)S(1)} collective-permute-done((bf16[1,136,512]{2,1,0:T(8,128)(2,1)S(1)}, bf16[1,136,512]{2,1,0:T(8,128)(2,1)S(1)}, u32[]{:S(2)}, u32[]{:S(2)}) %collective-permute-start.35) | collective-permute-done | bytes 139296 | tf_op jit(solution)/shard_map/ppermute | solution.py:625
  107.2 0.6 collective-permute-start.40
  107.9 1.2 collective-permute-start.41
  109.7 3.4 %collective-permute-start.42 = (bf16[1,104,512]{2,1,0:T(8,128)(2,1)S(1)}, bf16[1,104,512]{2,1,0:T(8,128)(2,1)S(1)}, u32[]{:S(2)}, u32[]{:S(2)}) collective-permute-start(bf16[1,104,512]{2,1,0:T(8,128)(2,1)S(1)} %bitcast.17), channel_id=1, source_target_pairs={{0,16},{4,20},{8,24},{12,28},{16,0},{20,4},{24,8},{28,12},{1,17},{... | collective-permute-start | bytes 319496 | tf_op jit(solution)/shard_map/ppermute | solution.py:625
  113.7 1.2 collective-permute-start.43
  114.9 1.5 %collective-permute-start.44 = (bf16[4,64,512]{2,1,0:T(8,128)(2,1)S(1)}, bf16[4,64,512]{2,1,0:T(8,128)(2,1)S(1)}, u32[]{:S(2)}, u32[]{:S(2)}) collective-permute-start(bf16[4,64,512]{2,1,0:T(8,128)(2,1)S(1)} %get-tuple-element.271.held2), channel_id=1, source_target_pairs={{0,8},{4,12},{8,0},{12,4},{16,24},{20,28},{24,16},{28,20},{1,9},{5... | collective-permute-start | bytes 786440 | tf_op jit(solution)/shard_map/ppermute | solution.py:625
  116.4 1.5 %collective-permute-done.42.recv = bf16[1,104,512]{2,1,0:T(8,128)(2,1)S(1)} collective-permute-done((bf16[1,104,512]{2,1,0:T(8,128)(2,1)S(1)}, bf16[1,104,512]{2,1,0:T(8,128)(2,1)S(1)}, u32[]{:S(2)}, u32[]{:S(2)}) %collective-permute-start.42) | collective-permute-done | bytes 106528 | tf_op jit(solution)/shard_map/ppermute | solution.py:625
  118.7 0.9 collective-permute-start.46
  119.6 4.1 %collective-permute-done.44.recv2 = bf16[4,64,512]{2,1,0:T(8,128)(2,1)S(1)} collective-permute-done((bf16[4,64,512]{2,1,0:T(8,128)(2,1)S(1)}, bf16[4,64,512]{2,1,0:T(8,128)(2,1)S(1)}, u32[]{:S(2)}, u32[]{:S(2)}) %collective-permute-start.44) | collective-permute-done | bytes 262176 | tf_op jit(solution)/shard_map/ppermute | solution.py:625
  123.7 2.1 %unpack.2 = (f32[512,512]{1,0:T(8,128)}, f32[512,512]{1,0:T(8,128)}, f32[8,512]{1,0:T(8,128)S(1)}) custom-call(s32[8]{0:T(128)S(1)} %copy-done, bf16[4,72,512]{2,1,0:T(8,128)(2,1)S(1)} %get-tuple-element.267.held1, bf16[4,72,512]{2,1,0:T(8,128)(2,1)S(1)} %collective-permute-done.43.recv1, bf16[4,64,512]{2,1,0:T(8,128)(2,1)S(1)} %get-tuple-element.271.held2, ...), custom_call_target="tpu_custom_call" | custom-call | flops 10000000000 | tf_op jit(solution)/shard_map/unpack/pallas_call | solution.py:42
  126.4 1.3 collective-permute-start.47
  127.6 0.6 collective-permute-start.48
  128.8 4.5 %collective-permute-done.48.recv2 = bf16[4,48,512]{2,1,0:T(8,128)(2,1)S(1)} collective-permute-done((bf16[4,48,512]{2,1,0:T(8,128)(2,1)S(1)}, bf16[4,48,512]{2,1,0:T(8,128)(2,1)S(1)}, u32[]{:S(2)}, u32[]{:S(2)}) %collective-permute-start.48) | collective-permute-done | bytes 196640 | tf_op jit(solution)/shard_map/ppermute | solution.py:625
  133.3 1.9 %unpack.3 = (f32[512,128]{1,0:T(8,128)}, f32[512,128]{1,0:T(8,128)}, f32[512,128]{1,0:T(8,128)}, f32[128,512]{1,0:T(8,128)}, f32[128,512]{1,0:T(8,128)}, /*index=5*/f32[128,512]{1,0:T(8,128)}, f32[8,512]{1,0:T(8,128)S(1)}) custom-call(s32[8]{0:T(128)S(1)} %copy-done, bf16[4,56,512]{2,1,0:T(8,128)(2,1)S(1)} %get-tuple-element.275.held1, ...), custom_call_target="tpu_custom_call" | custom-call | flops 10000000000 | tf_op jit(solution)/shard_map/unpack/pallas_call | solution.py:42
  135.8 0.6 fusion
  (89 shorter events, 11.6 us)
Async XLA Ops:
  0.7 9.6 %collective-permute-start = (bf16[256,512]{1,0:T(8,128)(2,1)}, bf16[256,512]{1,0:T(8,128)(2,1)S(1)}, u32[]{:S(2)}, u32[]{:S(2)}) collective-permute-start(bf16[256,512]{1,0:T(8,128)(2,1)} %x0.5), channel_id=1, source_target_pairs={{0,2},{1,3},{2,0},{3,1},{4,6},{5,7},{6,4},{7,5},{8,10},{9,11},{10,... | collective-permute-start | bytes 786440 | tf_op jit(solution)/shard_map/ppermute | solution.py:622
  4.9 4.3 %copy-start.7 = (bf16[256,512]{1,0:T(8,128)(2,1)S(1)}, bf16[256,512]{1,0:T(8,128)(2,1)}, u32[]{:S(2)}) copy-start(bf16[256,512]{1,0:T(8,128)(2,1)} %x0.5) | copy-start | bytes 786436
  4.9 7.4 %copy-start = (s32[8]{0:T(128)S(1)}, s32[8]{0:T(128)}, u32[]{:S(2)}) copy-start(s32[8]{0:T(128)} %compare_select_fusion.pos.tb) | copy-start | bytes 100
  4.9 7.4 %copy-start.8 = (s32[1,1024]{1,0:T(1,128)S(1)}, s32[1,1024]{1,0:T(1,128)}, u32[]{:S(2)}) copy-start(s32[1,1024]{1,0:T(1,128)} %segs.7) | copy-start | bytes 12292
  9.1 3.1 %collective-permute-start.3 = (bf16[520,384]{1,0:T(8,128)(2,1)}, bf16[520,384]{1,0:T(8,128)(2,1)S(1)}, u32[]{:S(2)}, u32[]{:S(2)}) collective-permute-start(bf16[520,384]{1,0:T(8,128)(2,1)} %get-tuple-element.157.qkv0), channel_id=1, source_target_pairs={{0,1},{1,0},{2,3},{3,2},{4,5},{5,4},{6,7},{7,6},{8,9},{9,8},{10,11... | collective-permute-start | bytes 1198088 | tf_op jit(solution)/shard_map/ppermute | solution.py:622
  9.2 3.0 %collective-permute-start.1 = (bf16[256,512]{1,0:T(8,128)(2,1)S(1)}, bf16[256,512]{1,0:T(8,128)(2,1)S(1)}, u32[]{:S(2)}, u32[]{:S(2)}) collective-permute-start(bf16[256,512]{1,0:T(8,128)(2,1)S(1)} %copy-done.7), channel_id=1, source_target_pairs={{0,1},{1,0},{2,3},{3,2},{4,5},{5,4},{6,7},{7,6},{8,9},{9,8},{10,11... | collective-permute-start | bytes 786440 | tf_op jit(solution)/shard_map/ppermute | solution.py:622
  10.2 2.0 %collective-permute-start.2 = (bf16[256,512]{1,0:T(8,128)(2,1)S(1)}, bf16[256,512]{1,0:T(8,128)(2,1)S(1)}, u32[]{:S(2)}, u32[]{:S(2)}) collective-permute-start(bf16[256,512]{1,0:T(8,128)(2,1)S(1)} %collective-permute-done.x1), channel_id=1, source_target_pairs={{0,1},{1,0},{2,3},{3,2},{4,5},{5,4},{6,7},{7,6},{8,9},{9,8},{10,11... | collective-permute-start | bytes 786440 | tf_op jit(solution)/shard_map/ppermute | solution.py:622
  10.2 9.5 %collective-permute-start.8 = (bf16[264,512]{1,0:T(8,128)(2,1)}, bf16[264,512]{1,0:T(8,128)(2,1)S(1)}, u32[]{:S(2)}, u32[]{:S(2)}) collective-permute-start(bf16[264,512]{1,0:T(8,128)(2,1)} %get-tuple-element.154), channel_id=1, source_target_pairs={{0,2},{1,3},{2,0},{3,1},{4,6},{5,7},{6,4},{7,5},{8,10},{9,11},{10,... | collective-permute-start | bytes 811016 | tf_op jit(solution)/shard_map/ppermute | solution.py:622
  11.9 16.4 %collective-permute-start.5 = (bf16[392,512]{1,0:T(8,128)(2,1)}, bf16[392,512]{1,0:T(8,128)(2,1)S(1)}, u32[]{:S(2)}, u32[]{:S(2)}) collective-permute-start(bf16[392,512]{1,0:T(8,128)(2,1)} %get-tuple-element.170.e0), channel_id=1, source_target_pairs={{0,2},{1,3},{2,0},{3,1},{4,6},{5,7},{6,4},{7,5},{8,10},{9,11},{10,... | collective-permute-start | bytes 1204232 | tf_op jit(solution)/shard_map/ppermute | solution.py:622
  12.2 19.1 %collective-permute-start.6 = (bf16[1416,512]{1,0:T(8,128)(2,1)}, bf16[1416,512]{1,0:T(8,128)(2,1)S(1)}, u32[]{:S(2)}, u32[]{:S(2)}) collective-permute-start(bf16[1416,512]{1,0:T(8,128)(2,1)} %get-tuple-element.172), channel_id=1, source_target_pairs={{0,1},{1,0},{2,3},{3,2},{4,5},{5,4},{6,7},{7,6},{8,9},{9,8},{10,11... | collective-permute-start | bytes 4349960 | tf_op jit(solution)/shard_map/ppermute | solution.py:622
  12.3 1.0 copy-start.4
  13.3 0.8 copy-start.9
  18.9 11.9 %collective-permute-start.4 = (bf16[256,256]{1,0:T(8,128)(2,1)S(1)}, bf16[256,256]{1,0:T(8,128)(2,1)S(1)}, u32[]{:S(2)}, u32[]{:S(2)}) collective-permute-start(bf16[256,256]{1,0:T(8,128)(2,1)S(1)} %get-tuple-element.168), channel_id=1, source_target_pairs={{0,2},{1,3},{2,0},{3,1},{4,6},{5,7},{6,4},{7,5},{8,10},{9,11},{10,... | collective-permute-start | bytes 393224 | tf_op jit(solution)/shard_map/ppermute | solution.py:622
  19.7 11.0 %collective-permute-start.12 = (bf16[264,512]{1,0:T(8,128)(2,1)S(1)}, bf16[264,512]{1,0:T(8,128)(2,1)S(1)}, u32[]{:S(2)}, u32[]{:S(2)}) collective-permute-start(bf16[264,512]{1,0:T(8,128)(2,1)S(1)} %collective-permute-done.8.s0), channel_id=1, source_target_pairs={{0,8},{4,12},{8,0},{12,4},{16,24},{20,28},{24,16},{28,20},{1,9},{5... | collective-permute-start | bytes 811016 | tf_op jit(solution)/shard_map/ppermute | solution.py:625
  21.5 9.7 %collective-permute-start.10 = (bf16[264,512]{1,0:T(8,128)(2,1)S(1)}, bf16[264,512]{1,0:T(8,128)(2,1)S(1)}, u32[]{:S(2)}, u32[]{:S(2)}) collective-permute-start(bf16[264,512]{1,0:T(8,128)(2,1)S(1)} %collective-permute-done.8.s0), channel_id=1, source_target_pairs={{0,4},{4,0},{8,12},{12,8},{16,20},{20,16},{24,28},{28,24},{1,5},{5... | collective-permute-start | bytes 811016 | tf_op jit(solution)/shard_map/ppermute | solution.py:625
  23.0 5.3 %copy-start.5 = (bf16[520,384]{1,0:T(8,128)(2,1)S(1)}, bf16[520,384]{1,0:T(8,128)(2,1)}, u32[]{:S(2)}) copy-start(bf16[520,384]{1,0:T(8,128)(2,1)} %get-tuple-element.157.qkv0) | copy-start | bytes 1198084
  24.6 6.7 %copy-start.3 = (bf16[392,512]{1,0:T(8,128)(2,1)S(1)}, bf16[392,512]{1,0:T(8,128)(2,1)}, u32[]{:S(2)}) copy-start(bf16[392,512]{1,0:T(8,128)(2,1)} %get-tuple-element.170.e0) | copy-start | bytes 1204228
  28.3 3.0 %collective-permute-start.7 = (bf16[392,512]{1,0:T(8,128)(2,1)S(1)}, bf16[392,512]{1,0:T(8,128)(2,1)S(1)}, u32[]{:S(2)}, u32[]{:S(2)}) collective-permute-start(bf16[392,512]{1,0:T(8,128)(2,1)S(1)} %collective-permute-done.5.e1), channel_id=1, source_target_pairs={{0,1},{1,0},{2,3},{3,2},{4,5},{5,4},{6,7},{7,6},{8,9},{9,8},{10,11... | collective-permute-start | bytes 1204232 | tf_op jit(solution)/shard_map/ppermute | solution.py:622
  30.7 12.7 %collective-permute-start.9 = (bf16[264,512]{1,0:T(8,128)(2,1)S(1)}, bf16[264,512]{1,0:T(8,128)(2,1)S(1)}, u32[]{:S(2)}, u32[]{:S(2)}) collective-permute-start(bf16[264,512]{1,0:T(8,128)(2,1)S(1)} %collective-permute-done.8.s0), channel_id=1, source_target_pairs={{0,1},{1,0},{2,3},{3,2},{4,5},{5,4},{6,7},{7,6},{8,9},{9,8},{10,11... | collective-permute-start | bytes 811016 | tf_op jit(solution)/shard_map/ppermute | solution.py:622
  30.7 12.7 %collective-permute-start.13 = (bf16[264,512]{1,0:T(8,128)(2,1)S(1)}, bf16[264,512]{1,0:T(8,128)(2,1)S(1)}, u32[]{:S(2)}, u32[]{:S(2)}) collective-permute-start(bf16[264,512]{1,0:T(8,128)(2,1)S(1)} %collective-permute-done.12.s4), channel_id=1, source_target_pairs={{0,1},{1,0},{2,3},{3,2},{4,5},{5,4},{6,7},{7,6},{8,9},{9,8},{10,11... | collective-permute-start | bytes 811016 | tf_op jit(solution)/shard_map/ppermute | solution.py:622
  31.2 12.2 %collective-permute-start.11 = (bf16[264,512]{1,0:T(8,128)(2,1)S(1)}, bf16[264,512]{1,0:T(8,128)(2,1)S(1)}, u32[]{:S(2)}, u32[]{:S(2)}) collective-permute-start(bf16[264,512]{1,0:T(8,128)(2,1)S(1)} %collective-permute-done.10.s2), channel_id=1, source_target_pairs={{0,1},{1,0},{2,3},{3,2},{4,5},{5,4},{6,7},{7,6},{8,9},{9,8},{10,11... | collective-permute-start | bytes 811016 | tf_op jit(solution)/shard_map/ppermute | solution.py:622
  31.3 3.2 %copy-start.1 = (bf16[512,512]{1,0:T(8,128)(2,1)S(1)}, bf16[512,512]{1,0:T(8,128)(2,1)}, u32[]{:S(2)}) copy-start(bf16[512,512]{1,0:T(8,128)(2,1)} %win0.5) | copy-start | bytes 1572868
  31.3 3.2 %copy-start.2 = (bf16[512,512]{1,0:T(8,128)(2,1)S(1)}, bf16[512,512]{1,0:T(8,128)(2,1)}, u32[]{:S(2)}) copy-start(bf16[512,512]{1,0:T(8,128)(2,1)} %wback0.5) | copy-start | bytes 1572868
  32.7 10.7 %copy-start.6 = (bf16[256,512]{1,0:T(8,128)(2,1)S(1)}, bf16[256,512]{1,0:T(8,128)(2,1)}, u32[]{:S(2)}) copy-start(bf16[256,512]{1,0:T(8,128)(2,1)} %ct.3) | copy-start | bytes 786436
  32.8 8.9 %collective-permute-start.14 = (bf16[264,512]{1,0:T(8,128)(2,1)S(1)}, bf16[264,512]{1,0:T(8,128)(2,1)S(1)}, u32[]{:S(2)}, u32[]{:S(2)}) collective-permute-start(bf16[264,512]{1,0:T(8,128)(2,1)S(1)} %collective-permute-done.12.s4), channel_id=1, source_target_pairs={{0,4},{4,0},{8,12},{12,8},{16,20},{20,16},{24,28},{28,24},{1,5},{5... | collective-permute-start | bytes 811016 | tf_op jit(solution)/shard_map/ppermute | solution.py:625
  41.6 1.8 %collective-permute-start.15 = (bf16[264,512]{1,0:T(8,128)(2,1)S(1)}, bf16[264,512]{1,0:T(8,128)(2,1)S(1)}, u32[]{:S(2)}, u32[]{:S(2)}) collective-permute-start(bf16[264,512]{1,0:T(8,128)(2,1)S(1)} %collective-permute-done.14.s6), channel_id=1, source_target_pairs={{0,1},{1,0},{2,3},{3,2},{4,5},{5,4},{6,7},{7,6},{8,9},{9,8},{10,11... | collective-permute-start | bytes 811016 | tf_op jit(solution)/shard_map/ppermute | solution.py:622
  41.6 14.2 %collective-permute-start.16 = (bf16[256,512]{1,0:T(8,128)(2,1)S(1)}, bf16[256,512]{1,0:T(8,128)(2,1)S(1)}, u32[]{:S(2)}, u32[]{:S(2)}) collective-permute-start(bf16[256,512]{1,0:T(8,128)(2,1)S(1)} %get-tuple-element.174.n2), channel_id=1, source_target_pairs={{0,2},{1,3},{2,0},{3,1},{4,6},{5,7},{6,4},{7,5},{8,10},{9,11},{10,... | collective-permute-start | bytes 786440 | tf_op jit(solution)/shard_map/ppermute | solution.py:622
  46.3 9.7 %collective-permute-start.17 = (bf16[256,512]{1,0:T(8,128)(2,1)S(1)}, bf16[256,512]{1,0:T(8,128)(2,1)S(1)}, u32[]{:S(2)}, u32[]{:S(2)}) collective-permute-start(bf16[256,512]{1,0:T(8,128)(2,1)S(1)} %get-tuple-element.184.fg), channel_id=1, source_target_pairs={{0,2},{1,3},{2,0},{3,1},{4,6},{5,7},{6,4},{7,5},{8,10},{9,11},{10,... | collective-permute-start | bytes 786440 | tf_op jit(solution)/shard_map/ppermute | solution.py:622
  53.3 6.9 %collective-permute-start.18 = (bf16[256,256]{1,0:T(8,128)(2,1)S(1)}, bf16[256,256]{1,0:T(8,128)(2,1)S(1)}, u32[]{:S(2)}, u32[]{:S(2)}) collective-permute-start(bf16[256,256]{1,0:T(8,128)(2,1)S(1)} %get-tuple-element.203), channel_id=1, source_target_pairs={{0,2},{1,3},{2,0},{3,1},{4,6},{5,7},{6,4},{7,5},{8,10},{9,11},{10,... | collective-permute-start | bytes 393224 | tf_op jit(solution)/shard_map/ppermute | solution.py:622
  60.2 2.3 %collective-permute-start.19 = (bf16[512,512]{1,0:T(8,128)(2,1)S(1)}, bf16[512,512]{1,0:T(8,128)(2,1)S(1)}, u32[]{:S(2)}, u32[]{:S(2)}) collective-permute-start(bf16[512,512]{1,0:T(8,128)(2,1)S(1)} %get-tuple-element.210), channel_id=1, source_target_pairs={{0,1},{1,0},{2,3},{3,2},{4,5},{5,4},{6,7},{7,6},{8,9},{9,8},{10,11... | collective-permute-start | bytes 1572872 | tf_op jit(solution)/shard_map/ppermute | solution.py:622
  60.7 2.3 %collective-permute-start.20 = (bf16[520,512]{1,0:T(8,128)(2,1)S(1)}, bf16[520,512]{1,0:T(8,128)(2,1)S(1)}, u32[]{:S(2)}, u32[]{:S(2)}) collective-permute-start(bf16[520,512]{1,0:T(8,128)(2,1)S(1)} %get-tuple-element.211), channel_id=1, source_target_pairs={{0,1},{1,0},{2,3},{3,2},{4,5},{5,4},{6,7},{7,6},{8,9},{9,8},{10,11... | collective-permute-start | bytes 1597448 | tf_op jit(solution)/shard_map/ppermute | solution.py:622
  62.0 5.3 %collective-permute-start.21 = (bf16[776,512]{1,0:T(8,128)(2,1)S(1)}, bf16[776,512]{1,0:T(8,128)(2,1)S(1)}, u32[]{:S(2)}, u32[]{:S(2)}) collective-permute-start(bf16[776,512]{1,0:T(8,128)(2,1)S(1)} %get-tuple-element.214), channel_id=1, source_target_pairs={{0,1},{1,0},{2,3},{3,2},{4,5},{5,4},{6,7},{7,6},{8,9},{9,8},{10,11... | collective-permute-start | bytes 2383880 | tf_op jit(solution)/shard_map/ppermute | solution.py:622
  64.0 12.2 %collective-permute-start.22 = (bf16[256,512]{1,0:T(8,128)(2,1)S(1)}, bf16[256,512]{1,0:T(8,128)(2,1)S(1)}, u32[]{:S(2)}, u32[]{:S(2)}) collective-permute-start(bf16[256,512]{1,0:T(8,128)(2,1)S(1)} %get-tuple-element.228), channel_id=1, source_target_pairs={{0,4},{4,0},{8,12},{12,8},{16,20},{20,16},{24,28},{28,24},{1,5},{5... | collective-permute-start | bytes 786440 | tf_op jit(solution)/shard_map/ppermute | solution.py:625
  65.7 10.5 %collective-permute-start.23 = (bf16[256,512]{1,0:T(8,128)(2,1)S(1)}, bf16[256,512]{1,0:T(8,128)(2,1)S(1)}, u32[]{:S(2)}, u32[]{:S(2)}) collective-permute-start(bf16[256,512]{1,0:T(8,128)(2,1)S(1)} %get-tuple-element.230), channel_id=1, source_target_pairs={{0,8},{4,12},{8,0},{12,4},{16,24},{20,28},{24,16},{28,20},{1,9},{5... | collective-permute-start | bytes 786440 | tf_op jit(solution)/shard_map/ppermute | solution.py:625
  67.9 11.0 %collective-permute-start.25 = (bf16[392,512]{1,0:T(8,128)(2,1)S(1)}, bf16[392,512]{1,0:T(8,128)(2,1)S(1)}, u32[]{:S(2)}, u32[]{:S(2)}) collective-permute-start(bf16[392,512]{1,0:T(8,128)(2,1)S(1)} %half_rows.1), channel_id=1, source_target_pairs={{0,2},{1,3},{2,0},{3,1},{4,6},{5,7},{6,4},{7,5},{8,10},{9,11},{10,... | collective-permute-start | bytes 1204232 | tf_op jit(solution)/shard_map/ppermute | solution.py:622
  75.8 2.2 %collective-permute-start.24 = (bf16[392,512]{1,0:T(8,128)(2,1)S(1)}, bf16[392,512]{1,0:T(8,128)(2,1)S(1)}, u32[]{:S(2)}, u32[]{:S(2)}) collective-permute-start(bf16[392,512]{1,0:T(8,128)(2,1)S(1)} %get-tuple-element.234), channel_id=1, source_target_pairs={{0,1},{1,0},{2,3},{3,2},{4,5},{5,4},{6,7},{7,6},{8,9},{9,8},{10,11... | collective-permute-start | bytes 1204232 | tf_op jit(solution)/shard_map/ppermute | solution.py:622
  76.9 6.2 %collective-permute-start.27 = (bf16[128,512]{1,0:T(8,128)(2,1)S(1)}, bf16[128,512]{1,0:T(8,128)(2,1)S(1)}, u32[]{:S(2)}, u32[]{:S(2)}) collective-permute-start(bf16[128,512]{1,0:T(8,128)(2,1)S(1)} %get-tuple-element.240), channel_id=1, source_target_pairs={{0,8},{4,12},{8,0},{12,4},{16,24},{20,28},{24,16},{28,20},{1,9},{5... | collective-permute-start | bytes 393224 | tf_op jit(solution)/shard_map/ppermute | solution.py:625
  77.4 6.0 %collective-permute-start.28 = (bf16[128,512]{1,0:T(8,128)(2,1)S(1)}, bf16[128,512]{1,0:T(8,128)(2,1)S(1)}, u32[]{:S(2)}, u32[]{:S(2)}) collective-permute-start(bf16[128,512]{1,0:T(8,128)(2,1)S(1)} %get-tuple-element.242), channel_id=1, source_target_pairs={{0,4},{4,0},{8,12},{12,8},{16,20},{20,16},{24,28},{28,24},{1,5},{5... | collective-permute-start | bytes 393224 | tf_op jit(solution)/shard_map/ppermute | solution.py:625
  78.0 4.1 %collective-permute-start.26 = (bf16[512,512]{1,0:T(8,128)(2,1)S(1)}, bf16[512,512]{1,0:T(8,128)(2,1)S(1)}, u32[]{:S(2)}, u32[]{:S(2)}) collective-permute-start(bf16[512,512]{1,0:T(8,128)(2,1)S(1)} %get-tuple-element.238), channel_id=1, source_target_pairs={{0,1},{1,0},{2,3},{3,2},{4,5},{5,4},{6,7},{7,6},{8,9},{9,8},{10,11... | collective-permute-start | bytes 1572872 | tf_op jit(solution)/shard_map/ppermute | solution.py:622
  79.8 7.2 %collective-permute-start.29 = (bf16[192,512]{1,0:T(8,128)(2,1)S(1)}, bf16[192,512]{1,0:T(8,128)(2,1)S(1)}, u32[]{:S(2)}, u32[]{:S(2)}) collective-permute-start(bf16[192,512]{1,0:T(8,128)(2,1)S(1)} %get-tuple-element.245), channel_id=1, source_target_pairs={{0,4},{4,0},{8,12},{12,8},{16,20},{20,16},{24,28},{28,24},{1,5},{5... | collective-permute-start | bytes 589832 | tf_op jit(solution)/shard_map/ppermute | solution.py:625
  80.5 9.0 %collective-permute-start.30 = (bf16[192,512]{1,0:T(8,128)(2,1)S(1)}, bf16[192,512]{1,0:T(8,128)(2,1)S(1)}, u32[]{:S(2)}, u32[]{:S(2)}) collective-permute-start(bf16[192,512]{1,0:T(8,128)(2,1)S(1)} %get-tuple-element.247), channel_id=1, source_target_pairs={{0,8},{4,12},{8,0},{12,4},{16,24},{20,28},{24,16},{28,20},{1,9},{5... | collective-permute-start | bytes 589832 | tf_op jit(solution)/shard_map/ppermute | solution.py:625
  82.7 8.2 %collective-permute-start.31 = (bf16[512,256]{1,0:T(8,128)(2,1)S(1)}, bf16[512,256]{1,0:T(8,128)(2,1)S(1)}, u32[]{:S(2)}, u32[]{:S(2)}) collective-permute-start(bf16[512,256]{1,0:T(8,128)(2,1)S(1)} %half_columns.1), channel_id=1, source_target_pairs={{0,2},{1,3},{2,0},{3,1},{4,6},{5,7},{6,4},{7,5},{8,10},{9,11},{10,... | collective-permute-start | bytes 786440 | tf_op jit(solution)/shard_map/ppermute | solution.py:622
  84.1 9.1 %collective-permute-start.32 = (bf16[128,512]{1,0:T(8,128)(2,1)S(1)}, bf16[128,512]{1,0:T(8,128)(2,1)S(1)}, u32[]{:S(2)}, u32[]{:S(2)}) collective-permute-start(bf16[128,512]{1,0:T(8,128)(2,1)S(1)} %get-tuple-element.253), channel_id=1, source_target_pairs={{0,16},{4,20},{8,24},{12,28},{16,0},{20,4},{24,8},{28,12},{1,17},{... | collective-permute-start | bytes 393224 | tf_op jit(solution)/shard_map/ppermute | solution.py:625
  90.2 6.8 %collective-permute-start.33 = (bf16[96,512]{1,0:T(8,128)(2,1)S(1)}, bf16[96,512]{1,0:T(8,128)(2,1)S(1)}, u32[]{:S(2)}, u32[]{:S(2)}) collective-permute-start(bf16[96,512]{1,0:T(8,128)(2,1)S(1)} %get-tuple-element.255), channel_id=1, source_target_pairs={{0,8},{4,12},{8,0},{12,4},{16,24},{20,28},{24,16},{28,20},{1,9},{5... | collective-permute-start | bytes 294920 | tf_op jit(solution)/shard_map/ppermute | solution.py:625
  90.3 6.8 %collective-permute-start.34 = (bf16[96,512]{1,0:T(8,128)(2,1)S(1)}, bf16[96,512]{1,0:T(8,128)(2,1)S(1)}, u32[]{:S(2)}, u32[]{:S(2)}) collective-permute-start(bf16[96,512]{1,0:T(8,128)(2,1)S(1)} %get-tuple-element.257), channel_id=1, source_target_pairs={{0,4},{4,0},{8,12},{12,8},{16,20},{20,16},{24,28},{28,24},{1,5},{5... | collective-permute-start | bytes 294920 | tf_op jit(solution)/shard_map/ppermute | solution.py:625
  92.9 6.2 %collective-permute-start.38 = (f32[8,512]{1,0:T(8,128)S(1)}, f32[8,512]{1,0:T(8,128)S(1)}, u32[]{:S(2)}, u32[]{:S(2)}) collective-permute-start(f32[8,512]{1,0:T(8,128)S(1)} %get-tuple-element.263.refs_0_), channel_id=1, source_target_pairs={{0,2},{1,3},{2,0},{3,1},{4,6},{5,7},{6,4},{7,5},{8,10},{9,11},{10,... | collective-permute-start | bytes 49160 | tf_op jit(solution)/shard_map/ppermute | solution.py:622
  93.2 15.9 %collective-permute-start.37 = (f32[8,512]{1,0:T(8,128)S(1)}, f32[8,512]{1,0:T(8,128)S(1)}, u32[]{:S(2)}, u32[]{:S(2)}) collective-permute-start(f32[8,512]{1,0:T(8,128)S(1)} %get-tuple-element.263.refs_0_), channel_id=1, source_target_pairs={{0,1},{1,0},{2,3},{3,2},{4,5},{5,4},{6,7},{7,6},{8,9},{9,8},{10,11... | collective-permute-start | bytes 49160 | tf_op jit(solution)/shard_map/ppermute | solution.py:622
  93.8 12.9 %collective-permute-start.35 = (bf16[1,136,512]{2,1,0:T(8,128)(2,1)S(1)}, bf16[1,136,512]{2,1,0:T(8,128)(2,1)S(1)}, u32[]{:S(2)}, u32[]{:S(2)}) collective-permute-start(bf16[1,136,512]{2,1,0:T(8,128)(2,1)S(1)} %bitcast.15), channel_id=1, source_target_pairs={{0,16},{4,20},{8,24},{12,28},{16,0},{20,4},{24,8},{28,12},{1,17},{... | collective-permute-start | bytes 417800 | tf_op jit(solution)/shard_map/ppermute | solution.py:625
  97.7 11.4 %collective-permute-start.36 = (bf16[96,512]{1,0:T(8,128)(2,1)S(1)}, bf16[96,512]{1,0:T(8,128)(2,1)S(1)}, u32[]{:S(2)}, u32[]{:S(2)}) collective-permute-start(bf16[96,512]{1,0:T(8,128)(2,1)S(1)} %get-tuple-element.262), channel_id=1, source_target_pairs={{0,16},{4,20},{8,24},{12,28},{16,0},{20,4},{24,8},{28,12},{1,17},{... | collective-permute-start | bytes 294920 | tf_op jit(solution)/shard_map/ppermute | solution.py:625
  99.1 10.0 %collective-permute-start.39 = (f32[8,512]{1,0:T(8,128)S(1)}, f32[8,512]{1,0:T(8,128)S(1)}, u32[]{:S(2)}, u32[]{:S(2)}) collective-permute-start(f32[8,512]{1,0:T(8,128)S(1)} %collective-permute-done.38.refs_2_), channel_id=1, source_target_pairs={{0,1},{1,0},{2,3},{3,2},{4,5},{5,4},{6,7},{7,6},{8,9},{9,8},{10,11... | collective-permute-start | bytes 49160 | tf_op jit(solution)/shard_map/ppermute | solution.py:622
  107.2 5.9 %collective-permute-start.40 = (bf16[2,72,512]{2,1,0:T(8,128)(2,1)S(1)}, bf16[2,72,512]{2,1,0:T(8,128)(2,1)S(1)}, u32[]{:S(2)}, u32[]{:S(2)}) collective-permute-start(bf16[2,72,512]{2,1,0:T(8,128)(2,1)S(1)} %get-tuple-element.260.held1), channel_id=1, source_target_pairs={{0,8},{4,12},{8,0},{12,4},{16,24},{20,28},{24,16},{28,20},{1,9},{5... | collective-permute-start | bytes 442376 | tf_op jit(solution)/shard_map/ppermute | solution.py:625
  107.9 5.3 %collective-permute-start.41 = (bf16[2,64,512]{2,1,0:T(8,128)(2,1)S(1)}, bf16[2,64,512]{2,1,0:T(8,128)(2,1)S(1)}, u32[]{:S(2)}, u32[]{:S(2)}) collective-permute-start(bf16[2,64,512]{2,1,0:T(8,128)(2,1)S(1)} %get-tuple-element.266.held2), channel_id=1, source_target_pairs={{0,4},{4,0},{8,12},{12,8},{16,20},{20,16},{24,28},{28,24},{1,5},{5... | collective-permute-start | bytes 393224 | tf_op jit(solution)/shard_map/ppermute | solution.py:625
  109.7 8.3 %collective-permute-start.42 = (bf16[1,104,512]{2,1,0:T(8,128)(2,1)S(1)}, bf16[1,104,512]{2,1,0:T(8,128)(2,1)S(1)}, u32[]{:S(2)}, u32[]{:S(2)}) collective-permute-start(bf16[1,104,512]{2,1,0:T(8,128)(2,1)S(1)} %bitcast.17), channel_id=1, source_target_pairs={{0,16},{4,20},{8,24},{12,28},{16,0},{20,4},{24,8},{28,12},{1,17},{... | collective-permute-start | bytes 319496 | tf_op jit(solution)/shard_map/ppermute | solution.py:625
  113.7 9.9 %collective-permute-start.43 = (bf16[4,72,512]{2,1,0:T(8,128)(2,1)S(1)}, bf16[4,72,512]{2,1,0:T(8,128)(2,1)S(1)}, u32[]{:S(2)}, u32[]{:S(2)}) collective-permute-start(bf16[4,72,512]{2,1,0:T(8,128)(2,1)S(1)} %get-tuple-element.267.held1), channel_id=1, source_target_pairs={{0,4},{4,0},{8,12},{12,8},{16,20},{20,16},{24,28},{28,24},{1,5},{5... | collective-permute-start | bytes 884744 | tf_op jit(solution)/shard_map/ppermute | solution.py:625
  114.9 8.8 %collective-permute-start.44 = (bf16[4,64,512]{2,1,0:T(8,128)(2,1)S(1)}, bf16[4,64,512]{2,1,0:T(8,128)(2,1)S(1)}, u32[]{:S(2)}, u32[]{:S(2)}) collective-permute-start(bf16[4,64,512]{2,1,0:T(8,128)(2,1)S(1)} %get-tuple-element.271.held2), channel_id=1, source_target_pairs={{0,8},{4,12},{8,0},{12,4},{16,24},{20,28},{24,16},{28,20},{1,9},{5... | collective-permute-start | bytes 786440 | tf_op jit(solution)/shard_map/ppermute | solution.py:625
  118.5 7.3 %collective-permute-start.45 = (bf16[2,56,512]{2,1,0:T(8,128)(2,1)S(1)}, bf16[2,56,512]{2,1,0:T(8,128)(2,1)S(1)}, u32[]{:S(2)}, u32[]{:S(2)}) collective-permute-start(bf16[2,56,512]{2,1,0:T(8,128)(2,1)S(1)} %get-tuple-element.269.held1), channel_id=1, source_target_pairs={{0,8},{4,12},{8,0},{12,4},{16,24},{20,28},{24,16},{28,20},{1,9},{5... | collective-permute-start | bytes 344072 | tf_op jit(solution)/shard_map/ppermute | solution.py:625
  118.7 7.1 %collective-permute-start.46 = (bf16[2,48,512]{2,1,0:T(8,128)(2,1)S(1)}, bf16[2,48,512]{2,1,0:T(8,128)(2,1)S(1)}, u32[]{:S(2)}, u32[]{:S(2)}) collective-permute-start(bf16[2,48,512]{2,1,0:T(8,128)(2,1)S(1)} %get-tuple-element.274.held2), channel_id=1, source_target_pairs={{0,4},{4,0},{8,12},{12,8},{16,20},{20,16},{24,28},{28,24},{1,5},{5... | collective-permute-start | bytes 294920 | tf_op jit(solution)/shard_map/ppermute | solution.py:625
  126.4 7.0 %collective-permute-start.47 = (bf16[4,56,512]{2,1,0:T(8,128)(2,1)S(1)}, bf16[4,56,512]{2,1,0:T(8,128)(2,1)S(1)}, u32[]{:S(2)}, u32[]{:S(2)}) collective-permute-start(bf16[4,56,512]{2,1,0:T(8,128)(2,1)S(1)} %get-tuple-element.275.held1), channel_id=1, source_target_pairs={{0,4},{4,0},{8,12},{12,8},{16,20},{20,16},{24,28},{28,24},{1,5},{5... | collective-permute-start | bytes 688136 | tf_op jit(solution)/shard_map/ppermute | solution.py:625
  127.6 5.7 %collective-permute-start.48 = (bf16[4,48,512]{2,1,0:T(8,128)(2,1)S(1)}, bf16[4,48,512]{2,1,0:T(8,128)(2,1)S(1)}, u32[]{:S(2)}, u32[]{:S(2)}) collective-permute-start(bf16[4,48,512]{2,1,0:T(8,128)(2,1)S(1)} %get-tuple-element.277.held2), channel_id=1, source_target_pairs={{0,8},{4,12},{8,0},{12,4},{16,24},{20,28},{24,16},{28,20},{1,9},{5... | collective-permute-start | bytes 589832 | tf_op jit(solution)/shard_map/ppermute | solution.py:625

commit v4 on v3

--- a/solution.py
+++ b/solution.py
@@ -16,7 +16,9 @@
 PX = 2
 LOCAL = (0, PX, 1, 1 ^ PX)
 SPARE = 4 * 1024 * 1024
-COST = 10**10
+HEAVY = 10**10
+LIGHT = 0
+EASY = ("pair_a", "part_f", "halves_f", "halves_a", "input_grad")
 
 
 def nn(a, b):
@@ -35,7 +37,7 @@
 SM = pl.BlockSpec(memory_space=pltpu.SMEM)
 
 
-def call(body, outs, args, smem=0, scratch=(), name=None, space=VM, limit=None):
+def call(body, outs, args, smem=0, scratch=(), name=None, space=VM, limit=None, cost=0):
     nbytes = sum(a.size * a.dtype.itemsize for a in args) + sum(o.size * o.dtype.itemsize for o in outs)
     held = sum(math.prod(s.shape) * 4 for s in scratch)
     limit = limit or nbytes + held + SPARE
@@ -46,7 +48,7 @@
         out_specs=tuple([VM] * len(outs)),
         scratch_shapes=list(scratch),
         compiler_params=pltpu.CompilerParams(vmem_limit_bytes=limit),
-        cost_estimate=pl.CostEstimate(flops=COST, bytes_accessed=0, transcendentals=0),
+        cost_estimate=pl.CostEstimate(flops=cost, bytes_accessed=0, transcendentals=0),
         name=name,
     )(*args)
 
@@ -141,24 +143,56 @@
         segc[256 * t : 256 * t + 256, :] = row.T
 
 
-def first_kernel(
-    tb, segs, segv, x0, x1, x2, x3, vecs, qkv0, qkv1,
-    n_ref, qt0_ref, qt1_ref, k_ref, vt_ref, p_ref, ot_ref, att_ref, invl_ref,
-    qz, s_sc, m_sc, l_sc, o_sc, segc,
-):
-    for i, x in enumerate((x0, x1, x2, x3)):
+def weight_of(w, part):
+    cols = slice(128 * part, 128 * part + 128)
+    return jnp.concatenate([w[0][:, cols], w[1][0:256, cols]], axis=0)
+
+
+def bias_of(w, part):
+    return w[1][256:257, 128 * part : 128 * part + 128].astype(F32)
+
+
+def project(n, w, c, k_ref, vt_ref, blocks):
+    cols = slice(128 * c, 128 * c + 128)
+    k = nn(n, weight_of(w, 1)).astype(BF16)
+    vt = (nn(n, weight_of(w, 2)) + bias_of(w, 2)).T.astype(BF16)
+    for i, at in enumerate(blocks):
+        k_ref[at : at + 256, cols] = k[256 * i : 256 * i + 256]
+        vt_ref[cols, at : at + 256] = vt[:, 256 * i : 256 * i + 256]
+
+
+def query_of(n, w):
+    q = nn(n, weight_of(w, 0)) + bias_of(w, 0)
+    return (q.astype(BF16).astype(F32) * HD ** (-0.5)).T.astype(BF16)
+
+
+def chip_kernel(pos, x0, x2, vecs, qa0, qb0, qa1, qb1, n_ref, qt_ref, k_ref, vt_ref):
+    for i, x in enumerate((x0, x2)):
         unit, _ = norm_unit(x[...].astype(F32))
         n_ref[256 * i : 256 * i + 256, :] = (unit * vecs[0:1, :] + vecs[1:2, :]).astype(BF16)
     n = n_ref[...]
-    for c, w in enumerate((qkv0, qkv1)):
-        cols = slice(128 * c, 128 * c + 128)
-        q = nn(n[0:512], w[0:512, 0:128]) + w[512:513, 0:128].astype(F32)
-        qt = (q.astype(BF16).astype(F32) * HD ** (-0.5)).T.astype(BF16)
-        qt0_ref[cols, :] = qt[:, 0:256]
-        qt1_ref[cols, :] = qt[:, 256:512]
-        k_ref[:, cols] = nn(n, w[0:512, 128:256]).astype(BF16)
-        v = nn(n, w[0:512, 256:384]) + w[512:513, 256:384].astype(F32)
-        vt_ref[cols, :] = v.T.astype(BF16)
+    for c, w in enumerate(((qa0, qb0), (qa1, qb1))):
+        qt_ref[128 * c : 128 * c + 128, :] = query_of(n[0:256], w)
+        project(n, w, c, k_ref, vt_ref, (0, 256))
+
+
+def first_kernel(
+    tb, segs, segv, x1, x3, vecs, qa0, qb0, qa1, qb1, na, ka, vta,
+    n_ref, qt1_ref, k_ref, vt_ref, p_ref, ot_ref, att_ref, invl_ref,
+    qz, s_sc, m_sc, l_sc, o_sc, segc,
+):
+    for i, x in enumerate((x1, x3)):
+        unit, _ = norm_unit(x[...].astype(F32))
+        n_ref[512 * i + 256 : 512 * i + 512, :] = (unit * vecs[0:1, :] + vecs[1:2, :]).astype(BF16)
+    n = jnp.concatenate([n_ref[256:512, :], n_ref[768:1024, :]], axis=0)
+    for c, w in enumerate(((qa0, qb0), (qa1, qb1))):
+        qt1_ref[128 * c : 128 * c + 128, :] = query_of(n[0:256], w)
+        project(n, w, c, k_ref, vt_ref, (256, 768))
+    for i in range(2):
+        src, dst = slice(256 * i, 256 * i + 256), slice(512 * i, 512 * i + 256)
+        n_ref[dst, :] = na[src, :]
+        k_ref[dst, :] = ka[src, :]
+        vt_ref[:, dst] = vta[:, src]
     fill_segc(segc, segv)
     fill_qz(qz, qt1_ref)
     attend_query_block(1, tb, segs, segv, qz, k_ref, vt_ref, p_ref, ot_ref, invl_ref, s_sc, m_sc, l_sc, o_sc, segc)
@@ -189,6 +223,16 @@
 def gather_gate(tb, pieces, start, scratch):
     for i, piece in enumerate(pieces):
         scratch[pl.ds(pl.multiple_of(tb[i] * 128, 128), 128), :] = piece[start : start + 128, :]
+
+
+def gather_gate_two(pos, g2, c2, pieces, scratch):
+    scratch[pl.ds(pl.multiple_of(pos[0] * 128, 128), 128), :] = g2[...]
+    scratch[pl.ds(pl.multiple_of(pos[2] * 128, 128), 128), :] = c2[256:384, :]
+    for i, piece in enumerate(pieces):
+        quarter = (pos[4] ^ (i // 2)) & 3
+        at = pos[1 + 2 * (i % 2)] * 128 + quarter * 32
+        rows = piece.shape[0]
+        scratch[pl.ds(pl.multiple_of(at, 32), 32), :] = piece[rows - 32 : rows, :]
 
 
 def out_kernel(
@@ -213,13 +257,18 @@
     return jnp.concatenate([a[start : start + 128, :], b[start : start + 128, :]], axis=0)
 
 
-def pair_bias(a, b):
-    return jnp.concatenate([a[256:257, 0:128], b[256:257, 0:128]], axis=1).astype(F32)
+def pair_bias(a, b, row=256):
+    return jnp.concatenate([a[row : row + 1, 0:128], b[row : row + 1, 0:128]], axis=1).astype(F32)
+
+
+def cut_kernel(pos, sx, sz, a_ref, b_ref):
+    a_ref[...] = sz[0:128, :]
+    b_ref[...] = sx[128:296, :]
 
 
 def ffn_first_kernel(
-    tb, n2, vecs, win0, wback0, c2,
-    total_ref, hid_ref, slope_ref,
+    tb, n2, vecs, win0, wback0, c2, s0, s1, s2, s3, s4, s5,
+    total_ref, hid_ref, slope_ref, slope1_ref,
 ):
     n2v = n2[...]
     total = jnp.zeros((256, 512), F32)
@@ -229,22 +278,22 @@
         hid_ref[:, 512 * i : 512 * i + 512] = value
         slope_ref[:, 512 * i : 512 * i + 512] = slope.astype(BF16)
         total = total + nn(value, wb)
+    for i, (a, b) in enumerate(((s0, s1), (s2, s3), (s4, s5))):
+        value, slope = gelu_parts(nt(n2v, pair_up(a, b, 0)) + pair_bias(a, b))
+        slope1_ref[:, 256 * i : 256 * i + 256] = slope.astype(BF16)
+        total = total + nn(value.astype(BF16), pair_up(a, b, 128))
     total_ref[...] = total
 
 
 def ffn_kernel(
-    tb, n2, mid, ct, vecs, e0, e1, e2, e3, total0, s0, s1, s2, s3, s4, s5, s6, s7,
-    out_ref, fg_ref, ltg_ref, slope_ref,
-    gw,
-):
-    gather_gate(tb, (e0, e1, e2, e3), 256, gw)
+    tb, n2, mid, ct, vecs, g2, c2, total0, s0, s1, s2, s3, s4, s5, a6, a7, b6, b7,
+    out_ref, fg_ref, ltg_ref, slope_ref, gw,
+):
+    gather_gate_two(tb, g2, c2, (s0, s1, s2, s3, s4, s5, b6, b7), gw)
     n2v = n2[...]
-    total = total0[...]
-    for i, (a, b) in enumerate(((s0, s1), (s2, s3), (s4, s5), (s6, s7))):
-        value, slope = gelu_parts(nt(n2v, pair_up(a, b, 0)) + pair_bias(a, b))
-        slope_ref[:, 256 * i : 256 * i + 256] = slope.astype(BF16)
-        total = total + nn(value.astype(BF16), pair_up(a, b, 128))
-    ffn = total + vecs[6:7, :]
+    value, slope = gelu_parts(nt(n2v, pair_up(a6, a7, 0)) + pair_bias(b6, b7, 128))
+    slope_ref[...] = slope.astype(BF16)
+    ffn = total0[...] + nn(value.astype(BF16), pair_up(b6, b7, 0)) + vecs[6:7, :]
     gate = sigmoid(nn(n2v, gw[...]) + vecs[7:8, :])
     up = ct[...].astype(F32)
     out_ref[...] = (mid[...] + gate * ffn).astype(BF16)
@@ -253,12 +302,12 @@
 
 
 def back_kernel(
-    tb, fg, ltg, slope0, slope1, mid, branch, gate, ct, vecs, e0, e1, e2, e3,
-    win0, wback0, s0, s1, s2, s3, s4, s5, s6, s7,
+    tb, fg, ltg, slope0, slope1, slope2, mid, branch, gate, ct, vecs, e0, e1, e2, e3, g2,
+    win0, wback0, s0, s1, s2, s3, s4, s5, a6, a7, b6, b7,
     dot_ref, dotp_ref, mg_ref, bg_ref, log_ref, hg_ref, sums_ref,
     gw,
 ):
-    gather_gate(tb, (e0, e1, e2, e3), 256, gw)
+    gather_gate_two(tb, g2, e2, (s0, s1, s2, s3, s4, s5, b6, b7), gw)
     fgv = fg[...]
     ltgv = ltg[...]
     ng = nt(ltgv, gw[...])
@@ -266,9 +315,12 @@
         hg = (nt(fgv, wb) * slope0[:, 512 * i : 512 * i + 512].astype(F32)).astype(BF16)
         hg_ref[:, 512 * i : 512 * i + 512] = hg
         ng = ng + nt(hg, w)
-    for i, (a, b) in enumerate(((s0, s1), (s2, s3), (s4, s5), (s6, s7))):
-        hg = (nt(fgv, pair_up(a, b, 128)) * slope1[:, 256 * i : 256 * i + 256].astype(F32)).astype(BF16)
+    for i, (a, b) in enumerate(((s0, s1), (s2, s3), (s4, s5))):
+        part = slope1[:, 256 * i : 256 * i + 256]
+        hg = (nt(fgv, pair_up(a, b, 128)) * part.astype(F32)).astype(BF16)
         ng = ng + nn(hg, pair_up(a, b, 0))
+    hg = (nt(fgv, pair_up(b6, b7, 0)) * slope2[...].astype(F32)).astype(BF16)
+    ng = ng + nn(hg, pair_up(a6, a7, 0))
     unit, inverse = norm_unit(mid[...])
     g = ng * vecs[4:5, :]
     back = inverse * (g - jnp.mean(g, axis=-1, keepdims=True) - unit * jnp.mean(g * unit, axis=-1, keepdims=True))
@@ -339,10 +391,10 @@
         dst[base + 256 : base + 384, :] = wo[i].astype(dst.dtype)
 
 
-def prepare_kernel(tb, n, k, qkv0, qkv1, v_ref, kt_ref):
+def prepare_kernel(tb, n, k, qa0, qb0, qa1, qb1, v_ref, kt_ref):
     nv = n[...]
-    for c, w in enumerate((qkv0, qkv1)):
-        v = nn(nv, w[0:512, 256:384]) + w[512:513, 256:384].astype(F32)
+    for c, w in enumerate(((qa0, qb0), (qa1, qb1))):
+        v = nn(nv, weight_of(w, 2)) + bias_of(w, 2)
         v_ref[:, 128 * c : 128 * c + 128] = v.astype(BF16)
     kt_ref[...] = k[...].astype(F32).T.astype(BF16)
 
@@ -419,10 +471,9 @@
     send_ref[384:392, :] = jnp.concatenate([bq[:, 128:256], bv[:, 128:256], empty], axis=1).astype(BF16)
 
 
-def input_kernel(tb, dqt, dkt, dvt, qkv0, qkv1, own_ref, par_ref, send_ref):
+def input_kernel(tb, dqt, dkt, dvt, qa0, qb0, qa1, qb1, own_ref, par_ref, send_ref):
     def weight(part):
-        cols = slice(128 * part, 128 * part + 128)
-        return jnp.concatenate([qkv0[0:512, cols], qkv1[0:512, cols]], axis=1)
+        return jnp.concatenate([weight_of((qa0, qb0), part), weight_of((qa1, qb1), part)], axis=1)
 
     wk, wv = weight(1), weight(2)
     g = nn(wk, dkt[...]) + nn(wv, dvt[...])
@@ -445,30 +496,41 @@
     sums_ref[1:2, :] = jnp.sum(ng, axis=0, keepdims=True)
 
 
-def pack_kernel(
-    pos, w_in, w_back, w_out, g1, g2, wq, wk, wv, *refs,
-):
-    vectors, (s_ref, e_ref, c_ref, qkv_ref, vecs), (sems, cut, *lines) = refs[:11], refs[11:16], refs[16:]
+def run_copies(moves, sems):
+    copies = [pltpu.make_async_copy(src, dst, sems.at[i]) for i, (src, dst) in enumerate(moves)]
+    for copy in copies:
+        copy.start()
+    for copy in copies:
+        copy.wait()
+
+
+def pack_kernel(pos, w_in, w_back, w_out, g1, g2, wq, wk, wv, *refs):
+    vectors, (s_ref, e_ref, c_ref, qa_ref, qb_ref, vecs), (sems, cut, *lines) = refs[:11], refs[11:17], refs[17:]
     start = pl.multiple_of((pos[4] & 3) * 128, 128)
+    gate = pl.multiple_of((pos[4] & 3) * 32, 32)
     moves = [
         (w_in.at[:, pl.ds(start, 128)], cut),
         (w_back.at[pl.ds(start, 128), :], s_ref.at[128:256, :]),
+        (g2.at[pl.ds(gate, 32), :], s_ref.at[264:296, :]),
+    ]
+    for i, w in enumerate((wq, wk, wv)):
+        cols = slice(128 * i, 128 * i + 128)
+        moves.append((w.at[0:256, :], qa_ref.at[:, cols]))
+        moves.append((w.at[256:512, :], qb_ref.at[0:256, cols]))
+    late = [
         (w_out, e_ref.at[0:128, :]),
         (g1, e_ref.at[128:256, :]),
-        (g2, e_ref.at[256:384, :]),
         (w_out, c_ref.at[0:128, :]),
         (g1, c_ref.at[128:256, :]),
         (g2, c_ref.at[256:384, :]),
         (w_in, c_ref.at[392:904, :]),
         (w_back, c_ref.at[904:1416, :]),
-        (wq, qkv_ref.at[0:512, 0:128]),
-        (wk, qkv_ref.at[0:512, 128:256]),
-        (wv, qkv_ref.at[0:512, 256:384]),
-    ] + list(zip(vectors, lines))
+    ]
+    moves = moves + list(zip(vectors, lines)) + late
     copies = [pltpu.make_async_copy(src, dst, sems.at[i]) for i, (src, dst) in enumerate(moves)]
     for copy in copies:
         copy.start()
-    for copy in copies:
+    for copy in copies[: len(moves) - len(late)]:
         copy.wait()
     for i, v in enumerate(lines[:9]):
         vecs[i : i + 1, :] = v[...].astype(F32).reshape(1, 512)
@@ -478,11 +540,11 @@
     s_ref[0:128, :] = cut[...].astype(F32).T.astype(BF16)
     bias = vecs[8:9, pl.ds(start, 128)]
     s_ref[256:264, :] = jnp.broadcast_to(jnp.concatenate([bias] * 4, axis=1), (8, 512)).astype(BF16)
-    b_in = jnp.broadcast_to(vecs[8:9, :], (8, 512)).astype(BF16)
-    e_ref[384:392, :] = b_in
-    c_ref[384:392, :] = b_in
+    c_ref[384:392, :] = jnp.broadcast_to(vecs[8:9, :], (8, 512)).astype(BF16)
     for i, bias in enumerate((bq, jnp.zeros_like(bq), bv)):
-        qkv_ref[512:520, 128 * i : 128 * i + 128] = jnp.broadcast_to(bias, (8, 128)).astype(BF16)
+        qb_ref[256:264, 128 * i : 128 * i + 128] = jnp.broadcast_to(bias, (8, 128)).astype(BF16)
+    for copy in copies[len(moves) - len(late) :]:
+        copy.wait()
 
 
 def half_rows_kernel(tb, keep, recv, out_ref):
@@ -547,6 +609,24 @@
         cut_rows(total, 0, rows, bit_of(pos, bit), own, i * rows // 2, send, i * rows // 2)
 
 
+def round_kernel(pos, *refs, count, small):
+    out = refs[-1]
+    at = 0
+    for i in range(0, count, 2):
+        rows = refs[i].shape[0]
+        out[at : at + rows, :] = (refs[i][...] + refs[i + 1][...].astype(F32)).astype(BF16)
+        at += rows
+    out[at : at + 8, :] = jnp.zeros((8, 512), BF16)
+    used = count
+    for first, size, starts in small:
+        value = None
+        for ref, start in zip(refs[used : used + len(starts)], starts):
+            block = ref[start : start + size, :].astype(F32)
+            value = block if value is None else value + block
+        out[at + first : at + first + size, :] = value.astype(BF16)
+        used += len(starts)
+
+
 def both_kernel(pos, own0, recv0, own, send, total, *, bit):
     rows = own0.shape[0] // 2
     total[...] = own0[...] + recv0[...].astype(F32)
@@ -554,19 +634,8 @@
         cut_rows(total, i * rows, rows, bit_of(pos, bit), own, i * rows // 2, send, i * rows // 2)
 
 
-def fold_kernel(pos, own, recv, *refs, small):
-    out = refs[-1]
-    rows = own.shape[0]
-    out[0:rows, :] = (own[...] + recv[...].astype(F32)).astype(BF16)
-    out[rows : rows + 8, :] = jnp.zeros((8, 512), BF16)
-    at = 0
-    for first, size, starts in small:
-        value = None
-        for ref, start in zip(refs[at : at + len(starts)], starts):
-            block = ref[start : start + size, :].astype(F32)
-            value = block if value is None else value + block
-        out[rows + first : rows + first + size, :] = value.astype(BF16)
-        at += len(starts)
+def settle_kernel(pos, own, recv, out):
+    out[...] = (own[...].astype(F32) + recv[...].astype(F32)).astype(BF16)
 
 
 def stack_kernel(pos, held, recv, out):
@@ -575,13 +644,23 @@
     out[size:] = recv[...]
 
 
+def part_rows(value, at, rows, out1, out2):
+    out1[at, 0:rows, :] = value[0:rows]
+    out1[at, rows : rows + 8, :] = value[2 * rows :]
+    out2[at] = value[rows : 2 * rows]
+
+
+def settle_part_kernel(pos, own, recv, out1, out2):
+    rows = (own.shape[0] - 8) // 2
+    value = (own[...].astype(F32) + recv[...].astype(F32)).astype(BF16)
+    part_rows(value, 0, rows, out1, out2)
+
+
 def part_kernel(pos, held, recv, out1, out2):
     size, rows = held.shape[0], (held.shape[1] - 8) // 2
     for i, r in enumerate((held, recv)):
-        at = slice(i * size, i * size + size)
-        out1[at, 0:rows, :] = r[:, 0:rows, :]
-        out1[at, rows : rows + 8, :] = r[:, 2 * rows :, :]
-        out2[at] = r[:, rows : 2 * rows, :]
+        for j in range(size):
+            part_rows(r[j], i * size + j, rows, out1, out2)
 
 
 def pair_kernel(pos, held1, recv1, held2, recv2, out1, out2):
@@ -591,8 +670,8 @@
         out[size:] = r[...]
 
 
-def unpack_kernel(pos, held1, recv1, held2, recv2, *refs, plans, orders):
-    outs, scratch = refs[:-1], refs[-1]
+def unpack_kernel(pos, held1, recv1, held2, recv2, *refs, plans, orders, small):
+    outs, scratch, sums = refs[:-2], refs[-2], refs[-1]
     rows = held2.shape[1]
     used = 0
     for plan, order, blocks in zip(plans, orders, ((held1, recv1), (held2, recv2))):
@@ -610,7 +689,9 @@
     total = jnp.zeros((8, 512), F32)
     for r in (held1, recv1):
         total = total + jnp.sum(r[:, rows:, :].astype(F32), axis=0)
-    outs[used][...] = total
+    sums[...] = total
+    for i, (row, start, size) in enumerate(small):
+        outs[used + i][...] = sums[row : row + 1, start : start + size].reshape(size)
 
 
 def body(
@@ -634,52 +715,60 @@
     x0 = layer_input
     last = [None]
 
-    def step(kernel, outs, args, name, scratch=(), smem=1, space=VM, then=(), limit=None):
+    def step(kernel, outs, args, name, scratch=(), smem=1, space=VM, then=(), limit=None, cost=HEAVY):
         pos = tb if last[0] is None else after(tb, last[0], *then)
-        got = call(kernel, outs, [pos] + args, smem=smem, scratch=scratch, name=name, space=space, limit=limit)
+        got = call(kernel, outs, [pos] + args, smem=smem, scratch=scratch, name=name, space=space, limit=limit, cost=LIGHT if name in EASY else cost)
         last[0] = got[0]
         return got
 
     x1 = hop(x0, PX)
     x2 = hop(x0, 1)
-    s0, e0, c0, qkv0, vecs = step(
+    hbm = dict(space=pl.BlockSpec(memory_space=pltpu.MemorySpace.HBM), cost=LIGHT)
+    s0, e0, c0, qa0, qb0, vecs = step(
         pack_kernel,
-        [sds((264, 512), BF16), sds((392, 512), BF16), sds((1416, 512), BF16), sds((520, 384), BF16), sds((16, 512), F32)],
-        [w_in, w_back, w_out, gate1_w, gate2_w, w_query, w_key, w_value, norm1_gain, norm1_bias, b_out, gate1_b,
-         norm2_gain, norm2_bias, b_back, gate2_b, b_in, b_query, b_value],
+        [sds((296, 512), BF16), sds((256, 512), BF16), sds((1416, 512), BF16), sds((256, 384), BF16),
+         sds((264, 384), BF16), sds((16, 512), F32)],
+        [pltpu.with_memory_space_constraint(w, pltpu.MemorySpace.HBM) for w in
+         (w_in, w_back, w_out, gate1_w, gate2_w, w_query, w_key, w_value, norm1_gain, norm1_bias, b_out, gate1_b,
+          norm2_gain, norm2_bias, b_back, gate2_b, b_in, b_query, b_value)],
         "pack",
-        [pltpu.SemaphoreType.DMA((24,)), pltpu.VMEM((512, 128), BF16)]
-        + [pltpu.VMEM((512,), BF16)] * 9 + [pltpu.VMEM((128,), BF16)] * 2,
-        space=pl.BlockSpec(memory_space=pltpu.MemorySpace.HBM), limit=60 * 1024 * 1024,
-    )
-    qkv1 = hop(qkv0, 1)
+        [pltpu.SemaphoreType.DMA((27,)), pltpu.VMEM((512, 128), BF16)]
+        + [pltpu.VMEM((512,), BF16)] * 9 + [pltpu.VMEM((128,), BF16)] * 2, **hbm,
+    )
+    qkv = [qa0, qb0, hop(qa0, 1), hop(qb0, 1)]
     sy = hop(s0, PX)
-    x3 = hop(x1, 1)
-    e1 = hop(after(e0, x1), PX)
-    c2 = hop(after(c0, qkv1), 1)
-
-    n, qt0, qt1, k, vt, p1, ot1, att1, invl1 = step(
+    c2 = hop(c0, 1)
+    na, qt0, ka, vta = step(
+        chip_kernel,
+        [sds((512, 512), BF16), sds((256, 256), BF16), sds((512, 256), BF16), sds((256, 512), BF16)],
+        [x0, x2, vecs] + qkv, "chip", cost=LIGHT,
+    )
+    x3 = hop(after(x1, na), 1)
+    e1 = hop(after(e0, x3), PX)
+    n, qt1, k, vt, p1, ot1, att1, invl1 = step(
         first_kernel,
         [
-            sds((1024, 512), BF16), sds((256, 256), BF16), sds((256, 256), BF16), sds((1024, 256), BF16),
+            sds((1024, 512), BF16), sds((256, 256), BF16), sds((1024, 256), BF16),
             sds((256, 1024), BF16), sds((4, 1024, 256), BF16), sds((256, 256), BF16), sds((256, 256), BF16),
             sds((4, 8, 256), F32),
         ],
-        [seg, seg, x0, x1, x2, x3, vecs, qkv0, qkv1],
+        [seg, seg, x1, x3, vecs] + qkv + [na, ka, vta],
         "first", ATT_SCRATCH, 2,
     )
     attp = hop(att1, PX)
     sy = after(sy, att1)
     sx = dhop(sy, 1)
     sz = dhop(sy, 2)
-    e3 = hop(after(e1, att1), 1)
     p0, ot0, att0, invl0 = step(
         second_kernel,
         [sds((4, 1024, 256), BF16), sds((256, 256), BF16), sds((256, 256), BF16), sds((4, 8, 256), F32)],
         [seg, seg, qt0, k, vt],
         "second", ATT_SCRATCH, 2,
     )
-    v, kt = step(prepare_kernel, [sds((1024, 256), BF16), sds((256, 1024), BF16)], [n, k, qkv0, qkv1], "prepare")
+    e3 = hop(after(e1, att0), 1)
+    v, kt = step(prepare_kernel, [sds((1024, 256), BF16), sds((256, 1024), BF16)], [n, k] + qkv, "prepare")
+    cut_a, cut_b = step(cut_kernel, [sds((128, 512), BF16), sds((168, 512), BF16)], [sx, sz], "cut")
+    sxz_a, sxz_b = dhop(cut_a, 1), dhop(cut_b, 2)
     n2, mid, branch, gate = step(
         out_kernel,
         [sds((256, 512), BF16), sds((256, 512), F32), sds((256, 512), F32), sds((256, 512), F32)],
@@ -687,20 +776,19 @@
         "out", [pltpu.VMEM((512, 512), BF16)],
     )
     n2p = hop(n2, PX)
-    sxz = dhop(after(sz, n2), 1)
-    total0, hid, slope0 = step(
+    quarters = [sy, hop(sy, 1), sx, hop(sx, 1), sz, hop(sz, 1)]
+    total0, hid, slope0, slope1 = step(
         ffn_first_kernel,
-        [sds((256, 512), F32), sds((256, 1024), BF16), sds((256, 1024), BF16)],
-        [n2, vecs, w_in, w_back, c2],
-        "ffn_first",
-    )
-    quarters = [sy, hop(sy, 1), sx, hop(sx, 1), sz, hop(sz, 1)]
-    sxz = after(sxz, total0)
-    quarters = quarters + [sxz, hop(sxz, 1)]
-    result, fg, ltg, slope1 = step(
+        [sds((256, 512), F32), sds((256, 1024), BF16), sds((256, 1024), BF16), sds((256, 768), BF16)],
+        [n2, vecs, w_in, w_back, c2] + quarters,
+        "ffn_first", cost=LIGHT,
+    )
+    sxz_a, sxz_b = lax.optimization_barrier((sxz_a, sxz_b, total0))[0:2]
+    quarters = quarters + [sxz_a, hop(sxz_a, 1), sxz_b, hop(sxz_b, 1)]
+    result, fg, ltg, slope2 = step(
         ffn_kernel,
-        [sds((256, 512), BF16), sds((256, 512), BF16), sds((256, 512), BF16), sds((256, 1024), BF16)],
-        [n2, mid, cotangent, vecs, e0, e1, c2, e3, total0] + quarters,
+        [sds((256, 512), BF16), sds((256, 512), BF16), sds((256, 512), BF16), sds((256, 256), BF16)],
+        [n2, mid, cotangent, vecs, gate2_w, c2, total0] + quarters,
         "ffn", [pltpu.VMEM((512, 512), BF16)],
     )
     fgp = hop(fg, PX)
@@ -710,10 +798,18 @@
             sds((256, 256), BF16), sds((256, 256), BF16), sds((256, 512), F32), sds((256, 512), BF16),
             sds((256, 512), BF16), sds((256, 1024), BF16), sds((8, 512), F32),
         ],
-        [fg, ltg, slope0, slope1, mid, branch, gate, cotangent, vecs, e0, e1, c2, e3, w_in, w_back] + quarters,
+        [fg, ltg, slope0, slope1, slope2, mid, branch, gate, cotangent, vecs, e0, e1, c2, e3, gate2_w, w_in, w_back]
+        + quarters,
         "back", [pltpu.VMEM((512, 512), BF16)],
     )
     dot1 = hop(dotp, PX)
+    skeep, ssend = step(
+        small_weight_kernel,
+        [sds((776, 512), F32), sds((776, 512), BF16)],
+        [n, n2, ltg, log, att0, attp, bg, sums],
+        "small_weight", [pltpu.VMEM((512, 512), F32), pltpu.VMEM((512, 512), F32)],
+    )
+    srecv = hop(ssend, 1)
     back_scratch = [
         pltpu.VMEM((256, 256), F32), pltpu.VMEM((4, 128, 256), BF16), pltpu.VMEM((256, 256), BF16),
         pltpu.VMEM((4, 8, 256), F32),
@@ -724,6 +820,8 @@
         [seg, p0, dot0, ot0, invl0, qt0, kt, v],
         "attn_back0", back_scratch, 2,
     )
+    (spar,) = step(half_rows_kernel, [sds((392, 512), BF16)], [skeep, srecv], "half_rows")
+    sparr = hop(spar, PX)
     bkeep, bsend, slopep = step(
         ffn_back_weight_kernel,
         [sds((512, 512), F32), sds((512, 512), BF16), sds((256, 1024), BF16)],
@@ -738,16 +836,9 @@
         "ffn_in_weight",
     )
     irecv = hop(isend, 1)
-    skeep, ssend = step(
-        small_weight_kernel,
-        [sds((776, 512), F32), sds((776, 512), BF16)],
-        [n, n2, ltg, log, att0, attp, bg, sums],
-        "small_weight", [pltpu.VMEM((512, 512), F32), pltpu.VMEM((512, 512), F32)], then=(dot1,),
-    )
-    srecv = hop(ssend, 1)
     bits = n_dp.bit_length() - 1
 
-    def halves(parts1, parts2, rows):
+    def halves(tag, parts1, parts2, rows):
         arrays = [a for parts in (parts1, parts2) for _, group in parts for a, _ in group]
         static = tuple(
             tuple((m, tuple(start for _, start in group)) for m, group in parts) for parts in (parts1, parts2)
@@ -755,69 +846,67 @@
         shapes = [sds((rows // 2, 512), F32), sds((rows // 2, 512), BF16)] * 2
         o1, s1, o2, s2 = step(
             functools.partial(halves_kernel, parts=static, rows=rows, bits=(0, 1)),
-            shapes, arrays, "halves", [pltpu.VMEM((rows, 512), F32)],
+            shapes, arrays, "halves_" + tag, [pltpu.VMEM((rows, 512), F32)],
         )
         return o1, dhop(s1, 1), o2, dhop(s2, 2)
 
-    def quarter_step(o1, r1, o2, r2):
+    def quarter_step(tag, o1, r1, o2, r2):
         rows = o1.shape[0]
         shapes = [sds((rows // 2, 512), F32), sds((rows // 2, 512), BF16)] * 2
         o1, s1, o2, s2 = step(
             functools.partial(halves_kernel, parts=(((rows, (0, 0)),),) * 2, rows=rows, bits=(1, 0)),
-            shapes, [o1, r1, o2, r2], "quarters", [pltpu.VMEM((rows, 512), F32)],
+            shapes, [o1, r1, o2, r2], "quarters_" + tag, [pltpu.VMEM((rows, 512), F32)],
         )
         return o1, dhop(s1, 2), o2, dhop(s2, 1)
 
-    def merge_step(o1, r1, o2, r2):
+    def merge_step(tag, o1, r1, o2, r2, small):
         rows = o1.shape[0]
-        own, sent = step(
-            functools.partial(merge_kernel, bit=2), [sds((rows, 512), F32), sds((rows, 512), BF16)],
-            [o1, r1, o2, r2], "merge", [pltpu.VMEM((rows, 512), F32)],
-        )
-        pair = own, dhop(sent, 4)
-        for b in range(3, bits):
-            rows = rows // 2
+        pairs = [o1, r1, o2, r2]
+        for b in range(2, bits - 1):
+            kernel = merge_kernel if b == 2 else both_kernel
             own, sent = step(
-                functools.partial(both_kernel, bit=b), [sds((rows, 512), F32), sds((rows, 512), BF16)],
-                list(pair), "both", [pltpu.VMEM((2 * rows, 512), F32)],
+                functools.partial(kernel, bit=b), [sds((rows, 512), F32), sds((rows, 512), BF16)],
+                pairs, "cut_" + tag, [pltpu.VMEM((rows if b == 2 else 2 * rows, 512), F32)],
             )
-            pair = own, dhop(sent, 1 << b)
-        return pair
-
-    def fold_step(own, recv, small):
-        rows = own.shape[0]
+            pairs, rows = [own, dhop(sent, 1 << b)], rows // 2
         static = tuple((f, m, tuple(start for _, start in group)) for f, m, group in small)
         arrays = [a for _, _, group in small for a, _ in group]
-        held = step(
-            functools.partial(fold_kernel, small=static), [sds((rows + 8, 512), BF16)], [own, recv] + arrays, "fold"
-        )[0][None]
-        for b in range(bits - 1, 2, -1):
-            shape = (2 * held.shape[0],) + held.shape[1:]
-            held = step(stack_kernel, [sds(shape, BF16)], [held, dhop(held, 1 << b)], "stack")[0]
-        return held, dhop(held, 4)
-
-    def part_step(held, recv):
-        size, rows = 2 * held.shape[0], (held.shape[1] - 8) // 2
-        h1, h2 = step(part_kernel, [sds((size, rows + 8, 512), BF16), sds((size, rows, 512), BF16)], [held, recv], "part")
+        own = step(
+            functools.partial(round_kernel, count=len(pairs), small=static), [sds((2 * rows + 8, 512), BF16)],
+            pairs + arrays, "merge_" + tag,
+        )[0]
+        return own, dhop(own, 1 << (bits - 1))
+
+    def part_step(tag, own, recv):
+        rows = (own.shape[0] - 8) // 2
+        if bits > 3:
+            held = step(settle_kernel, [sds(own.shape, BF16)], [own, recv], "settle")[0][None]
+            for b in range(bits - 2, 2, -1):
+                shape = (2 * held.shape[0],) + held.shape[1:]
+                held = step(stack_kernel, [sds(shape, BF16)], [held, dhop(held, 1 << b)], "stack")[0]
+            size = 2 * held.shape[0]
+            kernel, args = part_kernel, [held, dhop(held, 4)]
+        else:
+            size, kernel, args = 1, settle_part_kernel, [own, recv]
+        h1, h2 = step(kernel, [sds((size, rows + 8, 512), BF16), sds((size, rows, 512), BF16)], args, "part_" + tag)
         return h1, dhop(h1, 2), h2, dhop(h2, 1)
 
-    def pair_step(h1, r1, h2, r2):
+    def pair_step(tag, h1, r1, h2, r2):
         shapes = [sds((2 * h.shape[0],) + h.shape[1:], BF16) for h in (h1, h2)]
-        h1, h2 = step(pair_kernel, shapes, [h1, r1, h2, r2], "pair")
+        h1, h2 = step(pair_kernel, shapes, [h1, r1, h2, r2], "pair_" + tag)
         return h1, dhop(h1, 1), h2, dhop(h2, 2)
 
-    def unpack_step(h1, r1, h2, r2, plans):
+    def unpack_step(tag, h1, r1, h2, r2, plans, small):
         shapes = [sds((512, size) if flip else (size, 512), F32) for plan in plans for _, size, flip in plan]
-        rest = tuple(range(2, bits))
+        rest = tuple(range(2, bits - 1))
         rows = 2 * h2.shape[0] * h2.shape[1]
         return step(
-            functools.partial(unpack_kernel, plans=plans, orders=((0, 1) + rest, (1, 0) + rest)),
-            shapes + [sds((8, 512), F32)], [h1, r1, h2, r2], "unpack", [pltpu.VMEM((rows, 512), F32)],
+            functools.partial(unpack_kernel, plans=plans, orders=((0, 1) + rest, (1, 0) + rest), small=small),
+            shapes + [sds((size,), F32) for _, _, size in small], [h1, r1, h2, r2], "unpack_" + tag,
+            [pltpu.VMEM((rows, 512), F32), pltpu.VMEM((8, 512), F32)],
         )
 
-    f = halves([(512, [(bkeep, 0), (brecv, 0)])], [(512, [(ikeep, 0), (irecv, 0)])], padded(512, n_dp))
-    (spar,) = step(half_rows_kernel, [sds((392, 512), BF16)], [skeep, srecv], "half_rows")
-    sparr = hop(spar, PX)
+    f = halves("f", [(512, [(bkeep, 0), (brecv, 0)])], [(512, [(ikeep, 0), (irecv, 0)])], padded(512, n_dp))
 
     dqt, dkt, dvt, akeep, asend = step(
         back_second_kernel,
@@ -832,18 +921,19 @@
     gown, gpar, gsend = step(
         input_kernel,
         [sds((512, 256), F32), sds((512, 256), F32), sds((512, 512), BF16)],
-        [dqt, dkt, dvt, qkv0, qkv1],
+        [dqt, dkt, dvt] + qkv,
         "input_grad",
     )
     gsib = hop(gsend, 1)
-    f = quarter_step(*f)
+    f = quarter_step("f", *f)
     a = halves(
-        [(384, [(akeep, 0), (arecv, 0)])], [(384, [(skeep, 0), (srecv, 0), (sparr, 0)])], padded(384, n_dp)
+        "a", [(384, [(akeep, 0), (arecv, 0)])], [(384, [(skeep, 0), (srecv, 0), (sparr, 0)])], padded(384, n_dp)
     )
     (gsum,) = step(half_columns_kernel, [sds((512, 256), BF16)], [gpar, gsib], "half_columns")
     gp = hop(gsum, PX)
-    f = merge_step(*f)
-    a = quarter_step(*a)
+    tail = [(skeep, 773), (srecv, 773), (sparr, 389)]
+    f = merge_step("f", *f, [(0, 1, [(ikeep, 512), (irecv, 512)]), (1, 1, tail)])
+    a = quarter_step("a", *a)
     input_grad, sums1 = step(
         last_kernel,
         [sds((256, 512), F32), sds((8, 512), F32)],
@@ -852,48 +942,31 @@
     )
     sums1_b = hop(sums1, PX)
     sums1_a = hop(sums1, 1)
-    tail = [(skeep, 773), (srecv, 773), (sparr, 389)]
-    f = fold_step(*f, [(0, 1, [(ikeep, 512), (irecv, 512)]), (1, 1, tail)])
-    a = merge_step(*a)
-    sums1_c = hop(after(sums1_b, a[0]), 1)
-    f = part_step(*f)
+    sums1_c = hop(sums1, PX ^ 1)
+    f = part_step("f", *f)
     group = [(skeep, 768), (srecv, 768), (sparr, 384)]
-    a = fold_step(
-        *a,
+    a = merge_step(
+        "a", *a,
         [(0, 2, [(sums1, 0), (sums1_a, 0), (sums1_b, 0), (sums1_c, 0)]), (2, 1, [(akeep, 384), (arecv, 384)]),
          (3, 5, group)],
     )
-    f = pair_step(*f)
-    a = part_step(*a)
-    g_wback, g_win, f_small = unpack_step(*f, (((0, 512, False),), ((0, 512, False),)))
-    a = pair_step(*a)
+    f = pair_step("f", *f)
+    a = part_step("a", *a)
+    a = pair_step("a", *a)
+    g_wback, g_win, d_b_in, d_n2b = unpack_step(
+        "f", *f, (((0, 512, False),), ((0, 512, False),)), ((0, 0, 512), (1, 0, 512))
+    )
     plans = (
         ((0, 128, True), (128, 128, True), (256, 128, True)),
         ((0, 128, False), (128, 128, False), (256, 128, False)),
     )
-    g_q, g_k, g_v, g_g2, g_g1, g_wo, a_small = unpack_step(*a, plans)
+    small = ((0, 0, 512), (1, 0, 512), (2, 0, 128), (2, 128, 128)) + tuple((i, 0, 512) for i in range(3, 8))
+    g_q, g_k, g_v, g_g2, g_g1, g_wo, d_n1g, d_n1b, d_bq, d_bv, d_b_back, d_g2b, d_b_out, d_g1b, d_n2g = unpack_step(
+        "a", *a, plans, small
+    )
     return (
-        result,
-        input_grad,
-        a_small[0],
-        a_small[1],
-        g_q,
-        a_small[2, 0:128],
-        g_k,
-        g_v,
-        a_small[2, 128:256],
-        g_wo,
-        a_small[5],
-        g_g1,
-        a_small[6],
-        a_small[7],
-        f_small[1],
-        g_win,
-        f_small[0],
-        g_wback,
-        a_small[3],
-        g_g2,
-        a_small[4],
+        result, input_grad, d_n1g, d_n1b, g_q, d_bq, g_k, g_v, d_bv, g_wo, d_b_out, g_g1, d_g1b, d_n2g, d_n2b,
+        g_win, d_b_in, g_wback, d_b_back, g_g2, d_g2b,
     )
 
 

time: 137 us -> 125 us (0.912)
  starting transfers between devices: 47.1 us -> 43.1 us
  local copies, waits for them, and re-layouts: 3.5 us -> 0.03 us
  waiting for transfers between devices: 33.4 us -> 30.1 us
    ppermute x23 -> x22, waiting for transfers between devices: 26.2 us -> 19.1 us  [dhop(): return lax.ppermute(value, 'dp', [(i, i ^ mask) for i in range(n_dp)])]
    ppermute x23 -> x22, starting transfers between devices: 30.6 us -> 26.5 us  [dhop(): return lax.ppermute(value, 'dp', [(i, i ^ mask) for i in range(n_dp)])]
    ppermute x26 -> x28, waiting for transfers between devices: 7.21 us -> 11 us  [hop(): return lax.ppermute(value, 'tensor', [(i, i ^ mask) for i in range(4)])]
    unnamed x20 -> x12, local copies, waits for them, and re-layouts: 1.79 us -> 0.03 us
    ppermute x26 -> x28, starting transfers between devices: 16.5 us -> 16.7 us  [hop(): return lax.ppermute(value, 'tensor', [(i, i ^ mask) for i in range(4)])]
  transfers between devices with their start and end apart: 49 -> 50, of which waited for: 16 -> 18; matrix products, arithmetic and copies ran while one was open for 1% -> 1% of each run, Pallas kernels for 35% -> 35%
where the time goes in v4:
time: 125 us
  Pallas kernels  49.5 us (40%)
  starting transfers between devices  43.1 us (34%)
  waiting for transfers between devices  30.1 us (24%)
    pallas_call x31, Pallas kernels, call(): pl.pallas_call(body, out_shape=tuple(outs), in_specs=[SM] * smem + [space...  49.5 us
    ppermute x22, starting transfers between devices, dhop(): return lax.ppermute(value, 'dp', [(i, i ^ mask) for i in range(n_dp)])  26.5 us
    ppermute x22, waiting for transfers between devices, dhop(): return lax.ppermute(value, 'dp', [(i, i ^ mask) for i in range(n_dp)])  19.1 us
    ppermute x28, starting transfers between devices, hop(): return lax.ppermute(value, 'tensor', [(i, i ^ mask) for i in range(4)])  16.7 us
    ppermute x28, waiting for transfers between devices, hop(): return lax.ppermute(value, 'tensor', [(i, i ^ mask) for i in range(4)])  11 us
  transfers between devices with their start and end apart: 50, of which 18 were waited for; matrix products, arithmetic and copies ran while one was open for 1% of the time, Pallas kernels for 35%

profile of v4, /device:TPU:0, one launch (start us, length us, event | category | flops | bytes accessed | tf_op | source)
XLA Modules:
  0.0 124.6 jit_solution(13229069698784212781)
XLA Ops:
  0.7 3.0 %collective-permute-start.3 = (bf16[256,512]{1,0:T(8,128)(2,1)}, bf16[256,512]{1,0:T(8,128)(2,1)S(1)}, u32[]{:S(2)}, u32[]{:S(2)}) collective-permute-start(bf16[256,512]{1,0:T(8,128)(2,1)} %x0.5), channel_id=1, source_target_pairs={{0,2},{1,3},{2,0},{3,1},{4,6},{5,7},{6,4},{7,5},{8,10},{9,11},{10,... | collective-permute-start | bytes 786440 | tf_op jit(solution)/shard_map/ppermute | solution.py:703
  3.7 0.7 compare_select_fusion.pos.tb
  4.4 2.5 %pack.1 = (bf16[296,512]{1,0:T(8,128)(2,1)S(1)}, bf16[256,512]{1,0:T(8,128)(2,1)S(1)}, bf16[1416,512]{1,0:T(8,128)(2,1)S(1)}, bf16[256,384]{1,0:T(8,128)(2,1)S(1...) custom-call(s32[8]{0:T(128)S(1)} %compare_select_fusion.pos.tb, bf16[512,512]{1,0:T(8,128)(2,1)} %win0.5, ...), custom_call_target="tpu_custom_call" | custom-call | tf_op jit(solution)/shard_map/pack/pallas_call | solution.py:44
  7.6 1.4 %collective-permute-done.1.qa1 = bf16[256,384]{1,0:T(8,128)(2,1)S(1)} collective-permute-done((bf16[256,384]{1,0:T(8,128)(2,1)S(1)}, bf16[256,384]{1,0:T(8,128)(2,1)S(1)}, u32[]{:S(2)}, u32[]{:S(2)}) %collective-permute-start.1) | collective-permute-done | bytes 196640 | tf_op jit(solution)/shard_map/ppermute | solution.py:703
  8.9 1.8 %chip.1 = (bf16[512,512]{1,0:T(8,128)(2,1)S(1)}, bf16[256,256]{1,0:T(8,128)(2,1)S(1)}, bf16[512,256]{1,0:T(8,128)(2,1)S(1)}, bf16[256,512]{1,0:T(8,128)(2,1)S(1)}) custom-call(s32[8]{0:T(128)S(1)} %compare_select_fusion.pos.tb, bf16[256,512]{1,0:T(8,128)(2,1)S(1)} %copy-done.2, bf16[256,512]{1,0:T(8,128)(2,1)S(1)} %collective-permute-done.x2, ...), custom_call_target="tpu_custom_call" | custom-call | tf_op jit(solution)/shard_map/chip/pallas_call | solution.py:44
  11.1 0.9 collective-permute-start.5
  12.4 4.1 %first.1 = (bf16[1024,512]{1,0:T(8,128)(2,1)S(1)}, bf16[256,256]{1,0:T(8,128)(2,1)S(1)}, bf16[1024,256]{1,0:T(8,128)(2,1)S(1)}, bf16[256,1024]{1,0:T(8,128)(2,1)...) custom-call(s32[8]{0:T(128)S(1)} %compare_select_fusion.pos.tb, ...), custom_call_target="tpu_custom_call" | custom-call | flops 10000000000 | tf_op jit(solution)/shard_map/first/pallas_call | solution.py:44
  16.6 4.1 %collective-permute-done.5.s0 = bf16[296,512]{1,0:T(8,128)(2,1)S(1)} collective-permute-done((bf16[296,512]{1,0:T(8,128)(2,1)S(1)}, bf16[296,512]{1,0:T(8,128)(2,1)S(1)}, u32[]{:S(2)}, u32[]{:S(2)}) %collective-permute-start.5) | collective-permute-done | bytes 303136 | tf_op jit(solution)/shard_map/ppermute | solution.py:703
  20.7 1.6 %collective-permute-start.7 = (bf16[296,512]{1,0:T(8,128)(2,1)S(1)}, bf16[296,512]{1,0:T(8,128)(2,1)S(1)}, u32[]{:S(2)}, u32[]{:S(2)}) collective-permute-start(bf16[296,512]{1,0:T(8,128)(2,1)S(1)} %collective-permute-done.5.s0), channel_id=1, source_target_pairs={{0,8},{4,12},{8,0},{12,4},{16,24},{20,28},{24,16},{28,20},{1,9},{5... | collective-permute-start | bytes 909320 | tf_op jit(solution)/shard_map/ppermute | solution.py:706
  22.3 1.5 %collective-permute-start.6 = (bf16[296,512]{1,0:T(8,128)(2,1)S(1)}, bf16[296,512]{1,0:T(8,128)(2,1)S(1)}, u32[]{:S(2)}, u32[]{:S(2)}) collective-permute-start(bf16[296,512]{1,0:T(8,128)(2,1)S(1)} %collective-permute-done.5.s0), channel_id=1, source_target_pairs={{0,4},{4,0},{8,12},{12,8},{16,20},{20,16},{24,28},{28,24},{1,5},{5... | collective-permute-start | bytes 909320 | tf_op jit(solution)/shard_map/ppermute | solution.py:706
  23.8 1.2 collective-permute-start.9
  25.0 1.6 %second.1 = (bf16[4,1024,256]{2,1,0:T(8,128)(2,1)S(1)}, bf16[256,256]{1,0:T(8,128)(2,1)S(1)}, bf16[256,256]{1,0:T(8,128)(2,1)S(1)}, f32[4,8,256]{2,1,0:T(8,128)S(1)}) custom-call(s32[8]{0:T(128)S(1)} %compare_select_fusion.pos.tb, s32[1,1024]{1,0:T(1,128)S(1)} %copy-done.5, s32[1,1024]{1,0:T(1,128)S(1)} %copy-done.5, ...), custom_call_target="tpu_custom_call" | custom-call | flops 10000000000 | tf_op jit(solution)/shard_map/second/pallas_call | solution.py:44
  26.7 1.3 %prepare.1 = (bf16[1024,256]{1,0:T(8,128)(2,1)S(1)}, bf16[256,1024]{1,0:T(8,128)(2,1)S(1)}) custom-call(s32[8]{0:T(128)S(1)} %compare_select_fusion.pos.tb, bf16[1024,512]{1,0:T(8,128)(2,1)S(1)} %get-tuple-element.175.n, bf16[1024,256]{1,0:T(8,128)(2,1)S(1)} %get-tuple-element.178.k, bf16[256,384]{1,0:T(8,128)(2,1)S(1)} %get-tuple-element.168.qa0, ...), custom_call_target="tpu_custom_call" | custom-call | flops 10000000000 | tf_op jit(solution)/shard_map/prepare/pallas_call | solution.py:44
  27.9 2.6 %collective-permute-done.9.e1 = bf16[256,512]{1,0:T(8,128)(2,1)S(1)} collective-permute-done((bf16[256,512]{1,0:T(8,128)(2,1)S(1)}, bf16[256,512]{1,0:T(8,128)(2,1)S(1)}, u32[]{:S(2)}, u32[]{:S(2)}) %collective-permute-start.9) | collective-permute-done | bytes 262176 | tf_op jit(solution)/shard_map/ppermute | solution.py:703
  31.6 0.7 collective-permute-start.15
  32.3 0.7 collective-permute-start.16
  33.6 1.4 %out.1 = (bf16[256,512]{1,0:T(8,128)(2,1)S(1)}, f32[256,512]{1,0:T(8,128)S(1)}, f32[256,512]{1,0:T(8,128)S(1)}, f32[256,512]{1,0:T(8,128)S(1)}) custom-call(s32[8]{0:T(128)S(1)} %compare_select_fusion.pos.tb, bf16[256,512]{1,0:T(8,128)(2,1)S(1)} %copy-done.2, bf16[1024,512]{1,0:T(8,128)(2,1)S(1)} %get-tuple-element.175.n, ...), custom_call_target="tpu_custom_call" | custom-call | flops 10000000000 | tf_op jit(solution)/shard_map/out/pallas_call | solution.py:44
  35.1 2.7 %ffn_first.1 = (f32[256,512]{1,0:T(8,128)S(1)}, bf16[256,1024]{1,0:T(8,128)(2,1)S(1)}, bf16[256,1024]{1,0:T(8,128)(2,1)S(1)}, bf16[256,768]{1,0:T(8,128)(2,1)S(1)}) custom-call(s32[8]{0:T(128)S(1)} %compare_select_fusion.pos.tb, bf16[256,512]{1,0:T(8,128)(2,1)S(1)} %get-tuple-element.193.n2, f32[16,512]{1,0:T(8,128)S(1)} %get-tuple-element.167.vecs, ...), custom_call_target="tpu_custom_call" | custom-call | tf_op jit(solution)/shard_map/ffn_first/pallas_call | solution.py:44
  38.8 1.5 %collective-permute-start.20 = (bf16[256,512]{1,0:T(8,128)(2,1)S(1)}, bf16[256,512]{1,0:T(8,128)(2,1)S(1)}, u32[]{:S(2)}, u32[]{:S(2)}) collective-permute-start(bf16[256,512]{1,0:T(8,128)(2,1)S(1)} %get-tuple-element.193.n2), channel_id=1, source_target_pairs={{0,2},{1,3},{2,0},{3,1},{4,6},{5,7},{6,4},{7,5},{8,10},{9,11},{10,... | collective-permute-start | bytes 786440 | tf_op jit(solution)/shard_map/ppermute | solution.py:703
  40.2 2.1 %ffn.1 = (bf16[256,512]{1,0:T(8,128)(2,1)}, bf16[256,512]{1,0:T(8,128)(2,1)S(1)}, bf16[256,512]{1,0:T(8,128)(2,1)S(1)}, bf16[256,256]{1,0:T(8,128)(2,1)S(1)}) custom-call(s32[8]{0:T(128)S(1)} %compare_select_fusion.pos.tb, bf16[256,512]{1,0:T(8,128)(2,1)S(1)} %get-tuple-element.193.n2, f32[256,512]{1,0:T(8,128)S(1)} %get-tuple-element.197.mid, ...), custom_call_target="tpu_custom_call" | custom-call | flops 10000000000 | tf_op jit(solution)/shard_map/ffn/pallas_call | solution.py:44
  42.4 1.1 collective-permute-start.21
  43.5 3.5 %back.1 = (bf16[256,256]{1,0:T(8,128)(2,1)S(1)}, bf16[256,256]{1,0:T(8,128)(2,1)S(1)}, f32[256,512]{1,0:T(8,128)S(1)}, bf16[256,512]{1,0:T(8,128)(2,1)S(1)}, bf1...) custom-call(s32[8]{0:T(128)S(1)} %compare_select_fusion.pos.tb, ...), custom_call_target="tpu_custom_call" | custom-call | flops 10000000000 | tf_op jit(solution)/shard_map/back/pallas_call | solution.py:44
  46.9 1.2 small_weight.1
  48.2 2.1 %attn_back0.1 = (f32[256,1024]{1,0:T(8,128)S(1)}, f32[256,1024]{1,0:T(8,128)S(1)}, bf16[256,256]{1,0:T(8,128)(2,1)S(1)}) custom-call(s32[8]{0:T(128)S(1)} %compare_select_fusion.pos.tb, s32[1,1024]{1,0:T(1,128)S(1)} %copy-done.5, bf16[4,1024,256]{2,1,0:T(8,128)(2,1)S(1)} %get-tuple-element.180.p, bf16[256,256]{1,0:T(8,128)(2,1)S(1)} %get-tuple-element.210.dot, ...), custom_call_target="tpu_custom_call" | custom-call | flops 10000000000 | tf_op jit(solution)/shard_map/attn_back0/pallas_call | solution.py:44
  50.5 0.6 half_rows.1
  51.1 1.5 %collective-permute-done.21.fgp = bf16[256,512]{1,0:T(8,128)(2,1)S(1)} collective-permute-done((bf16[256,512]{1,0:T(8,128)(2,1)S(1)}, bf16[256,512]{1,0:T(8,128)(2,1)S(1)}, u32[]{:S(2)}, u32[]{:S(2)}) %collective-permute-start.21) | collective-permute-done | bytes 262176 | tf_op jit(solution)/shard_map/ppermute | solution.py:703
  52.6 2.3 %ffn_back_weight.1 = (f32[512,512]{1,0:T(8,128)S(1)}, bf16[512,512]{1,0:T(8,128)(2,1)S(1)}, bf16[256,1024]{1,0:T(8,128)(2,1)S(1)}) custom-call(s32[8]{0:T(128)S(1)} %compare_select_fusion.pos.tb, bf16[256,512]{1,0:T(8,128)(2,1)S(1)} %collective-permute-done.20.n2p, bf16[256,512]{1,0:T(8,128)(2,1)S(1)} %get-tuple-element.203.fg, ...), custom_call_target="tpu_custom_call" | custom-call | flops 10000000000 | tf_op jit(solution)/shard_map/ffn_back_weight/pallas_call | solution.py:44
  54.9 1.9 %ffn_in_weight.1 = (f32[520,512]{1,0:T(8,128)S(1)}, bf16[520,512]{1,0:T(8,128)(2,1)S(1)}) custom-call(s32[8]{0:T(128)S(1)} %compare_select_fusion.pos.tb, bf16[256,512]{1,0:T(8,128)(2,1)S(1)} %get-tuple-element.193.n2, bf16[256,512]{1,0:T(8,128)(2,1)S(1)} %collective-permute-done.20.n2p, bf16[256,512]{1,0:T(8,128)(2,1)S(1)} %collective-permute-done.21.fgp, ...), custom_call_target="tpu_custom_call" | custom-call | flops 10000000000 | tf_op jit(solution)/shard_map/ffn_in_weight/pallas_call | solution.py:44
  57.3 2.3 %collective-permute-start.24 = (bf16[256,256]{1,0:T(8,128)(2,1)S(1)}, bf16[256,256]{1,0:T(8,128)(2,1)S(1)}, u32[]{:S(2)}, u32[]{:S(2)}) collective-permute-start(bf16[256,256]{1,0:T(8,128)(2,1)S(1)} %get-tuple-element.236), channel_id=1, source_target_pairs={{0,2},{1,3},{2,0},{3,1},{4,6},{5,7},{6,4},{7,5},{8,10},{9,11},{10,... | collective-permute-start | bytes 393224 | tf_op jit(solution)/shard_map/ppermute | solution.py:703
  59.7 1.0 halves_f.1
  60.7 1.6 %collective-permute-start.25 = (bf16[256,512]{1,0:T(8,128)(2,1)S(1)}, bf16[256,512]{1,0:T(8,128)(2,1)S(1)}, u32[]{:S(2)}, u32[]{:S(2)}) collective-permute-start(bf16[256,512]{1,0:T(8,128)(2,1)S(1)} %get-tuple-element.248), channel_id=1, source_target_pairs={{0,4},{4,0},{8,12},{12,8},{16,20},{20,16},{24,28},{28,24},{1,5},{5... | collective-permute-start | bytes 786440 | tf_op jit(solution)/shard_map/ppermute | solution.py:706
  62.2 0.8 collective-permute-start.26
  63.1 0.9 collective-permute-done.24.dot
  64.0 4.8 %attn_back1.1 = (bf16[256,512]{1,0:T(8,128)(2,1)S(1)}, bf16[256,1024]{1,0:T(8,128)(2,1)S(1)}, bf16[256,1024]{1,0:T(8,128)(2,1)S(1)}, f32[392,512]{1,0:T(8,128)S(1)}, bf16[392,512]{1,0:T(8,128)(2,1)S(1)}) custom-call(s32[8]{0:T(128)S(1)} %compare_select_fusion.pos.tb, s32[1,1024]{1,0:T(1,128)S(1)} %copy-done.5, ...), custom_call_target="tpu_custom_call" | custom-call | flops 10000000000 | tf_op jit(solution)/shard_map/attn_back1/pallas_call | solution.py:44
  68.8 1.4 %input_grad.1 = (f32[512,256]{1,0:T(8,128)S(1)}, f32[512,256]{1,0:T(8,128)S(1)}, bf16[512,512]{1,0:T(8,128)(2,1)S(1)}) custom-call(s32[8]{0:T(128)S(1)} %compare_select_fusion.pos.tb, bf16[256,512]{1,0:T(8,128)(2,1)S(1)} %get-tuple-element.242.dqt, bf16[256,1024]{1,0:T(8,128)(2,1)S(1)} %get-tuple-element.244.dkt, ...), custom_call_target="tpu_custom_call" | custom-call | tf_op jit(solution)/shard_map/input_grad/pallas_call | solution.py:44
  70.1 0.6 collective-permute-start.27
  70.9 0.8 quarters_f.1
  71.6 1.0 collective-permute-start.30
  72.6 1.4 %collective-permute-start.31 = (bf16[128,512]{1,0:T(8,128)(2,1)S(1)}, bf16[128,512]{1,0:T(8,128)(2,1)S(1)}, u32[]{:S(2)}, u32[]{:S(2)}) collective-permute-start(bf16[128,512]{1,0:T(8,128)(2,1)S(1)} %get-tuple-element.262), channel_id=1, source_target_pairs={{0,4},{4,0},{8,12},{12,8},{16,20},{20,16},{24,28},{28,24},{1,5},{5... | collective-permute-start | bytes 393224 | tf_op jit(solution)/shard_map/ppermute | solution.py:706
  74.0 1.0 halves_a.1
  75.0 0.7 collective-permute-start.32
  75.7 1.1 collective-permute-start.33
  76.8 0.6 half_columns.1
  77.4 1.9 %collective-permute-start.34 = (bf16[512,256]{1,0:T(8,128)(2,1)S(1)}, bf16[512,256]{1,0:T(8,128)(2,1)S(1)}, u32[]{:S(2)}, u32[]{:S(2)}) collective-permute-start(bf16[512,256]{1,0:T(8,128)(2,1)S(1)} %half_columns.1), channel_id=1, source_target_pairs={{0,2},{1,3},{2,0},{3,1},{4,6},{5,7},{6,4},{7,5},{8,10},{9,11},{10,... | collective-permute-start | bytes 786440 | tf_op jit(solution)/shard_map/ppermute | solution.py:703
  79.3 0.6 merge_f.1.own
  79.9 2.6 %collective-permute-start.35 = (bf16[264,512]{1,0:T(8,128)(2,1)S(1)}, bf16[264,512]{1,0:T(8,128)(2,1)S(1)}, u32[]{:S(2)}, u32[]{:S(2)}) collective-permute-start(bf16[264,512]{1,0:T(8,128)(2,1)S(1)} %merge_f.1.own), channel_id=1, source_target_pairs={{0,16},{4,20},{8,24},{12,28},{16,0},{20,4},{24,8},{28,12},{1,17},{... | collective-permute-start | bytes 811016 | tf_op jit(solution)/shard_map/ppermute | solution.py:706
  82.6 0.8 collective-permute-done.33.refs_3_
  83.4 0.7 quarters_a.1
  84.3 1.5 %collective-permute-start.37 = (bf16[96,512]{1,0:T(8,128)(2,1)S(1)}, bf16[96,512]{1,0:T(8,128)(2,1)S(1)}, u32[]{:S(2)}, u32[]{:S(2)}) collective-permute-start(bf16[96,512]{1,0:T(8,128)(2,1)S(1)} %get-tuple-element.276), channel_id=1, source_target_pairs={{0,4},{4,0},{8,12},{12,8},{16,20},{20,16},{24,28},{28,24},{1,5},{5... | collective-permute-start | bytes 294920 | tf_op jit(solution)/shard_map/ppermute | solution.py:706
  85.7 2.0 %last.1 = (f32[256,512]{1,0:T(8,128)}, f32[8,512]{1,0:T(8,128)S(1)}) custom-call(s32[8]{0:T(128)S(1)} %compare_select_fusion.pos.tb, f32[512,256]{1,0:T(8,128)S(1)} %get-tuple-element.246.own, bf16[512,512]{1,0:T(8,128)(2,1)S(1)} %collective-permute-done.29.recv.sib, bf16[512,256]{1,0:T(8,128)(2,1)S(1)} %collective-permute-done.34.par, ...), custom_call_target="tpu_custom_call" | custom-call | flops 10000000000 | tf_op jit(solution)/shard_map/last/pallas_call | solution.py:44
  88.3 5.0 %collective-permute-done.35.recv = bf16[264,512]{1,0:T(8,128)(2,1)S(1)} collective-permute-done((bf16[264,512]{1,0:T(8,128)(2,1)S(1)}, bf16[264,512]{1,0:T(8,128)(2,1)S(1)}, u32[]{:S(2)}, u32[]{:S(2)}) %collective-permute-start.35) | collective-permute-done | bytes 270368 | tf_op jit(solution)/shard_map/ppermute | solution.py:706
  93.3 0.6 part_f.1
  94.3 1.5 %collective-permute-start.42 = (bf16[1,128,512]{2,1,0:T(8,128)(2,1)S(1)}, bf16[1,128,512]{2,1,0:T(8,128)(2,1)S(1)}, u32[]{:S(2)}, u32[]{:S(2)}) collective-permute-start(bf16[1,128,512]{2,1,0:T(8,128)(2,1)S(1)} %get-tuple-element.279.held2), channel_id=1, source_target_pairs={{0,4},{4,0},{8,12},{12,8},{16,20},{20,16},{24,28},{28,24},{1,5},{5... | collective-permute-start | bytes 393224 | tf_op jit(solution)/shard_map/ppermute | solution.py:706
  95.8 0.6 merge_a.1.own
  96.4 3.4 %collective-permute-start.43 = (bf16[200,512]{1,0:T(8,128)(2,1)S(1)}, bf16[200,512]{1,0:T(8,128)(2,1)S(1)}, u32[]{:S(2)}, u32[]{:S(2)}) collective-permute-start(bf16[200,512]{1,0:T(8,128)(2,1)S(1)} %merge_a.1.own), channel_id=1, source_target_pairs={{0,16},{4,20},{8,24},{12,28},{16,0},{20,4},{24,8},{28,12},{1,17},{... | collective-permute-start | bytes 614408 | tf_op jit(solution)/shard_map/ppermute | solution.py:706
  100.7 3.3 %collective-permute-start.46 = (bf16[2,136,512]{2,1,0:T(8,128)(2,1)S(1)}, bf16[2,136,512]{2,1,0:T(8,128)(2,1)S(1)}, u32[]{:S(2)}, u32[]{:S(2)}) collective-permute-start(bf16[2,136,512]{2,1,0:T(8,128)(2,1)S(1)} %get-tuple-element.280.held1), channel_id=1, source_target_pairs={{0,4},{4,0},{8,12},{12,8},{16,20},{20,16},{24,28},{28,24},{1,5},{5... | collective-permute-start | bytes 835592 | tf_op jit(solution)/shard_map/ppermute | solution.py:706
  104.0 5.6 %collective-permute-done.43.recv = bf16[200,512]{1,0:T(8,128)(2,1)S(1)} collective-permute-done((bf16[200,512]{1,0:T(8,128)(2,1)S(1)}, bf16[200,512]{1,0:T(8,128)(2,1)S(1)}, u32[]{:S(2)}, u32[]{:S(2)}) %collective-permute-start.43) | collective-permute-done | bytes 204832 | tf_op jit(solution)/shard_map/ppermute | solution.py:706
  110.2 0.7 collective-permute-start.45
  110.8 4.0 %collective-permute-done.45.recv2 = bf16[1,96,512]{2,1,0:T(8,128)(2,1)S(1)} collective-permute-done((bf16[1,96,512]{2,1,0:T(8,128)(2,1)S(1)}, bf16[1,96,512]{2,1,0:T(8,128)(2,1)S(1)}, u32[]{:S(2)}, u32[]{:S(2)}) %collective-permute-start.45) | collective-permute-done | bytes 98336 | tf_op jit(solution)/shard_map/ppermute | solution.py:706
  114.9 0.7 collective-permute-done.44.recv1
  116.2 1.8 %collective-permute-start.49 = (bf16[2,96,512]{2,1,0:T(8,128)(2,1)S(1)}, bf16[2,96,512]{2,1,0:T(8,128)(2,1)S(1)}, u32[]{:S(2)}, u32[]{:S(2)}) collective-permute-start(bf16[2,96,512]{2,1,0:T(8,128)(2,1)S(1)} %get-tuple-element.290.held2), channel_id=1, source_target_pairs={{0,8},{4,12},{8,0},{12,4},{16,24},{20,28},{24,16},{28,20},{1,9},{5... | collective-permute-start | bytes 589832 | tf_op jit(solution)/shard_map/ppermute | solution.py:706
  118.1 2.1 %unpack_f.1 = (f32[512,512]{1,0:T(8,128)}, f32[512,512]{1,0:T(8,128)}, f32[512]{0:T(512)}, f32[512]{0:T(512)}) custom-call(s32[8]{0:T(128)S(1)} %compare_select_fusion.pos.tb, bf16[2,136,512]{2,1,0:T(8,128)(2,1)S(1)} %get-tuple-element.280.held1, bf16[2,136,512]{2,1,0:T(8,128)(2,1)S(1)} %collective-permute-done.46.recv1, ...), custom_call_target="tpu_custom_call" | custom-call | flops 10000000000 | tf_op jit(solution)/shard_map/unpack_f/pallas_call | solution.py:44
  120.2 2.0 %collective-permute-done.49.recv2 = bf16[2,96,512]{2,1,0:T(8,128)(2,1)S(1)} collective-permute-done((bf16[2,96,512]{2,1,0:T(8,128)(2,1)S(1)}, bf16[2,96,512]{2,1,0:T(8,128)(2,1)S(1)}, u32[]{:S(2)}, u32[]{:S(2)}) %collective-permute-start.49) | collective-permute-done | bytes 196640 | tf_op jit(solution)/shard_map/ppermute | solution.py:706
  122.4 2.0 %unpack_a.1 = (f32[512,128]{1,0:T(8,128)}, f32[512,128]{1,0:T(8,128)}, f32[512,128]{1,0:T(8,128)}, f32[128,512]{1,0:T(8,128)}, f32[128,512]{1,0:T(8,128)}, /*ind...) custom-call(s32[8]{0:T(128)S(1)} %compare_select_fusion.pos.tb, ...), custom_call_target="tpu_custom_call" | custom-call | flops 10000000000 | tf_op jit(solution)/shard_map/unpack_a/pallas_call | solution.py:44
  (80 shorter events, 8.6 us)
Async XLA Ops:
  0.7 8.3 %copy-start.2 = (bf16[256,512]{1,0:T(8,128)(2,1)S(1)}, bf16[256,512]{1,0:T(8,128)(2,1)}, u32[]{:S(2)}) copy-start(bf16[256,512]{1,0:T(8,128)(2,1)} %x0.5) | copy-start | bytes 786436
  0.7 10.1 %collective-permute-start.3 = (bf16[256,512]{1,0:T(8,128)(2,1)}, bf16[256,512]{1,0:T(8,128)(2,1)S(1)}, u32[]{:S(2)}, u32[]{:S(2)}) collective-permute-start(bf16[256,512]{1,0:T(8,128)(2,1)} %x0.5), channel_id=1, source_target_pairs={{0,2},{1,3},{2,0},{3,1},{4,6},{5,7},{6,4},{7,5},{8,10},{9,11},{10,... | collective-permute-start | bytes 786440 | tf_op jit(solution)/shard_map/ppermute | solution.py:703
  3.7 5.2 %collective-permute-start = (bf16[256,512]{1,0:T(8,128)(2,1)}, bf16[256,512]{1,0:T(8,128)(2,1)S(1)}, u32[]{:S(2)}, u32[]{:S(2)}) collective-permute-start(bf16[256,512]{1,0:T(8,128)(2,1)} %x0.5), channel_id=1, source_target_pairs={{0,1},{1,0},{2,3},{3,2},{4,5},{5,4},{6,7},{7,6},{8,9},{9,8},{10,11... | collective-permute-start | bytes 786440 | tf_op jit(solution)/shard_map/ppermute | solution.py:703
  4.4 8.0 %copy-start.5 = (s32[1,1024]{1,0:T(1,128)S(1)}, s32[1,1024]{1,0:T(1,128)}, u32[]{:S(2)}) copy-start(s32[1,1024]{1,0:T(1,128)} %segs.7) | copy-start | bytes 12292
  6.9 2.0 %collective-permute-start.2 = (bf16[264,384]{1,0:T(8,128)(2,1)S(1)}, bf16[264,384]{1,0:T(8,128)(2,1)S(1)}, u32[]{:S(2)}, u32[]{:S(2)}) collective-permute-start(bf16[264,384]{1,0:T(8,128)(2,1)S(1)} %get-tuple-element.169.qb0), channel_id=1, source_target_pairs={{0,1},{1,0},{2,3},{3,2},{4,5},{5,4},{6,7},{7,6},{8,9},{9,8},{10,11... | collective-permute-start | bytes 608264 | tf_op jit(solution)/shard_map/ppermute | solution.py:703
  7.5 1.4 %collective-permute-start.1 = (bf16[256,384]{1,0:T(8,128)(2,1)S(1)}, bf16[256,384]{1,0:T(8,128)(2,1)S(1)}, u32[]{:S(2)}, u32[]{:S(2)}) collective-permute-start(bf16[256,384]{1,0:T(8,128)(2,1)S(1)} %get-tuple-element.168.qa0), channel_id=1, source_target_pairs={{0,1},{1,0},{2,3},{3,2},{4,5},{5,4},{6,7},{7,6},{8,9},{9,8},{10,11... | collective-permute-start | bytes 589832 | tf_op jit(solution)/shard_map/ppermute | solution.py:703
  10.8 1.6 %collective-permute-start.4 = (bf16[256,512]{1,0:T(8,128)(2,1)S(1)}, bf16[256,512]{1,0:T(8,128)(2,1)S(1)}, u32[]{:S(2)}, u32[]{:S(2)}) collective-permute-start(bf16[256,512]{1,0:T(8,128)(2,1)S(1)} %collective-permute-done.3.x1), channel_id=1, source_target_pairs={{0,1},{1,0},{2,3},{3,2},{4,5},{5,4},{6,7},{7,6},{8,9},{9,8},{10,11... | collective-permute-start | bytes 786440 | tf_op jit(solution)/shard_map/ppermute | solution.py:703
  11.1 9.6 %collective-permute-start.5 = (bf16[296,512]{1,0:T(8,128)(2,1)S(1)}, bf16[296,512]{1,0:T(8,128)(2,1)S(1)}, u32[]{:S(2)}, u32[]{:S(2)}) collective-permute-start(bf16[296,512]{1,0:T(8,128)(2,1)S(1)} %get-tuple-element.165), channel_id=1, source_target_pairs={{0,2},{1,3},{2,0},{3,1},{4,6},{5,7},{6,4},{7,5},{8,10},{9,11},{10,... | collective-permute-start | bytes 909320 | tf_op jit(solution)/shard_map/ppermute | solution.py:703
  12.0 21.1 %collective-permute-start.10 = (bf16[1416,512]{1,0:T(8,128)(2,1)S(1)}, bf16[1416,512]{1,0:T(8,128)(2,1)S(1)}, u32[]{:S(2)}, u32[]{:S(2)}) collective-permute-start(bf16[1416,512]{1,0:T(8,128)(2,1)S(1)} %get-tuple-element.191), channel_id=1, source_target_pairs={{0,1},{1,0},{2,3},{3,2},{4,5},{5,4},{6,7},{7,6},{8,9},{9,8},{10,11... | collective-permute-start | bytes 4349960 | tf_op jit(solution)/shard_map/ppermute | solution.py:703
  16.5 15.8 %collective-permute-start.8 = (bf16[256,256]{1,0:T(8,128)(2,1)S(1)}, bf16[256,256]{1,0:T(8,128)(2,1)S(1)}, u32[]{:S(2)}, u32[]{:S(2)}) collective-permute-start(bf16[256,256]{1,0:T(8,128)(2,1)S(1)} %get-tuple-element.184), channel_id=1, source_target_pairs={{0,2},{1,3},{2,0},{3,1},{4,6},{5,7},{6,4},{7,5},{8,10},{9,11},{10,... | collective-permute-start | bytes 393224 | tf_op jit(solution)/shard_map/ppermute | solution.py:703
  20.7 9.8 %collective-permute-start.7 = (bf16[296,512]{1,0:T(8,128)(2,1)S(1)}, bf16[296,512]{1,0:T(8,128)(2,1)S(1)}, u32[]{:S(2)}, u32[]{:S(2)}) collective-permute-start(bf16[296,512]{1,0:T(8,128)(2,1)S(1)} %collective-permute-done.5.s0), channel_id=1, source_target_pairs={{0,8},{4,12},{8,0},{12,4},{16,24},{20,28},{24,16},{28,20},{1,9},{5... | collective-permute-start | bytes 909320 | tf_op jit(solution)/shard_map/ppermute | solution.py:706
  22.3 8.8 %collective-permute-start.6 = (bf16[296,512]{1,0:T(8,128)(2,1)S(1)}, bf16[296,512]{1,0:T(8,128)(2,1)S(1)}, u32[]{:S(2)}, u32[]{:S(2)}) collective-permute-start(bf16[296,512]{1,0:T(8,128)(2,1)S(1)} %collective-permute-done.5.s0), channel_id=1, source_target_pairs={{0,4},{4,0},{8,12},{12,8},{16,20},{20,16},{24,28},{28,24},{1,5},{5... | collective-permute-start | bytes 909320 | tf_op jit(solution)/shard_map/ppermute | solution.py:706
  23.8 6.8 %collective-permute-start.9 = (bf16[256,512]{1,0:T(8,128)(2,1)S(1)}, bf16[256,512]{1,0:T(8,128)(2,1)S(1)}, u32[]{:S(2)}, u32[]{:S(2)}) collective-permute-start(bf16[256,512]{1,0:T(8,128)(2,1)S(1)} %get-tuple-element.190.e0), channel_id=1, source_target_pairs={{0,2},{1,3},{2,0},{3,1},{4,6},{5,7},{6,4},{7,5},{8,10},{9,11},{10,... | collective-permute-start | bytes 786440 | tf_op jit(solution)/shard_map/ppermute | solution.py:703
  30.5 4.5 %collective-permute-start.12 = (bf16[296,512]{1,0:T(8,128)(2,1)S(1)}, bf16[296,512]{1,0:T(8,128)(2,1)S(1)}, u32[]{:S(2)}, u32[]{:S(2)}) collective-permute-start(bf16[296,512]{1,0:T(8,128)(2,1)S(1)} %collective-permute-done.5.s0), channel_id=1, source_target_pairs={{0,1},{1,0},{2,3},{3,2},{4,5},{5,4},{6,7},{7,6},{8,9},{9,8},{10,11... | collective-permute-start | bytes 909320 | tf_op jit(solution)/shard_map/ppermute | solution.py:703
  30.5 2.5 %collective-permute-start.11 = (bf16[256,512]{1,0:T(8,128)(2,1)S(1)}, bf16[256,512]{1,0:T(8,128)(2,1)S(1)}, u32[]{:S(2)}, u32[]{:S(2)}) collective-permute-start(bf16[256,512]{1,0:T(8,128)(2,1)S(1)} %collective-permute-done.9.e1), channel_id=1, source_target_pairs={{0,1},{1,0},{2,3},{3,2},{4,5},{5,4},{6,7},{7,6},{8,9},{9,8},{10,11... | collective-permute-start | bytes 786440 | tf_op jit(solution)/shard_map/ppermute | solution.py:703
  31.6 6.2 %collective-permute-start.15 = (bf16[128,512]{1,0:T(8,128)(2,1)S(1)}, bf16[128,512]{1,0:T(8,128)(2,1)S(1)}, u32[]{:S(2)}, u32[]{:S(2)}) collective-permute-start(bf16[128,512]{1,0:T(8,128)(2,1)S(1)} %get-tuple-element.186), channel_id=1, source_target_pairs={{0,4},{4,0},{8,12},{12,8},{16,20},{20,16},{24,28},{28,24},{1,5},{5... | collective-permute-start | bytes 393224 | tf_op jit(solution)/shard_map/ppermute | solution.py:706
  32.3 2.8 %copy-start = (bf16[512,512]{1,0:T(8,128)(2,1)S(1)}, bf16[512,512]{1,0:T(8,128)(2,1)}, u32[]{:S(2)}) copy-start(bf16[512,512]{1,0:T(8,128)(2,1)} %win0.5) | copy-start | bytes 1572868
  32.3 2.8 %copy-start.1 = (bf16[512,512]{1,0:T(8,128)(2,1)S(1)}, bf16[512,512]{1,0:T(8,128)(2,1)}, u32[]{:S(2)}) copy-start(bf16[512,512]{1,0:T(8,128)(2,1)} %wback0.5) | copy-start | bytes 1572868
  32.3 5.9 %collective-permute-start.16 = (bf16[168,512]{1,0:T(8,128)(2,1)S(1)}, bf16[168,512]{1,0:T(8,128)(2,1)S(1)}, u32[]{:S(2)}, u32[]{:S(2)}) collective-permute-start(bf16[168,512]{1,0:T(8,128)(2,1)S(1)} %get-tuple-element.198), channel_id=1, source_target_pairs={{0,8},{4,12},{8,0},{12,4},{16,24},{20,28},{24,16},{28,20},{1,9},{5... | collective-permute-start | bytes 516104 | tf_op jit(solution)/shard_map/ppermute | solution.py:706
  33.1 1.9 %collective-permute-start.14 = (bf16[296,512]{1,0:T(8,128)(2,1)S(1)}, bf16[296,512]{1,0:T(8,128)(2,1)S(1)}, u32[]{:S(2)}, u32[]{:S(2)}) collective-permute-start(bf16[296,512]{1,0:T(8,128)(2,1)S(1)} %collective-permute-done.7.sz.s4), channel_id=1, source_target_pairs={{0,1},{1,0},{2,3},{3,2},{4,5},{5,4},{6,7},{7,6},{8,9},{9,8},{10,11... | collective-permute-start | bytes 909320 | tf_op jit(solution)/shard_map/ppermute | solution.py:703
  33.1 2.0 %collective-permute-start.13 = (bf16[296,512]{1,0:T(8,128)(2,1)S(1)}, bf16[296,512]{1,0:T(8,128)(2,1)S(1)}, u32[]{:S(2)}, u32[]{:S(2)}) collective-permute-start(bf16[296,512]{1,0:T(8,128)(2,1)S(1)} %collective-permute-done.6.sx.s2), channel_id=1, source_target_pairs={{0,1},{1,0},{2,3},{3,2},{4,5},{5,4},{6,7},{7,6},{8,9},{9,8},{10,11... | collective-permute-start | bytes 909320 | tf_op jit(solution)/shard_map/ppermute | solution.py:703
  35.0 5.3 %copy-start.3 = (bf16[128,512]{1,0:T(8,128)(2,1)S(1)}, bf16[128,512]{1,0:T(8,128)(2,1)}, u32[]{:S(2)}) copy-start(bf16[128,512]{1,0:T(8,128)(2,1)} %g2.5) | copy-start | bytes 393220
  35.0 5.2 %copy-start.4 = (bf16[256,512]{1,0:T(8,128)(2,1)S(1)}, bf16[256,512]{1,0:T(8,128)(2,1)}, u32[]{:S(2)}) copy-start(bf16[256,512]{1,0:T(8,128)(2,1)} %ct.3) | copy-start | bytes 786436
  38.2 2.0 %collective-permute-start.18 = (bf16[168,512]{1,0:T(8,128)(2,1)S(1)}, bf16[168,512]{1,0:T(8,128)(2,1)S(1)}, u32[]{:S(2)}, u32[]{:S(2)}) collective-permute-start(bf16[168,512]{1,0:T(8,128)(2,1)S(1)} %collective-permute-done.16.b6), channel_id=1, source_target_pairs={{0,1},{1,0},{2,3},{3,2},{4,5},{5,4},{6,7},{7,6},{8,9},{9,8},{10,11... | collective-permute-start | bytes 516104 | tf_op jit(solution)/shard_map/ppermute | solution.py:703
  38.3 2.0 %collective-permute-start.17 = (bf16[128,512]{1,0:T(8,128)(2,1)S(1)}, bf16[128,512]{1,0:T(8,128)(2,1)S(1)}, u32[]{:S(2)}, u32[]{:S(2)}) collective-permute-start(bf16[128,512]{1,0:T(8,128)(2,1)S(1)} %collective-permute-done.15.a6), channel_id=1, source_target_pairs={{0,1},{1,0},{2,3},{3,2},{4,5},{5,4},{6,7},{7,6},{8,9},{9,8},{10,11... | collective-permute-start | bytes 393224 | tf_op jit(solution)/shard_map/ppermute | solution.py:703
  38.8 12.4 %collective-permute-start.20 = (bf16[256,512]{1,0:T(8,128)(2,1)S(1)}, bf16[256,512]{1,0:T(8,128)(2,1)S(1)}, u32[]{:S(2)}, u32[]{:S(2)}) collective-permute-start(bf16[256,512]{1,0:T(8,128)(2,1)S(1)} %get-tuple-element.193.n2), channel_id=1, source_target_pairs={{0,2},{1,3},{2,0},{3,1},{4,6},{5,7},{6,4},{7,5},{8,10},{9,11},{10,... | collective-permute-start | bytes 786440 | tf_op jit(solution)/shard_map/ppermute | solution.py:703
  42.4 10.2 %collective-permute-start.21 = (bf16[256,512]{1,0:T(8,128)(2,1)S(1)}, bf16[256,512]{1,0:T(8,128)(2,1)S(1)}, u32[]{:S(2)}, u32[]{:S(2)}) collective-permute-start(bf16[256,512]{1,0:T(8,128)(2,1)S(1)} %get-tuple-element.203.fg), channel_id=1, source_target_pairs={{0,2},{1,3},{2,0},{3,1},{4,6},{5,7},{6,4},{7,5},{8,10},{9,11},{10,... | collective-permute-start | bytes 786440 | tf_op jit(solution)/shard_map/ppermute | solution.py:703
  48.1 2.4 %collective-permute-start.19 = (bf16[776,512]{1,0:T(8,128)(2,1)S(1)}, bf16[776,512]{1,0:T(8,128)(2,1)S(1)}, u32[]{:S(2)}, u32[]{:S(2)}) collective-permute-start(bf16[776,512]{1,0:T(8,128)(2,1)S(1)} %get-tuple-element.222), channel_id=1, source_target_pairs={{0,1},{1,0},{2,3},{3,2},{4,5},{5,4},{6,7},{7,6},{8,9},{9,8},{10,11... | collective-permute-start | bytes 2383880 | tf_op jit(solution)/shard_map/ppermute | solution.py:703
  56.8 2.9 %collective-permute-start.23 = (bf16[520,512]{1,0:T(8,128)(2,1)S(1)}, bf16[520,512]{1,0:T(8,128)(2,1)S(1)}, u32[]{:S(2)}, u32[]{:S(2)}) collective-permute-start(bf16[520,512]{1,0:T(8,128)(2,1)S(1)} %get-tuple-element.232), channel_id=1, source_target_pairs={{0,1},{1,0},{2,3},{3,2},{4,5},{5,4},{6,7},{7,6},{8,9},{9,8},{10,11... | collective-permute-start | bytes 1597448 | tf_op jit(solution)/shard_map/ppermute | solution.py:703
  56.8 2.8 %collective-permute-start.22 = (bf16[512,512]{1,0:T(8,128)(2,1)S(1)}, bf16[512,512]{1,0:T(8,128)(2,1)S(1)}, u32[]{:S(2)}, u32[]{:S(2)}) collective-permute-start(bf16[512,512]{1,0:T(8,128)(2,1)S(1)} %get-tuple-element.231), channel_id=1, source_target_pairs={{0,1},{1,0},{2,3},{3,2},{4,5},{5,4},{6,7},{7,6},{8,9},{9,8},{10,11... | collective-permute-start | bytes 1572872 | tf_op jit(solution)/shard_map/ppermute | solution.py:703
  57.3 6.7 %collective-permute-start.24 = (bf16[256,256]{1,0:T(8,128)(2,1)S(1)}, bf16[256,256]{1,0:T(8,128)(2,1)S(1)}, u32[]{:S(2)}, u32[]{:S(2)}) collective-permute-start(bf16[256,256]{1,0:T(8,128)(2,1)S(1)} %get-tuple-element.236), channel_id=1, source_target_pairs={{0,2},{1,3},{2,0},{3,1},{4,6},{5,7},{6,4},{7,5},{8,10},{9,11},{10,... | collective-permute-start | bytes 393224 | tf_op jit(solution)/shard_map/ppermute | solution.py:703
  59.7 14.4 %collective-permute-start.28 = (bf16[392,512]{1,0:T(8,128)(2,1)S(1)}, bf16[392,512]{1,0:T(8,128)(2,1)S(1)}, u32[]{:S(2)}, u32[]{:S(2)}) collective-permute-start(bf16[392,512]{1,0:T(8,128)(2,1)S(1)} %half_rows.1), channel_id=1, source_target_pairs={{0,2},{1,3},{2,0},{3,1},{4,6},{5,7},{6,4},{7,5},{8,10},{9,11},{10,... | collective-permute-start | bytes 1204232 | tf_op jit(solution)/shard_map/ppermute | solution.py:703
  60.7 10.2 %collective-permute-start.25 = (bf16[256,512]{1,0:T(8,128)(2,1)S(1)}, bf16[256,512]{1,0:T(8,128)(2,1)S(1)}, u32[]{:S(2)}, u32[]{:S(2)}) collective-permute-start(bf16[256,512]{1,0:T(8,128)(2,1)S(1)} %get-tuple-element.248), channel_id=1, source_target_pairs={{0,4},{4,0},{8,12},{12,8},{16,20},{20,16},{24,28},{28,24},{1,5},{5... | collective-permute-start | bytes 786440 | tf_op jit(solution)/shard_map/ppermute | solution.py:706
  62.2 8.6 %collective-permute-start.26 = (bf16[256,512]{1,0:T(8,128)(2,1)S(1)}, bf16[256,512]{1,0:T(8,128)(2,1)S(1)}, u32[]{:S(2)}, u32[]{:S(2)}) collective-permute-start(bf16[256,512]{1,0:T(8,128)(2,1)S(1)} %get-tuple-element.250), channel_id=1, source_target_pairs={{0,8},{4,12},{8,0},{12,4},{16,24},{20,28},{24,16},{28,20},{1,9},{5... | collective-permute-start | bytes 786440 | tf_op jit(solution)/shard_map/ppermute | solution.py:706
  70.1 3.9 %collective-permute-start.27 = (bf16[392,512]{1,0:T(8,128)(2,1)S(1)}, bf16[392,512]{1,0:T(8,128)(2,1)S(1)}, u32[]{:S(2)}, u32[]{:S(2)}) collective-permute-start(bf16[392,512]{1,0:T(8,128)(2,1)S(1)} %get-tuple-element.254), channel_id=1, source_target_pairs={{0,1},{1,0},{2,3},{3,2},{4,5},{5,4},{6,7},{7,6},{8,9},{9,8},{10,11... | collective-permute-start | bytes 1204232 | tf_op jit(solution)/shard_map/ppermute | solution.py:703
  70.8 6.0 %collective-permute-start.29 = (bf16[512,512]{1,0:T(8,128)(2,1)S(1)}, bf16[512,512]{1,0:T(8,128)(2,1)S(1)}, u32[]{:S(2)}, u32[]{:S(2)}) collective-permute-start(bf16[512,512]{1,0:T(8,128)(2,1)S(1)} %get-tuple-element.258), channel_id=1, source_target_pairs={{0,1},{1,0},{2,3},{3,2},{4,5},{5,4},{6,7},{7,6},{8,9},{9,8},{10,11... | collective-permute-start | bytes 1572872 | tf_op jit(solution)/shard_map/ppermute | solution.py:703
  71.6 7.7 %collective-permute-start.30 = (bf16[128,512]{1,0:T(8,128)(2,1)S(1)}, bf16[128,512]{1,0:T(8,128)(2,1)S(1)}, u32[]{:S(2)}, u32[]{:S(2)}) collective-permute-start(bf16[128,512]{1,0:T(8,128)(2,1)S(1)} %get-tuple-element.260), channel_id=1, source_target_pairs={{0,8},{4,12},{8,0},{12,4},{16,24},{20,28},{24,16},{28,20},{1,9},{5... | collective-permute-start | bytes 393224 | tf_op jit(solution)/shard_map/ppermute | solution.py:706
  72.6 6.7 %collective-permute-start.31 = (bf16[128,512]{1,0:T(8,128)(2,1)S(1)}, bf16[128,512]{1,0:T(8,128)(2,1)S(1)}, u32[]{:S(2)}, u32[]{:S(2)}) collective-permute-start(bf16[128,512]{1,0:T(8,128)(2,1)S(1)} %get-tuple-element.262), channel_id=1, source_target_pairs={{0,4},{4,0},{8,12},{12,8},{16,20},{20,16},{24,28},{28,24},{1,5},{5... | collective-permute-start | bytes 393224 | tf_op jit(solution)/shard_map/ppermute | solution.py:706
  75.0 7.6 %collective-permute-start.32 = (bf16[192,512]{1,0:T(8,128)(2,1)S(1)}, bf16[192,512]{1,0:T(8,128)(2,1)S(1)}, u32[]{:S(2)}, u32[]{:S(2)}) collective-permute-start(bf16[192,512]{1,0:T(8,128)(2,1)S(1)} %get-tuple-element.264), channel_id=1, source_target_pairs={{0,4},{4,0},{8,12},{12,8},{16,20},{20,16},{24,28},{28,24},{1,5},{5... | collective-permute-start | bytes 589832 | tf_op jit(solution)/shard_map/ppermute | solution.py:706
  75.7 7.7 %collective-permute-start.33 = (bf16[192,512]{1,0:T(8,128)(2,1)S(1)}, bf16[192,512]{1,0:T(8,128)(2,1)S(1)}, u32[]{:S(2)}, u32[]{:S(2)}) collective-permute-start(bf16[192,512]{1,0:T(8,128)(2,1)S(1)} %get-tuple-element.266), channel_id=1, source_target_pairs={{0,8},{4,12},{8,0},{12,4},{16,24},{20,28},{24,16},{28,20},{1,9},{5... | collective-permute-start | bytes 589832 | tf_op jit(solution)/shard_map/ppermute | solution.py:706
  77.4 8.4 %collective-permute-start.34 = (bf16[512,256]{1,0:T(8,128)(2,1)S(1)}, bf16[512,256]{1,0:T(8,128)(2,1)S(1)}, u32[]{:S(2)}, u32[]{:S(2)}) collective-permute-start(bf16[512,256]{1,0:T(8,128)(2,1)S(1)} %half_columns.1), channel_id=1, source_target_pairs={{0,2},{1,3},{2,0},{3,1},{4,6},{5,7},{6,4},{7,5},{8,10},{9,11},{10,... | collective-permute-start | bytes 786440 | tf_op jit(solution)/shard_map/ppermute | solution.py:703
  79.9 13.4 %collective-permute-start.35 = (bf16[264,512]{1,0:T(8,128)(2,1)S(1)}, bf16[264,512]{1,0:T(8,128)(2,1)S(1)}, u32[]{:S(2)}, u32[]{:S(2)}) collective-permute-start(bf16[264,512]{1,0:T(8,128)(2,1)S(1)} %merge_f.1.own), channel_id=1, source_target_pairs={{0,16},{4,20},{8,24},{12,28},{16,0},{20,4},{24,8},{28,12},{1,17},{... | collective-permute-start | bytes 811016 | tf_op jit(solution)/shard_map/ppermute | solution.py:706
  84.1 9.9 %collective-permute-start.36 = (bf16[96,512]{1,0:T(8,128)(2,1)S(1)}, bf16[96,512]{1,0:T(8,128)(2,1)S(1)}, u32[]{:S(2)}, u32[]{:S(2)}) collective-permute-start(bf16[96,512]{1,0:T(8,128)(2,1)S(1)} %get-tuple-element.274), channel_id=1, source_target_pairs={{0,8},{4,12},{8,0},{12,4},{16,24},{20,28},{24,16},{28,20},{1,9},{5... | collective-permute-start | bytes 294920 | tf_op jit(solution)/shard_map/ppermute | solution.py:706
  84.3 10.0 %collective-permute-start.37 = (bf16[96,512]{1,0:T(8,128)(2,1)S(1)}, bf16[96,512]{1,0:T(8,128)(2,1)S(1)}, u32[]{:S(2)}, u32[]{:S(2)}) collective-permute-start(bf16[96,512]{1,0:T(8,128)(2,1)S(1)} %get-tuple-element.276), channel_id=1, source_target_pairs={{0,4},{4,0},{8,12},{12,8},{16,20},{20,16},{24,28},{28,24},{1,5},{5... | collective-permute-start | bytes 294920 | tf_op jit(solution)/shard_map/ppermute | solution.py:706
  87.7 8.0 %collective-permute-start.40 = (f32[8,512]{1,0:T(8,128)S(1)}, f32[8,512]{1,0:T(8,128)S(1)}, u32[]{:S(2)}, u32[]{:S(2)}) collective-permute-start(f32[8,512]{1,0:T(8,128)S(1)} %get-tuple-element.277.refs_4_), channel_id=1, source_target_pairs={{0,3},{1,2},{2,1},{3,0},{4,7},{5,6},{6,5},{7,4},{8,11},{9,10},{10,... | collective-permute-start | bytes 49160 | tf_op jit(solution)/shard_map/ppermute | solution.py:703
  87.7 8.0 %collective-permute-start.39 = (f32[8,512]{1,0:T(8,128)S(1)}, f32[8,512]{1,0:T(8,128)S(1)}, u32[]{:S(2)}, u32[]{:S(2)}) collective-permute-start(f32[8,512]{1,0:T(8,128)S(1)} %get-tuple-element.277.refs_4_), channel_id=1, source_target_pairs={{0,2},{1,3},{2,0},{3,1},{4,6},{5,7},{6,4},{7,5},{8,10},{9,11},{10,... | collective-permute-start | bytes 49160 | tf_op jit(solution)/shard_map/ppermute | solution.py:703
  93.3 2.4 %collective-permute-start.38 = (f32[8,512]{1,0:T(8,128)S(1)}, f32[8,512]{1,0:T(8,128)S(1)}, u32[]{:S(2)}, u32[]{:S(2)}) collective-permute-start(f32[8,512]{1,0:T(8,128)S(1)} %get-tuple-element.277.refs_4_), channel_id=1, source_target_pairs={{0,1},{1,0},{2,3},{3,2},{4,5},{5,4},{6,7},{7,6},{8,9},{9,8},{10,11... | collective-permute-start | bytes 49160 | tf_op jit(solution)/shard_map/ppermute | solution.py:703
  94.0 6.1 %collective-permute-start.41 = (bf16[1,136,512]{2,1,0:T(8,128)(2,1)S(1)}, bf16[1,136,512]{2,1,0:T(8,128)(2,1)S(1)}, u32[]{:S(2)}, u32[]{:S(2)}) collective-permute-start(bf16[1,136,512]{2,1,0:T(8,128)(2,1)S(1)} %get-tuple-element.272.held1), channel_id=1, source_target_pairs={{0,8},{4,12},{8,0},{12,4},{16,24},{20,28},{24,16},{28,20},{1,9},{5... | collective-permute-start | bytes 417800 | tf_op jit(solution)/shard_map/ppermute | solution.py:706
  94.3 5.7 %collective-permute-start.42 = (bf16[1,128,512]{2,1,0:T(8,128)(2,1)S(1)}, bf16[1,128,512]{2,1,0:T(8,128)(2,1)S(1)}, u32[]{:S(2)}, u32[]{:S(2)}) collective-permute-start(bf16[1,128,512]{2,1,0:T(8,128)(2,1)S(1)} %get-tuple-element.279.held2), channel_id=1, source_target_pairs={{0,4},{4,0},{8,12},{12,8},{16,20},{20,16},{24,28},{28,24},{1,5},{5... | collective-permute-start | bytes 393224 | tf_op jit(solution)/shard_map/ppermute | solution.py:706
  96.4 13.1 %collective-permute-start.43 = (bf16[200,512]{1,0:T(8,128)(2,1)S(1)}, bf16[200,512]{1,0:T(8,128)(2,1)S(1)}, u32[]{:S(2)}, u32[]{:S(2)}) collective-permute-start(bf16[200,512]{1,0:T(8,128)(2,1)S(1)} %merge_a.1.own), channel_id=1, source_target_pairs={{0,16},{4,20},{8,24},{12,28},{16,0},{20,4},{24,8},{28,12},{1,17},{... | collective-permute-start | bytes 614408 | tf_op jit(solution)/shard_map/ppermute | solution.py:706
  100.7 17.4 %collective-permute-start.46 = (bf16[2,136,512]{2,1,0:T(8,128)(2,1)S(1)}, bf16[2,136,512]{2,1,0:T(8,128)(2,1)S(1)}, u32[]{:S(2)}, u32[]{:S(2)}) collective-permute-start(bf16[2,136,512]{2,1,0:T(8,128)(2,1)S(1)} %get-tuple-element.280.held1), channel_id=1, source_target_pairs={{0,4},{4,0},{8,12},{12,8},{16,20},{20,16},{24,28},{28,24},{1,5},{5... | collective-permute-start | bytes 835592 | tf_op jit(solution)/shard_map/ppermute | solution.py:706
  104.0 14.1 %collective-permute-start.47 = (bf16[2,128,512]{2,1,0:T(8,128)(2,1)S(1)}, bf16[2,128,512]{2,1,0:T(8,128)(2,1)S(1)}, u32[]{:S(2)}, u32[]{:S(2)}) collective-permute-start(bf16[2,128,512]{2,1,0:T(8,128)(2,1)S(1)} %get-tuple-element.287.held2), channel_id=1, source_target_pairs={{0,8},{4,12},{8,0},{12,4},{16,24},{20,28},{24,16},{28,20},{1,9},{5... | collective-permute-start | bytes 786440 | tf_op jit(solution)/shard_map/ppermute | solution.py:706
  110.1 5.5 %collective-permute-start.44 = (bf16[1,104,512]{2,1,0:T(8,128)(2,1)S(1)}, bf16[1,104,512]{2,1,0:T(8,128)(2,1)S(1)}, u32[]{:S(2)}, u32[]{:S(2)}) collective-permute-start(bf16[1,104,512]{2,1,0:T(8,128)(2,1)S(1)} %get-tuple-element.282.held1), channel_id=1, source_target_pairs={{0,8},{4,12},{8,0},{12,4},{16,24},{20,28},{24,16},{28,20},{1,9},{5... | collective-permute-start | bytes 319496 | tf_op jit(solution)/shard_map/ppermute | solution.py:706
  110.2 4.7 %collective-permute-start.45 = (bf16[1,96,512]{2,1,0:T(8,128)(2,1)S(1)}, bf16[1,96,512]{2,1,0:T(8,128)(2,1)S(1)}, u32[]{:S(2)}, u32[]{:S(2)}) collective-permute-start(bf16[1,96,512]{2,1,0:T(8,128)(2,1)S(1)} %get-tuple-element.284.held2), channel_id=1, source_target_pairs={{0,4},{4,0},{8,12},{12,8},{16,20},{20,16},{24,28},{28,24},{1,5},{5... | collective-permute-start | bytes 294920 | tf_op jit(solution)/shard_map/ppermute | solution.py:706
  116.1 6.3 %collective-permute-start.48 = (bf16[2,104,512]{2,1,0:T(8,128)(2,1)S(1)}, bf16[2,104,512]{2,1,0:T(8,128)(2,1)S(1)}, u32[]{:S(2)}, u32[]{:S(2)}) collective-permute-start(bf16[2,104,512]{2,1,0:T(8,128)(2,1)S(1)} %get-tuple-element.285.held1), channel_id=1, source_target_pairs={{0,4},{4,0},{8,12},{12,8},{16,20},{20,16},{24,28},{28,24},{1,5},{5... | collective-permute-start | bytes 638984 | tf_op jit(solution)/shard_map/ppermute | solution.py:706
  116.2 5.9 %collective-permute-start.49 = (bf16[2,96,512]{2,1,0:T(8,128)(2,1)S(1)}, bf16[2,96,512]{2,1,0:T(8,128)(2,1)S(1)}, u32[]{:S(2)}, u32[]{:S(2)}) collective-permute-start(bf16[2,96,512]{2,1,0:T(8,128)(2,1)S(1)} %get-tuple-element.290.held2), channel_id=1, source_target_pairs={{0,8},{4,12},{8,0},{12,4},{16,24},{20,28},{24,16},{28,20},{1,9},{5... | collective-permute-start | bytes 589832 | tf_op jit(solution)/shard_map/ppermute | solution.py:706

commit v5 on v4

--- a/solution.py
+++ b/solution.py
@@ -18,7 +18,7 @@
 SPARE = 4 * 1024 * 1024
 HEAVY = 10**10
 LIGHT = 0
-EASY = ("pair_a", "part_f", "halves_f", "halves_a", "input_grad")
+COSTS = {"halves_f": 0, "halves_a": 0, "input_grad": 0, "pair_a": 2*10**10, "part_f": 0, "merge_a": 0, "last": 0, "pair_f": 0, "part_a": 0,"unpack_f":0, "first": 0, "ffn": 0}
 
 
 def nn(a, b):
@@ -717,7 +717,7 @@
 
     def step(kernel, outs, args, name, scratch=(), smem=1, space=VM, then=(), limit=None, cost=HEAVY):
         pos = tb if last[0] is None else after(tb, last[0], *then)
-        got = call(kernel, outs, [pos] + args, smem=smem, scratch=scratch, name=name, space=space, limit=limit, cost=LIGHT if name in EASY else cost)
+        got = call(kernel, outs, [pos] + args, smem=smem, scratch=scratch, name=name, space=space, limit=limit, cost=COSTS.get(name, cost))
         last[0] = got[0]
         return got
 
@@ -744,7 +744,7 @@
         [x0, x2, vecs] + qkv, "chip", cost=LIGHT,
     )
     x3 = hop(after(x1, na), 1)
-    e1 = hop(after(e0, x3), PX)
+    e1 = hop(after(e0, na), PX)
     n, qt1, k, vt, p1, ot1, att1, invl1 = step(
         first_kernel,
         [
@@ -767,16 +767,16 @@
     )
     e3 = hop(after(e1, att0), 1)
     v, kt = step(prepare_kernel, [sds((1024, 256), BF16), sds((256, 1024), BF16)], [n, k] + qkv, "prepare")
-    cut_a, cut_b = step(cut_kernel, [sds((128, 512), BF16), sds((168, 512), BF16)], [sx, sz], "cut")
-    sxz_a, sxz_b = dhop(cut_a, 1), dhop(cut_b, 2)
     n2, mid, branch, gate = step(
         out_kernel,
         [sds((256, 512), BF16), sds((256, 512), F32), sds((256, 512), F32), sds((256, 512), F32)],
         [x0, n, att0, attp, vecs, e0, e1, c2, e3],
         "out", [pltpu.VMEM((512, 512), BF16)],
     )
-    n2p = hop(n2, PX)
-    quarters = [sy, hop(sy, 1), sx, hop(sx, 1), sz, hop(sz, 1)]
+    cut_a, cut_b = step(cut_kernel, [sds((128, 512), BF16), sds((168, 512), BF16)], [sx, sz], "cut")
+    sxz_a, sxz_b = dhop(cut_a, 1), dhop(cut_b, 2)
+    n2p = hop(after(n2, cut_a), PX)
+    quarters = [sy, hop(after(sy, cut_a), 1), sx, hop(after(sx, cut_a), 1), sz, hop(after(sz, cut_a), 1)]
     total0, hid, slope0, slope1 = step(
         ffn_first_kernel,
         [sds((256, 512), F32), sds((256, 1024), BF16), sds((256, 1024), BF16), sds((256, 768), BF16)],
@@ -800,7 +800,7 @@
         ],
         [fg, ltg, slope0, slope1, slope2, mid, branch, gate, cotangent, vecs, e0, e1, c2, e3, gate2_w, w_in, w_back]
         + quarters,
-        "back", [pltpu.VMEM((512, 512), BF16)],
+        "back", [pltpu.VMEM((512, 512), BF16)], then=(n2p,),
     )
     dot1 = hop(dotp, PX)
     skeep, ssend = step(
@@ -943,13 +943,13 @@
     sums1_b = hop(sums1, PX)
     sums1_a = hop(sums1, 1)
     sums1_c = hop(sums1, PX ^ 1)
-    f = part_step("f", *f)
     group = [(skeep, 768), (srecv, 768), (sparr, 384)]
     a = merge_step(
         "a", *a,
         [(0, 2, [(sums1, 0), (sums1_a, 0), (sums1_b, 0), (sums1_c, 0)]), (2, 1, [(akeep, 384), (arecv, 384)]),
          (3, 5, group)],
     )
+    f = part_step("f", *f)
     f = pair_step("f", *f)
     a = part_step("a", *a)
     a = pair_step("a", *a)

time: 125 us -> 121 us (0.968)
  waiting for transfers between devices: 30.1 us -> 23.5 us
  starting transfers between devices: 43.1 us -> 45.9 us
    ppermute x28, waiting for transfers between devices: 11 us -> 7.41 us  [hop(): return lax.ppermute(value, 'tensor', [(i, i ^ mask) for i in range(4)])]
    ppermute x22, waiting for transfers between devices: 19.1 us -> 16 us  [dhop(): return lax.ppermute(value, 'dp', [(i, i ^ mask) for i in range(n_dp)])]
    ppermute x28, starting transfers between devices: 16.7 us -> 18.3 us  [hop(): return lax.ppermute(value, 'tensor', [(i, i ^ mask) for i in range(4)])]
  transfers between devices with their start and end apart: 50 -> 50, of which waited for: 18 -> 20; matrix products, arithmetic and copies ran while one was open for 1% -> 1% of each run, Pallas kernels for 35% -> 35%
where the time goes in v5:
time: 121 us
  Pallas kernels  49.4 us (41%)
  starting transfers between devices  45.9 us (38%)
  waiting for transfers between devices  23.5 us (19%)
    pallas_call x31, Pallas kernels, call(): pl.pallas_call(body, out_shape=tuple(outs), in_specs=[SM] * smem + [space...  49.4 us
    ppermute x22, starting transfers between devices, dhop(): return lax.ppermute(value, 'dp', [(i, i ^ mask) for i in range(n_dp)])  27.6 us
    ppermute x28, starting transfers between devices, hop(): return lax.ppermute(value, 'tensor', [(i, i ^ mask) for i in range(4)])  18.3 us
    ppermute x22, waiting for transfers between devices, dhop(): return lax.ppermute(value, 'dp', [(i, i ^ mask) for i in range(n_dp)])  16 us
    ppermute x28, waiting for transfers between devices, hop(): return lax.ppermute(value, 'tensor', [(i, i ^ mask) for i in range(4)])  7.41 us
  transfers between devices with their start and end apart: 50, of which 20 were waited for; matrix products, arithmetic and copies ran while one was open for 1% of the time, Pallas kernels for 35%

profile of v5, /device:TPU:0, one launch (start us, length us, event | category | flops | bytes accessed | tf_op | source)
XLA Modules:
  0.0 120.5 jit_solution(11031152273978057870)
XLA Ops:
  0.7 3.0 %collective-permute-start.3 = (bf16[256,512]{1,0:T(8,128)(2,1)}, bf16[256,512]{1,0:T(8,128)(2,1)S(1)}, u32[]{:S(2)}, u32[]{:S(2)}) collective-permute-start(bf16[256,512]{1,0:T(8,128)(2,1)} %x0.5), channel_id=1, source_target_pairs={{0,2},{1,3},{2,0},{3,1},{4,6},{5,7},{6,4},{7,5},{8,10},{9,11},{10,... | collective-permute-start | bytes 786440 | tf_op jit(solution)/shard_map/ppermute | solution.py:703
  4.4 2.5 %pack.1 = (bf16[296,512]{1,0:T(8,128)(2,1)S(1)}, bf16[256,512]{1,0:T(8,128)(2,1)S(1)}, bf16[1416,512]{1,0:T(8,128)(2,1)S(1)}, bf16[256,384]{1,0:T(8,128)(2,1)S(1...) custom-call(s32[8]{0:T(128)S(1)} %compare_select_fusion.pos.tb, bf16[512,512]{1,0:T(8,128)(2,1)} %win0.5, ...), custom_call_target="tpu_custom_call" | custom-call | tf_op jit(solution)/shard_map/pack/pallas_call | solution.py:44
  7.7 1.3 %collective-permute-done.1.qa1 = bf16[256,384]{1,0:T(8,128)(2,1)S(1)} collective-permute-done((bf16[256,384]{1,0:T(8,128)(2,1)S(1)}, bf16[256,384]{1,0:T(8,128)(2,1)S(1)}, u32[]{:S(2)}, u32[]{:S(2)}) %collective-permute-start.1) | collective-permute-done | bytes 196640 | tf_op jit(solution)/shard_map/ppermute | solution.py:703
  8.9 1.8 %chip.1 = (bf16[512,512]{1,0:T(8,128)(2,1)S(1)}, bf16[256,256]{1,0:T(8,128)(2,1)S(1)}, bf16[512,256]{1,0:T(8,128)(2,1)S(1)}, bf16[256,512]{1,0:T(8,128)(2,1)S(1)}) custom-call(s32[8]{0:T(128)S(1)} %compare_select_fusion.pos.tb, bf16[256,512]{1,0:T(8,128)(2,1)S(1)} %copy-done.2, bf16[256,512]{1,0:T(8,128)(2,1)S(1)} %collective-permute-done.x2, ...), custom_call_target="tpu_custom_call" | custom-call | tf_op jit(solution)/shard_map/chip/pallas_call | solution.py:44
  11.3 2.1 %collective-permute-start.6 = (bf16[256,512]{1,0:T(8,128)(2,1)S(1)}, bf16[256,512]{1,0:T(8,128)(2,1)S(1)}, u32[]{:S(2)}, u32[]{:S(2)}) collective-permute-start(bf16[256,512]{1,0:T(8,128)(2,1)S(1)} %get-tuple-element.191.e0), channel_id=1, source_target_pairs={{0,2},{1,3},{2,0},{3,1},{4,6},{5,7},{6,4},{7,5},{8,10},{9,11},{10,... | collective-permute-start | bytes 786440 | tf_op jit(solution)/shard_map/ppermute | solution.py:703
  13.5 4.1 %first.1 = (bf16[1024,512]{1,0:T(8,128)(2,1)S(1)}, bf16[256,256]{1,0:T(8,128)(2,1)S(1)}, bf16[1024,256]{1,0:T(8,128)(2,1)S(1)}, bf16[256,1024]{1,0:T(8,128)(2,1)...) custom-call(s32[8]{0:T(128)S(1)} %compare_select_fusion.pos.tb, ...), custom_call_target="tpu_custom_call" | custom-call | tf_op jit(solution)/shard_map/first/pallas_call | solution.py:44
  17.7 1.4 %collective-permute-start.11 = (bf16[296,512]{1,0:T(8,128)(2,1)S(1)}, bf16[296,512]{1,0:T(8,128)(2,1)S(1)}, u32[]{:S(2)}, u32[]{:S(2)}) collective-permute-start(bf16[296,512]{1,0:T(8,128)(2,1)S(1)} %collective-permute-done.9.s0), channel_id=1, source_target_pairs={{0,8},{4,12},{8,0},{12,4},{16,24},{20,28},{24,16},{28,20},{1,9},{5... | collective-permute-start | bytes 909320 | tf_op jit(solution)/shard_map/ppermute | solution.py:706
  19.1 1.5 %collective-permute-start.10 = (bf16[296,512]{1,0:T(8,128)(2,1)S(1)}, bf16[296,512]{1,0:T(8,128)(2,1)S(1)}, u32[]{:S(2)}, u32[]{:S(2)}) collective-permute-start(bf16[296,512]{1,0:T(8,128)(2,1)S(1)} %collective-permute-done.9.s0), channel_id=1, source_target_pairs={{0,4},{4,0},{8,12},{12,8},{16,20},{20,16},{24,28},{28,24},{1,5},{5... | collective-permute-start | bytes 909320 | tf_op jit(solution)/shard_map/ppermute | solution.py:706
  20.6 1.6 %second.1 = (bf16[4,1024,256]{2,1,0:T(8,128)(2,1)S(1)}, bf16[256,256]{1,0:T(8,128)(2,1)S(1)}, bf16[256,256]{1,0:T(8,128)(2,1)S(1)}, f32[4,8,256]{2,1,0:T(8,128)S(1)}) custom-call(s32[8]{0:T(128)S(1)} %compare_select_fusion.pos.tb, s32[1,1024]{1,0:T(1,128)S(1)} %copy-done.5, s32[1,1024]{1,0:T(1,128)S(1)} %copy-done.5, ...), custom_call_target="tpu_custom_call" | custom-call | flops 10000000000 | tf_op jit(solution)/shard_map/second/pallas_call | solution.py:44
  22.3 0.9 collective-permute-done.6.e1
  23.2 1.2 %prepare.1 = (bf16[1024,256]{1,0:T(8,128)(2,1)S(1)}, bf16[256,1024]{1,0:T(8,128)(2,1)S(1)}) custom-call(s32[8]{0:T(128)S(1)} %compare_select_fusion.pos.tb, bf16[1024,512]{1,0:T(8,128)(2,1)S(1)} %get-tuple-element.179.n, bf16[1024,256]{1,0:T(8,128)(2,1)S(1)} %get-tuple-element.182.k, bf16[256,384]{1,0:T(8,128)(2,1)S(1)} %get-tuple-element.172.qa0, ...), custom_call_target="tpu_custom_call" | custom-call | flops 10000000000 | tf_op jit(solution)/shard_map/prepare/pallas_call | solution.py:44
  24.4 1.1 collective-permute-done.5.attp
  25.5 1.4 %out.1 = (bf16[256,512]{1,0:T(8,128)(2,1)S(1)}, f32[256,512]{1,0:T(8,128)S(1)}, f32[256,512]{1,0:T(8,128)S(1)}, f32[256,512]{1,0:T(8,128)S(1)}) custom-call(s32[8]{0:T(128)S(1)} %compare_select_fusion.pos.tb, bf16[256,512]{1,0:T(8,128)(2,1)S(1)} %copy-done.2, bf16[1024,512]{1,0:T(8,128)(2,1)S(1)} %get-tuple-element.179.n, ...), custom_call_target="tpu_custom_call" | custom-call | flops 10000000000 | tf_op jit(solution)/shard_map/out/pallas_call | solution.py:44
  27.2 1.1 collective-permute-done.10.sx.s2
  29.5 0.7 collective-permute-start.16
  30.1 1.3 %collective-permute-start.15 = (bf16[128,512]{1,0:T(8,128)(2,1)S(1)}, bf16[128,512]{1,0:T(8,128)(2,1)S(1)}, u32[]{:S(2)}, u32[]{:S(2)}) collective-permute-start(bf16[128,512]{1,0:T(8,128)(2,1)S(1)} %get-tuple-element.197), channel_id=1, source_target_pairs={{0,4},{4,0},{8,12},{12,8},{16,20},{20,16},{24,28},{28,24},{1,5},{5... | collective-permute-start | bytes 393224 | tf_op jit(solution)/shard_map/ppermute | solution.py:706
  31.4 1.7 %collective-permute-start.19 = (bf16[256,512]{1,0:T(8,128)(2,1)S(1)}, bf16[256,512]{1,0:T(8,128)(2,1)S(1)}, u32[]{:S(2)}, u32[]{:S(2)}) collective-permute-start(bf16[256,512]{1,0:T(8,128)(2,1)S(1)} %get-tuple-element.209.n2), channel_id=1, source_target_pairs={{0,2},{1,3},{2,0},{3,1},{4,6},{5,7},{6,4},{7,5},{8,10},{9,11},{10,... | collective-permute-start | bytes 786440 | tf_op jit(solution)/shard_map/ppermute | solution.py:703
  33.1 2.7 %ffn_first.1 = (f32[256,512]{1,0:T(8,128)S(1)}, bf16[256,1024]{1,0:T(8,128)(2,1)S(1)}, bf16[256,1024]{1,0:T(8,128)(2,1)S(1)}, bf16[256,768]{1,0:T(8,128)(2,1)S(1)}) custom-call(s32[8]{0:T(128)S(1)} %compare_select_fusion.pos.tb, bf16[256,512]{1,0:T(8,128)(2,1)S(1)} %get-tuple-element.209.n2, f32[16,512]{1,0:T(8,128)S(1)} %get-tuple-element.171.vecs, ...), custom_call_target="tpu_custom_call" | custom-call | tf_op jit(solution)/shard_map/ffn_first/pallas_call | solution.py:44
  36.7 1.1 collective-permute-done.17.a7
  37.8 2.1 %ffn.1 = (bf16[256,512]{1,0:T(8,128)(2,1)}, bf16[256,512]{1,0:T(8,128)(2,1)S(1)}, bf16[256,512]{1,0:T(8,128)(2,1)S(1)}, bf16[256,256]{1,0:T(8,128)(2,1)S(1)}) custom-call(s32[8]{0:T(128)S(1)} %compare_select_fusion.pos.tb, bf16[256,512]{1,0:T(8,128)(2,1)S(1)} %get-tuple-element.209.n2, f32[256,512]{1,0:T(8,128)S(1)} %get-tuple-element.204.mid, ...), custom_call_target="tpu_custom_call" | custom-call | tf_op jit(solution)/shard_map/ffn/pallas_call | solution.py:44
  39.9 1.7 %collective-permute-start.21 = (bf16[256,512]{1,0:T(8,128)(2,1)S(1)}, bf16[256,512]{1,0:T(8,128)(2,1)S(1)}, u32[]{:S(2)}, u32[]{:S(2)}) collective-permute-start(bf16[256,512]{1,0:T(8,128)(2,1)S(1)} %get-tuple-element.211.fg), channel_id=1, source_target_pairs={{0,2},{1,3},{2,0},{3,1},{4,6},{5,7},{6,4},{7,5},{8,10},{9,11},{10,... | collective-permute-start | bytes 786440 | tf_op jit(solution)/shard_map/ppermute | solution.py:703
  41.6 3.4 %back.1 = (bf16[256,256]{1,0:T(8,128)(2,1)S(1)}, bf16[256,256]{1,0:T(8,128)(2,1)S(1)}, f32[256,512]{1,0:T(8,128)S(1)}, bf16[256,512]{1,0:T(8,128)(2,1)S(1)}, bf1...) custom-call(s32[8]{0:T(128)S(1)} %compare_select_fusion.pos.tb, ...), custom_call_target="tpu_custom_call" | custom-call | flops 10000000000 | tf_op jit(solution)/shard_map/back/pallas_call | solution.py:44
  45.1 1.2 small_weight.1
  46.3 2.1 %attn_back0.1 = (f32[256,1024]{1,0:T(8,128)S(1)}, f32[256,1024]{1,0:T(8,128)S(1)}, bf16[256,256]{1,0:T(8,128)(2,1)S(1)}) custom-call(s32[8]{0:T(128)S(1)} %compare_select_fusion.pos.tb, s32[1,1024]{1,0:T(1,128)S(1)} %copy-done.5, bf16[4,1024,256]{2,1,0:T(8,128)(2,1)S(1)} %get-tuple-element.184.p, bf16[256,256]{1,0:T(8,128)(2,1)S(1)} %get-tuple-element.218.dot, ...), custom_call_target="tpu_custom_call" | custom-call | flops 10000000000 | tf_op jit(solution)/shard_map/attn_back0/pallas_call | solution.py:44
  49.2 2.3 %ffn_back_weight.1 = (f32[512,512]{1,0:T(8,128)S(1)}, bf16[512,512]{1,0:T(8,128)(2,1)S(1)}, bf16[256,1024]{1,0:T(8,128)(2,1)S(1)}) custom-call(s32[8]{0:T(128)S(1)} %compare_select_fusion.pos.tb, bf16[256,512]{1,0:T(8,128)(2,1)S(1)} %collective-permute-done.19.n2p, bf16[256,512]{1,0:T(8,128)(2,1)S(1)} %get-tuple-element.211.fg, ...), custom_call_target="tpu_custom_call" | custom-call | flops 10000000000 | tf_op jit(solution)/shard_map/ffn_back_weight/pallas_call | solution.py:44
  51.5 1.9 %ffn_in_weight.1 = (f32[520,512]{1,0:T(8,128)S(1)}, bf16[520,512]{1,0:T(8,128)(2,1)S(1)}) custom-call(s32[8]{0:T(128)S(1)} %compare_select_fusion.pos.tb, bf16[256,512]{1,0:T(8,128)(2,1)S(1)} %get-tuple-element.209.n2, bf16[256,512]{1,0:T(8,128)(2,1)S(1)} %collective-permute-done.19.n2p, bf16[256,512]{1,0:T(8,128)(2,1)S(1)} %collective-permute-done.21.fgp, ...), custom_call_target="tpu_custom_call" | custom-call | flops 10000000000 | tf_op jit(solution)/shard_map/ffn_in_weight/pallas_call | solution.py:44
  53.4 1.3 %collective-permute-start.23 = (bf16[520,512]{1,0:T(8,128)(2,1)S(1)}, bf16[520,512]{1,0:T(8,128)(2,1)S(1)}, u32[]{:S(2)}, u32[]{:S(2)}) collective-permute-start(bf16[520,512]{1,0:T(8,128)(2,1)S(1)} %get-tuple-element.240), channel_id=1, source_target_pairs={{0,1},{1,0},{2,3},{3,2},{4,5},{5,4},{6,7},{7,6},{8,9},{9,8},{10,11... | collective-permute-start | bytes 1597448 | tf_op jit(solution)/shard_map/ppermute | solution.py:703
  54.8 2.3 %collective-permute-start.24 = (bf16[256,256]{1,0:T(8,128)(2,1)S(1)}, bf16[256,256]{1,0:T(8,128)(2,1)S(1)}, u32[]{:S(2)}, u32[]{:S(2)}) collective-permute-start(bf16[256,256]{1,0:T(8,128)(2,1)S(1)} %get-tuple-element.244), channel_id=1, source_target_pairs={{0,2},{1,3},{2,0},{3,1},{4,6},{5,7},{6,4},{7,5},{8,10},{9,11},{10,... | collective-permute-start | bytes 393224 | tf_op jit(solution)/shard_map/ppermute | solution.py:703
  57.1 1.0 halves_f.1
  58.1 1.6 %collective-permute-start.25 = (bf16[256,512]{1,0:T(8,128)(2,1)S(1)}, bf16[256,512]{1,0:T(8,128)(2,1)S(1)}, u32[]{:S(2)}, u32[]{:S(2)}) collective-permute-start(bf16[256,512]{1,0:T(8,128)(2,1)S(1)} %get-tuple-element.256), channel_id=1, source_target_pairs={{0,4},{4,0},{8,12},{12,8},{16,20},{20,16},{24,28},{28,24},{1,5},{5... | collective-permute-start | bytes 786440 | tf_op jit(solution)/shard_map/ppermute | solution.py:706
  59.7 0.9 collective-permute-start.26
  60.6 0.9 collective-permute-done.24.dot
  61.5 4.7 %attn_back1.1 = (bf16[256,512]{1,0:T(8,128)(2,1)S(1)}, bf16[256,1024]{1,0:T(8,128)(2,1)S(1)}, bf16[256,1024]{1,0:T(8,128)(2,1)S(1)}, f32[392,512]{1,0:T(8,128)S(1)}, bf16[392,512]{1,0:T(8,128)(2,1)S(1)}) custom-call(s32[8]{0:T(128)S(1)} %compare_select_fusion.pos.tb, s32[1,1024]{1,0:T(1,128)S(1)} %copy-done.5, ...), custom_call_target="tpu_custom_call" | custom-call | flops 10000000000 | tf_op jit(solution)/shard_map/attn_back1/pallas_call | solution.py:44
  66.2 1.4 %input_grad.1 = (f32[512,256]{1,0:T(8,128)S(1)}, f32[512,256]{1,0:T(8,128)S(1)}, bf16[512,512]{1,0:T(8,128)(2,1)S(1)}) custom-call(s32[8]{0:T(128)S(1)} %compare_select_fusion.pos.tb, bf16[256,512]{1,0:T(8,128)(2,1)S(1)} %get-tuple-element.250.dqt, bf16[256,1024]{1,0:T(8,128)(2,1)S(1)} %get-tuple-element.252.dkt, ...), custom_call_target="tpu_custom_call" | custom-call | tf_op jit(solution)/shard_map/input_grad/pallas_call | solution.py:44
  68.3 0.7 quarters_f.1
  69.1 1.3 %collective-permute-start.30 = (bf16[128,512]{1,0:T(8,128)(2,1)S(1)}, bf16[128,512]{1,0:T(8,128)(2,1)S(1)}, u32[]{:S(2)}, u32[]{:S(2)}) collective-permute-start(bf16[128,512]{1,0:T(8,128)(2,1)S(1)} %get-tuple-element.268), channel_id=1, source_target_pairs={{0,8},{4,12},{8,0},{12,4},{16,24},{20,28},{24,16},{28,20},{1,9},{5... | collective-permute-start | bytes 393224 | tf_op jit(solution)/shard_map/ppermute | solution.py:706
  70.4 1.1 collective-permute-start.31
  71.5 1.0 halves_a.1
  72.5 1.0 collective-permute-start.32
  73.5 0.8 collective-permute-start.33
  74.8 1.9 %collective-permute-start.34 = (bf16[512,256]{1,0:T(8,128)(2,1)S(1)}, bf16[512,256]{1,0:T(8,128)(2,1)S(1)}, u32[]{:S(2)}, u32[]{:S(2)}) collective-permute-start(bf16[512,256]{1,0:T(8,128)(2,1)S(1)} %half_columns.1), channel_id=1, source_target_pairs={{0,2},{1,3},{2,0},{3,1},{4,6},{5,7},{6,4},{7,5},{8,10},{9,11},{10,... | collective-permute-start | bytes 786440 | tf_op jit(solution)/shard_map/ppermute | solution.py:703
  77.4 2.7 %collective-permute-start.40 = (bf16[264,512]{1,0:T(8,128)(2,1)S(1)}, bf16[264,512]{1,0:T(8,128)(2,1)S(1)}, u32[]{:S(2)}, u32[]{:S(2)}) collective-permute-start(bf16[264,512]{1,0:T(8,128)(2,1)S(1)} %merge_f.1.own), channel_id=1, source_target_pairs={{0,16},{4,20},{8,24},{12,28},{16,0},{20,4},{24,8},{28,12},{1,17},{... | collective-permute-start | bytes 811016 | tf_op jit(solution)/shard_map/ppermute | solution.py:706
  80.2 1.0 collective-permute-done.33.refs_3_
  81.2 0.7 quarters_a.1
  82.0 1.2 %collective-permute-start.36 = (bf16[96,512]{1,0:T(8,128)(2,1)S(1)}, bf16[96,512]{1,0:T(8,128)(2,1)S(1)}, u32[]{:S(2)}, u32[]{:S(2)}) collective-permute-start(bf16[96,512]{1,0:T(8,128)(2,1)S(1)} %get-tuple-element.282), channel_id=1, source_target_pairs={{0,4},{4,0},{8,12},{12,8},{16,20},{20,16},{24,28},{28,24},{1,5},{5... | collective-permute-start | bytes 294920 | tf_op jit(solution)/shard_map/ppermute | solution.py:706
  83.2 2.0 %last.1 = (f32[256,512]{1,0:T(8,128)}, f32[8,512]{1,0:T(8,128)S(1)}) custom-call(s32[8]{0:T(128)S(1)} %compare_select_fusion.pos.tb, f32[512,256]{1,0:T(8,128)S(1)} %get-tuple-element.254.own, bf16[512,512]{1,0:T(8,128)(2,1)S(1)} %collective-permute-done.29.recv.sib, bf16[512,256]{1,0:T(8,128)(2,1)S(1)} %collective-permute-done.34.par, ...), custom_call_target="tpu_custom_call" | custom-call | tf_op jit(solution)/shard_map/last/pallas_call | solution.py:44
  85.8 1.1 collective-permute-done.35.refs_1_
  87.1 1.3 %collective-permute-done.39.refs_7_ = f32[8,512]{1,0:T(8,128)S(1)} collective-permute-done((f32[8,512]{1,0:T(8,128)S(1)}, f32[8,512]{1,0:T(8,128)S(1)}, u32[]{:S(2)}, u32[]{:S(2)}) %collective-permute-start.39) | collective-permute-done | bytes 16416 | tf_op jit(solution)/shard_map/ppermute | solution.py:703
  89.6 2.8 %collective-permute-start.43 = (bf16[200,512]{1,0:T(8,128)(2,1)S(1)}, bf16[200,512]{1,0:T(8,128)(2,1)S(1)}, u32[]{:S(2)}, u32[]{:S(2)}) collective-permute-start(bf16[200,512]{1,0:T(8,128)(2,1)S(1)} %merge_a.1.own), channel_id=1, source_target_pairs={{0,16},{4,20},{8,24},{12,28},{16,0},{20,4},{24,8},{28,12},{1,17},{... | collective-permute-start | bytes 614408 | tf_op jit(solution)/shard_map/ppermute | solution.py:706
  93.0 2.0 %collective-permute-start.41 = (bf16[1,136,512]{2,1,0:T(8,128)(2,1)S(1)}, bf16[1,136,512]{2,1,0:T(8,128)(2,1)S(1)}, u32[]{:S(2)}, u32[]{:S(2)}) collective-permute-start(bf16[1,136,512]{2,1,0:T(8,128)(2,1)S(1)} %get-tuple-element.285.held1), channel_id=1, source_target_pairs={{0,8},{4,12},{8,0},{12,4},{16,24},{20,28},{24,16},{28,20},{1,9},{5... | collective-permute-start | bytes 417800 | tf_op jit(solution)/shard_map/ppermute | solution.py:706
  95.0 0.9 collective-permute-start.42
  95.8 4.1 %collective-permute-done.42.recv2 = bf16[1,128,512]{2,1,0:T(8,128)(2,1)S(1)} collective-permute-done((bf16[1,128,512]{2,1,0:T(8,128)(2,1)S(1)}, bf16[1,128,512]{2,1,0:T(8,128)(2,1)S(1)}, u32[]{:S(2)}, u32[]{:S(2)}) %collective-permute-start.42) | collective-permute-done | bytes 131104 | tf_op jit(solution)/shard_map/ppermute | solution.py:706
  100.5 1.5 %collective-permute-done.43.recv = bf16[200,512]{1,0:T(8,128)(2,1)S(1)} collective-permute-done((bf16[200,512]{1,0:T(8,128)(2,1)S(1)}, bf16[200,512]{1,0:T(8,128)(2,1)S(1)}, u32[]{:S(2)}, u32[]{:S(2)}) %collective-permute-start.43) | collective-permute-done | bytes 204832 | tf_op jit(solution)/shard_map/ppermute | solution.py:706
  102.6 1.0 collective-permute-start.44
  103.7 1.1 collective-permute-start.45
  104.7 0.9 collective-permute-start.46
  105.7 1.1 collective-permute-start.47
  106.7 2.7 %collective-permute-done.45.recv2 = bf16[1,96,512]{2,1,0:T(8,128)(2,1)S(1)} collective-permute-done((bf16[1,96,512]{2,1,0:T(8,128)(2,1)S(1)}, bf16[1,96,512]{2,1,0:T(8,128)(2,1)S(1)}, u32[]{:S(2)}, u32[]{:S(2)}) %collective-permute-start.45) | collective-permute-done | bytes 98336 | tf_op jit(solution)/shard_map/ppermute | solution.py:706
  110.0 1.2 collective-permute-start.48
  111.1 1.3 %collective-permute-start.49 = (bf16[2,96,512]{2,1,0:T(8,128)(2,1)S(1)}, bf16[2,96,512]{2,1,0:T(8,128)(2,1)S(1)}, u32[]{:S(2)}, u32[]{:S(2)}) collective-permute-start(bf16[2,96,512]{2,1,0:T(8,128)(2,1)S(1)} %get-tuple-element.298.held2), channel_id=1, source_target_pairs={{0,8},{4,12},{8,0},{12,4},{16,24},{20,28},{24,16},{28,20},{1,9},{5... | collective-permute-start | bytes 589832 | tf_op jit(solution)/shard_map/ppermute | solution.py:706
  112.4 2.5 %collective-permute-done.47.recv2 = bf16[2,128,512]{2,1,0:T(8,128)(2,1)S(1)} collective-permute-done((bf16[2,128,512]{2,1,0:T(8,128)(2,1)S(1)}, bf16[2,128,512]{2,1,0:T(8,128)(2,1)S(1)}, u32[]{:S(2)}, u32[]{:S(2)}) %collective-permute-start.47) | collective-permute-done | bytes 262176 | tf_op jit(solution)/shard_map/ppermute | solution.py:706
  115.4 2.1 %unpack_f.1 = (f32[512,512]{1,0:T(8,128)}, f32[512,512]{1,0:T(8,128)}, f32[512]{0:T(512)}, f32[512]{0:T(512)}) custom-call(s32[8]{0:T(128)S(1)} %compare_select_fusion.pos.tb, bf16[2,136,512]{2,1,0:T(8,128)(2,1)S(1)} %get-tuple-element.288.held1, bf16[2,136,512]{2,1,0:T(8,128)(2,1)S(1)} %collective-permute-done.46.recv1, ...), custom_call_target="tpu_custom_call" | custom-call | tf_op jit(solution)/shard_map/unpack_f/pallas_call | solution.py:44
  117.4 0.9 collective-permute-done.48.recv1
  118.4 2.0 %unpack_a.1 = (f32[512,128]{1,0:T(8,128)}, f32[512,128]{1,0:T(8,128)}, f32[512,128]{1,0:T(8,128)}, f32[128,512]{1,0:T(8,128)}, f32[128,512]{1,0:T(8,128)}, /*ind...) custom-call(s32[8]{0:T(128)S(1)} %compare_select_fusion.pos.tb, ...), custom_call_target="tpu_custom_call" | custom-call | flops 10000000000 | tf_op jit(solution)/shard_map/unpack_a/pallas_call | solution.py:44
  (80 shorter events, 12.4 us)
Async XLA Ops:
  0.7 8.3 %copy-start.2 = (bf16[256,512]{1,0:T(8,128)(2,1)S(1)}, bf16[256,512]{1,0:T(8,128)(2,1)}, u32[]{:S(2)}) copy-start(bf16[256,512]{1,0:T(8,128)(2,1)} %x0.5) | copy-start | bytes 786436
  0.7 10.1 %collective-permute-start.3 = (bf16[256,512]{1,0:T(8,128)(2,1)}, bf16[256,512]{1,0:T(8,128)(2,1)S(1)}, u32[]{:S(2)}, u32[]{:S(2)}) collective-permute-start(bf16[256,512]{1,0:T(8,128)(2,1)} %x0.5), channel_id=1, source_target_pairs={{0,2},{1,3},{2,0},{3,1},{4,6},{5,7},{6,4},{7,5},{8,10},{9,11},{10,... | collective-permute-start | bytes 786440 | tf_op jit(solution)/shard_map/ppermute | solution.py:703
  3.7 5.2 %collective-permute-start = (bf16[256,512]{1,0:T(8,128)(2,1)}, bf16[256,512]{1,0:T(8,128)(2,1)S(1)}, u32[]{:S(2)}, u32[]{:S(2)}) collective-permute-start(bf16[256,512]{1,0:T(8,128)(2,1)} %x0.5), channel_id=1, source_target_pairs={{0,1},{1,0},{2,3},{3,2},{4,5},{5,4},{6,7},{7,6},{8,9},{9,8},{10,11... | collective-permute-start | bytes 786440 | tf_op jit(solution)/shard_map/ppermute | solution.py:703
  4.4 9.1 %copy-start.5 = (s32[1,1024]{1,0:T(1,128)S(1)}, s32[1,1024]{1,0:T(1,128)}, u32[]{:S(2)}) copy-start(s32[1,1024]{1,0:T(1,128)} %segs.7) | copy-start | bytes 12292
  6.9 2.0 %collective-permute-start.2 = (bf16[264,384]{1,0:T(8,128)(2,1)S(1)}, bf16[264,384]{1,0:T(8,128)(2,1)S(1)}, u32[]{:S(2)}, u32[]{:S(2)}) collective-permute-start(bf16[264,384]{1,0:T(8,128)(2,1)S(1)} %get-tuple-element.173.qb0), channel_id=1, source_target_pairs={{0,1},{1,0},{2,3},{3,2},{4,5},{5,4},{6,7},{7,6},{8,9},{9,8},{10,11... | collective-permute-start | bytes 608264 | tf_op jit(solution)/shard_map/ppermute | solution.py:703
  7.5 1.4 %collective-permute-start.1 = (bf16[256,384]{1,0:T(8,128)(2,1)S(1)}, bf16[256,384]{1,0:T(8,128)(2,1)S(1)}, u32[]{:S(2)}, u32[]{:S(2)}) collective-permute-start(bf16[256,384]{1,0:T(8,128)(2,1)S(1)} %get-tuple-element.172.qa0), channel_id=1, source_target_pairs={{0,1},{1,0},{2,3},{3,2},{4,5},{5,4},{6,7},{7,6},{8,9},{9,8},{10,11... | collective-permute-start | bytes 589832 | tf_op jit(solution)/shard_map/ppermute | solution.py:703
  7.6 10.1 %collective-permute-start.9 = (bf16[296,512]{1,0:T(8,128)(2,1)S(1)}, bf16[296,512]{1,0:T(8,128)(2,1)S(1)}, u32[]{:S(2)}, u32[]{:S(2)}) collective-permute-start(bf16[296,512]{1,0:T(8,128)(2,1)S(1)} %get-tuple-element.169), channel_id=1, source_target_pairs={{0,2},{1,3},{2,0},{3,1},{4,6},{5,7},{6,4},{7,5},{8,10},{9,11},{10,... | collective-permute-start | bytes 909320 | tf_op jit(solution)/shard_map/ppermute | solution.py:703
  10.8 2.7 %collective-permute-start.4 = (bf16[256,512]{1,0:T(8,128)(2,1)S(1)}, bf16[256,512]{1,0:T(8,128)(2,1)S(1)}, u32[]{:S(2)}, u32[]{:S(2)}) collective-permute-start(bf16[256,512]{1,0:T(8,128)(2,1)S(1)} %collective-permute-done.3.x1), channel_id=1, source_target_pairs={{0,1},{1,0},{2,3},{3,2},{4,5},{5,4},{6,7},{7,6},{8,9},{9,8},{10,11... | collective-permute-start | bytes 786440 | tf_op jit(solution)/shard_map/ppermute | solution.py:703
  11.1 14.4 %collective-permute-start.7 = (bf16[1416,512]{1,0:T(8,128)(2,1)S(1)}, bf16[1416,512]{1,0:T(8,128)(2,1)S(1)}, u32[]{:S(2)}, u32[]{:S(2)}) collective-permute-start(bf16[1416,512]{1,0:T(8,128)(2,1)S(1)} %get-tuple-element.192), channel_id=1, source_target_pairs={{0,1},{1,0},{2,3},{3,2},{4,5},{5,4},{6,7},{7,6},{8,9},{9,8},{10,11... | collective-permute-start | bytes 4349960 | tf_op jit(solution)/shard_map/ppermute | solution.py:703
  11.3 11.8 %collective-permute-start.6 = (bf16[256,512]{1,0:T(8,128)(2,1)S(1)}, bf16[256,512]{1,0:T(8,128)(2,1)S(1)}, u32[]{:S(2)}, u32[]{:S(2)}) collective-permute-start(bf16[256,512]{1,0:T(8,128)(2,1)S(1)} %get-tuple-element.191.e0), channel_id=1, source_target_pairs={{0,2},{1,3},{2,0},{3,1},{4,6},{5,7},{6,4},{7,5},{8,10},{9,11},{10,... | collective-permute-start | bytes 786440 | tf_op jit(solution)/shard_map/ppermute | solution.py:703
  17.6 7.9 %collective-permute-start.5 = (bf16[256,256]{1,0:T(8,128)(2,1)S(1)}, bf16[256,256]{1,0:T(8,128)(2,1)S(1)}, u32[]{:S(2)}, u32[]{:S(2)}) collective-permute-start(bf16[256,256]{1,0:T(8,128)(2,1)S(1)} %get-tuple-element.189), channel_id=1, source_target_pairs={{0,2},{1,3},{2,0},{3,1},{4,6},{5,7},{6,4},{7,5},{8,10},{9,11},{10,... | collective-permute-start | bytes 393224 | tf_op jit(solution)/shard_map/ppermute | solution.py:703
  17.7 9.5 %collective-permute-start.11 = (bf16[296,512]{1,0:T(8,128)(2,1)S(1)}, bf16[296,512]{1,0:T(8,128)(2,1)S(1)}, u32[]{:S(2)}, u32[]{:S(2)}) collective-permute-start(bf16[296,512]{1,0:T(8,128)(2,1)S(1)} %collective-permute-done.9.s0), channel_id=1, source_target_pairs={{0,8},{4,12},{8,0},{12,4},{16,24},{20,28},{24,16},{28,20},{1,9},{5... | collective-permute-start | bytes 909320 | tf_op jit(solution)/shard_map/ppermute | solution.py:706
  19.1 9.1 %collective-permute-start.10 = (bf16[296,512]{1,0:T(8,128)(2,1)S(1)}, bf16[296,512]{1,0:T(8,128)(2,1)S(1)}, u32[]{:S(2)}, u32[]{:S(2)}) collective-permute-start(bf16[296,512]{1,0:T(8,128)(2,1)S(1)} %collective-permute-done.9.s0), channel_id=1, source_target_pairs={{0,4},{4,0},{8,12},{12,8},{16,20},{20,16},{24,28},{28,24},{1,5},{5... | collective-permute-start | bytes 909320 | tf_op jit(solution)/shard_map/ppermute | solution.py:706
  23.2 2.4 %collective-permute-start.8 = (bf16[256,512]{1,0:T(8,128)(2,1)S(1)}, bf16[256,512]{1,0:T(8,128)(2,1)S(1)}, u32[]{:S(2)}, u32[]{:S(2)}) collective-permute-start(bf16[256,512]{1,0:T(8,128)(2,1)S(1)} %collective-permute-done.6.e1), channel_id=1, source_target_pairs={{0,1},{1,0},{2,3},{3,2},{4,5},{5,4},{6,7},{7,6},{8,9},{9,8},{10,11... | collective-permute-start | bytes 786440 | tf_op jit(solution)/shard_map/ppermute | solution.py:703
  26.9 6.2 %copy-start = (bf16[512,512]{1,0:T(8,128)(2,1)S(1)}, bf16[512,512]{1,0:T(8,128)(2,1)}, u32[]{:S(2)}) copy-start(bf16[512,512]{1,0:T(8,128)(2,1)} %win0.5) | copy-start | bytes 1572868
  26.9 6.2 %copy-start.1 = (bf16[512,512]{1,0:T(8,128)(2,1)S(1)}, bf16[512,512]{1,0:T(8,128)(2,1)}, u32[]{:S(2)}) copy-start(bf16[512,512]{1,0:T(8,128)(2,1)} %wback0.5) | copy-start | bytes 1572868
  28.8 2.6 %collective-permute-start.12 = (bf16[296,512]{1,0:T(8,128)(2,1)S(1)}, bf16[296,512]{1,0:T(8,128)(2,1)S(1)}, u32[]{:S(2)}, u32[]{:S(2)}) collective-permute-start(bf16[296,512]{1,0:T(8,128)(2,1)S(1)} %collective-permute-done.9.s0), channel_id=1, source_target_pairs={{0,1},{1,0},{2,3},{3,2},{4,5},{5,4},{6,7},{7,6},{8,9},{9,8},{10,11... | collective-permute-start | bytes 909320 | tf_op jit(solution)/shard_map/ppermute | solution.py:703
  28.9 4.2 %collective-permute-start.13 = (bf16[296,512]{1,0:T(8,128)(2,1)S(1)}, bf16[296,512]{1,0:T(8,128)(2,1)S(1)}, u32[]{:S(2)}, u32[]{:S(2)}) collective-permute-start(bf16[296,512]{1,0:T(8,128)(2,1)S(1)} %collective-permute-done.10.sx.s2), channel_id=1, source_target_pairs={{0,1},{1,0},{2,3},{3,2},{4,5},{5,4},{6,7},{7,6},{8,9},{9,8},{10,11... | collective-permute-start | bytes 909320 | tf_op jit(solution)/shard_map/ppermute | solution.py:703
  29.4 3.7 %collective-permute-start.14 = (bf16[296,512]{1,0:T(8,128)(2,1)S(1)}, bf16[296,512]{1,0:T(8,128)(2,1)S(1)}, u32[]{:S(2)}, u32[]{:S(2)}) collective-permute-start(bf16[296,512]{1,0:T(8,128)(2,1)S(1)} %collective-permute-done.11.sz.s4), channel_id=1, source_target_pairs={{0,1},{1,0},{2,3},{3,2},{4,5},{5,4},{6,7},{7,6},{8,9},{9,8},{10,11... | collective-permute-start | bytes 909320 | tf_op jit(solution)/shard_map/ppermute | solution.py:703
  29.5 8.3 %copy-start.3 = (bf16[128,512]{1,0:T(8,128)(2,1)S(1)}, bf16[128,512]{1,0:T(8,128)(2,1)}, u32[]{:S(2)}) copy-start(bf16[128,512]{1,0:T(8,128)(2,1)} %g2.5) | copy-start | bytes 393220
  29.5 8.3 %copy-start.4 = (bf16[256,512]{1,0:T(8,128)(2,1)S(1)}, bf16[256,512]{1,0:T(8,128)(2,1)}, u32[]{:S(2)}) copy-start(bf16[256,512]{1,0:T(8,128)(2,1)} %ct.3) | copy-start | bytes 786436
  29.5 6.7 %collective-permute-start.16 = (bf16[168,512]{1,0:T(8,128)(2,1)S(1)}, bf16[168,512]{1,0:T(8,128)(2,1)S(1)}, u32[]{:S(2)}, u32[]{:S(2)}) collective-permute-start(bf16[168,512]{1,0:T(8,128)(2,1)S(1)} %get-tuple-element.205), channel_id=1, source_target_pairs={{0,8},{4,12},{8,0},{12,4},{16,24},{20,28},{24,16},{28,20},{1,9},{5... | collective-permute-start | bytes 516104 | tf_op jit(solution)/shard_map/ppermute | solution.py:706
  30.1 5.7 %collective-permute-start.15 = (bf16[128,512]{1,0:T(8,128)(2,1)S(1)}, bf16[128,512]{1,0:T(8,128)(2,1)S(1)}, u32[]{:S(2)}, u32[]{:S(2)}) collective-permute-start(bf16[128,512]{1,0:T(8,128)(2,1)S(1)} %get-tuple-element.197), channel_id=1, source_target_pairs={{0,4},{4,0},{8,12},{12,8},{16,20},{20,16},{24,28},{28,24},{1,5},{5... | collective-permute-start | bytes 393224 | tf_op jit(solution)/shard_map/ppermute | solution.py:706
  31.4 8.5 %collective-permute-start.19 = (bf16[256,512]{1,0:T(8,128)(2,1)S(1)}, bf16[256,512]{1,0:T(8,128)(2,1)S(1)}, u32[]{:S(2)}, u32[]{:S(2)}) collective-permute-start(bf16[256,512]{1,0:T(8,128)(2,1)S(1)} %get-tuple-element.209.n2), channel_id=1, source_target_pairs={{0,2},{1,3},{2,0},{3,1},{4,6},{5,7},{6,4},{7,5},{8,10},{9,11},{10,... | collective-permute-start | bytes 786440 | tf_op jit(solution)/shard_map/ppermute | solution.py:703
  36.2 1.6 %collective-permute-start.18 = (bf16[168,512]{1,0:T(8,128)(2,1)S(1)}, bf16[168,512]{1,0:T(8,128)(2,1)S(1)}, u32[]{:S(2)}, u32[]{:S(2)}) collective-permute-start(bf16[168,512]{1,0:T(8,128)(2,1)S(1)} %collective-permute-done.16.b6), channel_id=1, source_target_pairs={{0,1},{1,0},{2,3},{3,2},{4,5},{5,4},{6,7},{7,6},{8,9},{9,8},{10,11... | collective-permute-start | bytes 516104 | tf_op jit(solution)/shard_map/ppermute | solution.py:703
  36.2 1.6 %collective-permute-start.17 = (bf16[128,512]{1,0:T(8,128)(2,1)S(1)}, bf16[128,512]{1,0:T(8,128)(2,1)S(1)}, u32[]{:S(2)}, u32[]{:S(2)}) collective-permute-start(bf16[128,512]{1,0:T(8,128)(2,1)S(1)} %collective-permute-done.15.a6), channel_id=1, source_target_pairs={{0,1},{1,0},{2,3},{3,2},{4,5},{5,4},{6,7},{7,6},{8,9},{9,8},{10,11... | collective-permute-start | bytes 393224 | tf_op jit(solution)/shard_map/ppermute | solution.py:703
  39.9 9.3 %collective-permute-start.21 = (bf16[256,512]{1,0:T(8,128)(2,1)S(1)}, bf16[256,512]{1,0:T(8,128)(2,1)S(1)}, u32[]{:S(2)}, u32[]{:S(2)}) collective-permute-start(bf16[256,512]{1,0:T(8,128)(2,1)S(1)} %get-tuple-element.211.fg), channel_id=1, source_target_pairs={{0,2},{1,3},{2,0},{3,1},{4,6},{5,7},{6,4},{7,5},{8,10},{9,11},{10,... | collective-permute-start | bytes 786440 | tf_op jit(solution)/shard_map/ppermute | solution.py:703
  46.3 2.4 %collective-permute-start.20 = (bf16[776,512]{1,0:T(8,128)(2,1)S(1)}, bf16[776,512]{1,0:T(8,128)(2,1)S(1)}, u32[]{:S(2)}, u32[]{:S(2)}) collective-permute-start(bf16[776,512]{1,0:T(8,128)(2,1)S(1)} %get-tuple-element.230), channel_id=1, source_target_pairs={{0,1},{1,0},{2,3},{3,2},{4,5},{5,4},{6,7},{7,6},{8,9},{9,8},{10,11... | collective-permute-start | bytes 2383880 | tf_op jit(solution)/shard_map/ppermute | solution.py:703
  53.4 3.7 %collective-permute-start.23 = (bf16[520,512]{1,0:T(8,128)(2,1)S(1)}, bf16[520,512]{1,0:T(8,128)(2,1)S(1)}, u32[]{:S(2)}, u32[]{:S(2)}) collective-permute-start(bf16[520,512]{1,0:T(8,128)(2,1)S(1)} %get-tuple-element.240), channel_id=1, source_target_pairs={{0,1},{1,0},{2,3},{3,2},{4,5},{5,4},{6,7},{7,6},{8,9},{9,8},{10,11... | collective-permute-start | bytes 1597448 | tf_op jit(solution)/shard_map/ppermute | solution.py:703
  54.7 2.4 %collective-permute-start.22 = (bf16[512,512]{1,0:T(8,128)(2,1)S(1)}, bf16[512,512]{1,0:T(8,128)(2,1)S(1)}, u32[]{:S(2)}, u32[]{:S(2)}) collective-permute-start(bf16[512,512]{1,0:T(8,128)(2,1)S(1)} %get-tuple-element.239), channel_id=1, source_target_pairs={{0,1},{1,0},{2,3},{3,2},{4,5},{5,4},{6,7},{7,6},{8,9},{9,8},{10,11... | collective-permute-start | bytes 1572872 | tf_op jit(solution)/shard_map/ppermute | solution.py:703
  54.8 6.7 %collective-permute-start.24 = (bf16[256,256]{1,0:T(8,128)(2,1)S(1)}, bf16[256,256]{1,0:T(8,128)(2,1)S(1)}, u32[]{:S(2)}, u32[]{:S(2)}) collective-permute-start(bf16[256,256]{1,0:T(8,128)(2,1)S(1)} %get-tuple-element.244), channel_id=1, source_target_pairs={{0,2},{1,3},{2,0},{3,1},{4,6},{5,7},{6,4},{7,5},{8,10},{9,11},{10,... | collective-permute-start | bytes 393224 | tf_op jit(solution)/shard_map/ppermute | solution.py:703
  57.1 14.4 %collective-permute-start.28 = (bf16[392,512]{1,0:T(8,128)(2,1)S(1)}, bf16[392,512]{1,0:T(8,128)(2,1)S(1)}, u32[]{:S(2)}, u32[]{:S(2)}) collective-permute-start(bf16[392,512]{1,0:T(8,128)(2,1)S(1)} %half_rows.1), channel_id=1, source_target_pairs={{0,2},{1,3},{2,0},{3,1},{4,6},{5,7},{6,4},{7,5},{8,10},{9,11},{10,... | collective-permute-start | bytes 1204232 | tf_op jit(solution)/shard_map/ppermute | solution.py:703
  58.1 10.2 %collective-permute-start.25 = (bf16[256,512]{1,0:T(8,128)(2,1)S(1)}, bf16[256,512]{1,0:T(8,128)(2,1)S(1)}, u32[]{:S(2)}, u32[]{:S(2)}) collective-permute-start(bf16[256,512]{1,0:T(8,128)(2,1)S(1)} %get-tuple-element.256), channel_id=1, source_target_pairs={{0,4},{4,0},{8,12},{12,8},{16,20},{20,16},{24,28},{28,24},{1,5},{5... | collective-permute-start | bytes 786440 | tf_op jit(solution)/shard_map/ppermute | solution.py:706
  59.7 8.6 %collective-permute-start.26 = (bf16[256,512]{1,0:T(8,128)(2,1)S(1)}, bf16[256,512]{1,0:T(8,128)(2,1)S(1)}, u32[]{:S(2)}, u32[]{:S(2)}) collective-permute-start(bf16[256,512]{1,0:T(8,128)(2,1)S(1)} %get-tuple-element.258), channel_id=1, source_target_pairs={{0,8},{4,12},{8,0},{12,4},{16,24},{20,28},{24,16},{28,20},{1,9},{5... | collective-permute-start | bytes 786440 | tf_op jit(solution)/shard_map/ppermute | solution.py:706
  67.6 3.9 %collective-permute-start.27 = (bf16[392,512]{1,0:T(8,128)(2,1)S(1)}, bf16[392,512]{1,0:T(8,128)(2,1)S(1)}, u32[]{:S(2)}, u32[]{:S(2)}) collective-permute-start(bf16[392,512]{1,0:T(8,128)(2,1)S(1)} %get-tuple-element.262), channel_id=1, source_target_pairs={{0,1},{1,0},{2,3},{3,2},{4,5},{5,4},{6,7},{7,6},{8,9},{9,8},{10,11... | collective-permute-start | bytes 1204232 | tf_op jit(solution)/shard_map/ppermute | solution.py:703
  68.2 6.0 %collective-permute-start.29 = (bf16[512,512]{1,0:T(8,128)(2,1)S(1)}, bf16[512,512]{1,0:T(8,128)(2,1)S(1)}, u32[]{:S(2)}, u32[]{:S(2)}) collective-permute-start(bf16[512,512]{1,0:T(8,128)(2,1)S(1)} %get-tuple-element.266), channel_id=1, source_target_pairs={{0,1},{1,0},{2,3},{3,2},{4,5},{5,4},{6,7},{7,6},{8,9},{9,8},{10,11... | collective-permute-start | bytes 1572872 | tf_op jit(solution)/shard_map/ppermute | solution.py:703
  69.1 7.7 %collective-permute-start.30 = (bf16[128,512]{1,0:T(8,128)(2,1)S(1)}, bf16[128,512]{1,0:T(8,128)(2,1)S(1)}, u32[]{:S(2)}, u32[]{:S(2)}) collective-permute-start(bf16[128,512]{1,0:T(8,128)(2,1)S(1)} %get-tuple-element.268), channel_id=1, source_target_pairs={{0,8},{4,12},{8,0},{12,4},{16,24},{20,28},{24,16},{28,20},{1,9},{5... | collective-permute-start | bytes 393224 | tf_op jit(solution)/shard_map/ppermute | solution.py:706
  70.4 6.4 %collective-permute-start.31 = (bf16[128,512]{1,0:T(8,128)(2,1)S(1)}, bf16[128,512]{1,0:T(8,128)(2,1)S(1)}, u32[]{:S(2)}, u32[]{:S(2)}) collective-permute-start(bf16[128,512]{1,0:T(8,128)(2,1)S(1)} %get-tuple-element.270), channel_id=1, source_target_pairs={{0,4},{4,0},{8,12},{12,8},{16,20},{20,16},{24,28},{28,24},{1,5},{5... | collective-permute-start | bytes 393224 | tf_op jit(solution)/shard_map/ppermute | solution.py:706
  72.5 7.7 %collective-permute-start.32 = (bf16[192,512]{1,0:T(8,128)(2,1)S(1)}, bf16[192,512]{1,0:T(8,128)(2,1)S(1)}, u32[]{:S(2)}, u32[]{:S(2)}) collective-permute-start(bf16[192,512]{1,0:T(8,128)(2,1)S(1)} %get-tuple-element.272), channel_id=1, source_target_pairs={{0,4},{4,0},{8,12},{12,8},{16,20},{20,16},{24,28},{28,24},{1,5},{5... | collective-permute-start | bytes 589832 | tf_op jit(solution)/shard_map/ppermute | solution.py:706
  73.5 7.7 %collective-permute-start.33 = (bf16[192,512]{1,0:T(8,128)(2,1)S(1)}, bf16[192,512]{1,0:T(8,128)(2,1)S(1)}, u32[]{:S(2)}, u32[]{:S(2)}) collective-permute-start(bf16[192,512]{1,0:T(8,128)(2,1)S(1)} %get-tuple-element.274), channel_id=1, source_target_pairs={{0,8},{4,12},{8,0},{12,4},{16,24},{20,28},{24,16},{28,20},{1,9},{5... | collective-permute-start | bytes 589832 | tf_op jit(solution)/shard_map/ppermute | solution.py:706
  74.8 8.4 %collective-permute-start.34 = (bf16[512,256]{1,0:T(8,128)(2,1)S(1)}, bf16[512,256]{1,0:T(8,128)(2,1)S(1)}, u32[]{:S(2)}, u32[]{:S(2)}) collective-permute-start(bf16[512,256]{1,0:T(8,128)(2,1)S(1)} %half_columns.1), channel_id=1, source_target_pairs={{0,2},{1,3},{2,0},{3,1},{4,6},{5,7},{6,4},{7,5},{8,10},{9,11},{10,... | collective-permute-start | bytes 786440 | tf_op jit(solution)/shard_map/ppermute | solution.py:703
  77.4 15.0 %collective-permute-start.40 = (bf16[264,512]{1,0:T(8,128)(2,1)S(1)}, bf16[264,512]{1,0:T(8,128)(2,1)S(1)}, u32[]{:S(2)}, u32[]{:S(2)}) collective-permute-start(bf16[264,512]{1,0:T(8,128)(2,1)S(1)} %merge_f.1.own), channel_id=1, source_target_pairs={{0,16},{4,20},{8,24},{12,28},{16,0},{20,4},{24,8},{28,12},{1,17},{... | collective-permute-start | bytes 811016 | tf_op jit(solution)/shard_map/ppermute | solution.py:706
  81.9 4.9 %collective-permute-start.35 = (bf16[96,512]{1,0:T(8,128)(2,1)S(1)}, bf16[96,512]{1,0:T(8,128)(2,1)S(1)}, u32[]{:S(2)}, u32[]{:S(2)}) collective-permute-start(bf16[96,512]{1,0:T(8,128)(2,1)S(1)} %get-tuple-element.280), channel_id=1, source_target_pairs={{0,8},{4,12},{8,0},{12,4},{16,24},{20,28},{24,16},{28,20},{1,9},{5... | collective-permute-start | bytes 294920 | tf_op jit(solution)/shard_map/ppermute | solution.py:706
  82.0 5.1 %collective-permute-start.36 = (bf16[96,512]{1,0:T(8,128)(2,1)S(1)}, bf16[96,512]{1,0:T(8,128)(2,1)S(1)}, u32[]{:S(2)}, u32[]{:S(2)}) collective-permute-start(bf16[96,512]{1,0:T(8,128)(2,1)S(1)} %get-tuple-element.282), channel_id=1, source_target_pairs={{0,4},{4,0},{8,12},{12,8},{16,20},{20,16},{24,28},{28,24},{1,5},{5... | collective-permute-start | bytes 294920 | tf_op jit(solution)/shard_map/ppermute | solution.py:706
  85.2 3.2 %collective-permute-start.39 = (f32[8,512]{1,0:T(8,128)S(1)}, f32[8,512]{1,0:T(8,128)S(1)}, u32[]{:S(2)}, u32[]{:S(2)}) collective-permute-start(f32[8,512]{1,0:T(8,128)S(1)} %get-tuple-element.283.refs_4_), channel_id=1, source_target_pairs={{0,3},{1,2},{2,1},{3,0},{4,7},{5,6},{6,5},{7,4},{8,11},{9,10},{10,... | collective-permute-start | bytes 49160 | tf_op jit(solution)/shard_map/ppermute | solution.py:703
  85.2 3.8 %collective-permute-start.38 = (f32[8,512]{1,0:T(8,128)S(1)}, f32[8,512]{1,0:T(8,128)S(1)}, u32[]{:S(2)}, u32[]{:S(2)}) collective-permute-start(f32[8,512]{1,0:T(8,128)S(1)} %get-tuple-element.283.refs_4_), channel_id=1, source_target_pairs={{0,2},{1,3},{2,0},{3,1},{4,6},{5,7},{6,4},{7,5},{8,10},{9,11},{10,... | collective-permute-start | bytes 49160 | tf_op jit(solution)/shard_map/ppermute | solution.py:703
  86.8 2.2 %collective-permute-start.37 = (f32[8,512]{1,0:T(8,128)S(1)}, f32[8,512]{1,0:T(8,128)S(1)}, u32[]{:S(2)}, u32[]{:S(2)}) collective-permute-start(f32[8,512]{1,0:T(8,128)S(1)} %get-tuple-element.283.refs_4_), channel_id=1, source_target_pairs={{0,1},{1,0},{2,3},{3,2},{4,5},{5,4},{6,7},{7,6},{8,9},{9,8},{10,11... | collective-permute-start | bytes 49160 | tf_op jit(solution)/shard_map/ppermute | solution.py:703
  89.6 12.4 %collective-permute-start.43 = (bf16[200,512]{1,0:T(8,128)(2,1)S(1)}, bf16[200,512]{1,0:T(8,128)(2,1)S(1)}, u32[]{:S(2)}, u32[]{:S(2)}) collective-permute-start(bf16[200,512]{1,0:T(8,128)(2,1)S(1)} %merge_a.1.own), channel_id=1, source_target_pairs={{0,16},{4,20},{8,24},{12,28},{16,0},{20,4},{24,8},{28,12},{1,17},{... | collective-permute-start | bytes 614408 | tf_op jit(solution)/shard_map/ppermute | solution.py:706
  93.0 7.0 %collective-permute-start.41 = (bf16[1,136,512]{2,1,0:T(8,128)(2,1)S(1)}, bf16[1,136,512]{2,1,0:T(8,128)(2,1)S(1)}, u32[]{:S(2)}, u32[]{:S(2)}) collective-permute-start(bf16[1,136,512]{2,1,0:T(8,128)(2,1)S(1)} %get-tuple-element.285.held1), channel_id=1, source_target_pairs={{0,8},{4,12},{8,0},{12,4},{16,24},{20,28},{24,16},{28,20},{1,9},{5... | collective-permute-start | bytes 417800 | tf_op jit(solution)/shard_map/ppermute | solution.py:706
  95.0 5.0 %collective-permute-start.42 = (bf16[1,128,512]{2,1,0:T(8,128)(2,1)S(1)}, bf16[1,128,512]{2,1,0:T(8,128)(2,1)S(1)}, u32[]{:S(2)}, u32[]{:S(2)}) collective-permute-start(bf16[1,128,512]{2,1,0:T(8,128)(2,1)S(1)} %get-tuple-element.287.held2), channel_id=1, source_target_pairs={{0,4},{4,0},{8,12},{12,8},{16,20},{20,16},{24,28},{28,24},{1,5},{5... | collective-permute-start | bytes 393224 | tf_op jit(solution)/shard_map/ppermute | solution.py:706
  102.6 6.8 %collective-permute-start.44 = (bf16[1,104,512]{2,1,0:T(8,128)(2,1)S(1)}, bf16[1,104,512]{2,1,0:T(8,128)(2,1)S(1)}, u32[]{:S(2)}, u32[]{:S(2)}) collective-permute-start(bf16[1,104,512]{2,1,0:T(8,128)(2,1)S(1)} %get-tuple-element.290.held1), channel_id=1, source_target_pairs={{0,8},{4,12},{8,0},{12,4},{16,24},{20,28},{24,16},{28,20},{1,9},{5... | collective-permute-start | bytes 319496 | tf_op jit(solution)/shard_map/ppermute | solution.py:706
  103.7 5.7 %collective-permute-start.45 = (bf16[1,96,512]{2,1,0:T(8,128)(2,1)S(1)}, bf16[1,96,512]{2,1,0:T(8,128)(2,1)S(1)}, u32[]{:S(2)}, u32[]{:S(2)}) collective-permute-start(bf16[1,96,512]{2,1,0:T(8,128)(2,1)S(1)} %get-tuple-element.292.held2), channel_id=1, source_target_pairs={{0,4},{4,0},{8,12},{12,8},{16,20},{20,16},{24,28},{28,24},{1,5},{5... | collective-permute-start | bytes 294920 | tf_op jit(solution)/shard_map/ppermute | solution.py:706
  104.7 10.6 %collective-permute-start.46 = (bf16[2,136,512]{2,1,0:T(8,128)(2,1)S(1)}, bf16[2,136,512]{2,1,0:T(8,128)(2,1)S(1)}, u32[]{:S(2)}, u32[]{:S(2)}) collective-permute-start(bf16[2,136,512]{2,1,0:T(8,128)(2,1)S(1)} %get-tuple-element.288.held1), channel_id=1, source_target_pairs={{0,4},{4,0},{8,12},{12,8},{16,20},{20,16},{24,28},{28,24},{1,5},{5... | collective-permute-start | bytes 835592 | tf_op jit(solution)/shard_map/ppermute | solution.py:706
  105.7 9.2 %collective-permute-start.47 = (bf16[2,128,512]{2,1,0:T(8,128)(2,1)S(1)}, bf16[2,128,512]{2,1,0:T(8,128)(2,1)S(1)}, u32[]{:S(2)}, u32[]{:S(2)}) collective-permute-start(bf16[2,128,512]{2,1,0:T(8,128)(2,1)S(1)} %get-tuple-element.295.held2), channel_id=1, source_target_pairs={{0,8},{4,12},{8,0},{12,4},{16,24},{20,28},{24,16},{28,20},{1,9},{5... | collective-permute-start | bytes 786440 | tf_op jit(solution)/shard_map/ppermute | solution.py:706
  110.0 8.4 %collective-permute-start.48 = (bf16[2,104,512]{2,1,0:T(8,128)(2,1)S(1)}, bf16[2,104,512]{2,1,0:T(8,128)(2,1)S(1)}, u32[]{:S(2)}, u32[]{:S(2)}) collective-permute-start(bf16[2,104,512]{2,1,0:T(8,128)(2,1)S(1)} %get-tuple-element.293.held1), channel_id=1, source_target_pairs={{0,4},{4,0},{8,12},{12,8},{16,20},{20,16},{24,28},{28,24},{1,5},{5... | collective-permute-start | bytes 638984 | tf_op jit(solution)/shard_map/ppermute | solution.py:706
  111.1 6.3 %collective-permute-start.49 = (bf16[2,96,512]{2,1,0:T(8,128)(2,1)S(1)}, bf16[2,96,512]{2,1,0:T(8,128)(2,1)S(1)}, u32[]{:S(2)}, u32[]{:S(2)}) collective-permute-start(bf16[2,96,512]{2,1,0:T(8,128)(2,1)S(1)} %get-tuple-element.298.held2), channel_id=1, source_target_pairs={{0,8},{4,12},{8,0},{12,4},{16,24},{20,28},{24,16},{28,20},{1,9},{5... | collective-permute-start | bytes 589832 | tf_op jit(solution)/shard_map/ppermute | solution.py:706

commit v6 on v5

--- a/solution.py
+++ b/solution.py
@@ -18,7 +18,8 @@
 SPARE = 4 * 1024 * 1024
 HEAVY = 10**10
 LIGHT = 0
-COSTS = {"halves_f": 0, "halves_a": 0, "input_grad": 0, "pair_a": 2*10**10, "part_f": 0, "merge_a": 0, "last": 0, "pair_f": 0, "part_a": 0,"unpack_f":0, "first": 0, "ffn": 0}
+AHEAD = ("a", "f")
+COSTS = {"halves_f": 0, "halves_a": 0, "input_grad": 0, "part_f": 0, "merge_a": 0, "last": 0, "first": 0, "ffn": 0, "part_a": 0, "unpack_f": 2*10**10}
 
 
 def nn(a, b):
@@ -670,16 +671,17 @@
         out[size:] = r[...]
 
 
-def unpack_kernel(pos, held1, recv1, held2, recv2, *refs, plans, orders, small):
+def unpack_kernel(pos, *refs, count, plans, orders, small):
+    blocks1, blocks2, refs = refs[:count], refs[count : 2 * count], refs[2 * count :]
     outs, scratch, sums = refs[:-2], refs[-2], refs[-1]
-    rows = held2.shape[1]
+    rows = blocks2[0].shape[1]
     used = 0
-    for plan, order, blocks in zip(plans, orders, ((held1, recv1), (held2, recv2))):
+    for plan, order, blocks in zip(plans, orders, (blocks1, blocks2)):
         place = 0
         for b in order:
             place = place * 2 + bit_of(pos, b)
         each = blocks[0].shape[0]
-        for i in range(2 * each):
+        for i in range(count * each):
             at = pl.multiple_of((place ^ i) * rows, 8)
             scratch[pl.ds(at, rows), :] = blocks[i // each][i % each, 0:rows, :].astype(F32)
         for start, size, flip in plan:
@@ -687,7 +689,7 @@
             outs[used][...] = block.T if flip else block
             used += 1
     total = jnp.zeros((8, 512), F32)
-    for r in (held1, recv1):
+    for r in blocks1:
         total = total + jnp.sum(r[:, rows:, :].astype(F32), axis=0)
     sums[...] = total
     for i, (row, start, size) in enumerate(small):
@@ -889,6 +891,10 @@
         else:
             size, kernel, args = 1, settle_part_kernel, [own, recv]
         h1, h2 = step(kernel, [sds((size, rows + 8, 512), BF16), sds((size, rows, 512), BF16)], args, "part_" + tag)
+        if tag in AHEAD:
+            far1, far2 = dhop(h1, 1), dhop(h2, 2)
+            r1, r2 = dhop(h1, 2), dhop(h2, 1)
+            return h1, r1, far1, h2, r2, far2
         return h1, dhop(h1, 2), h2, dhop(h2, 1)
 
     def pair_step(tag, h1, r1, h2, r2):
@@ -896,13 +902,16 @@
         h1, h2 = step(pair_kernel, shapes, [h1, r1, h2, r2], "pair_" + tag)
         return h1, dhop(h1, 1), h2, dhop(h2, 2)
 
-    def unpack_step(tag, h1, r1, h2, r2, plans, small):
+    def unpack_step(tag, blocks, plans, small):
         shapes = [sds((512, size) if flip else (size, 512), F32) for plan in plans for _, size, flip in plan]
         rest = tuple(range(2, bits - 1))
-        rows = 2 * h2.shape[0] * h2.shape[1]
+        half = len(blocks) // 2
+        rows = half * blocks[half].shape[0] * blocks[half].shape[1]
         return step(
-            functools.partial(unpack_kernel, plans=plans, orders=((0, 1) + rest, (1, 0) + rest), small=small),
-            shapes + [sds((size,), F32) for _, _, size in small], [h1, r1, h2, r2], "unpack_" + tag,
+            functools.partial(
+                unpack_kernel, count=half, plans=plans, orders=((0, 1) + rest, (1, 0) + rest), small=small
+            ),
+            shapes + [sds((size,), F32) for _, _, size in small], list(blocks), "unpack_" + tag,
             [pltpu.VMEM((rows, 512), F32), pltpu.VMEM((8, 512), F32)],
         )
 
@@ -950,11 +959,16 @@
          (3, 5, group)],
     )
     f = part_step("f", *f)
-    f = pair_step("f", *f)
+    h1, r1, far1, h2, r2, far2 = f
+    f = [h1, r1, far1, dhop(r1, 1), h2, r2, far2, dhop(r2, 2)]
     a = part_step("a", *a)
-    a = pair_step("a", *a)
+    if "a" in AHEAD:
+        h1, r1, far1, h2, r2, far2 = a
+        a = [h1, r1, far1, dhop(r1, 1), h2, r2, far2, dhop(r2, 2)]
+    else:
+        a = pair_step("a", *a)
     g_wback, g_win, d_b_in, d_n2b = unpack_step(
-        "f", *f, (((0, 512, False),), ((0, 512, False),)), ((0, 0, 512), (1, 0, 512))
+        "f", f, (((0, 512, False),), ((0, 512, False),)), ((0, 0, 512), (1, 0, 512))
     )
     plans = (
         ((0, 128, True), (128, 128, True), (256, 128, True)),
@@ -962,7 +976,7 @@
     )
     small = ((0, 0, 512), (1, 0, 512), (2, 0, 128), (2, 128, 128)) + tuple((i, 0, 512) for i in range(3, 8))
     g_q, g_k, g_v, g_g2, g_g1, g_wo, d_n1g, d_n1b, d_bq, d_bv, d_b_back, d_g2b, d_b_out, d_g1b, d_n2g = unpack_step(
-        "a", *a, plans, small
+        "a", a, plans, small
     )
     return (
         result, input_grad, d_n1g, d_n1b, g_q, d_bq, g_k, g_v, d_bv, g_wo, d_b_out, g_g1, d_g1b, d_n2g, d_n2b,

time: 121 us -> 119 us (0.983)
  waiting for transfers between devices: 23.5 us -> 19.1 us
  starting transfers between devices: 45.9 us -> 49.4 us
    ppermute x22 -> x26, waiting for transfers between devices: 16 us -> 11.6 us  [dhop(): return lax.ppermute(value, 'dp', [(i, i ^ mask) for i in range(n_dp)])]
    ppermute x22 -> x26, starting transfers between devices: 27.6 us -> 31.1 us  [dhop(): return lax.ppermute(value, 'dp', [(i, i ^ mask) for i in range(n_dp)])]
    pallas_call x31 -> x29, Pallas kernels: 49.4 us -> 48.2 us  [call(): pl.pallas_call(body, out_shape=tuple(outs), in_specs=[SM] * smem + [space...]
  transfers between devices with their start and end apart: 50 -> 54, of which waited for: 20 -> 19; matrix products, arithmetic and copies ran while one was open for 1% -> 1% of each run, Pallas kernels for 35% -> 35%
where the time goes in v6:
time: 119 us; the launch traced here: 118 us
  starting transfers between devices  49.4 us (42%)
  Pallas kernels  48.2 us (41%)
  waiting for transfers between devices  19.1 us (16%)
    pallas_call x29, Pallas kernels, call(): pl.pallas_call(body, out_shape=tuple(outs), in_specs=[SM] * smem + [space...  48.2 us
    ppermute x26, starting transfers between devices, dhop(): return lax.ppermute(value, 'dp', [(i, i ^ mask) for i in range(n_dp)])  31.1 us
    ppermute x28, starting transfers between devices, hop(): return lax.ppermute(value, 'tensor', [(i, i ^ mask) for i in range(4)])  18.3 us
    ppermute x26, waiting for transfers between devices, dhop(): return lax.ppermute(value, 'dp', [(i, i ^ mask) for i in range(n_dp)])  11.6 us
    ppermute x28, waiting for transfers between devices, hop(): return lax.ppermute(value, 'tensor', [(i, i ^ mask) for i in range(4)])  7.41 us
  transfers between devices with their start and end apart: 54, of which 19 were waited for; matrix products, arithmetic and copies ran while one was open for 1% of the time, Pallas kernels for 35%

profile of v6, /device:TPU:0, one launch (start us, length us, event | category | flops | bytes accessed | tf_op | source)
XLA Modules:
  0.0 118.5 jit_solution(610866299331897748)
XLA Ops:
  0.7 3.0 %collective-permute-start.3 = (bf16[256,512]{1,0:T(8,128)(2,1)}, bf16[256,512]{1,0:T(8,128)(2,1)S(1)}, u32[]{:S(2)}, u32[]{:S(2)}) collective-permute-start(bf16[256,512]{1,0:T(8,128)(2,1)} %x0.5), channel_id=1, source_target_pairs={{0,2},{1,3},{2,0},{3,1},{4,6},{5,7},{6,4},{7,5},{8,10},{9,11},{10,... | collective-permute-start | bytes 786440 | tf_op jit(solution)/shard_map/ppermute | solution.py:705
  4.4 2.5 %pack.1 = (bf16[296,512]{1,0:T(8,128)(2,1)S(1)}, bf16[256,512]{1,0:T(8,128)(2,1)S(1)}, bf16[1416,512]{1,0:T(8,128)(2,1)S(1)}, bf16[256,384]{1,0:T(8,128)(2,1)S(1...) custom-call(s32[8]{0:T(128)S(1)} %compare_select_fusion.pos.tb, bf16[512,512]{1,0:T(8,128)(2,1)} %win0.5, ...), custom_call_target="tpu_custom_call" | custom-call | tf_op jit(solution)/shard_map/pack/pallas_call | solution.py:45
  7.7 1.3 %collective-permute-done.1.qa1 = bf16[256,384]{1,0:T(8,128)(2,1)S(1)} collective-permute-done((bf16[256,384]{1,0:T(8,128)(2,1)S(1)}, bf16[256,384]{1,0:T(8,128)(2,1)S(1)}, u32[]{:S(2)}, u32[]{:S(2)}) %collective-permute-start.1) | collective-permute-done | bytes 196640 | tf_op jit(solution)/shard_map/ppermute | solution.py:705
  8.9 1.8 %chip.1 = (bf16[512,512]{1,0:T(8,128)(2,1)S(1)}, bf16[256,256]{1,0:T(8,128)(2,1)S(1)}, bf16[512,256]{1,0:T(8,128)(2,1)S(1)}, bf16[256,512]{1,0:T(8,128)(2,1)S(1)}) custom-call(s32[8]{0:T(128)S(1)} %compare_select_fusion.pos.tb, bf16[256,512]{1,0:T(8,128)(2,1)S(1)} %copy-done.2, bf16[256,512]{1,0:T(8,128)(2,1)S(1)} %collective-permute-done.x2, ...), custom_call_target="tpu_custom_call" | custom-call | tf_op jit(solution)/shard_map/chip/pallas_call | solution.py:45
  11.3 2.1 %collective-permute-start.6 = (bf16[256,512]{1,0:T(8,128)(2,1)S(1)}, bf16[256,512]{1,0:T(8,128)(2,1)S(1)}, u32[]{:S(2)}, u32[]{:S(2)}) collective-permute-start(bf16[256,512]{1,0:T(8,128)(2,1)S(1)} %get-tuple-element.185.e0), channel_id=1, source_target_pairs={{0,2},{1,3},{2,0},{3,1},{4,6},{5,7},{6,4},{7,5},{8,10},{9,11},{10,... | collective-permute-start | bytes 786440 | tf_op jit(solution)/shard_map/ppermute | solution.py:705
  13.5 4.1 %first.1 = (bf16[1024,512]{1,0:T(8,128)(2,1)S(1)}, bf16[256,256]{1,0:T(8,128)(2,1)S(1)}, bf16[1024,256]{1,0:T(8,128)(2,1)S(1)}, bf16[256,1024]{1,0:T(8,128)(2,1)...) custom-call(s32[8]{0:T(128)S(1)} %compare_select_fusion.pos.tb, ...), custom_call_target="tpu_custom_call" | custom-call | tf_op jit(solution)/shard_map/first/pallas_call | solution.py:45
  17.7 1.4 %collective-permute-start.11 = (bf16[296,512]{1,0:T(8,128)(2,1)S(1)}, bf16[296,512]{1,0:T(8,128)(2,1)S(1)}, u32[]{:S(2)}, u32[]{:S(2)}) collective-permute-start(bf16[296,512]{1,0:T(8,128)(2,1)S(1)} %collective-permute-done.9.s0), channel_id=1, source_target_pairs={{0,8},{4,12},{8,0},{12,4},{16,24},{20,28},{24,16},{28,20},{1,9},{5... | collective-permute-start | bytes 909320 | tf_op jit(solution)/shard_map/ppermute | solution.py:708
  19.1 1.5 %collective-permute-start.10 = (bf16[296,512]{1,0:T(8,128)(2,1)S(1)}, bf16[296,512]{1,0:T(8,128)(2,1)S(1)}, u32[]{:S(2)}, u32[]{:S(2)}) collective-permute-start(bf16[296,512]{1,0:T(8,128)(2,1)S(1)} %collective-permute-done.9.s0), channel_id=1, source_target_pairs={{0,4},{4,0},{8,12},{12,8},{16,20},{20,16},{24,28},{28,24},{1,5},{5... | collective-permute-start | bytes 909320 | tf_op jit(solution)/shard_map/ppermute | solution.py:708
  20.6 1.6 %second.1 = (bf16[4,1024,256]{2,1,0:T(8,128)(2,1)S(1)}, bf16[256,256]{1,0:T(8,128)(2,1)S(1)}, bf16[256,256]{1,0:T(8,128)(2,1)S(1)}, f32[4,8,256]{2,1,0:T(8,128)S(1)}) custom-call(s32[8]{0:T(128)S(1)} %compare_select_fusion.pos.tb, s32[1,1024]{1,0:T(1,128)S(1)} %copy-done.5, s32[1,1024]{1,0:T(1,128)S(1)} %copy-done.5, ...), custom_call_target="tpu_custom_call" | custom-call | flops 10000000000 | tf_op jit(solution)/shard_map/second/pallas_call | solution.py:45
  22.3 0.9 collective-permute-done.6.e1
  23.2 1.2 %prepare.1 = (bf16[1024,256]{1,0:T(8,128)(2,1)S(1)}, bf16[256,1024]{1,0:T(8,128)(2,1)S(1)}) custom-call(s32[8]{0:T(128)S(1)} %compare_select_fusion.pos.tb, bf16[1024,512]{1,0:T(8,128)(2,1)S(1)} %get-tuple-element.173.n, bf16[1024,256]{1,0:T(8,128)(2,1)S(1)} %get-tuple-element.176.k, bf16[256,384]{1,0:T(8,128)(2,1)S(1)} %get-tuple-element.166.qa0, ...), custom_call_target="tpu_custom_call" | custom-call | flops 10000000000 | tf_op jit(solution)/shard_map/prepare/pallas_call | solution.py:45
  24.4 1.1 collective-permute-done.5.attp
  25.5 1.4 %out.1 = (bf16[256,512]{1,0:T(8,128)(2,1)S(1)}, f32[256,512]{1,0:T(8,128)S(1)}, f32[256,512]{1,0:T(8,128)S(1)}, f32[256,512]{1,0:T(8,128)S(1)}) custom-call(s32[8]{0:T(128)S(1)} %compare_select_fusion.pos.tb, bf16[256,512]{1,0:T(8,128)(2,1)S(1)} %copy-done.2, bf16[1024,512]{1,0:T(8,128)(2,1)S(1)} %get-tuple-element.173.n, ...), custom_call_target="tpu_custom_call" | custom-call | flops 10000000000 | tf_op jit(solution)/shard_map/out/pallas_call | solution.py:45
  27.2 1.1 collective-permute-done.10.sx.s2
  30.1 1.3 %collective-permute-start.15 = (bf16[128,512]{1,0:T(8,128)(2,1)S(1)}, bf16[128,512]{1,0:T(8,128)(2,1)S(1)}, u32[]{:S(2)}, u32[]{:S(2)}) collective-permute-start(bf16[128,512]{1,0:T(8,128)(2,1)S(1)} %get-tuple-element.191), channel_id=1, source_target_pairs={{0,4},{4,0},{8,12},{12,8},{16,20},{20,16},{24,28},{28,24},{1,5},{5... | collective-permute-start | bytes 393224 | tf_op jit(solution)/shard_map/ppermute | solution.py:708
  31.4 1.7 %collective-permute-start.19 = (bf16[256,512]{1,0:T(8,128)(2,1)S(1)}, bf16[256,512]{1,0:T(8,128)(2,1)S(1)}, u32[]{:S(2)}, u32[]{:S(2)}) collective-permute-start(bf16[256,512]{1,0:T(8,128)(2,1)S(1)} %get-tuple-element.203.n2), channel_id=1, source_target_pairs={{0,2},{1,3},{2,0},{3,1},{4,6},{5,7},{6,4},{7,5},{8,10},{9,11},{10,... | collective-permute-start | bytes 786440 | tf_op jit(solution)/shard_map/ppermute | solution.py:705
  33.1 2.7 %ffn_first.1 = (f32[256,512]{1,0:T(8,128)S(1)}, bf16[256,1024]{1,0:T(8,128)(2,1)S(1)}, bf16[256,1024]{1,0:T(8,128)(2,1)S(1)}, bf16[256,768]{1,0:T(8,128)(2,1)S(1)}) custom-call(s32[8]{0:T(128)S(1)} %compare_select_fusion.pos.tb, bf16[256,512]{1,0:T(8,128)(2,1)S(1)} %get-tuple-element.203.n2, f32[16,512]{1,0:T(8,128)S(1)} %get-tuple-element.165.vecs, ...), custom_call_target="tpu_custom_call" | custom-call | tf_op jit(solution)/shard_map/ffn_first/pallas_call | solution.py:45
  36.7 1.1 collective-permute-done.17.a7
  37.8 2.1 %ffn.1 = (bf16[256,512]{1,0:T(8,128)(2,1)}, bf16[256,512]{1,0:T(8,128)(2,1)S(1)}, bf16[256,512]{1,0:T(8,128)(2,1)S(1)}, bf16[256,256]{1,0:T(8,128)(2,1)S(1)}) custom-call(s32[8]{0:T(128)S(1)} %compare_select_fusion.pos.tb, bf16[256,512]{1,0:T(8,128)(2,1)S(1)} %get-tuple-element.203.n2, f32[256,512]{1,0:T(8,128)S(1)} %get-tuple-element.198.mid, ...), custom_call_target="tpu_custom_call" | custom-call | tf_op jit(solution)/shard_map/ffn/pallas_call | solution.py:45
  39.9 1.7 %collective-permute-start.21 = (bf16[256,512]{1,0:T(8,128)(2,1)S(1)}, bf16[256,512]{1,0:T(8,128)(2,1)S(1)}, u32[]{:S(2)}, u32[]{:S(2)}) collective-permute-start(bf16[256,512]{1,0:T(8,128)(2,1)S(1)} %get-tuple-element.205.fg), channel_id=1, source_target_pairs={{0,2},{1,3},{2,0},{3,1},{4,6},{5,7},{6,4},{7,5},{8,10},{9,11},{10,... | collective-permute-start | bytes 786440 | tf_op jit(solution)/shard_map/ppermute | solution.py:705
  41.6 3.4 %back.1 = (bf16[256,256]{1,0:T(8,128)(2,1)S(1)}, bf16[256,256]{1,0:T(8,128)(2,1)S(1)}, f32[256,512]{1,0:T(8,128)S(1)}, bf16[256,512]{1,0:T(8,128)(2,1)S(1)}, bf1...) custom-call(s32[8]{0:T(128)S(1)} %compare_select_fusion.pos.tb, ...), custom_call_target="tpu_custom_call" | custom-call | flops 10000000000 | tf_op jit(solution)/shard_map/back/pallas_call | solution.py:45
  45.1 1.2 %small_weight.1 = (f32[776,512]{1,0:T(8,128)S(1)}, bf16[776,512]{1,0:T(8,128)(2,1)S(1)}) custom-call(s32[8]{0:T(128)S(1)} %compare_select_fusion.pos.tb, bf16[1024,512]{1,0:T(8,128)(2,1)S(1)} %get-tuple-element.173.n, bf16[256,512]{1,0:T(8,128)(2,1)S(1)} %get-tuple-element.203.n2, bf16[256,512]{1,0:T(8,128)(2,1)S(1)} %get-tuple-element.206.ltg, ...), custom_call_target="tpu_custom_call" | custom-call | flops 10000000000 | tf_op jit(solution)/shard_map/small_weight/pallas_call | solution.py:45
  46.3 2.1 %attn_back0.1 = (f32[256,1024]{1,0:T(8,128)S(1)}, f32[256,1024]{1,0:T(8,128)S(1)}, bf16[256,256]{1,0:T(8,128)(2,1)S(1)}) custom-call(s32[8]{0:T(128)S(1)} %compare_select_fusion.pos.tb, s32[1,1024]{1,0:T(1,128)S(1)} %copy-done.5, bf16[4,1024,256]{2,1,0:T(8,128)(2,1)S(1)} %get-tuple-element.178.p, bf16[256,256]{1,0:T(8,128)(2,1)S(1)} %get-tuple-element.212.dot, ...), custom_call_target="tpu_custom_call" | custom-call | flops 10000000000 | tf_op jit(solution)/shard_map/attn_back0/pallas_call | solution.py:45
  49.2 2.3 %ffn_back_weight.1 = (f32[512,512]{1,0:T(8,128)S(1)}, bf16[512,512]{1,0:T(8,128)(2,1)S(1)}, bf16[256,1024]{1,0:T(8,128)(2,1)S(1)}) custom-call(s32[8]{0:T(128)S(1)} %compare_select_fusion.pos.tb, bf16[256,512]{1,0:T(8,128)(2,1)S(1)} %collective-permute-done.19.n2p, bf16[256,512]{1,0:T(8,128)(2,1)S(1)} %get-tuple-element.205.fg, ...), custom_call_target="tpu_custom_call" | custom-call | flops 10000000000 | tf_op jit(solution)/shard_map/ffn_back_weight/pallas_call | solution.py:45
  51.5 1.9 %ffn_in_weight.1 = (f32[520,512]{1,0:T(8,128)S(1)}, bf16[520,512]{1,0:T(8,128)(2,1)S(1)}) custom-call(s32[8]{0:T(128)S(1)} %compare_select_fusion.pos.tb, bf16[256,512]{1,0:T(8,128)(2,1)S(1)} %get-tuple-element.203.n2, bf16[256,512]{1,0:T(8,128)(2,1)S(1)} %collective-permute-done.19.n2p, bf16[256,512]{1,0:T(8,128)(2,1)S(1)} %collective-permute-done.21.fgp, ...), custom_call_target="tpu_custom_call" | custom-call | flops 10000000000 | tf_op jit(solution)/shard_map/ffn_in_weight/pallas_call | solution.py:45
  53.4 1.3 %collective-permute-start.23 = (bf16[520,512]{1,0:T(8,128)(2,1)S(1)}, bf16[520,512]{1,0:T(8,128)(2,1)S(1)}, u32[]{:S(2)}, u32[]{:S(2)}) collective-permute-start(bf16[520,512]{1,0:T(8,128)(2,1)S(1)} %get-tuple-element.234), channel_id=1, source_target_pairs={{0,1},{1,0},{2,3},{3,2},{4,5},{5,4},{6,7},{7,6},{8,9},{9,8},{10,11... | collective-permute-start | bytes 1597448 | tf_op jit(solution)/shard_map/ppermute | solution.py:705
  54.8 2.3 %collective-permute-start.24 = (bf16[256,256]{1,0:T(8,128)(2,1)S(1)}, bf16[256,256]{1,0:T(8,128)(2,1)S(1)}, u32[]{:S(2)}, u32[]{:S(2)}) collective-permute-start(bf16[256,256]{1,0:T(8,128)(2,1)S(1)} %get-tuple-element.238), channel_id=1, source_target_pairs={{0,2},{1,3},{2,0},{3,1},{4,6},{5,7},{6,4},{7,5},{8,10},{9,11},{10,... | collective-permute-start | bytes 393224 | tf_op jit(solution)/shard_map/ppermute | solution.py:705
  57.1 1.0 halves_f.1
  58.1 1.6 %collective-permute-start.25 = (bf16[256,512]{1,0:T(8,128)(2,1)S(1)}, bf16[256,512]{1,0:T(8,128)(2,1)S(1)}, u32[]{:S(2)}, u32[]{:S(2)}) collective-permute-start(bf16[256,512]{1,0:T(8,128)(2,1)S(1)} %get-tuple-element.250), channel_id=1, source_target_pairs={{0,4},{4,0},{8,12},{12,8},{16,20},{20,16},{24,28},{28,24},{1,5},{5... | collective-permute-start | bytes 786440 | tf_op jit(solution)/shard_map/ppermute | solution.py:708
  59.7 0.9 collective-permute-start.26
  60.6 0.9 collective-permute-done.24.dot
  61.5 4.7 %attn_back1.1 = (bf16[256,512]{1,0:T(8,128)(2,1)S(1)}, bf16[256,1024]{1,0:T(8,128)(2,1)S(1)}, bf16[256,1024]{1,0:T(8,128)(2,1)S(1)}, f32[392,512]{1,0:T(8,128)S(1)}, bf16[392,512]{1,0:T(8,128)(2,1)S(1)}) custom-call(s32[8]{0:T(128)S(1)} %compare_select_fusion.pos.tb, s32[1,1024]{1,0:T(1,128)S(1)} %copy-done.5, ...), custom_call_target="tpu_custom_call" | custom-call | flops 10000000000 | tf_op jit(solution)/shard_map/attn_back1/pallas_call | solution.py:45
  66.2 1.4 %input_grad.1 = (f32[512,256]{1,0:T(8,128)S(1)}, f32[512,256]{1,0:T(8,128)S(1)}, bf16[512,512]{1,0:T(8,128)(2,1)S(1)}) custom-call(s32[8]{0:T(128)S(1)} %compare_select_fusion.pos.tb, bf16[256,512]{1,0:T(8,128)(2,1)S(1)} %get-tuple-element.244.dqt, bf16[256,1024]{1,0:T(8,128)(2,1)S(1)} %get-tuple-element.246.dkt, ...), custom_call_target="tpu_custom_call" | custom-call | tf_op jit(solution)/shard_map/input_grad/pallas_call | solution.py:45
  68.3 0.7 quarters_f.1
  69.1 1.3 %collective-permute-start.30 = (bf16[128,512]{1,0:T(8,128)(2,1)S(1)}, bf16[128,512]{1,0:T(8,128)(2,1)S(1)}, u32[]{:S(2)}, u32[]{:S(2)}) collective-permute-start(bf16[128,512]{1,0:T(8,128)(2,1)S(1)} %get-tuple-element.262), channel_id=1, source_target_pairs={{0,8},{4,12},{8,0},{12,4},{16,24},{20,28},{24,16},{28,20},{1,9},{5... | collective-permute-start | bytes 393224 | tf_op jit(solution)/shard_map/ppermute | solution.py:708
  70.4 1.1 collective-permute-start.31
  71.5 1.0 halves_a.1
  72.5 1.0 collective-permute-start.32
  73.5 0.8 collective-permute-start.33
  74.8 1.9 %collective-permute-start.34 = (bf16[512,256]{1,0:T(8,128)(2,1)S(1)}, bf16[512,256]{1,0:T(8,128)(2,1)S(1)}, u32[]{:S(2)}, u32[]{:S(2)}) collective-permute-start(bf16[512,256]{1,0:T(8,128)(2,1)S(1)} %half_columns.1), channel_id=1, source_target_pairs={{0,2},{1,3},{2,0},{3,1},{4,6},{5,7},{6,4},{7,5},{8,10},{9,11},{10,... | collective-permute-start | bytes 786440 | tf_op jit(solution)/shard_map/ppermute | solution.py:705
  77.4 2.7 %collective-permute-start.40 = (bf16[264,512]{1,0:T(8,128)(2,1)S(1)}, bf16[264,512]{1,0:T(8,128)(2,1)S(1)}, u32[]{:S(2)}, u32[]{:S(2)}) collective-permute-start(bf16[264,512]{1,0:T(8,128)(2,1)S(1)} %merge_f.1.own), channel_id=1, source_target_pairs={{0,16},{4,20},{8,24},{12,28},{16,0},{20,4},{24,8},{28,12},{1,17},{... | collective-permute-start | bytes 811016 | tf_op jit(solution)/shard_map/ppermute | solution.py:708
  80.2 1.0 collective-permute-done.33.refs_3_
  81.2 0.7 quarters_a.1
  82.0 1.2 %collective-permute-start.36 = (bf16[96,512]{1,0:T(8,128)(2,1)S(1)}, bf16[96,512]{1,0:T(8,128)(2,1)S(1)}, u32[]{:S(2)}, u32[]{:S(2)}) collective-permute-start(bf16[96,512]{1,0:T(8,128)(2,1)S(1)} %get-tuple-element.276), channel_id=1, source_target_pairs={{0,4},{4,0},{8,12},{12,8},{16,20},{20,16},{24,28},{28,24},{1,5},{5... | collective-permute-start | bytes 294920 | tf_op jit(solution)/shard_map/ppermute | solution.py:708
  83.2 2.0 %last.1 = (f32[256,512]{1,0:T(8,128)}, f32[8,512]{1,0:T(8,128)S(1)}) custom-call(s32[8]{0:T(128)S(1)} %compare_select_fusion.pos.tb, f32[512,256]{1,0:T(8,128)S(1)} %get-tuple-element.248.own, bf16[512,512]{1,0:T(8,128)(2,1)S(1)} %collective-permute-done.29.recv.sib, bf16[512,256]{1,0:T(8,128)(2,1)S(1)} %collective-permute-done.34.par, ...), custom_call_target="tpu_custom_call" | custom-call | tf_op jit(solution)/shard_map/last/pallas_call | solution.py:45
  85.8 1.1 collective-permute-done.35.refs_1_
  87.1 1.3 %collective-permute-done.39.refs_7_ = f32[8,512]{1,0:T(8,128)S(1)} collective-permute-done((f32[8,512]{1,0:T(8,128)S(1)}, f32[8,512]{1,0:T(8,128)S(1)}, u32[]{:S(2)}, u32[]{:S(2)}) %collective-permute-start.39) | collective-permute-done | bytes 16416 | tf_op jit(solution)/shard_map/ppermute | solution.py:705
  89.6 2.8 %collective-permute-start.41 = (bf16[200,512]{1,0:T(8,128)(2,1)S(1)}, bf16[200,512]{1,0:T(8,128)(2,1)S(1)}, u32[]{:S(2)}, u32[]{:S(2)}) collective-permute-start(bf16[200,512]{1,0:T(8,128)(2,1)S(1)} %merge_a.1.own), channel_id=1, source_target_pairs={{0,16},{4,20},{8,24},{12,28},{16,0},{20,4},{24,8},{28,12},{1,17},{... | collective-permute-start | bytes 614408 | tf_op jit(solution)/shard_map/ppermute | solution.py:708
  93.0 2.0 %collective-permute-start.42 = (bf16[1,136,512]{2,1,0:T(8,128)(2,1)S(1)}, bf16[1,136,512]{2,1,0:T(8,128)(2,1)S(1)}, u32[]{:S(2)}, u32[]{:S(2)}) collective-permute-start(bf16[1,136,512]{2,1,0:T(8,128)(2,1)S(1)} %get-tuple-element.279.refs_0_), channel_id=1, source_target_pairs={{0,8},{4,12},{8,0},{12,4},{16,24},{20,28},{24,16},{28,20},{1,9},{5... | collective-permute-start | bytes 417800 | tf_op jit(solution)/shard_map/ppermute | solution.py:708
  95.0 0.9 collective-permute-start.45
  96.0 1.1 collective-permute-start.43
  97.1 3.8 %collective-permute-done.42.refs_1_ = bf16[1,136,512]{2,1,0:T(8,128)(2,1)S(1)} collective-permute-done((bf16[1,136,512]{2,1,0:T(8,128)(2,1)S(1)}, bf16[1,136,512]{2,1,0:T(8,128)(2,1)S(1)}, u32[]{:S(2)}, u32[]{:S(2)}) %collective-permute-start.42) | collective-permute-done | bytes 139296 | tf_op jit(solution)/shard_map/ppermute | solution.py:708
  100.8 2.7 %collective-permute-start.44 = (bf16[1,136,512]{2,1,0:T(8,128)(2,1)S(1)}, bf16[1,136,512]{2,1,0:T(8,128)(2,1)S(1)}, u32[]{:S(2)}, u32[]{:S(2)}) collective-permute-start(bf16[1,136,512]{2,1,0:T(8,128)(2,1)S(1)} %collective-permute-done.42.refs_1_), channel_id=1, source_target_pairs={{0,4},{4,0},{8,12},{12,8},{16,20},{20,16},{24,28},{28,24},{1,5},{5... | collective-permute-start | bytes 417800 | tf_op jit(solution)/shard_map/ppermute | solution.py:708
  103.6 0.7 collective-permute-start.47
  104.9 1.4 %collective-permute-start.48 = (bf16[1,104,512]{2,1,0:T(8,128)(2,1)S(1)}, bf16[1,104,512]{2,1,0:T(8,128)(2,1)S(1)}, u32[]{:S(2)}, u32[]{:S(2)}) collective-permute-start(bf16[1,104,512]{2,1,0:T(8,128)(2,1)S(1)} %get-tuple-element.281.refs_0_), channel_id=1, source_target_pairs={{0,8},{4,12},{8,0},{12,4},{16,24},{20,28},{24,16},{28,20},{1,9},{5... | collective-permute-start | bytes 319496 | tf_op jit(solution)/shard_map/ppermute | solution.py:708
  106.4 1.7 %collective-permute-start.52 = (bf16[1,96,512]{2,1,0:T(8,128)(2,1)S(1)}, bf16[1,96,512]{2,1,0:T(8,128)(2,1)S(1)}, u32[]{:S(2)}, u32[]{:S(2)}) collective-permute-start(bf16[1,96,512]{2,1,0:T(8,128)(2,1)S(1)} %get-tuple-element.286.refs_4_), channel_id=1, source_target_pairs={{0,8},{4,12},{8,0},{12,4},{16,24},{20,28},{24,16},{28,20},{1,9},{5... | collective-permute-start | bytes 294920 | tf_op jit(solution)/shard_map/ppermute | solution.py:708
  108.0 1.5 %collective-permute-done.47.refs_7_ = bf16[1,128,512]{2,1,0:T(8,128)(2,1)S(1)} collective-permute-done((bf16[1,128,512]{2,1,0:T(8,128)(2,1)S(1)}, bf16[1,128,512]{2,1,0:T(8,128)(2,1)S(1)}, u32[]{:S(2)}, u32[]{:S(2)}) %collective-permute-start.47) | collective-permute-done | bytes 131104 | tf_op jit(solution)/shard_map/ppermute | solution.py:708
  110.0 0.9 collective-permute-done.51.refs_5_
  110.9 0.7 collective-permute-start.53
  111.6 1.0 collective-permute-start.50
  112.7 2.1 %unpack_f.1 = (f32[512,512]{1,0:T(8,128)}, f32[512,512]{1,0:T(8,128)}, f32[512]{0:T(512)}, f32[512]{0:T(512)}) custom-call(s32[8]{0:T(128)S(1)} %compare_select_fusion.pos.tb, bf16[1,136,512]{2,1,0:T(8,128)(2,1)S(1)} %get-tuple-element.279.refs_0_, bf16[1,136,512]{2,1,0:T(8,128)(2,1)S(1)} %collective-permute-done.42.refs_1_, ...), custom_call_target="tpu_custom_call" | custom-call | flops 20000000000 | tf_op jit(solution)/shard_map/unpack_f/pallas_call | solution.py:45
  114.8 0.7 collective-permute-done.53.refs_7_
  115.5 0.8 collective-permute-done.50.refs_3_
  116.3 2.0 %unpack_a.1 = (f32[512,128]{1,0:T(8,128)}, f32[512,128]{1,0:T(8,128)}, f32[512,128]{1,0:T(8,128)}, f32[128,512]{1,0:T(8,128)}, f32[128,512]{1,0:T(8,128)}, /*ind...) custom-call(s32[8]{0:T(128)S(1)} %compare_select_fusion.pos.tb, ...), custom_call_target="tpu_custom_call" | custom-call | flops 10000000000 | tf_op jit(solution)/shard_map/unpack_a/pallas_call | solution.py:45
  (86 shorter events, 12.2 us)
Async XLA Ops:
  0.7 8.3 %copy-start.2 = (bf16[256,512]{1,0:T(8,128)(2,1)S(1)}, bf16[256,512]{1,0:T(8,128)(2,1)}, u32[]{:S(2)}) copy-start(bf16[256,512]{1,0:T(8,128)(2,1)} %x0.5) | copy-start | bytes 786436
  0.7 10.1 %collective-permute-start.3 = (bf16[256,512]{1,0:T(8,128)(2,1)}, bf16[256,512]{1,0:T(8,128)(2,1)S(1)}, u32[]{:S(2)}, u32[]{:S(2)}) collective-permute-start(bf16[256,512]{1,0:T(8,128)(2,1)} %x0.5), channel_id=1, source_target_pairs={{0,2},{1,3},{2,0},{3,1},{4,6},{5,7},{6,4},{7,5},{8,10},{9,11},{10,... | collective-permute-start | bytes 786440 | tf_op jit(solution)/shard_map/ppermute | solution.py:705
  3.7 5.2 %collective-permute-start = (bf16[256,512]{1,0:T(8,128)(2,1)}, bf16[256,512]{1,0:T(8,128)(2,1)S(1)}, u32[]{:S(2)}, u32[]{:S(2)}) collective-permute-start(bf16[256,512]{1,0:T(8,128)(2,1)} %x0.5), channel_id=1, source_target_pairs={{0,1},{1,0},{2,3},{3,2},{4,5},{5,4},{6,7},{7,6},{8,9},{9,8},{10,11... | collective-permute-start | bytes 786440 | tf_op jit(solution)/shard_map/ppermute | solution.py:705
  4.4 9.1 %copy-start.5 = (s32[1,1024]{1,0:T(1,128)S(1)}, s32[1,1024]{1,0:T(1,128)}, u32[]{:S(2)}) copy-start(s32[1,1024]{1,0:T(1,128)} %segs.7) | copy-start | bytes 12292
  6.9 2.0 %collective-permute-start.2 = (bf16[264,384]{1,0:T(8,128)(2,1)S(1)}, bf16[264,384]{1,0:T(8,128)(2,1)S(1)}, u32[]{:S(2)}, u32[]{:S(2)}) collective-permute-start(bf16[264,384]{1,0:T(8,128)(2,1)S(1)} %get-tuple-element.167.qb0), channel_id=1, source_target_pairs={{0,1},{1,0},{2,3},{3,2},{4,5},{5,4},{6,7},{7,6},{8,9},{9,8},{10,11... | collective-permute-start | bytes 608264 | tf_op jit(solution)/shard_map/ppermute | solution.py:705
  7.5 1.4 %collective-permute-start.1 = (bf16[256,384]{1,0:T(8,128)(2,1)S(1)}, bf16[256,384]{1,0:T(8,128)(2,1)S(1)}, u32[]{:S(2)}, u32[]{:S(2)}) collective-permute-start(bf16[256,384]{1,0:T(8,128)(2,1)S(1)} %get-tuple-element.166.qa0), channel_id=1, source_target_pairs={{0,1},{1,0},{2,3},{3,2},{4,5},{5,4},{6,7},{7,6},{8,9},{9,8},{10,11... | collective-permute-start | bytes 589832 | tf_op jit(solution)/shard_map/ppermute | solution.py:705
  7.6 10.1 %collective-permute-start.9 = (bf16[296,512]{1,0:T(8,128)(2,1)S(1)}, bf16[296,512]{1,0:T(8,128)(2,1)S(1)}, u32[]{:S(2)}, u32[]{:S(2)}) collective-permute-start(bf16[296,512]{1,0:T(8,128)(2,1)S(1)} %get-tuple-element.163), channel_id=1, source_target_pairs={{0,2},{1,3},{2,0},{3,1},{4,6},{5,7},{6,4},{7,5},{8,10},{9,11},{10,... | collective-permute-start | bytes 909320 | tf_op jit(solution)/shard_map/ppermute | solution.py:705
  10.8 2.7 %collective-permute-start.4 = (bf16[256,512]{1,0:T(8,128)(2,1)S(1)}, bf16[256,512]{1,0:T(8,128)(2,1)S(1)}, u32[]{:S(2)}, u32[]{:S(2)}) collective-permute-start(bf16[256,512]{1,0:T(8,128)(2,1)S(1)} %collective-permute-done.3.x1), channel_id=1, source_target_pairs={{0,1},{1,0},{2,3},{3,2},{4,5},{5,4},{6,7},{7,6},{8,9},{9,8},{10,11... | collective-permute-start | bytes 786440 | tf_op jit(solution)/shard_map/ppermute | solution.py:705
  11.1 14.4 %collective-permute-start.7 = (bf16[1416,512]{1,0:T(8,128)(2,1)S(1)}, bf16[1416,512]{1,0:T(8,128)(2,1)S(1)}, u32[]{:S(2)}, u32[]{:S(2)}) collective-permute-start(bf16[1416,512]{1,0:T(8,128)(2,1)S(1)} %get-tuple-element.186), channel_id=1, source_target_pairs={{0,1},{1,0},{2,3},{3,2},{4,5},{5,4},{6,7},{7,6},{8,9},{9,8},{10,11... | collective-permute-start | bytes 4349960 | tf_op jit(solution)/shard_map/ppermute | solution.py:705
  11.3 11.8 %collective-permute-start.6 = (bf16[256,512]{1,0:T(8,128)(2,1)S(1)}, bf16[256,512]{1,0:T(8,128)(2,1)S(1)}, u32[]{:S(2)}, u32[]{:S(2)}) collective-permute-start(bf16[256,512]{1,0:T(8,128)(2,1)S(1)} %get-tuple-element.185.e0), channel_id=1, source_target_pairs={{0,2},{1,3},{2,0},{3,1},{4,6},{5,7},{6,4},{7,5},{8,10},{9,11},{10,... | collective-permute-start | bytes 786440 | tf_op jit(solution)/shard_map/ppermute | solution.py:705
  17.6 7.9 %collective-permute-start.5 = (bf16[256,256]{1,0:T(8,128)(2,1)S(1)}, bf16[256,256]{1,0:T(8,128)(2,1)S(1)}, u32[]{:S(2)}, u32[]{:S(2)}) collective-permute-start(bf16[256,256]{1,0:T(8,128)(2,1)S(1)} %get-tuple-element.183), channel_id=1, source_target_pairs={{0,2},{1,3},{2,0},{3,1},{4,6},{5,7},{6,4},{7,5},{8,10},{9,11},{10,... | collective-permute-start | bytes 393224 | tf_op jit(solution)/shard_map/ppermute | solution.py:705
  17.7 9.5 %collective-permute-start.11 = (bf16[296,512]{1,0:T(8,128)(2,1)S(1)}, bf16[296,512]{1,0:T(8,128)(2,1)S(1)}, u32[]{:S(2)}, u32[]{:S(2)}) collective-permute-start(bf16[296,512]{1,0:T(8,128)(2,1)S(1)} %collective-permute-done.9.s0), channel_id=1, source_target_pairs={{0,8},{4,12},{8,0},{12,4},{16,24},{20,28},{24,16},{28,20},{1,9},{5... | collective-permute-start | bytes 909320 | tf_op jit(solution)/shard_map/ppermute | solution.py:708
  19.1 9.1 %collective-permute-start.10 = (bf16[296,512]{1,0:T(8,128)(2,1)S(1)}, bf16[296,512]{1,0:T(8,128)(2,1)S(1)}, u32[]{:S(2)}, u32[]{:S(2)}) collective-permute-start(bf16[296,512]{1,0:T(8,128)(2,1)S(1)} %collective-permute-done.9.s0), channel_id=1, source_target_pairs={{0,4},{4,0},{8,12},{12,8},{16,20},{20,16},{24,28},{28,24},{1,5},{5... | collective-permute-start | bytes 909320 | tf_op jit(solution)/shard_map/ppermute | solution.py:708
  23.2 2.4 %collective-permute-start.8 = (bf16[256,512]{1,0:T(8,128)(2,1)S(1)}, bf16[256,512]{1,0:T(8,128)(2,1)S(1)}, u32[]{:S(2)}, u32[]{:S(2)}) collective-permute-start(bf16[256,512]{1,0:T(8,128)(2,1)S(1)} %collective-permute-done.6.e1), channel_id=1, source_target_pairs={{0,1},{1,0},{2,3},{3,2},{4,5},{5,4},{6,7},{7,6},{8,9},{9,8},{10,11... | collective-permute-start | bytes 786440 | tf_op jit(solution)/shard_map/ppermute | solution.py:705
  26.9 6.2 %copy-start = (bf16[512,512]{1,0:T(8,128)(2,1)S(1)}, bf16[512,512]{1,0:T(8,128)(2,1)}, u32[]{:S(2)}) copy-start(bf16[512,512]{1,0:T(8,128)(2,1)} %win0.5) | copy-start | bytes 1572868
  26.9 6.2 %copy-start.1 = (bf16[512,512]{1,0:T(8,128)(2,1)S(1)}, bf16[512,512]{1,0:T(8,128)(2,1)}, u32[]{:S(2)}) copy-start(bf16[512,512]{1,0:T(8,128)(2,1)} %wback0.5) | copy-start | bytes 1572868
  28.8 2.6 %collective-permute-start.12 = (bf16[296,512]{1,0:T(8,128)(2,1)S(1)}, bf16[296,512]{1,0:T(8,128)(2,1)S(1)}, u32[]{:S(2)}, u32[]{:S(2)}) collective-permute-start(bf16[296,512]{1,0:T(8,128)(2,1)S(1)} %collective-permute-done.9.s0), channel_id=1, source_target_pairs={{0,1},{1,0},{2,3},{3,2},{4,5},{5,4},{6,7},{7,6},{8,9},{9,8},{10,11... | collective-permute-start | bytes 909320 | tf_op jit(solution)/shard_map/ppermute | solution.py:705
  28.9 4.2 %collective-permute-start.13 = (bf16[296,512]{1,0:T(8,128)(2,1)S(1)}, bf16[296,512]{1,0:T(8,128)(2,1)S(1)}, u32[]{:S(2)}, u32[]{:S(2)}) collective-permute-start(bf16[296,512]{1,0:T(8,128)(2,1)S(1)} %collective-permute-done.10.sx.s2), channel_id=1, source_target_pairs={{0,1},{1,0},{2,3},{3,2},{4,5},{5,4},{6,7},{7,6},{8,9},{9,8},{10,11... | collective-permute-start | bytes 909320 | tf_op jit(solution)/shard_map/ppermute | solution.py:705
  29.4 3.7 %collective-permute-start.14 = (bf16[296,512]{1,0:T(8,128)(2,1)S(1)}, bf16[296,512]{1,0:T(8,128)(2,1)S(1)}, u32[]{:S(2)}, u32[]{:S(2)}) collective-permute-start(bf16[296,512]{1,0:T(8,128)(2,1)S(1)} %collective-permute-done.11.sz.s4), channel_id=1, source_target_pairs={{0,1},{1,0},{2,3},{3,2},{4,5},{5,4},{6,7},{7,6},{8,9},{9,8},{10,11... | collective-permute-start | bytes 909320 | tf_op jit(solution)/shard_map/ppermute | solution.py:705
  29.5 8.3 %copy-start.3 = (bf16[128,512]{1,0:T(8,128)(2,1)S(1)}, bf16[128,512]{1,0:T(8,128)(2,1)}, u32[]{:S(2)}) copy-start(bf16[128,512]{1,0:T(8,128)(2,1)} %g2.5) | copy-start | bytes 393220
  29.5 8.3 %copy-start.4 = (bf16[256,512]{1,0:T(8,128)(2,1)S(1)}, bf16[256,512]{1,0:T(8,128)(2,1)}, u32[]{:S(2)}) copy-start(bf16[256,512]{1,0:T(8,128)(2,1)} %ct.3) | copy-start | bytes 786436
  29.5 6.7 %collective-permute-start.16 = (bf16[168,512]{1,0:T(8,128)(2,1)S(1)}, bf16[168,512]{1,0:T(8,128)(2,1)S(1)}, u32[]{:S(2)}, u32[]{:S(2)}) collective-permute-start(bf16[168,512]{1,0:T(8,128)(2,1)S(1)} %get-tuple-element.199), channel_id=1, source_target_pairs={{0,8},{4,12},{8,0},{12,4},{16,24},{20,28},{24,16},{28,20},{1,9},{5... | collective-permute-start | bytes 516104 | tf_op jit(solution)/shard_map/ppermute | solution.py:708
  30.1 5.7 %collective-permute-start.15 = (bf16[128,512]{1,0:T(8,128)(2,1)S(1)}, bf16[128,512]{1,0:T(8,128)(2,1)S(1)}, u32[]{:S(2)}, u32[]{:S(2)}) collective-permute-start(bf16[128,512]{1,0:T(8,128)(2,1)S(1)} %get-tuple-element.191), channel_id=1, source_target_pairs={{0,4},{4,0},{8,12},{12,8},{16,20},{20,16},{24,28},{28,24},{1,5},{5... | collective-permute-start | bytes 393224 | tf_op jit(solution)/shard_map/ppermute | solution.py:708
  31.4 8.5 %collective-permute-start.19 = (bf16[256,512]{1,0:T(8,128)(2,1)S(1)}, bf16[256,512]{1,0:T(8,128)(2,1)S(1)}, u32[]{:S(2)}, u32[]{:S(2)}) collective-permute-start(bf16[256,512]{1,0:T(8,128)(2,1)S(1)} %get-tuple-element.203.n2), channel_id=1, source_target_pairs={{0,2},{1,3},{2,0},{3,1},{4,6},{5,7},{6,4},{7,5},{8,10},{9,11},{10,... | collective-permute-start | bytes 786440 | tf_op jit(solution)/shard_map/ppermute | solution.py:705
  36.2 1.6 %collective-permute-start.18 = (bf16[168,512]{1,0:T(8,128)(2,1)S(1)}, bf16[168,512]{1,0:T(8,128)(2,1)S(1)}, u32[]{:S(2)}, u32[]{:S(2)}) collective-permute-start(bf16[168,512]{1,0:T(8,128)(2,1)S(1)} %collective-permute-done.16.b6), channel_id=1, source_target_pairs={{0,1},{1,0},{2,3},{3,2},{4,5},{5,4},{6,7},{7,6},{8,9},{9,8},{10,11... | collective-permute-start | bytes 516104 | tf_op jit(solution)/shard_map/ppermute | solution.py:705
  36.2 1.6 %collective-permute-start.17 = (bf16[128,512]{1,0:T(8,128)(2,1)S(1)}, bf16[128,512]{1,0:T(8,128)(2,1)S(1)}, u32[]{:S(2)}, u32[]{:S(2)}) collective-permute-start(bf16[128,512]{1,0:T(8,128)(2,1)S(1)} %collective-permute-done.15.a6), channel_id=1, source_target_pairs={{0,1},{1,0},{2,3},{3,2},{4,5},{5,4},{6,7},{7,6},{8,9},{9,8},{10,11... | collective-permute-start | bytes 393224 | tf_op jit(solution)/shard_map/ppermute | solution.py:705
  39.9 9.3 %collective-permute-start.21 = (bf16[256,512]{1,0:T(8,128)(2,1)S(1)}, bf16[256,512]{1,0:T(8,128)(2,1)S(1)}, u32[]{:S(2)}, u32[]{:S(2)}) collective-permute-start(bf16[256,512]{1,0:T(8,128)(2,1)S(1)} %get-tuple-element.205.fg), channel_id=1, source_target_pairs={{0,2},{1,3},{2,0},{3,1},{4,6},{5,7},{6,4},{7,5},{8,10},{9,11},{10,... | collective-permute-start | bytes 786440 | tf_op jit(solution)/shard_map/ppermute | solution.py:705
  46.3 2.4 %collective-permute-start.20 = (bf16[776,512]{1,0:T(8,128)(2,1)S(1)}, bf16[776,512]{1,0:T(8,128)(2,1)S(1)}, u32[]{:S(2)}, u32[]{:S(2)}) collective-permute-start(bf16[776,512]{1,0:T(8,128)(2,1)S(1)} %get-tuple-element.224), channel_id=1, source_target_pairs={{0,1},{1,0},{2,3},{3,2},{4,5},{5,4},{6,7},{7,6},{8,9},{9,8},{10,11... | collective-permute-start | bytes 2383880 | tf_op jit(solution)/shard_map/ppermute | solution.py:705
  53.4 3.7 %collective-permute-start.23 = (bf16[520,512]{1,0:T(8,128)(2,1)S(1)}, bf16[520,512]{1,0:T(8,128)(2,1)S(1)}, u32[]{:S(2)}, u32[]{:S(2)}) collective-permute-start(bf16[520,512]{1,0:T(8,128)(2,1)S(1)} %get-tuple-element.234), channel_id=1, source_target_pairs={{0,1},{1,0},{2,3},{3,2},{4,5},{5,4},{6,7},{7,6},{8,9},{9,8},{10,11... | collective-permute-start | bytes 1597448 | tf_op jit(solution)/shard_map/ppermute | solution.py:705
  54.7 2.4 %collective-permute-start.22 = (bf16[512,512]{1,0:T(8,128)(2,1)S(1)}, bf16[512,512]{1,0:T(8,128)(2,1)S(1)}, u32[]{:S(2)}, u32[]{:S(2)}) collective-permute-start(bf16[512,512]{1,0:T(8,128)(2,1)S(1)} %get-tuple-element.233), channel_id=1, source_target_pairs={{0,1},{1,0},{2,3},{3,2},{4,5},{5,4},{6,7},{7,6},{8,9},{9,8},{10,11... | collective-permute-start | bytes 1572872 | tf_op jit(solution)/shard_map/ppermute | solution.py:705
  54.8 6.7 %collective-permute-start.24 = (bf16[256,256]{1,0:T(8,128)(2,1)S(1)}, bf16[256,256]{1,0:T(8,128)(2,1)S(1)}, u32[]{:S(2)}, u32[]{:S(2)}) collective-permute-start(bf16[256,256]{1,0:T(8,128)(2,1)S(1)} %get-tuple-element.238), channel_id=1, source_target_pairs={{0,2},{1,3},{2,0},{3,1},{4,6},{5,7},{6,4},{7,5},{8,10},{9,11},{10,... | collective-permute-start | bytes 393224 | tf_op jit(solution)/shard_map/ppermute | solution.py:705
  57.1 14.4 %collective-permute-start.28 = (bf16[392,512]{1,0:T(8,128)(2,1)S(1)}, bf16[392,512]{1,0:T(8,128)(2,1)S(1)}, u32[]{:S(2)}, u32[]{:S(2)}) collective-permute-start(bf16[392,512]{1,0:T(8,128)(2,1)S(1)} %half_rows.1), channel_id=1, source_target_pairs={{0,2},{1,3},{2,0},{3,1},{4,6},{5,7},{6,4},{7,5},{8,10},{9,11},{10,... | collective-permute-start | bytes 1204232 | tf_op jit(solution)/shard_map/ppermute | solution.py:705
  58.1 10.2 %collective-permute-start.25 = (bf16[256,512]{1,0:T(8,128)(2,1)S(1)}, bf16[256,512]{1,0:T(8,128)(2,1)S(1)}, u32[]{:S(2)}, u32[]{:S(2)}) collective-permute-start(bf16[256,512]{1,0:T(8,128)(2,1)S(1)} %get-tuple-element.250), channel_id=1, source_target_pairs={{0,4},{4,0},{8,12},{12,8},{16,20},{20,16},{24,28},{28,24},{1,5},{5... | collective-permute-start | bytes 786440 | tf_op jit(solution)/shard_map/ppermute | solution.py:708
  59.7 8.6 %collective-permute-start.26 = (bf16[256,512]{1,0:T(8,128)(2,1)S(1)}, bf16[256,512]{1,0:T(8,128)(2,1)S(1)}, u32[]{:S(2)}, u32[]{:S(2)}) collective-permute-start(bf16[256,512]{1,0:T(8,128)(2,1)S(1)} %get-tuple-element.252), channel_id=1, source_target_pairs={{0,8},{4,12},{8,0},{12,4},{16,24},{20,28},{24,16},{28,20},{1,9},{5... | collective-permute-start | bytes 786440 | tf_op jit(solution)/shard_map/ppermute | solution.py:708
  67.6 3.9 %collective-permute-start.27 = (bf16[392,512]{1,0:T(8,128)(2,1)S(1)}, bf16[392,512]{1,0:T(8,128)(2,1)S(1)}, u32[]{:S(2)}, u32[]{:S(2)}) collective-permute-start(bf16[392,512]{1,0:T(8,128)(2,1)S(1)} %get-tuple-element.256), channel_id=1, source_target_pairs={{0,1},{1,0},{2,3},{3,2},{4,5},{5,4},{6,7},{7,6},{8,9},{9,8},{10,11... | collective-permute-start | bytes 1204232 | tf_op jit(solution)/shard_map/ppermute | solution.py:705
  68.2 6.0 %collective-permute-start.29 = (bf16[512,512]{1,0:T(8,128)(2,1)S(1)}, bf16[512,512]{1,0:T(8,128)(2,1)S(1)}, u32[]{:S(2)}, u32[]{:S(2)}) collective-permute-start(bf16[512,512]{1,0:T(8,128)(2,1)S(1)} %get-tuple-element.260), channel_id=1, source_target_pairs={{0,1},{1,0},{2,3},{3,2},{4,5},{5,4},{6,7},{7,6},{8,9},{9,8},{10,11... | collective-permute-start | bytes 1572872 | tf_op jit(solution)/shard_map/ppermute | solution.py:705
  69.1 7.7 %collective-permute-start.30 = (bf16[128,512]{1,0:T(8,128)(2,1)S(1)}, bf16[128,512]{1,0:T(8,128)(2,1)S(1)}, u32[]{:S(2)}, u32[]{:S(2)}) collective-permute-start(bf16[128,512]{1,0:T(8,128)(2,1)S(1)} %get-tuple-element.262), channel_id=1, source_target_pairs={{0,8},{4,12},{8,0},{12,4},{16,24},{20,28},{24,16},{28,20},{1,9},{5... | collective-permute-start | bytes 393224 | tf_op jit(solution)/shard_map/ppermute | solution.py:708
  70.4 6.4 %collective-permute-start.31 = (bf16[128,512]{1,0:T(8,128)(2,1)S(1)}, bf16[128,512]{1,0:T(8,128)(2,1)S(1)}, u32[]{:S(2)}, u32[]{:S(2)}) collective-permute-start(bf16[128,512]{1,0:T(8,128)(2,1)S(1)} %get-tuple-element.264), channel_id=1, source_target_pairs={{0,4},{4,0},{8,12},{12,8},{16,20},{20,16},{24,28},{28,24},{1,5},{5... | collective-permute-start | bytes 393224 | tf_op jit(solution)/shard_map/ppermute | solution.py:708
  72.5 7.7 %collective-permute-start.32 = (bf16[192,512]{1,0:T(8,128)(2,1)S(1)}, bf16[192,512]{1,0:T(8,128)(2,1)S(1)}, u32[]{:S(2)}, u32[]{:S(2)}) collective-permute-start(bf16[192,512]{1,0:T(8,128)(2,1)S(1)} %get-tuple-element.266), channel_id=1, source_target_pairs={{0,4},{4,0},{8,12},{12,8},{16,20},{20,16},{24,28},{28,24},{1,5},{5... | collective-permute-start | bytes 589832 | tf_op jit(solution)/shard_map/ppermute | solution.py:708
  73.5 7.7 %collective-permute-start.33 = (bf16[192,512]{1,0:T(8,128)(2,1)S(1)}, bf16[192,512]{1,0:T(8,128)(2,1)S(1)}, u32[]{:S(2)}, u32[]{:S(2)}) collective-permute-start(bf16[192,512]{1,0:T(8,128)(2,1)S(1)} %get-tuple-element.268), channel_id=1, source_target_pairs={{0,8},{4,12},{8,0},{12,4},{16,24},{20,28},{24,16},{28,20},{1,9},{5... | collective-permute-start | bytes 589832 | tf_op jit(solution)/shard_map/ppermute | solution.py:708
  74.8 8.4 %collective-permute-start.34 = (bf16[512,256]{1,0:T(8,128)(2,1)S(1)}, bf16[512,256]{1,0:T(8,128)(2,1)S(1)}, u32[]{:S(2)}, u32[]{:S(2)}) collective-permute-start(bf16[512,256]{1,0:T(8,128)(2,1)S(1)} %half_columns.1), channel_id=1, source_target_pairs={{0,2},{1,3},{2,0},{3,1},{4,6},{5,7},{6,4},{7,5},{8,10},{9,11},{10,... | collective-permute-start | bytes 786440 | tf_op jit(solution)/shard_map/ppermute | solution.py:705
  77.4 15.0 %collective-permute-start.40 = (bf16[264,512]{1,0:T(8,128)(2,1)S(1)}, bf16[264,512]{1,0:T(8,128)(2,1)S(1)}, u32[]{:S(2)}, u32[]{:S(2)}) collective-permute-start(bf16[264,512]{1,0:T(8,128)(2,1)S(1)} %merge_f.1.own), channel_id=1, source_target_pairs={{0,16},{4,20},{8,24},{12,28},{16,0},{20,4},{24,8},{28,12},{1,17},{... | collective-permute-start | bytes 811016 | tf_op jit(solution)/shard_map/ppermute | solution.py:708
  81.9 4.9 %collective-permute-start.35 = (bf16[96,512]{1,0:T(8,128)(2,1)S(1)}, bf16[96,512]{1,0:T(8,128)(2,1)S(1)}, u32[]{:S(2)}, u32[]{:S(2)}) collective-permute-start(bf16[96,512]{1,0:T(8,128)(2,1)S(1)} %get-tuple-element.274), channel_id=1, source_target_pairs={{0,8},{4,12},{8,0},{12,4},{16,24},{20,28},{24,16},{28,20},{1,9},{5... | collective-permute-start | bytes 294920 | tf_op jit(solution)/shard_map/ppermute | solution.py:708
  82.0 5.1 %collective-permute-start.36 = (bf16[96,512]{1,0:T(8,128)(2,1)S(1)}, bf16[96,512]{1,0:T(8,128)(2,1)S(1)}, u32[]{:S(2)}, u32[]{:S(2)}) collective-permute-start(bf16[96,512]{1,0:T(8,128)(2,1)S(1)} %get-tuple-element.276), channel_id=1, source_target_pairs={{0,4},{4,0},{8,12},{12,8},{16,20},{20,16},{24,28},{28,24},{1,5},{5... | collective-permute-start | bytes 294920 | tf_op jit(solution)/shard_map/ppermute | solution.py:708
  85.2 3.2 %collective-permute-start.39 = (f32[8,512]{1,0:T(8,128)S(1)}, f32[8,512]{1,0:T(8,128)S(1)}, u32[]{:S(2)}, u32[]{:S(2)}) collective-permute-start(f32[8,512]{1,0:T(8,128)S(1)} %get-tuple-element.277.refs_4_), channel_id=1, source_target_pairs={{0,3},{1,2},{2,1},{3,0},{4,7},{5,6},{6,5},{7,4},{8,11},{9,10},{10,... | collective-permute-start | bytes 49160 | tf_op jit(solution)/shard_map/ppermute | solution.py:705
  85.2 3.8 %collective-permute-start.38 = (f32[8,512]{1,0:T(8,128)S(1)}, f32[8,512]{1,0:T(8,128)S(1)}, u32[]{:S(2)}, u32[]{:S(2)}) collective-permute-start(f32[8,512]{1,0:T(8,128)S(1)} %get-tuple-element.277.refs_4_), channel_id=1, source_target_pairs={{0,2},{1,3},{2,0},{3,1},{4,6},{5,7},{6,4},{7,5},{8,10},{9,11},{10,... | collective-permute-start | bytes 49160 | tf_op jit(solution)/shard_map/ppermute | solution.py:705
  86.8 2.2 %collective-permute-start.37 = (f32[8,512]{1,0:T(8,128)S(1)}, f32[8,512]{1,0:T(8,128)S(1)}, u32[]{:S(2)}, u32[]{:S(2)}) collective-permute-start(f32[8,512]{1,0:T(8,128)S(1)} %get-tuple-element.277.refs_4_), channel_id=1, source_target_pairs={{0,1},{1,0},{2,3},{3,2},{4,5},{5,4},{6,7},{7,6},{8,9},{9,8},{10,11... | collective-permute-start | bytes 49160 | tf_op jit(solution)/shard_map/ppermute | solution.py:705
  89.6 14.7 %collective-permute-start.41 = (bf16[200,512]{1,0:T(8,128)(2,1)S(1)}, bf16[200,512]{1,0:T(8,128)(2,1)S(1)}, u32[]{:S(2)}, u32[]{:S(2)}) collective-permute-start(bf16[200,512]{1,0:T(8,128)(2,1)S(1)} %merge_a.1.own), channel_id=1, source_target_pairs={{0,16},{4,20},{8,24},{12,28},{16,0},{20,4},{24,8},{28,12},{1,17},{... | collective-permute-start | bytes 614408 | tf_op jit(solution)/shard_map/ppermute | solution.py:708
  93.0 7.9 %collective-permute-start.42 = (bf16[1,136,512]{2,1,0:T(8,128)(2,1)S(1)}, bf16[1,136,512]{2,1,0:T(8,128)(2,1)S(1)}, u32[]{:S(2)}, u32[]{:S(2)}) collective-permute-start(bf16[1,136,512]{2,1,0:T(8,128)(2,1)S(1)} %get-tuple-element.279.refs_0_), channel_id=1, source_target_pairs={{0,8},{4,12},{8,0},{12,4},{16,24},{20,28},{24,16},{28,20},{1,9},{5... | collective-permute-start | bytes 417800 | tf_op jit(solution)/shard_map/ppermute | solution.py:708
  95.0 8.6 %collective-permute-start.45 = (bf16[1,128,512]{2,1,0:T(8,128)(2,1)S(1)}, bf16[1,128,512]{2,1,0:T(8,128)(2,1)S(1)}, u32[]{:S(2)}, u32[]{:S(2)}) collective-permute-start(bf16[1,128,512]{2,1,0:T(8,128)(2,1)S(1)} %get-tuple-element.283.refs_4_), channel_id=1, source_target_pairs={{0,4},{4,0},{8,12},{12,8},{16,20},{20,16},{24,28},{28,24},{1,5},{5... | collective-permute-start | bytes 393224 | tf_op jit(solution)/shard_map/ppermute | solution.py:708
  95.9 10.4 %collective-permute-start.46 = (bf16[1,128,512]{2,1,0:T(8,128)(2,1)S(1)}, bf16[1,128,512]{2,1,0:T(8,128)(2,1)S(1)}, u32[]{:S(2)}, u32[]{:S(2)}) collective-permute-start(bf16[1,128,512]{2,1,0:T(8,128)(2,1)S(1)} %get-tuple-element.283.refs_4_), channel_id=1, source_target_pairs={{0,8},{4,12},{8,0},{12,4},{16,24},{20,28},{24,16},{28,20},{1,9},{5... | collective-permute-start | bytes 393224 | tf_op jit(solution)/shard_map/ppermute | solution.py:708
  96.0 10.3 %collective-permute-start.43 = (bf16[1,136,512]{2,1,0:T(8,128)(2,1)S(1)}, bf16[1,136,512]{2,1,0:T(8,128)(2,1)S(1)}, u32[]{:S(2)}, u32[]{:S(2)}) collective-permute-start(bf16[1,136,512]{2,1,0:T(8,128)(2,1)S(1)} %get-tuple-element.279.refs_0_), channel_id=1, source_target_pairs={{0,4},{4,0},{8,12},{12,8},{16,20},{20,16},{24,28},{28,24},{1,5},{5... | collective-permute-start | bytes 417800 | tf_op jit(solution)/shard_map/ppermute | solution.py:708
  100.8 11.8 %collective-permute-start.44 = (bf16[1,136,512]{2,1,0:T(8,128)(2,1)S(1)}, bf16[1,136,512]{2,1,0:T(8,128)(2,1)S(1)}, u32[]{:S(2)}, u32[]{:S(2)}) collective-permute-start(bf16[1,136,512]{2,1,0:T(8,128)(2,1)S(1)} %collective-permute-done.42.refs_1_), channel_id=1, source_target_pairs={{0,4},{4,0},{8,12},{12,8},{16,20},{20,16},{24,28},{28,24},{1,5},{5... | collective-permute-start | bytes 417800 | tf_op jit(solution)/shard_map/ppermute | solution.py:708
  103.6 6.0 %collective-permute-start.47 = (bf16[1,128,512]{2,1,0:T(8,128)(2,1)S(1)}, bf16[1,128,512]{2,1,0:T(8,128)(2,1)S(1)}, u32[]{:S(2)}, u32[]{:S(2)}) collective-permute-start(bf16[1,128,512]{2,1,0:T(8,128)(2,1)S(1)} %collective-permute-done.45.refs_5_), channel_id=1, source_target_pairs={{0,8},{4,12},{8,0},{12,4},{16,24},{20,28},{24,16},{28,20},{1,9},{5... | collective-permute-start | bytes 393224 | tf_op jit(solution)/shard_map/ppermute | solution.py:708
  104.9 6.7 %collective-permute-start.48 = (bf16[1,104,512]{2,1,0:T(8,128)(2,1)S(1)}, bf16[1,104,512]{2,1,0:T(8,128)(2,1)S(1)}, u32[]{:S(2)}, u32[]{:S(2)}) collective-permute-start(bf16[1,104,512]{2,1,0:T(8,128)(2,1)S(1)} %get-tuple-element.281.refs_0_), channel_id=1, source_target_pairs={{0,8},{4,12},{8,0},{12,4},{16,24},{20,28},{24,16},{28,20},{1,9},{5... | collective-permute-start | bytes 319496 | tf_op jit(solution)/shard_map/ppermute | solution.py:708
  106.3 4.6 %collective-permute-start.51 = (bf16[1,96,512]{2,1,0:T(8,128)(2,1)S(1)}, bf16[1,96,512]{2,1,0:T(8,128)(2,1)S(1)}, u32[]{:S(2)}, u32[]{:S(2)}) collective-permute-start(bf16[1,96,512]{2,1,0:T(8,128)(2,1)S(1)} %get-tuple-element.286.refs_4_), channel_id=1, source_target_pairs={{0,4},{4,0},{8,12},{12,8},{16,20},{20,16},{24,28},{28,24},{1,5},{5... | collective-permute-start | bytes 294920 | tf_op jit(solution)/shard_map/ppermute | solution.py:708
  106.4 8.4 %collective-permute-start.52 = (bf16[1,96,512]{2,1,0:T(8,128)(2,1)S(1)}, bf16[1,96,512]{2,1,0:T(8,128)(2,1)S(1)}, u32[]{:S(2)}, u32[]{:S(2)}) collective-permute-start(bf16[1,96,512]{2,1,0:T(8,128)(2,1)S(1)} %get-tuple-element.286.refs_4_), channel_id=1, source_target_pairs={{0,8},{4,12},{8,0},{12,4},{16,24},{20,28},{24,16},{28,20},{1,9},{5... | collective-permute-start | bytes 294920 | tf_op jit(solution)/shard_map/ppermute | solution.py:708
  109.6 5.2 %collective-permute-start.49 = (bf16[1,104,512]{2,1,0:T(8,128)(2,1)S(1)}, bf16[1,104,512]{2,1,0:T(8,128)(2,1)S(1)}, u32[]{:S(2)}, u32[]{:S(2)}) collective-permute-start(bf16[1,104,512]{2,1,0:T(8,128)(2,1)S(1)} %get-tuple-element.281.refs_0_), channel_id=1, source_target_pairs={{0,4},{4,0},{8,12},{12,8},{16,20},{20,16},{24,28},{28,24},{1,5},{5... | collective-permute-start | bytes 319496 | tf_op jit(solution)/shard_map/ppermute | solution.py:708
  110.9 4.6 %collective-permute-start.53 = (bf16[1,96,512]{2,1,0:T(8,128)(2,1)S(1)}, bf16[1,96,512]{2,1,0:T(8,128)(2,1)S(1)}, u32[]{:S(2)}, u32[]{:S(2)}) collective-permute-start(bf16[1,96,512]{2,1,0:T(8,128)(2,1)S(1)} %collective-permute-done.51.refs_5_), channel_id=1, source_target_pairs={{0,8},{4,12},{8,0},{12,4},{16,24},{20,28},{24,16},{28,20},{1,9},{5... | collective-permute-start | bytes 294920 | tf_op jit(solution)/shard_map/ppermute | solution.py:708
  111.6 4.7 %collective-permute-start.50 = (bf16[1,104,512]{2,1,0:T(8,128)(2,1)S(1)}, bf16[1,104,512]{2,1,0:T(8,128)(2,1)S(1)}, u32[]{:S(2)}, u32[]{:S(2)}) collective-permute-start(bf16[1,104,512]{2,1,0:T(8,128)(2,1)S(1)} %collective-permute-done.48.refs_1_), channel_id=1, source_target_pairs={{0,4},{4,0},{8,12},{12,8},{16,20},{20,16},{24,28},{28,24},{1,5},{5... | collective-permute-start | bytes 319496 | tf_op jit(solution)/shard_map/ppermute | solution.py:708

commit v7 on v6

--- a/solution.py
+++ b/solution.py
@@ -343,9 +343,10 @@
 
 
 def ffn_back_weight_kernel(
-    tb, n2p, fg, fgp, hid, vecs, win0, c2,
-    keep_ref, send_ref, slope_ref,
-):
+    tb, n2p, fg, fgp, hid, vecs, win0, c2, keep, recv,
+    keep_ref, send_ref, slope_ref, par_ref,
+):
+    par_ref[...] = (keep[384:, :] + recv[384:, :].astype(F32)).astype(BF16)
     fgv, fgpv, n2pv = fg[...], fgp[...], n2p[...]
     for i, (b, w) in enumerate(((vecs[8:9, :], win0[...]), (c2[384:385, :], c2[392:904, :]))):
         cols = slice(512 * i, 512 * i + 512)
@@ -373,10 +374,12 @@
 
 
 def small_weight_kernel(
-    tb, n, n2, ltg, log, att, attp, bg, sums,
-    keep_ref, send_ref,
-    g1, g2,
-):
+    tb, n, n2, ltg, log, att, attp, bg, sums, e0, e1, e2, e3,
+    keep_ref, send_ref, gate_ref,
+    g1, g2, gw,
+):
+    gather_gate(tb, (e0, e1, e2, e3), 128, gw)
+    gate_ref[...] = nt(log[...], gw[...])
     keep_ref[768:776, :] = sums[...]
     send_ref[768:776, :] = sums[...].astype(BF16)
     g2[...] = tn(n2[...], ltg[...])
@@ -484,10 +487,9 @@
     par_ref[...] = g0[:, 256:512]
 
 
-def last_kernel(tb, own, sib, par, x0, mg, log, vecs, e0, e1, e2, e3, grad_ref, sums_ref, gw):
-    gather_gate(tb, (e0, e1, e2, e3), 128, gw)
+def last_kernel(tb, own, sib, par, x0, mg, gate_part, vecs, grad_ref, sums_ref):
     total = own[...] + sib[:, 0:256].astype(F32) + par[...].astype(F32)
-    ng = total.T + nt(log[...], gw[...])
+    ng = total.T + gate_part[...]
     unit, inverse = norm_unit(x0[...].astype(F32))
     g = ng * vecs[0:1, :]
     back = inverse * (g - jnp.mean(g, axis=-1, keepdims=True) - unit * jnp.mean(g * unit, axis=-1, keepdims=True))
@@ -548,10 +550,6 @@
         copy.wait()
 
 
-def half_rows_kernel(tb, keep, recv, out_ref):
-    out_ref[...] = (keep[384:, :] + recv[384:, :].astype(F32)).astype(BF16)
-
-
 def half_columns_kernel(tb, keep, recv, out_ref):
     half = keep.shape[1]
     out_ref[...] = (keep[...] + recv[:, half:].astype(F32)).astype(BF16)
@@ -805,11 +803,11 @@
         "back", [pltpu.VMEM((512, 512), BF16)], then=(n2p,),
     )
     dot1 = hop(dotp, PX)
-    skeep, ssend = step(
+    skeep, ssend, gate_part = step(
         small_weight_kernel,
-        [sds((776, 512), F32), sds((776, 512), BF16)],
-        [n, n2, ltg, log, att0, attp, bg, sums],
-        "small_weight", [pltpu.VMEM((512, 512), F32), pltpu.VMEM((512, 512), F32)],
+        [sds((776, 512), F32), sds((776, 512), BF16), sds((256, 512), F32)],
+        [n, n2, ltg, log, att0, attp, bg, sums, e0, e1, c2, e3],
+        "small_weight", [pltpu.VMEM((512, 512), F32), pltpu.VMEM((512, 512), F32), pltpu.VMEM((512, 512), BF16)],
     )
     srecv = hop(ssend, 1)
     back_scratch = [
@@ -822,15 +820,14 @@
         [seg, p0, dot0, ot0, invl0, qt0, kt, v],
         "attn_back0", back_scratch, 2,
     )
-    (spar,) = step(half_rows_kernel, [sds((392, 512), BF16)], [skeep, srecv], "half_rows")
+    bkeep, bsend, slopep, spar = step(
+        ffn_back_weight_kernel,
+        [sds((512, 512), F32), sds((512, 512), BF16), sds((256, 1024), BF16), sds((392, 512), BF16)],
+        [n2p, fg, fgp, hid, vecs, w_in, c2, skeep, srecv],
+        "ffn_back_weight",
+    )
+    brecv = hop(bsend, 1)
     sparr = hop(spar, PX)
-    bkeep, bsend, slopep = step(
-        ffn_back_weight_kernel,
-        [sds((512, 512), F32), sds((512, 512), BF16), sds((256, 1024), BF16)],
-        [n2p, fg, fgp, hid, vecs, w_in, c2],
-        "ffn_back_weight",
-    )
-    brecv = hop(bsend, 1)
     ikeep, isend = step(
         ffn_in_weight_kernel,
         [sds((520, 512), F32), sds((520, 512), BF16)],
@@ -946,8 +943,8 @@
     input_grad, sums1 = step(
         last_kernel,
         [sds((256, 512), F32), sds((8, 512), F32)],
-        [gown, gsib, gp, x0, mg, log, vecs, e0, e1, c2, e3],
-        "last", [pltpu.VMEM((512, 512), BF16)],
+        [gown, gsib, gp, x0, mg, gate_part, vecs],
+        "last",
     )
     sums1_b = hop(sums1, PX)
     sums1_a = hop(sums1, 1)

time: 119 us -> 118 us (level)
    pallas_call x29 -> x28, Pallas kernels: 48.2 us -> 47.8 us  [call(): pl.pallas_call(body, out_shape=tuple(outs), in_specs=[SM] * smem + [space...]
where the time goes in v7:
time: 118 us
  starting transfers between devices  49.4 us (42%)
  Pallas kernels  47.8 us (41%)
  waiting for transfers between devices  19.1 us (16%)
    pallas_call x28, Pallas kernels, call(): pl.pallas_call(body, out_shape=tuple(outs), in_specs=[SM] * smem + [space...  47.8 us
    ppermute x26, starting transfers between devices, dhop(): return lax.ppermute(value, 'dp', [(i, i ^ mask) for i in range(n_dp)])  31.2 us
    ppermute x28, starting transfers between devices, hop(): return lax.ppermute(value, 'tensor', [(i, i ^ mask) for i in range(4)])  18.3 us
    ppermute x26, waiting for transfers between devices, dhop(): return lax.ppermute(value, 'dp', [(i, i ^ mask) for i in range(n_dp)])  11.7 us
    ppermute x28, waiting for transfers between devices, hop(): return lax.ppermute(value, 'tensor', [(i, i ^ mask) for i in range(4)])  7.37 us
  transfers between devices with their start and end apart: 54, of which 19 were waited for; matrix products, arithmetic and copies ran while one was open for 1% of the time, Pallas kernels for 35%

profile of v7, /device:TPU:0, one launch (start us, length us, event | category | flops | bytes accessed | tf_op | source)
XLA Modules:
  0.0 118.1 jit_solution(1677030624183981787)
XLA Ops:
  0.7 3.0 %collective-permute-start.3 = (bf16[256,512]{1,0:T(8,128)(2,1)}, bf16[256,512]{1,0:T(8,128)(2,1)S(1)}, u32[]{:S(2)}, u32[]{:S(2)}) collective-permute-start(bf16[256,512]{1,0:T(8,128)(2,1)} %x0.5), channel_id=1, source_target_pairs={{0,2},{1,3},{2,0},{3,1},{4,6},{5,7},{6,4},{7,5},{8,10},{9,11},{10,... | collective-permute-start | bytes 786440 | tf_op jit(solution)/shard_map/ppermute | solution.py:703
  4.4 2.5 %pack.1 = (bf16[296,512]{1,0:T(8,128)(2,1)S(1)}, bf16[256,512]{1,0:T(8,128)(2,1)S(1)}, bf16[1416,512]{1,0:T(8,128)(2,1)S(1)}, bf16[256,384]{1,0:T(8,128)(2,1)S(1...) custom-call(s32[8]{0:T(128)S(1)} %compare_select_fusion.pos.tb, bf16[512,512]{1,0:T(8,128)(2,1)} %win0.5, ...), custom_call_target="tpu_custom_call" | custom-call | tf_op jit(solution)/shard_map/pack/pallas_call | solution.py:45
  7.7 1.3 %collective-permute-done.1.qa1 = bf16[256,384]{1,0:T(8,128)(2,1)S(1)} collective-permute-done((bf16[256,384]{1,0:T(8,128)(2,1)S(1)}, bf16[256,384]{1,0:T(8,128)(2,1)S(1)}, u32[]{:S(2)}, u32[]{:S(2)}) %collective-permute-start.1) | collective-permute-done | bytes 196640 | tf_op jit(solution)/shard_map/ppermute | solution.py:703
  8.9 1.8 %chip.1 = (bf16[512,512]{1,0:T(8,128)(2,1)S(1)}, bf16[256,256]{1,0:T(8,128)(2,1)S(1)}, bf16[512,256]{1,0:T(8,128)(2,1)S(1)}, bf16[256,512]{1,0:T(8,128)(2,1)S(1)}) custom-call(s32[8]{0:T(128)S(1)} %compare_select_fusion.pos.tb, bf16[256,512]{1,0:T(8,128)(2,1)S(1)} %copy-done.2, bf16[256,512]{1,0:T(8,128)(2,1)S(1)} %collective-permute-done.x2, ...), custom_call_target="tpu_custom_call" | custom-call | tf_op jit(solution)/shard_map/chip/pallas_call | solution.py:45
  11.3 2.1 %collective-permute-start.6 = (bf16[256,512]{1,0:T(8,128)(2,1)S(1)}, bf16[256,512]{1,0:T(8,128)(2,1)S(1)}, u32[]{:S(2)}, u32[]{:S(2)}) collective-permute-start(bf16[256,512]{1,0:T(8,128)(2,1)S(1)} %get-tuple-element.186.e0), channel_id=1, source_target_pairs={{0,2},{1,3},{2,0},{3,1},{4,6},{5,7},{6,4},{7,5},{8,10},{9,11},{10,... | collective-permute-start | bytes 786440 | tf_op jit(solution)/shard_map/ppermute | solution.py:703
  13.5 4.1 %first.1 = (bf16[1024,512]{1,0:T(8,128)(2,1)S(1)}, bf16[256,256]{1,0:T(8,128)(2,1)S(1)}, bf16[1024,256]{1,0:T(8,128)(2,1)S(1)}, bf16[256,1024]{1,0:T(8,128)(2,1)...) custom-call(s32[8]{0:T(128)S(1)} %compare_select_fusion.pos.tb, ...), custom_call_target="tpu_custom_call" | custom-call | tf_op jit(solution)/shard_map/first/pallas_call | solution.py:45
  17.7 1.4 %collective-permute-start.11 = (bf16[296,512]{1,0:T(8,128)(2,1)S(1)}, bf16[296,512]{1,0:T(8,128)(2,1)S(1)}, u32[]{:S(2)}, u32[]{:S(2)}) collective-permute-start(bf16[296,512]{1,0:T(8,128)(2,1)S(1)} %collective-permute-done.9.s0), channel_id=1, source_target_pairs={{0,8},{4,12},{8,0},{12,4},{16,24},{20,28},{24,16},{28,20},{1,9},{5... | collective-permute-start | bytes 909320 | tf_op jit(solution)/shard_map/ppermute | solution.py:706
  19.1 1.5 %collective-permute-start.10 = (bf16[296,512]{1,0:T(8,128)(2,1)S(1)}, bf16[296,512]{1,0:T(8,128)(2,1)S(1)}, u32[]{:S(2)}, u32[]{:S(2)}) collective-permute-start(bf16[296,512]{1,0:T(8,128)(2,1)S(1)} %collective-permute-done.9.s0), channel_id=1, source_target_pairs={{0,4},{4,0},{8,12},{12,8},{16,20},{20,16},{24,28},{28,24},{1,5},{5... | collective-permute-start | bytes 909320 | tf_op jit(solution)/shard_map/ppermute | solution.py:706
  20.6 1.6 %second.1 = (bf16[4,1024,256]{2,1,0:T(8,128)(2,1)S(1)}, bf16[256,256]{1,0:T(8,128)(2,1)S(1)}, bf16[256,256]{1,0:T(8,128)(2,1)S(1)}, f32[4,8,256]{2,1,0:T(8,128)S(1)}) custom-call(s32[8]{0:T(128)S(1)} %compare_select_fusion.pos.tb, s32[1,1024]{1,0:T(1,128)S(1)} %copy-done.5, s32[1,1024]{1,0:T(1,128)S(1)} %copy-done.5, ...), custom_call_target="tpu_custom_call" | custom-call | flops 10000000000 | tf_op jit(solution)/shard_map/second/pallas_call | solution.py:45
  22.3 0.9 collective-permute-done.6.e1
  23.2 1.2 %prepare.1 = (bf16[1024,256]{1,0:T(8,128)(2,1)S(1)}, bf16[256,1024]{1,0:T(8,128)(2,1)S(1)}) custom-call(s32[8]{0:T(128)S(1)} %compare_select_fusion.pos.tb, bf16[1024,512]{1,0:T(8,128)(2,1)S(1)} %get-tuple-element.174.n, bf16[1024,256]{1,0:T(8,128)(2,1)S(1)} %get-tuple-element.177.k, bf16[256,384]{1,0:T(8,128)(2,1)S(1)} %get-tuple-element.167.qa0, ...), custom_call_target="tpu_custom_call" | custom-call | flops 10000000000 | tf_op jit(solution)/shard_map/prepare/pallas_call | solution.py:45
  24.4 1.1 collective-permute-done.5.attp
  25.5 1.4 %out.1 = (bf16[256,512]{1,0:T(8,128)(2,1)S(1)}, f32[256,512]{1,0:T(8,128)S(1)}, f32[256,512]{1,0:T(8,128)S(1)}, f32[256,512]{1,0:T(8,128)S(1)}) custom-call(s32[8]{0:T(128)S(1)} %compare_select_fusion.pos.tb, bf16[256,512]{1,0:T(8,128)(2,1)S(1)} %copy-done.2, bf16[1024,512]{1,0:T(8,128)(2,1)S(1)} %get-tuple-element.174.n, ...), custom_call_target="tpu_custom_call" | custom-call | flops 10000000000 | tf_op jit(solution)/shard_map/out/pallas_call | solution.py:45
  27.2 1.1 collective-permute-done.10.sx.s2
  29.5 0.7 collective-permute-start.16
  30.2 1.2 %collective-permute-start.15 = (bf16[128,512]{1,0:T(8,128)(2,1)S(1)}, bf16[128,512]{1,0:T(8,128)(2,1)S(1)}, u32[]{:S(2)}, u32[]{:S(2)}) collective-permute-start(bf16[128,512]{1,0:T(8,128)(2,1)S(1)} %get-tuple-element.192), channel_id=1, source_target_pairs={{0,4},{4,0},{8,12},{12,8},{16,20},{20,16},{24,28},{28,24},{1,5},{5... | collective-permute-start | bytes 393224 | tf_op jit(solution)/shard_map/ppermute | solution.py:706
  31.4 1.7 %collective-permute-start.19 = (bf16[256,512]{1,0:T(8,128)(2,1)S(1)}, bf16[256,512]{1,0:T(8,128)(2,1)S(1)}, u32[]{:S(2)}, u32[]{:S(2)}) collective-permute-start(bf16[256,512]{1,0:T(8,128)(2,1)S(1)} %get-tuple-element.204.n2), channel_id=1, source_target_pairs={{0,2},{1,3},{2,0},{3,1},{4,6},{5,7},{6,4},{7,5},{8,10},{9,11},{10,... | collective-permute-start | bytes 786440 | tf_op jit(solution)/shard_map/ppermute | solution.py:703
  33.1 2.7 %ffn_first.1 = (f32[256,512]{1,0:T(8,128)S(1)}, bf16[256,1024]{1,0:T(8,128)(2,1)S(1)}, bf16[256,1024]{1,0:T(8,128)(2,1)S(1)}, bf16[256,768]{1,0:T(8,128)(2,1)S(1)}) custom-call(s32[8]{0:T(128)S(1)} %compare_select_fusion.pos.tb, bf16[256,512]{1,0:T(8,128)(2,1)S(1)} %get-tuple-element.204.n2, f32[16,512]{1,0:T(8,128)S(1)} %get-tuple-element.166.vecs, ...), custom_call_target="tpu_custom_call" | custom-call | tf_op jit(solution)/shard_map/ffn_first/pallas_call | solution.py:45
  36.7 1.1 collective-permute-done.17.a7
  37.8 2.1 %ffn.1 = (bf16[256,512]{1,0:T(8,128)(2,1)}, bf16[256,512]{1,0:T(8,128)(2,1)S(1)}, bf16[256,512]{1,0:T(8,128)(2,1)S(1)}, bf16[256,256]{1,0:T(8,128)(2,1)S(1)}) custom-call(s32[8]{0:T(128)S(1)} %compare_select_fusion.pos.tb, bf16[256,512]{1,0:T(8,128)(2,1)S(1)} %get-tuple-element.204.n2, f32[256,512]{1,0:T(8,128)S(1)} %get-tuple-element.199.mid, ...), custom_call_target="tpu_custom_call" | custom-call | tf_op jit(solution)/shard_map/ffn/pallas_call | solution.py:45
  39.9 1.7 %collective-permute-start.20 = (bf16[256,512]{1,0:T(8,128)(2,1)S(1)}, bf16[256,512]{1,0:T(8,128)(2,1)S(1)}, u32[]{:S(2)}, u32[]{:S(2)}) collective-permute-start(bf16[256,512]{1,0:T(8,128)(2,1)S(1)} %get-tuple-element.206.fg), channel_id=1, source_target_pairs={{0,2},{1,3},{2,0},{3,1},{4,6},{5,7},{6,4},{7,5},{8,10},{9,11},{10,... | collective-permute-start | bytes 786440 | tf_op jit(solution)/shard_map/ppermute | solution.py:703
  41.6 3.5 %back.1 = (bf16[256,256]{1,0:T(8,128)(2,1)S(1)}, bf16[256,256]{1,0:T(8,128)(2,1)S(1)}, f32[256,512]{1,0:T(8,128)S(1)}, bf16[256,512]{1,0:T(8,128)(2,1)S(1)}, bf1...) custom-call(s32[8]{0:T(128)S(1)} %compare_select_fusion.pos.tb, ...), custom_call_target="tpu_custom_call" | custom-call | flops 10000000000 | tf_op jit(solution)/shard_map/back/pallas_call | solution.py:45
  45.0 1.4 %small_weight.1 = (f32[776,512]{1,0:T(8,128)S(1)}, bf16[776,512]{1,0:T(8,128)(2,1)S(1)}, f32[256,512]{1,0:T(8,128)S(1)}) custom-call(s32[8]{0:T(128)S(1)} %compare_select_fusion.pos.tb, bf16[1024,512]{1,0:T(8,128)(2,1)S(1)} %get-tuple-element.174.n, bf16[256,512]{1,0:T(8,128)(2,1)S(1)} %get-tuple-element.204.n2, ...), custom_call_target="tpu_custom_call" | custom-call | flops 10000000000 | tf_op jit(solution)/shard_map/small_weight/pallas_call | solution.py:45
  46.5 2.1 %attn_back0.1 = (f32[256,1024]{1,0:T(8,128)S(1)}, f32[256,1024]{1,0:T(8,128)S(1)}, bf16[256,256]{1,0:T(8,128)(2,1)S(1)}) custom-call(s32[8]{0:T(128)S(1)} %compare_select_fusion.pos.tb, s32[1,1024]{1,0:T(1,128)S(1)} %copy-done.5, bf16[4,1024,256]{2,1,0:T(8,128)(2,1)S(1)} %get-tuple-element.179.p, bf16[256,256]{1,0:T(8,128)(2,1)S(1)} %get-tuple-element.213.dot, ...), custom_call_target="tpu_custom_call" | custom-call | flops 10000000000 | tf_op jit(solution)/shard_map/attn_back0/pallas_call | solution.py:45
  48.8 2.4 %ffn_back_weight.1 = (f32[512,512]{1,0:T(8,128)S(1)}, bf16[512,512]{1,0:T(8,128)(2,1)S(1)}, bf16[256,1024]{1,0:T(8,128)(2,1)S(1)}, bf16[392,512]{1,0:T(8,128)(2,1)S(1)}) custom-call(s32[8]{0:T(128)S(1)} %compare_select_fusion.pos.tb, bf16[256,512]{1,0:T(8,128)(2,1)S(1)} %collective-permute-done.19.n2p, bf16[256,512]{1,0:T(8,128)(2,1)S(1)} %get-tuple-element.206.fg, ...), custom_call_target="tpu_custom_call" | custom-call | flops 10000000000 | tf_op jit(solution)/shard_map/ffn_back_weight/pallas_call | solution.py:45
  51.2 1.9 %ffn_in_weight.1 = (f32[520,512]{1,0:T(8,128)S(1)}, bf16[520,512]{1,0:T(8,128)(2,1)S(1)}) custom-call(s32[8]{0:T(128)S(1)} %compare_select_fusion.pos.tb, bf16[256,512]{1,0:T(8,128)(2,1)S(1)} %get-tuple-element.204.n2, bf16[256,512]{1,0:T(8,128)(2,1)S(1)} %collective-permute-done.19.n2p, bf16[256,512]{1,0:T(8,128)(2,1)S(1)} %collective-permute-done.20.fgp, ...), custom_call_target="tpu_custom_call" | custom-call | flops 10000000000 | tf_op jit(solution)/shard_map/ffn_in_weight/pallas_call | solution.py:45
  53.0 1.4 %collective-permute-start.23 = (bf16[520,512]{1,0:T(8,128)(2,1)S(1)}, bf16[520,512]{1,0:T(8,128)(2,1)S(1)}, u32[]{:S(2)}, u32[]{:S(2)}) collective-permute-start(bf16[520,512]{1,0:T(8,128)(2,1)S(1)} %get-tuple-element.234), channel_id=1, source_target_pairs={{0,1},{1,0},{2,3},{3,2},{4,5},{5,4},{6,7},{7,6},{8,9},{9,8},{10,11... | collective-permute-start | bytes 1597448 | tf_op jit(solution)/shard_map/ppermute | solution.py:703
  54.4 2.3 %collective-permute-start.24 = (bf16[256,256]{1,0:T(8,128)(2,1)S(1)}, bf16[256,256]{1,0:T(8,128)(2,1)S(1)}, u32[]{:S(2)}, u32[]{:S(2)}) collective-permute-start(bf16[256,256]{1,0:T(8,128)(2,1)S(1)} %get-tuple-element.238), channel_id=1, source_target_pairs={{0,2},{1,3},{2,0},{3,1},{4,6},{5,7},{6,4},{7,5},{8,10},{9,11},{10,... | collective-permute-start | bytes 393224 | tf_op jit(solution)/shard_map/ppermute | solution.py:703
  56.8 1.0 halves_f.1
  57.8 1.6 %collective-permute-start.25 = (bf16[256,512]{1,0:T(8,128)(2,1)S(1)}, bf16[256,512]{1,0:T(8,128)(2,1)S(1)}, u32[]{:S(2)}, u32[]{:S(2)}) collective-permute-start(bf16[256,512]{1,0:T(8,128)(2,1)S(1)} %get-tuple-element.250), channel_id=1, source_target_pairs={{0,4},{4,0},{8,12},{12,8},{16,20},{20,16},{24,28},{28,24},{1,5},{5... | collective-permute-start | bytes 786440 | tf_op jit(solution)/shard_map/ppermute | solution.py:706
  59.4 0.9 collective-permute-start.26
  60.2 0.9 collective-permute-done.24.dot
  61.1 4.8 %attn_back1.1 = (bf16[256,512]{1,0:T(8,128)(2,1)S(1)}, bf16[256,1024]{1,0:T(8,128)(2,1)S(1)}, bf16[256,1024]{1,0:T(8,128)(2,1)S(1)}, f32[392,512]{1,0:T(8,128)S(1)}, bf16[392,512]{1,0:T(8,128)(2,1)S(1)}) custom-call(s32[8]{0:T(128)S(1)} %compare_select_fusion.pos.tb, s32[1,1024]{1,0:T(1,128)S(1)} %copy-done.5, ...), custom_call_target="tpu_custom_call" | custom-call | flops 10000000000 | tf_op jit(solution)/shard_map/attn_back1/pallas_call | solution.py:45
  65.9 1.4 %input_grad.1 = (f32[512,256]{1,0:T(8,128)S(1)}, f32[512,256]{1,0:T(8,128)S(1)}, bf16[512,512]{1,0:T(8,128)(2,1)S(1)}) custom-call(s32[8]{0:T(128)S(1)} %compare_select_fusion.pos.tb, bf16[256,512]{1,0:T(8,128)(2,1)S(1)} %get-tuple-element.244.dqt, bf16[256,1024]{1,0:T(8,128)(2,1)S(1)} %get-tuple-element.246.dkt, ...), custom_call_target="tpu_custom_call" | custom-call | tf_op jit(solution)/shard_map/input_grad/pallas_call | solution.py:45
  68.0 0.7 quarters_f.1
  68.7 1.3 %collective-permute-start.30 = (bf16[128,512]{1,0:T(8,128)(2,1)S(1)}, bf16[128,512]{1,0:T(8,128)(2,1)S(1)}, u32[]{:S(2)}, u32[]{:S(2)}) collective-permute-start(bf16[128,512]{1,0:T(8,128)(2,1)S(1)} %get-tuple-element.263), channel_id=1, source_target_pairs={{0,8},{4,12},{8,0},{12,4},{16,24},{20,28},{24,16},{28,20},{1,9},{5... | collective-permute-start | bytes 393224 | tf_op jit(solution)/shard_map/ppermute | solution.py:706
  70.1 1.1 collective-permute-start.31
  71.2 0.9 halves_a.1
  72.1 1.0 collective-permute-start.32
  73.1 0.8 collective-permute-start.33
  74.5 1.9 %collective-permute-start.34 = (bf16[512,256]{1,0:T(8,128)(2,1)S(1)}, bf16[512,256]{1,0:T(8,128)(2,1)S(1)}, u32[]{:S(2)}, u32[]{:S(2)}) collective-permute-start(bf16[512,256]{1,0:T(8,128)(2,1)S(1)} %half_columns.1), channel_id=1, source_target_pairs={{0,2},{1,3},{2,0},{3,1},{4,6},{5,7},{6,4},{7,5},{8,10},{9,11},{10,... | collective-permute-start | bytes 786440 | tf_op jit(solution)/shard_map/ppermute | solution.py:703
  77.0 2.7 %collective-permute-start.40 = (bf16[264,512]{1,0:T(8,128)(2,1)S(1)}, bf16[264,512]{1,0:T(8,128)(2,1)S(1)}, u32[]{:S(2)}, u32[]{:S(2)}) collective-permute-start(bf16[264,512]{1,0:T(8,128)(2,1)S(1)} %merge_f.1.own), channel_id=1, source_target_pairs={{0,16},{4,20},{8,24},{12,28},{16,0},{20,4},{24,8},{28,12},{1,17},{... | collective-permute-start | bytes 811016 | tf_op jit(solution)/shard_map/ppermute | solution.py:706
  79.8 1.0 collective-permute-done.33.refs_3_
  80.8 0.7 quarters_a.1
  81.6 1.3 %collective-permute-start.36 = (bf16[96,512]{1,0:T(8,128)(2,1)S(1)}, bf16[96,512]{1,0:T(8,128)(2,1)S(1)}, u32[]{:S(2)}, u32[]{:S(2)}) collective-permute-start(bf16[96,512]{1,0:T(8,128)(2,1)S(1)} %get-tuple-element.278), channel_id=1, source_target_pairs={{0,4},{4,0},{8,12},{12,8},{16,20},{20,16},{24,28},{28,24},{1,5},{5... | collective-permute-start | bytes 294920 | tf_op jit(solution)/shard_map/ppermute | solution.py:706
  82.8 1.9 %last.1 = (f32[256,512]{1,0:T(8,128)}, f32[8,512]{1,0:T(8,128)S(1)}) custom-call(s32[8]{0:T(128)S(1)} %compare_select_fusion.pos.tb, f32[512,256]{1,0:T(8,128)S(1)} %get-tuple-element.248.own, bf16[512,512]{1,0:T(8,128)(2,1)S(1)} %collective-permute-done.29.recv.sib, bf16[512,256]{1,0:T(8,128)(2,1)S(1)} %collective-permute-done.34.par, ...), custom_call_target="tpu_custom_call" | custom-call | tf_op jit(solution)/shard_map/last/pallas_call | solution.py:45
  85.3 1.1 collective-permute-done.35.refs_1_
  86.6 1.3 %collective-permute-done.39.refs_7_ = f32[8,512]{1,0:T(8,128)S(1)} collective-permute-done((f32[8,512]{1,0:T(8,128)S(1)}, f32[8,512]{1,0:T(8,128)S(1)}, u32[]{:S(2)}, u32[]{:S(2)}) %collective-permute-start.39) | collective-permute-done | bytes 16416 | tf_op jit(solution)/shard_map/ppermute | solution.py:703
  89.1 2.8 %collective-permute-start.41 = (bf16[200,512]{1,0:T(8,128)(2,1)S(1)}, bf16[200,512]{1,0:T(8,128)(2,1)S(1)}, u32[]{:S(2)}, u32[]{:S(2)}) collective-permute-start(bf16[200,512]{1,0:T(8,128)(2,1)S(1)} %merge_a.1.own), channel_id=1, source_target_pairs={{0,16},{4,20},{8,24},{12,28},{16,0},{20,4},{24,8},{28,12},{1,17},{... | collective-permute-start | bytes 614408 | tf_op jit(solution)/shard_map/ppermute | solution.py:706
  92.5 2.0 %collective-permute-start.42 = (bf16[1,136,512]{2,1,0:T(8,128)(2,1)S(1)}, bf16[1,136,512]{2,1,0:T(8,128)(2,1)S(1)}, u32[]{:S(2)}, u32[]{:S(2)}) collective-permute-start(bf16[1,136,512]{2,1,0:T(8,128)(2,1)S(1)} %get-tuple-element.281.refs_0_), channel_id=1, source_target_pairs={{0,8},{4,12},{8,0},{12,4},{16,24},{20,28},{24,16},{28,20},{1,9},{5... | collective-permute-start | bytes 417800 | tf_op jit(solution)/shard_map/ppermute | solution.py:706
  94.5 0.8 collective-permute-start.45
  95.7 0.9 collective-permute-start.43
  96.6 3.7 %collective-permute-done.42.refs_1_ = bf16[1,136,512]{2,1,0:T(8,128)(2,1)S(1)} collective-permute-done((bf16[1,136,512]{2,1,0:T(8,128)(2,1)S(1)}, bf16[1,136,512]{2,1,0:T(8,128)(2,1)S(1)}, u32[]{:S(2)}, u32[]{:S(2)}) %collective-permute-start.42) | collective-permute-done | bytes 139296 | tf_op jit(solution)/shard_map/ppermute | solution.py:706
  100.3 2.9 %collective-permute-start.44 = (bf16[1,136,512]{2,1,0:T(8,128)(2,1)S(1)}, bf16[1,136,512]{2,1,0:T(8,128)(2,1)S(1)}, u32[]{:S(2)}, u32[]{:S(2)}) collective-permute-start(bf16[1,136,512]{2,1,0:T(8,128)(2,1)S(1)} %collective-permute-done.42.refs_1_), channel_id=1, source_target_pairs={{0,4},{4,0},{8,12},{12,8},{16,20},{20,16},{24,28},{28,24},{1,5},{5... | collective-permute-start | bytes 417800 | tf_op jit(solution)/shard_map/ppermute | solution.py:706
  103.2 0.7 collective-permute-start.47
  104.5 1.4 %collective-permute-start.48 = (bf16[1,104,512]{2,1,0:T(8,128)(2,1)S(1)}, bf16[1,104,512]{2,1,0:T(8,128)(2,1)S(1)}, u32[]{:S(2)}, u32[]{:S(2)}) collective-permute-start(bf16[1,104,512]{2,1,0:T(8,128)(2,1)S(1)} %get-tuple-element.283.refs_0_), channel_id=1, source_target_pairs={{0,8},{4,12},{8,0},{12,4},{16,24},{20,28},{24,16},{28,20},{1,9},{5... | collective-permute-start | bytes 319496 | tf_op jit(solution)/shard_map/ppermute | solution.py:706
  106.1 1.5 %collective-permute-start.52 = (bf16[1,96,512]{2,1,0:T(8,128)(2,1)S(1)}, bf16[1,96,512]{2,1,0:T(8,128)(2,1)S(1)}, u32[]{:S(2)}, u32[]{:S(2)}) collective-permute-start(bf16[1,96,512]{2,1,0:T(8,128)(2,1)S(1)} %get-tuple-element.288.refs_4_), channel_id=1, source_target_pairs={{0,8},{4,12},{8,0},{12,4},{16,24},{20,28},{24,16},{28,20},{1,9},{5... | collective-permute-start | bytes 294920 | tf_op jit(solution)/shard_map/ppermute | solution.py:706
  107.6 1.6 %collective-permute-done.47.refs_7_ = bf16[1,128,512]{2,1,0:T(8,128)(2,1)S(1)} collective-permute-done((bf16[1,128,512]{2,1,0:T(8,128)(2,1)S(1)}, bf16[1,128,512]{2,1,0:T(8,128)(2,1)S(1)}, u32[]{:S(2)}, u32[]{:S(2)}) %collective-permute-start.47) | collective-permute-done | bytes 131104 | tf_op jit(solution)/shard_map/ppermute | solution.py:706
  109.7 0.9 collective-permute-done.51.refs_5_
  111.2 1.0 collective-permute-start.50
  112.2 2.1 %unpack_f.1 = (f32[512,512]{1,0:T(8,128)}, f32[512,512]{1,0:T(8,128)}, f32[512]{0:T(512)}, f32[512]{0:T(512)}) custom-call(s32[8]{0:T(128)S(1)} %compare_select_fusion.pos.tb, bf16[1,136,512]{2,1,0:T(8,128)(2,1)S(1)} %get-tuple-element.281.refs_0_, bf16[1,136,512]{2,1,0:T(8,128)(2,1)S(1)} %collective-permute-done.42.refs_1_, ...), custom_call_target="tpu_custom_call" | custom-call | flops 20000000000 | tf_op jit(solution)/shard_map/unpack_f/pallas_call | solution.py:45
  114.3 0.9 collective-permute-done.53.refs_7_
  115.2 0.8 collective-permute-done.50.refs_3_
  115.9 2.0 %unpack_a.1 = (f32[512,128]{1,0:T(8,128)}, f32[512,128]{1,0:T(8,128)}, f32[512,128]{1,0:T(8,128)}, f32[128,512]{1,0:T(8,128)}, f32[128,512]{1,0:T(8,128)}, /*ind...) custom-call(s32[8]{0:T(128)S(1)} %compare_select_fusion.pos.tb, ...), custom_call_target="tpu_custom_call" | custom-call | flops 10000000000 | tf_op jit(solution)/shard_map/unpack_a/pallas_call | solution.py:45
  (85 shorter events, 11.9 us)
Async XLA Ops:
  0.7 8.3 %copy-start.2 = (bf16[256,512]{1,0:T(8,128)(2,1)S(1)}, bf16[256,512]{1,0:T(8,128)(2,1)}, u32[]{:S(2)}) copy-start(bf16[256,512]{1,0:T(8,128)(2,1)} %x0.5) | copy-start | bytes 786436
  0.7 10.1 %collective-permute-start.3 = (bf16[256,512]{1,0:T(8,128)(2,1)}, bf16[256,512]{1,0:T(8,128)(2,1)S(1)}, u32[]{:S(2)}, u32[]{:S(2)}) collective-permute-start(bf16[256,512]{1,0:T(8,128)(2,1)} %x0.5), channel_id=1, source_target_pairs={{0,2},{1,3},{2,0},{3,1},{4,6},{5,7},{6,4},{7,5},{8,10},{9,11},{10,... | collective-permute-start | bytes 786440 | tf_op jit(solution)/shard_map/ppermute | solution.py:703
  3.7 5.2 %collective-permute-start = (bf16[256,512]{1,0:T(8,128)(2,1)}, bf16[256,512]{1,0:T(8,128)(2,1)S(1)}, u32[]{:S(2)}, u32[]{:S(2)}) collective-permute-start(bf16[256,512]{1,0:T(8,128)(2,1)} %x0.5), channel_id=1, source_target_pairs={{0,1},{1,0},{2,3},{3,2},{4,5},{5,4},{6,7},{7,6},{8,9},{9,8},{10,11... | collective-permute-start | bytes 786440 | tf_op jit(solution)/shard_map/ppermute | solution.py:703
  4.4 9.1 %copy-start.5 = (s32[1,1024]{1,0:T(1,128)S(1)}, s32[1,1024]{1,0:T(1,128)}, u32[]{:S(2)}) copy-start(s32[1,1024]{1,0:T(1,128)} %segs.7) | copy-start | bytes 12292
  6.9 2.0 %collective-permute-start.2 = (bf16[264,384]{1,0:T(8,128)(2,1)S(1)}, bf16[264,384]{1,0:T(8,128)(2,1)S(1)}, u32[]{:S(2)}, u32[]{:S(2)}) collective-permute-start(bf16[264,384]{1,0:T(8,128)(2,1)S(1)} %get-tuple-element.168.qb0), channel_id=1, source_target_pairs={{0,1},{1,0},{2,3},{3,2},{4,5},{5,4},{6,7},{7,6},{8,9},{9,8},{10,11... | collective-permute-start | bytes 608264 | tf_op jit(solution)/shard_map/ppermute | solution.py:703
  7.5 1.4 %collective-permute-start.1 = (bf16[256,384]{1,0:T(8,128)(2,1)S(1)}, bf16[256,384]{1,0:T(8,128)(2,1)S(1)}, u32[]{:S(2)}, u32[]{:S(2)}) collective-permute-start(bf16[256,384]{1,0:T(8,128)(2,1)S(1)} %get-tuple-element.167.qa0), channel_id=1, source_target_pairs={{0,1},{1,0},{2,3},{3,2},{4,5},{5,4},{6,7},{7,6},{8,9},{9,8},{10,11... | collective-permute-start | bytes 589832 | tf_op jit(solution)/shard_map/ppermute | solution.py:703
  7.6 10.1 %collective-permute-start.9 = (bf16[296,512]{1,0:T(8,128)(2,1)S(1)}, bf16[296,512]{1,0:T(8,128)(2,1)S(1)}, u32[]{:S(2)}, u32[]{:S(2)}) collective-permute-start(bf16[296,512]{1,0:T(8,128)(2,1)S(1)} %get-tuple-element.164), channel_id=1, source_target_pairs={{0,2},{1,3},{2,0},{3,1},{4,6},{5,7},{6,4},{7,5},{8,10},{9,11},{10,... | collective-permute-start | bytes 909320 | tf_op jit(solution)/shard_map/ppermute | solution.py:703
  10.8 2.7 %collective-permute-start.4 = (bf16[256,512]{1,0:T(8,128)(2,1)S(1)}, bf16[256,512]{1,0:T(8,128)(2,1)S(1)}, u32[]{:S(2)}, u32[]{:S(2)}) collective-permute-start(bf16[256,512]{1,0:T(8,128)(2,1)S(1)} %collective-permute-done.3.x1), channel_id=1, source_target_pairs={{0,1},{1,0},{2,3},{3,2},{4,5},{5,4},{6,7},{7,6},{8,9},{9,8},{10,11... | collective-permute-start | bytes 786440 | tf_op jit(solution)/shard_map/ppermute | solution.py:703
  11.1 14.4 %collective-permute-start.7 = (bf16[1416,512]{1,0:T(8,128)(2,1)S(1)}, bf16[1416,512]{1,0:T(8,128)(2,1)S(1)}, u32[]{:S(2)}, u32[]{:S(2)}) collective-permute-start(bf16[1416,512]{1,0:T(8,128)(2,1)S(1)} %get-tuple-element.187), channel_id=1, source_target_pairs={{0,1},{1,0},{2,3},{3,2},{4,5},{5,4},{6,7},{7,6},{8,9},{9,8},{10,11... | collective-permute-start | bytes 4349960 | tf_op jit(solution)/shard_map/ppermute | solution.py:703
  11.3 11.8 %collective-permute-start.6 = (bf16[256,512]{1,0:T(8,128)(2,1)S(1)}, bf16[256,512]{1,0:T(8,128)(2,1)S(1)}, u32[]{:S(2)}, u32[]{:S(2)}) collective-permute-start(bf16[256,512]{1,0:T(8,128)(2,1)S(1)} %get-tuple-element.186.e0), channel_id=1, source_target_pairs={{0,2},{1,3},{2,0},{3,1},{4,6},{5,7},{6,4},{7,5},{8,10},{9,11},{10,... | collective-permute-start | bytes 786440 | tf_op jit(solution)/shard_map/ppermute | solution.py:703
  17.6 7.9 %collective-permute-start.5 = (bf16[256,256]{1,0:T(8,128)(2,1)S(1)}, bf16[256,256]{1,0:T(8,128)(2,1)S(1)}, u32[]{:S(2)}, u32[]{:S(2)}) collective-permute-start(bf16[256,256]{1,0:T(8,128)(2,1)S(1)} %get-tuple-element.184), channel_id=1, source_target_pairs={{0,2},{1,3},{2,0},{3,1},{4,6},{5,7},{6,4},{7,5},{8,10},{9,11},{10,... | collective-permute-start | bytes 393224 | tf_op jit(solution)/shard_map/ppermute | solution.py:703
  17.7 9.5 %collective-permute-start.11 = (bf16[296,512]{1,0:T(8,128)(2,1)S(1)}, bf16[296,512]{1,0:T(8,128)(2,1)S(1)}, u32[]{:S(2)}, u32[]{:S(2)}) collective-permute-start(bf16[296,512]{1,0:T(8,128)(2,1)S(1)} %collective-permute-done.9.s0), channel_id=1, source_target_pairs={{0,8},{4,12},{8,0},{12,4},{16,24},{20,28},{24,16},{28,20},{1,9},{5... | collective-permute-start | bytes 909320 | tf_op jit(solution)/shard_map/ppermute | solution.py:706
  19.1 9.1 %collective-permute-start.10 = (bf16[296,512]{1,0:T(8,128)(2,1)S(1)}, bf16[296,512]{1,0:T(8,128)(2,1)S(1)}, u32[]{:S(2)}, u32[]{:S(2)}) collective-permute-start(bf16[296,512]{1,0:T(8,128)(2,1)S(1)} %collective-permute-done.9.s0), channel_id=1, source_target_pairs={{0,4},{4,0},{8,12},{12,8},{16,20},{20,16},{24,28},{28,24},{1,5},{5... | collective-permute-start | bytes 909320 | tf_op jit(solution)/shard_map/ppermute | solution.py:706
  23.2 2.4 %collective-permute-start.8 = (bf16[256,512]{1,0:T(8,128)(2,1)S(1)}, bf16[256,512]{1,0:T(8,128)(2,1)S(1)}, u32[]{:S(2)}, u32[]{:S(2)}) collective-permute-start(bf16[256,512]{1,0:T(8,128)(2,1)S(1)} %collective-permute-done.6.e1), channel_id=1, source_target_pairs={{0,1},{1,0},{2,3},{3,2},{4,5},{5,4},{6,7},{7,6},{8,9},{9,8},{10,11... | collective-permute-start | bytes 786440 | tf_op jit(solution)/shard_map/ppermute | solution.py:703
  26.9 6.1 %copy-start = (bf16[512,512]{1,0:T(8,128)(2,1)S(1)}, bf16[512,512]{1,0:T(8,128)(2,1)}, u32[]{:S(2)}) copy-start(bf16[512,512]{1,0:T(8,128)(2,1)} %win0.5) | copy-start | bytes 1572868
  26.9 6.1 %copy-start.1 = (bf16[512,512]{1,0:T(8,128)(2,1)S(1)}, bf16[512,512]{1,0:T(8,128)(2,1)}, u32[]{:S(2)}) copy-start(bf16[512,512]{1,0:T(8,128)(2,1)} %wback0.5) | copy-start | bytes 1572868
  28.8 2.6 %collective-permute-start.12 = (bf16[296,512]{1,0:T(8,128)(2,1)S(1)}, bf16[296,512]{1,0:T(8,128)(2,1)S(1)}, u32[]{:S(2)}, u32[]{:S(2)}) collective-permute-start(bf16[296,512]{1,0:T(8,128)(2,1)S(1)} %collective-permute-done.9.s0), channel_id=1, source_target_pairs={{0,1},{1,0},{2,3},{3,2},{4,5},{5,4},{6,7},{7,6},{8,9},{9,8},{10,11... | collective-permute-start | bytes 909320 | tf_op jit(solution)/shard_map/ppermute | solution.py:703
  28.9 4.2 %collective-permute-start.13 = (bf16[296,512]{1,0:T(8,128)(2,1)S(1)}, bf16[296,512]{1,0:T(8,128)(2,1)S(1)}, u32[]{:S(2)}, u32[]{:S(2)}) collective-permute-start(bf16[296,512]{1,0:T(8,128)(2,1)S(1)} %collective-permute-done.10.sx.s2), channel_id=1, source_target_pairs={{0,1},{1,0},{2,3},{3,2},{4,5},{5,4},{6,7},{7,6},{8,9},{9,8},{10,11... | collective-permute-start | bytes 909320 | tf_op jit(solution)/shard_map/ppermute | solution.py:703
  29.4 3.7 %collective-permute-start.14 = (bf16[296,512]{1,0:T(8,128)(2,1)S(1)}, bf16[296,512]{1,0:T(8,128)(2,1)S(1)}, u32[]{:S(2)}, u32[]{:S(2)}) collective-permute-start(bf16[296,512]{1,0:T(8,128)(2,1)S(1)} %collective-permute-done.11.sz.s4), channel_id=1, source_target_pairs={{0,1},{1,0},{2,3},{3,2},{4,5},{5,4},{6,7},{7,6},{8,9},{9,8},{10,11... | collective-permute-start | bytes 909320 | tf_op jit(solution)/shard_map/ppermute | solution.py:703
  29.5 8.3 %copy-start.3 = (bf16[128,512]{1,0:T(8,128)(2,1)S(1)}, bf16[128,512]{1,0:T(8,128)(2,1)}, u32[]{:S(2)}) copy-start(bf16[128,512]{1,0:T(8,128)(2,1)} %g2.5) | copy-start | bytes 393220
  29.5 8.3 %copy-start.4 = (bf16[256,512]{1,0:T(8,128)(2,1)S(1)}, bf16[256,512]{1,0:T(8,128)(2,1)}, u32[]{:S(2)}) copy-start(bf16[256,512]{1,0:T(8,128)(2,1)} %ct.3) | copy-start | bytes 786436
  29.5 6.7 %collective-permute-start.16 = (bf16[168,512]{1,0:T(8,128)(2,1)S(1)}, bf16[168,512]{1,0:T(8,128)(2,1)S(1)}, u32[]{:S(2)}, u32[]{:S(2)}) collective-permute-start(bf16[168,512]{1,0:T(8,128)(2,1)S(1)} %get-tuple-element.200), channel_id=1, source_target_pairs={{0,8},{4,12},{8,0},{12,4},{16,24},{20,28},{24,16},{28,20},{1,9},{5... | collective-permute-start | bytes 516104 | tf_op jit(solution)/shard_map/ppermute | solution.py:706
  30.2 5.6 %collective-permute-start.15 = (bf16[128,512]{1,0:T(8,128)(2,1)S(1)}, bf16[128,512]{1,0:T(8,128)(2,1)S(1)}, u32[]{:S(2)}, u32[]{:S(2)}) collective-permute-start(bf16[128,512]{1,0:T(8,128)(2,1)S(1)} %get-tuple-element.192), channel_id=1, source_target_pairs={{0,4},{4,0},{8,12},{12,8},{16,20},{20,16},{24,28},{28,24},{1,5},{5... | collective-permute-start | bytes 393224 | tf_op jit(solution)/shard_map/ppermute | solution.py:706
  31.4 8.5 %collective-permute-start.19 = (bf16[256,512]{1,0:T(8,128)(2,1)S(1)}, bf16[256,512]{1,0:T(8,128)(2,1)S(1)}, u32[]{:S(2)}, u32[]{:S(2)}) collective-permute-start(bf16[256,512]{1,0:T(8,128)(2,1)S(1)} %get-tuple-element.204.n2), channel_id=1, source_target_pairs={{0,2},{1,3},{2,0},{3,1},{4,6},{5,7},{6,4},{7,5},{8,10},{9,11},{10,... | collective-permute-start | bytes 786440 | tf_op jit(solution)/shard_map/ppermute | solution.py:703
  36.2 1.6 %collective-permute-start.18 = (bf16[168,512]{1,0:T(8,128)(2,1)S(1)}, bf16[168,512]{1,0:T(8,128)(2,1)S(1)}, u32[]{:S(2)}, u32[]{:S(2)}) collective-permute-start(bf16[168,512]{1,0:T(8,128)(2,1)S(1)} %collective-permute-done.16.b6), channel_id=1, source_target_pairs={{0,1},{1,0},{2,3},{3,2},{4,5},{5,4},{6,7},{7,6},{8,9},{9,8},{10,11... | collective-permute-start | bytes 516104 | tf_op jit(solution)/shard_map/ppermute | solution.py:703
  36.2 1.6 %collective-permute-start.17 = (bf16[128,512]{1,0:T(8,128)(2,1)S(1)}, bf16[128,512]{1,0:T(8,128)(2,1)S(1)}, u32[]{:S(2)}, u32[]{:S(2)}) collective-permute-start(bf16[128,512]{1,0:T(8,128)(2,1)S(1)} %collective-permute-done.15.a6), channel_id=1, source_target_pairs={{0,1},{1,0},{2,3},{3,2},{4,5},{5,4},{6,7},{7,6},{8,9},{9,8},{10,11... | collective-permute-start | bytes 393224 | tf_op jit(solution)/shard_map/ppermute | solution.py:703
  39.9 8.7 %collective-permute-start.20 = (bf16[256,512]{1,0:T(8,128)(2,1)S(1)}, bf16[256,512]{1,0:T(8,128)(2,1)S(1)}, u32[]{:S(2)}, u32[]{:S(2)}) collective-permute-start(bf16[256,512]{1,0:T(8,128)(2,1)S(1)} %get-tuple-element.206.fg), channel_id=1, source_target_pairs={{0,2},{1,3},{2,0},{3,1},{4,6},{5,7},{6,4},{7,5},{8,10},{9,11},{10,... | collective-permute-start | bytes 786440 | tf_op jit(solution)/shard_map/ppermute | solution.py:703
  46.4 2.4 %collective-permute-start.21 = (bf16[776,512]{1,0:T(8,128)(2,1)S(1)}, bf16[776,512]{1,0:T(8,128)(2,1)S(1)}, u32[]{:S(2)}, u32[]{:S(2)}) collective-permute-start(bf16[776,512]{1,0:T(8,128)(2,1)S(1)} %get-tuple-element.226), channel_id=1, source_target_pairs={{0,1},{1,0},{2,3},{3,2},{4,5},{5,4},{6,7},{7,6},{8,9},{9,8},{10,11... | collective-permute-start | bytes 2383880 | tf_op jit(solution)/shard_map/ppermute | solution.py:703
  53.0 3.8 %collective-permute-start.23 = (bf16[520,512]{1,0:T(8,128)(2,1)S(1)}, bf16[520,512]{1,0:T(8,128)(2,1)S(1)}, u32[]{:S(2)}, u32[]{:S(2)}) collective-permute-start(bf16[520,512]{1,0:T(8,128)(2,1)S(1)} %get-tuple-element.234), channel_id=1, source_target_pairs={{0,1},{1,0},{2,3},{3,2},{4,5},{5,4},{6,7},{7,6},{8,9},{9,8},{10,11... | collective-permute-start | bytes 1597448 | tf_op jit(solution)/shard_map/ppermute | solution.py:703
  54.4 2.4 %collective-permute-start.22 = (bf16[512,512]{1,0:T(8,128)(2,1)S(1)}, bf16[512,512]{1,0:T(8,128)(2,1)S(1)}, u32[]{:S(2)}, u32[]{:S(2)}) collective-permute-start(bf16[512,512]{1,0:T(8,128)(2,1)S(1)} %get-tuple-element.233), channel_id=1, source_target_pairs={{0,1},{1,0},{2,3},{3,2},{4,5},{5,4},{6,7},{7,6},{8,9},{9,8},{10,11... | collective-permute-start | bytes 1572872 | tf_op jit(solution)/shard_map/ppermute | solution.py:703
  54.4 6.7 %collective-permute-start.24 = (bf16[256,256]{1,0:T(8,128)(2,1)S(1)}, bf16[256,256]{1,0:T(8,128)(2,1)S(1)}, u32[]{:S(2)}, u32[]{:S(2)}) collective-permute-start(bf16[256,256]{1,0:T(8,128)(2,1)S(1)} %get-tuple-element.238), channel_id=1, source_target_pairs={{0,2},{1,3},{2,0},{3,1},{4,6},{5,7},{6,4},{7,5},{8,10},{9,11},{10,... | collective-permute-start | bytes 393224 | tf_op jit(solution)/shard_map/ppermute | solution.py:703
  56.8 14.4 %collective-permute-start.28 = (bf16[392,512]{1,0:T(8,128)(2,1)S(1)}, bf16[392,512]{1,0:T(8,128)(2,1)S(1)}, u32[]{:S(2)}, u32[]{:S(2)}) collective-permute-start(bf16[392,512]{1,0:T(8,128)(2,1)S(1)} %get-tuple-element.257), channel_id=1, source_target_pairs={{0,2},{1,3},{2,0},{3,1},{4,6},{5,7},{6,4},{7,5},{8,10},{9,11},{10,... | collective-permute-start | bytes 1204232 | tf_op jit(solution)/shard_map/ppermute | solution.py:703
  57.8 10.2 %collective-permute-start.25 = (bf16[256,512]{1,0:T(8,128)(2,1)S(1)}, bf16[256,512]{1,0:T(8,128)(2,1)S(1)}, u32[]{:S(2)}, u32[]{:S(2)}) collective-permute-start(bf16[256,512]{1,0:T(8,128)(2,1)S(1)} %get-tuple-element.250), channel_id=1, source_target_pairs={{0,4},{4,0},{8,12},{12,8},{16,20},{20,16},{24,28},{28,24},{1,5},{5... | collective-permute-start | bytes 786440 | tf_op jit(solution)/shard_map/ppermute | solution.py:706
  59.4 8.6 %collective-permute-start.26 = (bf16[256,512]{1,0:T(8,128)(2,1)S(1)}, bf16[256,512]{1,0:T(8,128)(2,1)S(1)}, u32[]{:S(2)}, u32[]{:S(2)}) collective-permute-start(bf16[256,512]{1,0:T(8,128)(2,1)S(1)} %get-tuple-element.252), channel_id=1, source_target_pairs={{0,8},{4,12},{8,0},{12,4},{16,24},{20,28},{24,16},{28,20},{1,9},{5... | collective-permute-start | bytes 786440 | tf_op jit(solution)/shard_map/ppermute | solution.py:706
  67.3 3.9 %collective-permute-start.27 = (bf16[392,512]{1,0:T(8,128)(2,1)S(1)}, bf16[392,512]{1,0:T(8,128)(2,1)S(1)}, u32[]{:S(2)}, u32[]{:S(2)}) collective-permute-start(bf16[392,512]{1,0:T(8,128)(2,1)S(1)} %get-tuple-element.256), channel_id=1, source_target_pairs={{0,1},{1,0},{2,3},{3,2},{4,5},{5,4},{6,7},{7,6},{8,9},{9,8},{10,11... | collective-permute-start | bytes 1204232 | tf_op jit(solution)/shard_map/ppermute | solution.py:703
  67.9 6.0 %collective-permute-start.29 = (bf16[512,512]{1,0:T(8,128)(2,1)S(1)}, bf16[512,512]{1,0:T(8,128)(2,1)S(1)}, u32[]{:S(2)}, u32[]{:S(2)}) collective-permute-start(bf16[512,512]{1,0:T(8,128)(2,1)S(1)} %get-tuple-element.261), channel_id=1, source_target_pairs={{0,1},{1,0},{2,3},{3,2},{4,5},{5,4},{6,7},{7,6},{8,9},{9,8},{10,11... | collective-permute-start | bytes 1572872 | tf_op jit(solution)/shard_map/ppermute | solution.py:703
  68.7 7.7 %collective-permute-start.30 = (bf16[128,512]{1,0:T(8,128)(2,1)S(1)}, bf16[128,512]{1,0:T(8,128)(2,1)S(1)}, u32[]{:S(2)}, u32[]{:S(2)}) collective-permute-start(bf16[128,512]{1,0:T(8,128)(2,1)S(1)} %get-tuple-element.263), channel_id=1, source_target_pairs={{0,8},{4,12},{8,0},{12,4},{16,24},{20,28},{24,16},{28,20},{1,9},{5... | collective-permute-start | bytes 393224 | tf_op jit(solution)/shard_map/ppermute | solution.py:706
  70.1 6.4 %collective-permute-start.31 = (bf16[128,512]{1,0:T(8,128)(2,1)S(1)}, bf16[128,512]{1,0:T(8,128)(2,1)S(1)}, u32[]{:S(2)}, u32[]{:S(2)}) collective-permute-start(bf16[128,512]{1,0:T(8,128)(2,1)S(1)} %get-tuple-element.265), channel_id=1, source_target_pairs={{0,4},{4,0},{8,12},{12,8},{16,20},{20,16},{24,28},{28,24},{1,5},{5... | collective-permute-start | bytes 393224 | tf_op jit(solution)/shard_map/ppermute | solution.py:706
  72.1 7.7 %collective-permute-start.32 = (bf16[192,512]{1,0:T(8,128)(2,1)S(1)}, bf16[192,512]{1,0:T(8,128)(2,1)S(1)}, u32[]{:S(2)}, u32[]{:S(2)}) collective-permute-start(bf16[192,512]{1,0:T(8,128)(2,1)S(1)} %get-tuple-element.267), channel_id=1, source_target_pairs={{0,4},{4,0},{8,12},{12,8},{16,20},{20,16},{24,28},{28,24},{1,5},{5... | collective-permute-start | bytes 589832 | tf_op jit(solution)/shard_map/ppermute | solution.py:706
  73.1 7.7 %collective-permute-start.33 = (bf16[192,512]{1,0:T(8,128)(2,1)S(1)}, bf16[192,512]{1,0:T(8,128)(2,1)S(1)}, u32[]{:S(2)}, u32[]{:S(2)}) collective-permute-start(bf16[192,512]{1,0:T(8,128)(2,1)S(1)} %get-tuple-element.269), channel_id=1, source_target_pairs={{0,8},{4,12},{8,0},{12,4},{16,24},{20,28},{24,16},{28,20},{1,9},{5... | collective-permute-start | bytes 589832 | tf_op jit(solution)/shard_map/ppermute | solution.py:706
  74.5 8.4 %collective-permute-start.34 = (bf16[512,256]{1,0:T(8,128)(2,1)S(1)}, bf16[512,256]{1,0:T(8,128)(2,1)S(1)}, u32[]{:S(2)}, u32[]{:S(2)}) collective-permute-start(bf16[512,256]{1,0:T(8,128)(2,1)S(1)} %half_columns.1), channel_id=1, source_target_pairs={{0,2},{1,3},{2,0},{3,1},{4,6},{5,7},{6,4},{7,5},{8,10},{9,11},{10,... | collective-permute-start | bytes 786440 | tf_op jit(solution)/shard_map/ppermute | solution.py:703
  77.0 14.8 %collective-permute-start.40 = (bf16[264,512]{1,0:T(8,128)(2,1)S(1)}, bf16[264,512]{1,0:T(8,128)(2,1)S(1)}, u32[]{:S(2)}, u32[]{:S(2)}) collective-permute-start(bf16[264,512]{1,0:T(8,128)(2,1)S(1)} %merge_f.1.own), channel_id=1, source_target_pairs={{0,16},{4,20},{8,24},{12,28},{16,0},{20,4},{24,8},{28,12},{1,17},{... | collective-permute-start | bytes 811016 | tf_op jit(solution)/shard_map/ppermute | solution.py:706
  81.5 4.9 %collective-permute-start.35 = (bf16[96,512]{1,0:T(8,128)(2,1)S(1)}, bf16[96,512]{1,0:T(8,128)(2,1)S(1)}, u32[]{:S(2)}, u32[]{:S(2)}) collective-permute-start(bf16[96,512]{1,0:T(8,128)(2,1)S(1)} %get-tuple-element.276), channel_id=1, source_target_pairs={{0,8},{4,12},{8,0},{12,4},{16,24},{20,28},{24,16},{28,20},{1,9},{5... | collective-permute-start | bytes 294920 | tf_op jit(solution)/shard_map/ppermute | solution.py:706
  81.6 5.0 %collective-permute-start.36 = (bf16[96,512]{1,0:T(8,128)(2,1)S(1)}, bf16[96,512]{1,0:T(8,128)(2,1)S(1)}, u32[]{:S(2)}, u32[]{:S(2)}) collective-permute-start(bf16[96,512]{1,0:T(8,128)(2,1)S(1)} %get-tuple-element.278), channel_id=1, source_target_pairs={{0,4},{4,0},{8,12},{12,8},{16,20},{20,16},{24,28},{28,24},{1,5},{5... | collective-permute-start | bytes 294920 | tf_op jit(solution)/shard_map/ppermute | solution.py:706
  84.7 3.2 %collective-permute-start.39 = (f32[8,512]{1,0:T(8,128)S(1)}, f32[8,512]{1,0:T(8,128)S(1)}, u32[]{:S(2)}, u32[]{:S(2)}) collective-permute-start(f32[8,512]{1,0:T(8,128)S(1)} %get-tuple-element.279.refs_4_), channel_id=1, source_target_pairs={{0,3},{1,2},{2,1},{3,0},{4,7},{5,6},{6,5},{7,4},{8,11},{9,10},{10,... | collective-permute-start | bytes 49160 | tf_op jit(solution)/shard_map/ppermute | solution.py:703
  84.7 3.8 %collective-permute-start.38 = (f32[8,512]{1,0:T(8,128)S(1)}, f32[8,512]{1,0:T(8,128)S(1)}, u32[]{:S(2)}, u32[]{:S(2)}) collective-permute-start(f32[8,512]{1,0:T(8,128)S(1)} %get-tuple-element.279.refs_4_), channel_id=1, source_target_pairs={{0,2},{1,3},{2,0},{3,1},{4,6},{5,7},{6,4},{7,5},{8,10},{9,11},{10,... | collective-permute-start | bytes 49160 | tf_op jit(solution)/shard_map/ppermute | solution.py:703
  86.4 2.1 %collective-permute-start.37 = (f32[8,512]{1,0:T(8,128)S(1)}, f32[8,512]{1,0:T(8,128)S(1)}, u32[]{:S(2)}, u32[]{:S(2)}) collective-permute-start(f32[8,512]{1,0:T(8,128)S(1)} %get-tuple-element.279.refs_4_), channel_id=1, source_target_pairs={{0,1},{1,0},{2,3},{3,2},{4,5},{5,4},{6,7},{7,6},{8,9},{9,8},{10,11... | collective-permute-start | bytes 49160 | tf_op jit(solution)/shard_map/ppermute | solution.py:703
  89.1 14.8 %collective-permute-start.41 = (bf16[200,512]{1,0:T(8,128)(2,1)S(1)}, bf16[200,512]{1,0:T(8,128)(2,1)S(1)}, u32[]{:S(2)}, u32[]{:S(2)}) collective-permute-start(bf16[200,512]{1,0:T(8,128)(2,1)S(1)} %merge_a.1.own), channel_id=1, source_target_pairs={{0,16},{4,20},{8,24},{12,28},{16,0},{20,4},{24,8},{28,12},{1,17},{... | collective-permute-start | bytes 614408 | tf_op jit(solution)/shard_map/ppermute | solution.py:706
  92.5 7.9 %collective-permute-start.42 = (bf16[1,136,512]{2,1,0:T(8,128)(2,1)S(1)}, bf16[1,136,512]{2,1,0:T(8,128)(2,1)S(1)}, u32[]{:S(2)}, u32[]{:S(2)}) collective-permute-start(bf16[1,136,512]{2,1,0:T(8,128)(2,1)S(1)} %get-tuple-element.281.refs_0_), channel_id=1, source_target_pairs={{0,8},{4,12},{8,0},{12,4},{16,24},{20,28},{24,16},{28,20},{1,9},{5... | collective-permute-start | bytes 417800 | tf_op jit(solution)/shard_map/ppermute | solution.py:706
  94.5 8.7 %collective-permute-start.45 = (bf16[1,128,512]{2,1,0:T(8,128)(2,1)S(1)}, bf16[1,128,512]{2,1,0:T(8,128)(2,1)S(1)}, u32[]{:S(2)}, u32[]{:S(2)}) collective-permute-start(bf16[1,128,512]{2,1,0:T(8,128)(2,1)S(1)} %get-tuple-element.285.refs_4_), channel_id=1, source_target_pairs={{0,4},{4,0},{8,12},{12,8},{16,20},{20,16},{24,28},{28,24},{1,5},{5... | collective-permute-start | bytes 393224 | tf_op jit(solution)/shard_map/ppermute | solution.py:706
  95.3 10.6 %collective-permute-start.46 = (bf16[1,128,512]{2,1,0:T(8,128)(2,1)S(1)}, bf16[1,128,512]{2,1,0:T(8,128)(2,1)S(1)}, u32[]{:S(2)}, u32[]{:S(2)}) collective-permute-start(bf16[1,128,512]{2,1,0:T(8,128)(2,1)S(1)} %get-tuple-element.285.refs_4_), channel_id=1, source_target_pairs={{0,8},{4,12},{8,0},{12,4},{16,24},{20,28},{24,16},{28,20},{1,9},{5... | collective-permute-start | bytes 393224 | tf_op jit(solution)/shard_map/ppermute | solution.py:706
  95.7 10.4 %collective-permute-start.43 = (bf16[1,136,512]{2,1,0:T(8,128)(2,1)S(1)}, bf16[1,136,512]{2,1,0:T(8,128)(2,1)S(1)}, u32[]{:S(2)}, u32[]{:S(2)}) collective-permute-start(bf16[1,136,512]{2,1,0:T(8,128)(2,1)S(1)} %get-tuple-element.281.refs_0_), channel_id=1, source_target_pairs={{0,4},{4,0},{8,12},{12,8},{16,20},{20,16},{24,28},{28,24},{1,5},{5... | collective-permute-start | bytes 417800 | tf_op jit(solution)/shard_map/ppermute | solution.py:706
  100.3 11.9 %collective-permute-start.44 = (bf16[1,136,512]{2,1,0:T(8,128)(2,1)S(1)}, bf16[1,136,512]{2,1,0:T(8,128)(2,1)S(1)}, u32[]{:S(2)}, u32[]{:S(2)}) collective-permute-start(bf16[1,136,512]{2,1,0:T(8,128)(2,1)S(1)} %collective-permute-done.42.refs_1_), channel_id=1, source_target_pairs={{0,4},{4,0},{8,12},{12,8},{16,20},{20,16},{24,28},{28,24},{1,5},{5... | collective-permute-start | bytes 417800 | tf_op jit(solution)/shard_map/ppermute | solution.py:706
  103.2 5.9 %collective-permute-start.47 = (bf16[1,128,512]{2,1,0:T(8,128)(2,1)S(1)}, bf16[1,128,512]{2,1,0:T(8,128)(2,1)S(1)}, u32[]{:S(2)}, u32[]{:S(2)}) collective-permute-start(bf16[1,128,512]{2,1,0:T(8,128)(2,1)S(1)} %collective-permute-done.45.refs_5_), channel_id=1, source_target_pairs={{0,8},{4,12},{8,0},{12,4},{16,24},{20,28},{24,16},{28,20},{1,9},{5... | collective-permute-start | bytes 393224 | tf_op jit(solution)/shard_map/ppermute | solution.py:706
  104.5 6.7 %collective-permute-start.48 = (bf16[1,104,512]{2,1,0:T(8,128)(2,1)S(1)}, bf16[1,104,512]{2,1,0:T(8,128)(2,1)S(1)}, u32[]{:S(2)}, u32[]{:S(2)}) collective-permute-start(bf16[1,104,512]{2,1,0:T(8,128)(2,1)S(1)} %get-tuple-element.283.refs_0_), channel_id=1, source_target_pairs={{0,8},{4,12},{8,0},{12,4},{16,24},{20,28},{24,16},{28,20},{1,9},{5... | collective-permute-start | bytes 319496 | tf_op jit(solution)/shard_map/ppermute | solution.py:706
  105.9 4.6 %collective-permute-start.51 = (bf16[1,96,512]{2,1,0:T(8,128)(2,1)S(1)}, bf16[1,96,512]{2,1,0:T(8,128)(2,1)S(1)}, u32[]{:S(2)}, u32[]{:S(2)}) collective-permute-start(bf16[1,96,512]{2,1,0:T(8,128)(2,1)S(1)} %get-tuple-element.288.refs_4_), channel_id=1, source_target_pairs={{0,4},{4,0},{8,12},{12,8},{16,20},{20,16},{24,28},{28,24},{1,5},{5... | collective-permute-start | bytes 294920 | tf_op jit(solution)/shard_map/ppermute | solution.py:706
  106.1 8.3 %collective-permute-start.52 = (bf16[1,96,512]{2,1,0:T(8,128)(2,1)S(1)}, bf16[1,96,512]{2,1,0:T(8,128)(2,1)S(1)}, u32[]{:S(2)}, u32[]{:S(2)}) collective-permute-start(bf16[1,96,512]{2,1,0:T(8,128)(2,1)S(1)} %get-tuple-element.288.refs_4_), channel_id=1, source_target_pairs={{0,8},{4,12},{8,0},{12,4},{16,24},{20,28},{24,16},{28,20},{1,9},{5... | collective-permute-start | bytes 294920 | tf_op jit(solution)/shard_map/ppermute | solution.py:706
  109.1 5.2 %collective-permute-start.49 = (bf16[1,104,512]{2,1,0:T(8,128)(2,1)S(1)}, bf16[1,104,512]{2,1,0:T(8,128)(2,1)S(1)}, u32[]{:S(2)}, u32[]{:S(2)}) collective-permute-start(bf16[1,104,512]{2,1,0:T(8,128)(2,1)S(1)} %get-tuple-element.283.refs_0_), channel_id=1, source_target_pairs={{0,4},{4,0},{8,12},{12,8},{16,20},{20,16},{24,28},{28,24},{1,5},{5... | collective-permute-start | bytes 319496 | tf_op jit(solution)/shard_map/ppermute | solution.py:706
  110.6 4.6 %collective-permute-start.53 = (bf16[1,96,512]{2,1,0:T(8,128)(2,1)S(1)}, bf16[1,96,512]{2,1,0:T(8,128)(2,1)S(1)}, u32[]{:S(2)}, u32[]{:S(2)}) collective-permute-start(bf16[1,96,512]{2,1,0:T(8,128)(2,1)S(1)} %collective-permute-done.51.refs_5_), channel_id=1, source_target_pairs={{0,8},{4,12},{8,0},{12,4},{16,24},{20,28},{24,16},{28,20},{1,9},{5... | collective-permute-start | bytes 294920 | tf_op jit(solution)/shard_map/ppermute | solution.py:706
  111.2 4.7 %collective-permute-start.50 = (bf16[1,104,512]{2,1,0:T(8,128)(2,1)S(1)}, bf16[1,104,512]{2,1,0:T(8,128)(2,1)S(1)}, u32[]{:S(2)}, u32[]{:S(2)}) collective-permute-start(bf16[1,104,512]{2,1,0:T(8,128)(2,1)S(1)} %collective-permute-done.48.refs_1_), channel_id=1, source_target_pairs={{0,4},{4,0},{8,12},{12,8},{16,20},{20,16},{24,28},{28,24},{1,5},{5... | collective-permute-start | bytes 319496 | tf_op jit(solution)/shard_map/ppermute | solution.py:706
